TPU v7x, 32 devices: a whole 2x2x4 slice. The times are simulated.
32 devices in a mesh: dp: 8 (over z, y), section: 4 (over x, core).
Axes of the slice: x: 2, y: 2, z: 4, core: 2. Of those that a mesh axis runs over, the one named last changes fastest.
Arguments:
- tokens: bfloat16 [2, 8, 1024, 768], P(None, 'dp'), may hold values from -6 to 6
- lengths: int32 [2, 8], P(None, 'dp'), may hold values from 300 to 1024, as said below
- cotangent: bfloat16 [2, 8, 1024, 768], P(None, 'dp'), may hold values from -6 to 6
- attn_gain: bfloat16 [2, 768], P(None, 'dp'), may hold values from 0.5 to 1.5
- attn_shift: bfloat16 [2, 768], P(None, 'dp'), may hold values from -1.796875 to 1.796875
- qkv_weight: bfloat16 [2, 768, 2304], P(None, 'dp'), may hold values from -0.21875 to 0.21875
- qv_bias: bfloat16 [2, 1536], P(None, 'dp'), may hold values from -3 to 3
- out_weight: bfloat16 [2, 768, 768], P(None, 'dp'), may hold values from -3.5 to 3.5
- out_bias: bfloat16 [2, 768], P(None, 'dp'), may hold values from -1.796875 to 1.796875
- ffn_gain: bfloat16 [2, 768], P(None, 'dp'), may hold values from 0.5 to 1.5
- ffn_shift: bfloat16 [2, 768], P(None, 'dp'), may hold values from -1.796875 to 1.796875
- up_weight: bfloat16 [2, 768, 3072], P(None, 'dp'), may hold values from -0.21875 to 0.21875
- up_bias: bfloat16 [2, 3072], P(None, 'dp'), may hold values from -3 to 3
- down_weight: bfloat16 [2, 3072, 768], P(None, 'dp'), may hold values from -0.109375 to 0.109375
- down_bias: bfloat16 [2, 768], P(None, 'dp'), may hold values from -1.796875 to 1.796875
Outputs:
- encoded: bfloat16 [2, 8, 1024, 768], P(None, 'dp', 'section')
- grad_tokens: bfloat16 [2, 8, 1024, 768], P(None, 'dp', 'section')
- grad_attn_gain: float32 [2, 768], P(None, 'dp')
- grad_attn_shift: float32 [2, 768], P(None, 'dp')
- grad_qkv_weight: float32 [2, 768, 2304], P(None, 'dp')
- grad_qv_bias: float32 [2, 1536], P(None, 'dp')
- grad_out_weight: float32 [2, 768, 768], P(None, 'dp')
- grad_out_bias: float32 [2, 768], P(None, 'dp')
- grad_ffn_gain: float32 [2, 768], P(None, 'dp')
- grad_ffn_shift: float32 [2, 768], P(None, 'dp')
- grad_up_weight: float32 [2, 768, 3072], P(None, 'dp')
- grad_up_bias: float32 [2, 3072], P(None, 'dp')
- grad_down_weight: float32 [2, 3072, 768], P(None, 'dp')
- grad_down_bias: float32 [2, 768], P(None, 'dp')
Inputs may be any that keep to these rules, and one draw needn't show every extreme that they name: lengths[m, c] counts the expressed genes of cell c in micro-batch m; in every micro-batch some cell has exactly 1024.
All inputs are finite; a program needn't handle non-finite values.
Results may differ from a plain program's by a relative error of at most 0.013.
Values may be sent and summed in bfloat16 or wider, within the bound.
No kernel may reach another device: no remote copies, remote signals or barrier semaphores. Data moves between devices by JAX's collectives and lax.ppermute only.
A program may use at most 576 MiB of HBM per device.

v0:
```python
from functools import partial
import math

import jax
import jax.numpy as jnp
from jax import lax
from jax.sharding import PartitionSpec as P

HEADS = 12
HEAD = 64
QB = 512


NORM_EPS = 1e-05
MASK_FLOOR = -1e30


def shifted(block, axis, distance):
    devices = range(lax.axis_size(axis))
    route = [(i - distance, i) for i in devices if i - distance in devices]
    return lax.ppermute(block, axis, route)


def norm_rows(stream, norm_gain, norm_shift):
    center = stream - jnp.mean(stream, axis=-1, keepdims=True)
    spread = jnp.mean(center * center, axis=-1, keepdims=True)
    return center * lax.rsqrt(spread + NORM_EPS) * norm_gain + norm_shift


def block_scores(query_part, key_heads, key_valid):
    score_scale = 1.0 / math.sqrt(HEAD)
    scores = (
        jnp.einsum("cqhd,ckhd->chqk", query_part, key_heads, preferred_element_type=jnp.float32)
        * score_scale
    )
    return jnp.where(key_valid[:, None, None, :], scores, MASK_FLOOR)


def attend(queries, keys_all, values_all, key_valid):
    cell_count, seq_len = key_valid.shape
    block_count = seq_len // QB
    query_blocks = queries.reshape(cell_count, block_count, QB, HEADS, HEAD)
    key_heads = keys_all.reshape(cell_count, seq_len, HEADS, HEAD)
    value_heads = values_all.reshape(cell_count, seq_len, HEADS, HEAD)

    def one_block(block_id):
        query_part = lax.dynamic_index_in_dim(query_blocks, block_id, 1, keepdims=False)
        scores = block_scores(query_part, key_heads, key_valid)
        row_max = jnp.max(scores, axis=-1, keepdims=True)
        log_total = row_max + jnp.log(jnp.sum(jnp.exp(scores - row_max), axis=-1, keepdims=True))
        probs_low = jnp.exp(scores - log_total).astype(jnp.bfloat16)
        block_out = jnp.einsum(
            "chqk,ckhd->cqhd", probs_low, value_heads, preferred_element_type=jnp.float32
        )
        return (block_out, log_total)

    block_outs, log_totals = lax.map(one_block, jnp.arange(block_count))
    mixed_out = jnp.moveaxis(block_outs, 0, 1).reshape(cell_count * seq_len, HEADS * HEAD)
    return (mixed_out, log_totals)


def attend_back(queries, keys_all, values_all, key_valid, log_totals, grad_mixed):
    cell_count, seq_len = key_valid.shape
    block_count = seq_len // QB
    score_scale = 1.0 / math.sqrt(HEAD)
    query_blocks = queries.reshape(cell_count, block_count, QB, HEADS, HEAD)
    grad_blocks = grad_mixed.reshape(cell_count, block_count, QB, HEADS, HEAD)
    key_heads = keys_all.reshape(cell_count, seq_len, HEADS, HEAD)
    value_heads = values_all.reshape(cell_count, seq_len, HEADS, HEAD)

    def one_block(carry, block_id):
        grad_keys, grad_values = carry
        query_part = lax.dynamic_index_in_dim(query_blocks, block_id, 1, keepdims=False)
        grad_part = lax.dynamic_index_in_dim(grad_blocks, block_id, 1, keepdims=False)
        log_total = lax.dynamic_index_in_dim(log_totals, block_id, 0, keepdims=False)
        scores = block_scores(query_part, key_heads, key_valid)
        probs_full = jnp.exp(scores - log_total)
        grad_probs = jnp.einsum(
            "cqhd,ckhd->chqk", grad_part, value_heads, preferred_element_type=jnp.float32
        )
        inner = jnp.sum(probs_full * grad_probs, axis=-1, keepdims=True)
        grad_scores = (probs_full * (grad_probs - inner)).astype(jnp.bfloat16)
        grad_query = (
            jnp.einsum(
                "chqk,ckhd->cqhd", grad_scores, key_heads, preferred_element_type=jnp.float32
            )
            * score_scale
        )
        grad_keys = (
            grad_keys
            + jnp.einsum(
                "chqk,cqhd->ckhd", grad_scores, query_part, preferred_element_type=jnp.float32
            )
            * score_scale
        )
        grad_values = grad_values + jnp.einsum(
            "chqk,cqhd->ckhd",
            probs_full.astype(jnp.bfloat16),
            grad_part,
            preferred_element_type=jnp.float32,
        )
        return ((grad_keys, grad_values), grad_query)

    start_fill = jnp.zeros((cell_count, seq_len, HEADS, HEAD), jnp.float32)
    (grad_keys, grad_values), grad_queries = lax.scan(
        one_block, (start_fill, start_fill), jnp.arange(block_count)
    )
    row_count = cell_count * seq_len
    grad_queries = jnp.moveaxis(grad_queries, 0, 1).reshape(row_count, HEADS * HEAD)
    return (
        grad_queries,
        grad_keys.reshape(row_count, HEADS * HEAD),
        grad_values.reshape(row_count, HEADS * HEAD),
    )


def attention_block(stream_in, key_valid, weights, grad_out):
    norm_gain, norm_shift, qkv_weight, qv_bias, out_weight, out_bias = weights
    cell_count, seq_len, model_width = stream_in.shape
    row_count = cell_count * seq_len
    stream = stream_in.reshape(row_count, model_width).astype(jnp.float32)
    normed, norm_pull = jax.vjp(
        norm_rows, stream, norm_gain.astype(jnp.float32), norm_shift.astype(jnp.float32)
    )
    normed_low = normed.astype(jnp.bfloat16)
    projected = jnp.dot(normed_low, qkv_weight, preferred_element_type=jnp.float32)
    biases = qv_bias.astype(jnp.float32)
    queries = (projected[:, :model_width] + biases[:model_width]).astype(jnp.bfloat16)
    keys_all = projected[:, model_width : 2 * model_width].astype(jnp.bfloat16)
    values_all = (projected[:, 2 * model_width :] + biases[model_width:]).astype(jnp.bfloat16)
    mixed_out, log_totals = attend(queries, keys_all, values_all, key_valid)
    mixed_low = mixed_out.astype(jnp.bfloat16)
    if grad_out is None:
        branch_out = jnp.dot(
            mixed_low, out_weight, preferred_element_type=jnp.float32
        ) + out_bias.astype(jnp.float32)
        return (stream + branch_out).astype(jnp.bfloat16).reshape(stream_in.shape)
    grad_low = grad_out.reshape(row_count, model_width)
    grad_rows = grad_low.astype(jnp.float32)
    grad_out_bias = jnp.sum(grad_rows, axis=0)
    grad_out_weight = jnp.einsum(
        "rd,re->de", mixed_low, grad_low, preferred_element_type=jnp.float32
    )
    grad_mixed = jnp.einsum(
        "re,de->rd", grad_low, out_weight, preferred_element_type=jnp.float32
    ).astype(jnp.bfloat16)
    grad_q, grad_k, grad_v = attend_back(
        queries, keys_all, values_all, key_valid, log_totals, grad_mixed
    )
    grad_q = grad_q.astype(jnp.bfloat16)
    grad_k = grad_k.astype(jnp.bfloat16)
    grad_v = grad_v.astype(jnp.bfloat16)
    grad_qv_bias = jnp.concatenate(
        [jnp.sum(grad_q.astype(jnp.float32), axis=0), jnp.sum(grad_v.astype(jnp.float32), axis=0)]
    )
    grad_proj = jnp.concatenate([grad_q, grad_k, grad_v], axis=1)
    grad_qkv_weight = jnp.einsum(
        "rd,re->de", normed_low, grad_proj, preferred_element_type=jnp.float32
    )
    grad_normed = jnp.einsum("re,de->rd", grad_proj, qkv_weight, preferred_element_type=jnp.float32)
    grad_stream, grad_gain, grad_shift = norm_pull(grad_normed)
    grad_in = (grad_rows + grad_stream).astype(jnp.bfloat16).reshape(stream_in.shape)
    return (
        grad_in,
        (grad_gain, grad_shift, grad_qkv_weight, grad_qv_bias, grad_out_weight, grad_out_bias),
    )


def ffn_block(stream_in, weights, grad_out):
    norm_gain, norm_shift, up_weight, up_bias, down_weight, down_bias = weights
    cell_count, seq_len, model_width = stream_in.shape
    row_count = cell_count * seq_len
    stream = stream_in.reshape(row_count, model_width).astype(jnp.float32)
    normed, norm_pull = jax.vjp(
        norm_rows, stream, norm_gain.astype(jnp.float32), norm_shift.astype(jnp.float32)
    )
    normed_low = normed.astype(jnp.bfloat16)
    up_proj = jnp.dot(normed_low, up_weight, preferred_element_type=jnp.float32) + up_bias.astype(
        jnp.float32
    )
    hidden, gelu_pull = jax.vjp(partial(jax.nn.gelu, approximate=False), up_proj)
    hidden_low = hidden.astype(jnp.bfloat16)
    if grad_out is None:
        branch_out = jnp.dot(
            hidden_low, down_weight, preferred_element_type=jnp.float32
        ) + down_bias.astype(jnp.float32)
        return (stream + branch_out).astype(jnp.bfloat16).reshape(stream_in.shape)
    grad_low = grad_out.reshape(row_count, model_width)
    grad_rows = grad_low.astype(jnp.float32)
    grad_down_bias = jnp.sum(grad_rows, axis=0)
    grad_down_weight = jnp.einsum(
        "rf,rd->fd", hidden_low, grad_low, preferred_element_type=jnp.float32
    )
    grad_hidden = jnp.einsum("rd,fd->rf", grad_low, down_weight, preferred_element_type=jnp.float32)
    grad_up = gelu_pull(grad_hidden)[0].astype(jnp.bfloat16)
    grad_up_bias = jnp.sum(grad_up.astype(jnp.float32), axis=0)
    grad_up_weight = jnp.einsum(
        "rd,rf->df", normed_low, grad_up, preferred_element_type=jnp.float32
    )
    grad_normed = jnp.einsum("rf,df->rd", grad_up, up_weight, preferred_element_type=jnp.float32)
    grad_stream, grad_gain, grad_shift = norm_pull(grad_normed)
    grad_in = (grad_rows + grad_stream).astype(jnp.bfloat16).reshape(stream_in.shape)
    return (
        grad_in,
        (grad_gain, grad_shift, grad_up_weight, grad_up_bias, grad_down_weight, grad_down_bias),
    )


def local(
    tokens,
    lengths,
    cotangent,
    attn_gain,
    attn_shift,
    qkv_weight,
    qv_bias,
    out_weight,
    out_bias,
    ffn_gain,
    ffn_shift,
    up_weight,
    up_bias,
    down_weight,
    down_bias,
):
    section_id = lax.axis_index("section")
    section_count = lax.axis_size("section")
    group_size = lax.axis_size("dp")
    layer_id = section_id // 2
    attn_turn = section_id % 2 == 0
    micro_count = tokens.shape[0]
    tick_count = micro_count + section_count - 1
    positions = jnp.arange(tokens.shape[2], dtype=jnp.int32)

    def pick(stacked):
        return lax.dynamic_index_in_dim(stacked, layer_id, 0, keepdims=False)

    a_gain, a_shift, a_qkv, a_qvb, a_out, a_outb = (
        pick(attn_gain),
        pick(attn_shift),
        pick(qkv_weight),
        pick(qv_bias),
        pick(out_weight),
        pick(out_bias),
    )
    f_gain, f_shift, f_up, f_upb, f_down, f_downb = (
        pick(ffn_gain),
        pick(ffn_shift),
        pick(up_weight),
        pick(up_bias),
        pick(down_weight),
        pick(down_bias),
    )
    attn_local = (a_gain, a_shift, a_qkv, a_qvb, a_out, a_outb)
    ffn_local = (f_gain, f_shift, f_up, f_upb, f_down, f_downb)

    def full_zeros(local_set, kind):
        return tuple(
            (jnp.zeros((item.shape[0] * group_size,) + item.shape[1:], kind) for item in local_set)
        )

    def shard_zeros(local_set):
        return tuple((jnp.zeros(item.shape, jnp.float32) for item in local_set))

    def fetch_attn():
        fetched = (
            lax.all_gather(a_gain, "dp", axis=0, tiled=True),
            lax.all_gather(a_shift, "dp", axis=0, tiled=True),
            lax.all_gather(a_qkv, "dp", axis=0, tiled=True),
            lax.all_gather(a_qvb, "dp", axis=0, tiled=True),
            lax.all_gather(a_out, "dp", axis=0, tiled=True),
            lax.all_gather(a_outb, "dp", axis=0, tiled=True),
        )
        return (tuple(fetched), full_zeros(ffn_local, jnp.bfloat16))

    def fetch_ffn():
        fetched = (
            lax.all_gather(f_gain, "dp", axis=0, tiled=True),
            lax.all_gather(f_shift, "dp", axis=0, tiled=True),
            lax.all_gather(f_up, "dp", axis=0, tiled=True),
            lax.all_gather(f_upb, "dp", axis=0, tiled=True),
            lax.all_gather(f_down, "dp", axis=0, tiled=True),
            lax.all_gather(f_downb, "dp", axis=0, tiled=True),
        )
        return (full_zeros(attn_local, jnp.bfloat16), tuple(fetched))

    attn_full, ffn_full = lax.cond(attn_turn, fetch_attn, fetch_ffn)

    def reduce_attn(attn_terms):
        shards = (
            lax.psum_scatter(attn_terms[0], "dp", scatter_dimension=0, tiled=True),
            lax.psum_scatter(attn_terms[1], "dp", scatter_dimension=0, tiled=True),
            lax.psum_scatter(attn_terms[2], "dp", scatter_dimension=0, tiled=True),
            lax.psum_scatter(attn_terms[3], "dp", scatter_dimension=0, tiled=True),
            lax.psum_scatter(attn_terms[4], "dp", scatter_dimension=0, tiled=True),
            lax.psum_scatter(attn_terms[5], "dp", scatter_dimension=0, tiled=True),
        )
        return (tuple(shards), shard_zeros(ffn_local))

    def reduce_ffn(ffn_terms):
        shards = (
            lax.psum_scatter(ffn_terms[0], "dp", scatter_dimension=0, tiled=True),
            lax.psum_scatter(ffn_terms[1], "dp", scatter_dimension=0, tiled=True),
            lax.psum_scatter(ffn_terms[2], "dp", scatter_dimension=0, tiled=True),
            lax.psum_scatter(ffn_terms[3], "dp", scatter_dimension=0, tiled=True),
            lax.psum_scatter(ffn_terms[4], "dp", scatter_dimension=0, tiled=True),
            lax.psum_scatter(ffn_terms[5], "dp", scatter_dimension=0, tiled=True),
        )
        return (shard_zeros(attn_local), tuple(shards))

    def key_mask(slot_id):
        cell_lengths = lax.dynamic_index_in_dim(lengths, slot_id, 0, keepdims=False)
        return positions[None, :] < cell_lengths[:, None]

    saved_inputs = jnp.zeros(tokens.shape, jnp.bfloat16)
    out_store = jnp.zeros(tokens.shape, jnp.bfloat16)
    incoming = jnp.zeros(tokens.shape[1:], jnp.bfloat16)
    for tick_no in range(tick_count):
        micro_id = tick_no - section_id
        active = (micro_id >= 0) & (micro_id < micro_count)
        slot_id = jnp.clip(micro_id, 0, micro_count - 1)
        first_input = lax.dynamic_index_in_dim(tokens, slot_id, 0, keepdims=False)
        stream_in = jnp.where(section_id == 0, first_input, incoming)
        key_valid = key_mask(slot_id)
        block_out = lax.cond(
            attn_turn,
            lambda: attention_block(stream_in, key_valid, attn_full, None),
            lambda: ffn_block(stream_in, ffn_full, None),
        )
        saved_inputs = jnp.where(
            active,
            lax.dynamic_update_index_in_dim(saved_inputs, stream_in, slot_id, 0),
            saved_inputs,
        )
        out_store = jnp.where(
            active & (section_id == section_count - 1),
            lax.dynamic_update_index_in_dim(out_store, block_out, slot_id, 0),
            out_store,
        )
        if tick_no + 1 < tick_count:
            incoming = shifted(block_out, "section", 1)
    attn_shards = shard_zeros(attn_local)
    ffn_shards = shard_zeros(ffn_local)
    grad_store = jnp.zeros(tokens.shape, jnp.bfloat16)
    grad_incoming = jnp.zeros(tokens.shape[1:], jnp.bfloat16)
    for tick_no in range(tick_count):
        micro_id = tick_no - (section_count - 1 - section_id)
        active = (micro_id >= 0) & (micro_id < micro_count)
        slot_id = jnp.clip(micro_id, 0, micro_count - 1)
        seed_grad = lax.dynamic_index_in_dim(cotangent, slot_id, 0, keepdims=False)
        grad_out = jnp.where(section_id == section_count - 1, seed_grad, grad_incoming)
        stream_in = lax.dynamic_index_in_dim(saved_inputs, slot_id, 0, keepdims=False)
        key_valid = key_mask(slot_id)

        def attn_side():
            grad_in, attn_terms = attention_block(stream_in, key_valid, attn_full, grad_out)
            return (
                grad_in,
                attn_terms,
                tuple((jnp.zeros(item.shape, jnp.float32) for item in ffn_full)),
            )

        def ffn_side():
            grad_in, ffn_terms = ffn_block(stream_in, ffn_full, grad_out)
            return (
                grad_in,
                tuple((jnp.zeros(item.shape, jnp.float32) for item in attn_full)),
                ffn_terms,
            )

        grad_in, attn_terms, ffn_terms = lax.cond(attn_turn, attn_side, ffn_side)
        attn_terms = tuple((jnp.where(active, item, 0.0) for item in attn_terms))
        ffn_terms = tuple((jnp.where(active, item, 0.0) for item in ffn_terms))
        step_attn, step_ffn = lax.cond(
            attn_turn, lambda: reduce_attn(attn_terms), lambda: reduce_ffn(ffn_terms)
        )
        attn_shards = tuple((total + item for total, item in zip(attn_shards, step_attn)))
        ffn_shards = tuple((total + item for total, item in zip(ffn_shards, step_ffn)))
        grad_store = jnp.where(
            active & (section_id == 0),
            lax.dynamic_update_index_in_dim(grad_store, grad_in, slot_id, 0),
            grad_store,
        )
        if tick_no + 1 < tick_count:
            grad_incoming = shifted(grad_in, "section", -1)
    layer_total = section_count // 2

    def place(shard):
        base_fill = jnp.zeros((layer_total,) + shard.shape, jnp.float32)
        return lax.dynamic_update_index_in_dim(base_fill, shard, layer_id, 0)

    summed = (
        lax.psum(place(attn_shards[0]).astype(jnp.bfloat16), "section").astype(jnp.float32),
        lax.psum(place(attn_shards[1]).astype(jnp.bfloat16), "section").astype(jnp.float32),
        lax.psum(place(attn_shards[2]).astype(jnp.bfloat16), "section").astype(jnp.float32),
        lax.psum(place(attn_shards[3]).astype(jnp.bfloat16), "section").astype(jnp.float32),
        lax.psum(place(attn_shards[4]).astype(jnp.bfloat16), "section").astype(jnp.float32),
        lax.psum(place(attn_shards[5]).astype(jnp.bfloat16), "section").astype(jnp.float32),
        lax.psum(place(ffn_shards[0]).astype(jnp.bfloat16), "section").astype(jnp.float32),
        lax.psum(place(ffn_shards[1]).astype(jnp.bfloat16), "section").astype(jnp.float32),
        lax.psum(place(ffn_shards[2]).astype(jnp.bfloat16), "section").astype(jnp.float32),
        lax.psum(place(ffn_shards[3]).astype(jnp.bfloat16), "section").astype(jnp.float32),
        lax.psum(place(ffn_shards[4]).astype(jnp.bfloat16), "section").astype(jnp.float32),
        lax.psum(place(ffn_shards[5]).astype(jnp.bfloat16), "section").astype(jnp.float32),
    )
    out_parts, grad_parts = (
        lax.all_to_all(out_store, "section", split_axis=2, concat_axis=0, tiled=True),
        lax.all_to_all(grad_store, "section", split_axis=2, concat_axis=0, tiled=True),
    )
    out_mine = out_parts[(section_count - 1) * micro_count : section_count * micro_count]
    grad_mine = grad_parts[0:micro_count]
    return (out_mine, grad_mine) + tuple(summed)


def solution(mesh):
    in_specs = (
        P(None, "dp", None, None),
        P(None, "dp"),
        P(None, "dp", None, None),
        P(None, "dp"),
        P(None, "dp"),
        P(None, "dp", None),
        P(None, "dp"),
        P(None, "dp", None),
        P(None, "dp"),
        P(None, "dp"),
        P(None, "dp"),
        P(None, "dp", None),
        P(None, "dp"),
        P(None, "dp", None),
        P(None, "dp"),
    )
    out_specs = (
        P(None, "dp", "section", None),
        P(None, "dp", "section", None),
        P(None, "dp"),
        P(None, "dp"),
        P(None, "dp", None),
        P(None, "dp"),
        P(None, "dp", None),
        P(None, "dp"),
        P(None, "dp"),
        P(None, "dp"),
        P(None, "dp", None),
        P(None, "dp"),
        P(None, "dp", None),
        P(None, "dp"),
    )
    return jax.shard_map(local, mesh=mesh, in_specs=in_specs, out_specs=out_specs, check_vma=False)
```

profile of v0, /device:TPU:0, one launch (start us, length us, event | category | flops | bytes accessed | tf_op | source)
XLA Modules:
  0.0 4074.1 jit_solution(2566674823854947512)
XLA Ops:
  8.1 136.5 %conditional.24 = (bf16[768]{0:T(1024)(128)(2,1)S(1)}, bf16[768]{0:T(1024)(128)(2,1)S(1)}, bf16[768,2304]{1,0:T(8,128)(2,1)}, bf16[1536]{0:T(1024)(128)(2,1)S(1)...) conditional(s32[]{:T(128)} %convert_element_type.1493, ...), branch_computations={%region_0.1_spmd, %region_1.2_spmd} | conditional | flops 3844 | bytes 38984608 | solution.py:287
  17.1 39.5 all-reduce.58
  60.6 78.6 %all-gather.21.cloned.1.call-done = bf16[1,768,2304]{2,1,0:T(8,128)(2,1)} async-done(((bf16[1,96,2304]{2,1,0:T(8,128)(2,1)}), bf16[1,768,2304]{2,1,0:T(8,128)(2,1)}) %all-gather.21.cloned.1.call-update) | async-done | bytes 3538960 | tf_op jit(solution)/shard_map/cond/branch_1_fun/all_gather | solution.py:269
  148.7 101.7 %conditional.25 = (f32[1024,768]{1,0:T(8,128)}, f32[1024,768]{1,0:T(8,128)S(1)}, bf16[768]{0:T(1024)(128)(2,1)S(1)}) conditional(s32[]{:T(128)} %convert_element_type.1493, (bf16[1,1024,768]{2,1,0:T(8,128)(2,1)S(1)}, bf16[768]{0:T(1024)(128)(2,1)S(1)}, bf16[768]{0:T(1024)(128)(2,1)S(1)}, bf16[768,3072]{1,0:T(8,128)(2,1)}, ...), branch_computations={%region_2.5_spmd, %region_5.12_spmd} | conditional | flops 9879951360 | bytes 194519552
  172.7 72.4 %while.326 = (s32[]{:T(128)}, bf16[2,1,512,12,64]{2,4,3,1,0:T(8,128)(2,1)}, pred[1,1024]{1,0:T(4,128)(4,1)S(1)}, s32[2]{0:T(128)S(1)}, bf16[1,2,512,12,64]{2,4,3...) while((s32[]{:T(128)}, ...), condition=%wide.region_11.11_spmd, body=%wide.region_8.10_spmd.sunk | while | flops 1679812608 | bytes 100062456 | solution.py:57
  267.9 104.7 %conditional.26 = (f32[1024,768]{1,0:T(8,128)}, f32[1024,768]{1,0:T(8,128)S(1)}, bf16[768]{0:T(1024)(128)(2,1)S(1)}) conditional(s32[]{:T(128)} %convert_element_type.1493, (bf16[1,1024,768]{2,1,0:T(8,128)(2,1)}, bf16[768]{0:T(1024)(128)(2,1)S(1)}, bf16[768]{0:T(1024)(128)(2,1)S(1)}, bf16[768,3072]{1,0:T(8,128)(2,1)}, ...), branch_computations={%region_12.15_spmd, %region_15.22_spmd} | conditional | flops 9879951360 | bytes 194556576
  294.9 72.4 %while.327 = (s32[]{:T(128)}, bf16[2,1,512,12,64]{2,4,3,1,0:T(8,128)(2,1)}, pred[1,1024]{1,0:T(4,128)(4,1)S(1)}, s32[2]{0:T(128)S(1)}, bf16[1,2,512,12,64]{2,4,3...) while((s32[]{:T(128)}, ...), condition=%wide.region_21.21_spmd, body=%wide.region_18.20_spmd.sunk | while | flops 1679812608 | bytes 100062456 | solution.py:57
  389.8 105.0 %conditional.27 = (f32[1024,768]{1,0:T(8,128)}, f32[1024,768]{1,0:T(8,128)S(1)}, bf16[768]{0:T(1024)(128)(2,1)S(1)}) conditional(s32[]{:T(128)} %convert_element_type.1493, (bf16[1,1024,768]{2,1,0:T(8,128)(2,1)}, bf16[768]{0:T(1024)(128)(2,1)S(1)}, bf16[768]{0:T(1024)(128)(2,1)S(1)}, bf16[768,3072]{1,0:T(8,128)(2,1)}, ...), branch_computations={%region_22.25_spmd, %region_25.32_spmd} | conditional | flops 9879951360 | bytes 194556576
  417.1 72.4 %while.328 = (s32[]{:T(128)}, bf16[2,1,512,12,64]{2,4,3,1,0:T(8,128)(2,1)}, pred[1,1024]{1,0:T(4,128)(4,1)S(1)}, s32[2]{0:T(128)S(1)}, bf16[1,2,512,12,64]{2,4,3...) while((s32[]{:T(128)}, ...), condition=%wide.region_31.31_spmd, body=%wide.region_28.30_spmd.sunk | while | flops 1679812608 | bytes 100062456 | solution.py:57
  512.0 105.0 %conditional.28 = (f32[1024,768]{1,0:T(8,128)}, f32[1024,768]{1,0:T(8,128)S(1)}, bf16[768]{0:T(1024)(128)(2,1)S(1)}) conditional(s32[]{:T(128)} %convert_element_type.1493, (bf16[1,1024,768]{2,1,0:T(8,128)(2,1)}, bf16[768]{0:T(1024)(128)(2,1)S(1)}, bf16[768]{0:T(1024)(128)(2,1)S(1)}, bf16[768,3072]{1,0:T(8,128)(2,1)}, ...), branch_computations={%region_32.35_spmd, %region_35.42_spmd} | conditional | flops 9879951360 | bytes 194556576
  539.3 72.4 %while.329 = (s32[]{:T(128)}, bf16[2,1,512,12,64]{2,4,3,1,0:T(8,128)(2,1)}, pred[1,1024]{1,0:T(4,128)(4,1)S(1)}, s32[2]{0:T(128)S(1)}, bf16[1,2,512,12,64]{2,4,3...) while((s32[]{:T(128)}, ...), condition=%wide.region_41.41_spmd, body=%wide.region_38.40_spmd.sunk | while | flops 1679812608 | bytes 100062456 | solution.py:57
  637.7 317.3 %conditional.40 = (f32[768]{0:T(1024)}, f32[768]{0:T(1024)}, f32[768,2304]{1,0:T(8,128)}, f32[1536]{0:T(1024)}, f32[768,768]{1,0:T(8,128)}, /*index=5*/f32[768]{...) conditional(s32[]{:T(128)} %convert_element_type.1493, ...), branch_computations={%region_52.60_spmd, %region_60.76_spmd} | conditional | flops 24451749888 | bytes 521000512
  679.4 72.4 %while.333 = (s32[]{:T(128)}, bf16[2,1,512,12,64]{2,4,3,1,0:T(8,128)(2,1)}, f32[2,1,12,512,1]{3,2,4,1,0:T(8,128)S(1)}, pred[1,1024]{1,0:T(4,128)(4,1)S(1)}, s32[...) while((s32[]{:T(128)}, ...), condition=%wide.region_66.66_spmd, body=%wide.region_63.65_spmd.sunk | while | flops 1679812608 | bytes 100119824 | solution.py:57
  751.8 167.2 %while.334 = (s32[]{:T(128)}, f32[1,1024,12,64]{1,3,2,0:T(8,128)}, f32[1,1024,12,64]{1,3,2,0:T(8,128)}, bf16[2,1,512,12,64]{2,4,3,1,0:T(8,128)(2,1)}, s32[2]{0:T...) while((s32[]{:T(128)}, f32[1,1024,12,64]{1,3,2,0:T(8,128)}, ...), condition=%wide.region_69.69_spmd.clone, body=%wide.region_67.68_spmd.clone.sunk | while | flops 4125222912 | bytes 217240848 | solution.py:105
  794.9 21.4 multiply_convert_fusion.23
  860.9 17.5 multiply_reduce_fusion.21
  878.4 21.4 multiply_convert_fusion.23
  977.0 338.5 %conditional.41 = (f32[768]{0:T(1024)}, f32[768]{0:T(1024)}, f32[768,2304]{1,0:T(8,128)}, f32[1536]{0:T(1024)}, f32[768,768]{1,0:T(8,128)}, /*index=5*/f32[768]{...) conditional(s32[]{:T(128)} %convert_element_type.1493, ...), branch_computations={%region_77.85_spmd, %region_85.101_spmd} | conditional | flops 24451749888 | bytes 527291968
  1020.2 85.2 %while.335 = (s32[]{:T(128)}, bf16[2,1,512,12,64]{2,4,3,1,0:T(8,128)(2,1)}, f32[2,1,12,512,1]{3,2,4,1,0:T(8,128)S(1)}, pred[1,1024]{1,0:T(4,128)(4,1)S(1)}, s32[...) while((s32[]{:T(128)}, ...), condition=%wide.region_91.91_spmd, body=%wide.region_88.90_spmd.sunk | while | flops 1679812608 | bytes 100119824 | solution.py:57
  1105.3 166.8 %while.336 = (s32[]{:T(128)}, f32[1,1024,12,64]{1,3,2,0:T(8,128)}, f32[1,1024,12,64]{1,3,2,0:T(8,128)}, bf16[2,1,512,12,64]{2,4,3,1,0:T(8,128)(2,1)}, s32[2]{0:T...) while((s32[]{:T(128)}, f32[1,1024,12,64]{1,3,2,0:T(8,128)}, ...), condition=%wide.region_94.94_spmd.clone, body=%wide.region_92.93_spmd.clone.sunk | while | flops 4125222912 | bytes 217240848 | solution.py:105
  1148.3 21.5 multiply_convert_fusion.22
  1231.6 21.5 multiply_convert_fusion.22
  1331.0 340.4 %conditional.42 = (f32[768]{0:T(1024)}, f32[768]{0:T(1024)}, f32[768,2304]{1,0:T(8,128)}, f32[1536]{0:T(1024)}, f32[768,768]{1,0:T(8,128)}, /*index=5*/f32[768]{...) conditional(s32[]{:T(128)} %convert_element_type.1493, ...), branch_computations={%region_102.110_spmd, %region_110.126_spmd} | conditional | flops 24451749888 | bytes 527291968
  1374.2 86.2 %while.337 = (s32[]{:T(128)}, bf16[2,1,512,12,64]{2,4,3,1,0:T(8,128)(2,1)}, f32[2,1,12,512,1]{3,2,4,1,0:T(8,128)S(1)}, pred[1,1024]{1,0:T(4,128)(4,1)S(1)}, s32[...) while((s32[]{:T(128)}, ...), condition=%wide.region_116.116_spmd, body=%wide.region_113.115_spmd.sunk | while | flops 1679812608 | bytes 100119824 | solution.py:57
  1460.4 167.7 %while.338 = (s32[]{:T(128)}, f32[1,1024,12,64]{1,3,2,0:T(8,128)}, f32[1,1024,12,64]{1,3,2,0:T(8,128)}, bf16[2,1,512,12,64]{2,4,3,1,0:T(8,128)(2,1)}, s32[2]{0:T...) while((s32[]{:T(128)}, f32[1,1024,12,64]{1,3,2,0:T(8,128)}, ...), condition=%wide.region_119.119_spmd.clone, body=%wide.region_117.118_spmd.clone.sunk | while | flops 4125222912 | bytes 217240848 | solution.py:105
  1486.3 17.5 multiply_reduce_fusion.19
  1503.8 21.4 multiply_convert_fusion.21
  1570.0 17.5 multiply_reduce_fusion.19
  1587.6 21.4 multiply_convert_fusion.21
  1687.3 340.0 %conditional.43 = (f32[768]{0:T(1024)}, f32[768]{0:T(1024)}, f32[768,2304]{1,0:T(8,128)}, f32[1536]{0:T(1024)}, f32[768,768]{1,0:T(8,128)}, /*index=5*/f32[768]{...) conditional(s32[]{:T(128)} %convert_element_type.1493, ...), branch_computations={%region_127.135_spmd, %region_135.151_spmd} | conditional | flops 24451749888 | bytes 521000512
  1731.6 85.6 %while.339 = (s32[]{:T(128)}, bf16[2,1,512,12,64]{2,4,3,1,0:T(8,128)(2,1)}, f32[2,1,12,512,1]{3,2,4,1,0:T(8,128)S(1)}, pred[1,1024]{1,0:T(4,128)(4,1)S(1)}, s32[...) while((s32[]{:T(128)}, ...), condition=%wide.region_141.141_spmd, body=%wide.region_138.140_spmd.sunk | while | flops 1679812608 | bytes 100119824 | solution.py:57
  1817.2 166.9 %while.340 = (s32[]{:T(128)}, f32[1,1024,12,64]{1,3,2,0:T(8,128)}, f32[1,1024,12,64]{1,3,2,0:T(8,128)}, bf16[2,1,512,12,64]{2,4,3,1,0:T(8,128)(2,1)}, s32[2]{0:T...) while((s32[]{:T(128)}, f32[1,1024,12,64]{1,3,2,0:T(8,128)}, ...), condition=%wide.region_144.144_spmd.clone, body=%wide.region_142.143_spmd.clone.sunk | while | flops 4125222912 | bytes 217240848 | solution.py:105
  1860.3 21.4 multiply_convert_fusion.20
  1943.6 21.4 multiply_convert_fusion.20
  2036.4 104.6 %conditional.29 = (bf16[1,1,1024,768]{3,2,1,0:T(8,128)(2,1)S(1)}) conditional(s32[]{:T(128)} %convert_element_type.1493, (bf16[1,1024,768]{2,1,0:T(8,128)(2,1)S(1)}, bf16[768]{0:T(1024)(128)(2,1)S(1)}, bf16[768]{0:T(1024)(128)(2,1)S(1)}, bf16[768,3072]{1,0:T(8,128)(2,1)}, bf16[3072]{0:T(1024)(128)(2,1)S(1)}, ...), branch_computations={%region_42.45_spmd, %region_45.52_spmd} | conditional | flops 9883883520 | bytes 163060608 | solution.py:325
  2061.1 74.6 %while.330 = (s32[]{:T(128)}, bf16[2,1,512,12,64]{2,4,3,1,0:T(8,128)(2,1)}, pred[1,1024]{1,0:T(4,128)(4,1)S(1)}, s32[2]{0:T(128)S(1)}, bf16[1,2,512,12,64]{2,4,3...) while((s32[]{:T(128)}, ...), condition=%wide.region_51.51_spmd, body=%wide.region_48.50_spmd.sunk | while | flops 1679812608 | bytes 100062456 | solution.py:57
  2150.7 114.0 %all-to-all-start = ((bf16[2,1,1024,768]{3,0,1,2:T(2,128)(2,1)}), bf16[2,1,1024,768]{3,0,1,2:T(2,128)(2,1)}, u32[]{:S(2)}, u32[]{:S(2)}) async-start(bf16[2,1,1024,768]{3,0,1,2:T(2,128)(2,1)} %copy.394), calls=%async_computation.20 | async-start | bytes 6291456 | tf_op jit(solution)/shard_map/all_to_all | solution.py:407
  2277.6 262.2 %conditional.35 = (f32[96]{0:T(128)S(1)}, f32[96]{0:T(128)S(1)}, f32[96,2304]{1,0:T(8,128)}, f32[192]{0:T(256)S(1)}, f32[96,768]{1,0:T(8,128)}, /*index=5*/f32[9...) conditional(s32[]{:T(128)} %convert_element_type.1493, ...), branch_computations={%region_178.185_spmd, %region_185.192_spmd} | conditional | flops 4729348 | bytes 121613232 | solution.py:374
  2288.8 36.8 all-reduce.48
  2325.9 58.7 %reduce-scatter.27.cloned.1.call-done = f32[96,768]{1,0:T(8,128)} async-done(((f32[768,768]{1,0:T(8,128)}), f32[96,768]{1,0:T(8,128)}) %reduce-scatter.27.cloned.1.call-update) | async-done | bytes 294928 | tf_op jit(solution)/shard_map/cond/branch_1_fun/reduce_scatter | solution.py:295
  2384.7 152.7 %reduce-scatter.25.cloned.1.call-done = f32[96,2304]{1,0:T(8,128)} async-done(((f32[768,2304]{1,0:T(8,128)}), f32[96,2304]{1,0:T(8,128)}) %reduce-scatter.25.cloned.1.call-update) | async-done | bytes 884752 | tf_op jit(solution)/shard_map/cond/branch_1_fun/reduce_scatter | solution.py:293
  2540.7 265.5 %conditional.36 = (f32[96]{0:T(128)S(1)}, f32[96]{0:T(128)S(1)}, f32[96,2304]{1,0:T(8,128)}, f32[192]{0:T(256)S(1)}, f32[96,768]{1,0:T(8,128)}, /*index=5*/f32[9...) conditional(s32[]{:T(128)} %convert_element_type.1493, ...), branch_computations={%region_192.199_spmd, %region_199.206_spmd} | conditional | flops 4729348 | bytes 121613232 | solution.py:374
  2551.9 36.4 all-reduce.50
  2588.6 62.1 %reduce-scatter.35.cloned.1.call-done = f32[96,768]{1,0:T(8,128)} async-done(((f32[768,768]{1,0:T(8,128)}), f32[96,768]{1,0:T(8,128)}) %reduce-scatter.35.cloned.1.call-update) | async-done | bytes 294928 | tf_op jit(solution)/shard_map/cond/branch_1_fun/reduce_scatter | solution.py:295
  2650.6 153.2 %reduce-scatter.33.cloned.1.call-done = f32[96,2304]{1,0:T(8,128)} async-done(((f32[768,2304]{1,0:T(8,128)}), f32[96,2304]{1,0:T(8,128)}) %reduce-scatter.33.cloned.1.call-update) | async-done | bytes 884752 | tf_op jit(solution)/shard_map/cond/branch_1_fun/reduce_scatter | solution.py:293
  2806.9 265.4 %conditional.37 = (f32[96]{0:T(128)S(1)}, f32[96]{0:T(128)S(1)}, f32[96,2304]{1,0:T(8,128)}, f32[192]{0:T(256)S(1)}, f32[96,768]{1,0:T(8,128)}, /*index=5*/f32[9...) conditional(s32[]{:T(128)} %convert_element_type.1493, ...), branch_computations={%region_206.213_spmd, %region_213.220_spmd} | conditional | flops 4729348 | bytes 121613232 | solution.py:374
  2818.2 36.3 all-reduce.52
  2854.8 62.1 %reduce-scatter.43.cloned.1.call-done = f32[96,768]{1,0:T(8,128)} async-done(((f32[768,768]{1,0:T(8,128)}), f32[96,768]{1,0:T(8,128)}) %reduce-scatter.43.cloned.1.call-update) | async-done | bytes 294928 | tf_op jit(solution)/shard_map/cond/branch_1_fun/reduce_scatter | solution.py:295
  2916.8 152.9 %reduce-scatter.41.cloned.1.call-done = f32[96,2304]{1,0:T(8,128)} async-done(((f32[768,2304]{1,0:T(8,128)}), f32[96,2304]{1,0:T(8,128)}) %reduce-scatter.41.cloned.1.call-update) | async-done | bytes 884752 | tf_op jit(solution)/shard_map/cond/branch_1_fun/reduce_scatter | solution.py:293
  3073.0 265.6 %conditional.38 = (f32[96]{0:T(128)S(1)}, f32[96]{0:T(128)S(1)}, f32[96,2304]{1,0:T(8,128)}, f32[192]{0:T(256)S(1)}, f32[96,768]{1,0:T(8,128)}, /*index=5*/f32[9...) conditional(s32[]{:T(128)} %convert_element_type.1493, ...), branch_computations={%region_220.227_spmd, %region_227.234_spmd} | conditional | flops 4729348 | bytes 121613232 | solution.py:374
  3085.8 36.2 all-reduce.54
  3122.3 60.9 %reduce-scatter.51.cloned.1.call-done = f32[96,768]{1,0:T(8,128)} async-done(((f32[768,768]{1,0:T(8,128)}), f32[96,768]{1,0:T(8,128)}) %reduce-scatter.51.cloned.1.call-update) | async-done | bytes 294928 | tf_op jit(solution)/shard_map/cond/branch_1_fun/reduce_scatter | solution.py:295
  3183.1 153.2 %reduce-scatter.49.cloned.1.call-done = f32[96,2304]{1,0:T(8,128)} async-done(((f32[768,2304]{1,0:T(8,128)}), f32[96,2304]{1,0:T(8,128)}) %reduce-scatter.49.cloned.1.call-update) | async-done | bytes 884752 | tf_op jit(solution)/shard_map/cond/branch_1_fun/reduce_scatter | solution.py:293
  3345.3 322.2 %conditional.34 = (f32[768]{0:T(1024)}, f32[768]{0:T(1024)}, f32[768,2304]{1,0:T(8,128)}, f32[1536]{0:T(1024)}, f32[768,768]{1,0:T(8,128)}, /*index=5*/f32[768]{...) conditional(s32[]{:T(128)} %convert_element_type.1493, ...), branch_computations={%region_152.161_spmd, %region_161.178_spmd} | conditional | flops 24460400640 | bytes 530461216 | solution.py:371
  3383.5 72.7 %while.331 = (s32[]{:T(128)}, bf16[2,1,512,12,64]{2,4,3,1,0:T(8,128)(2,1)}, f32[2,1,12,512,1]{3,2,4,1,0:T(8,128)S(1)}, pred[1,1024]{1,0:T(4,128)(4,1)S(1)}, s32[...) while((s32[]{:T(128)}, ...), condition=%wide.region_167.167_spmd, body=%wide.region_164.166_spmd.sunk | while | flops 1679812608 | bytes 100119824 | solution.py:57
  3457.6 167.2 %while.332 = (s32[]{:T(128)}, f32[1,1024,12,64]{1,3,2,0:T(8,128)}, f32[1,1024,12,64]{1,3,2,0:T(8,128)}, bf16[2,1,512,12,64]{2,4,3,1,0:T(8,128)(2,1)}, s32[2]{0:T...) while((s32[]{:T(128)}, f32[1,1024,12,64]{1,3,2,0:T(8,128)}, ...), condition=%wide.region_170.170_spmd.clone, body=%wide.region_168.169_spmd.clone.sunk | while | flops 4125222912 | bytes 217240848 | solution.py:105
  3500.9 21.4 multiply_convert_fusion.24
  3584.2 21.4 multiply_convert_fusion.24
  3681.2 257.4 %conditional.39 = (f32[96]{0:T(128)S(1)}, f32[96]{0:T(128)S(1)}, f32[96,2304]{1,0:T(8,128)}, f32[192]{0:T(256)S(1)}, f32[96,768]{1,0:T(8,128)}, /*index=5*/f32[9...) conditional(s32[]{:T(128)} %convert_element_type.1493, ...), branch_computations={%region_234.241_spmd, %region_241.248_spmd} | conditional | flops 4729348 | bytes 121637872 | solution.py:374
  3695.5 36.5 all-reduce.56
  3732.3 51.3 %reduce-scatter.59.cloned.1.call-done = f32[96,768]{1,0:T(8,128)} async-done(((f32[768,768]{1,0:T(8,128)}), f32[96,768]{1,0:T(8,128)}) %reduce-scatter.59.cloned.1.call-update) | async-done | bytes 294928 | tf_op jit(solution)/shard_map/cond/branch_1_fun/reduce_scatter | solution.py:295
  3783.6 152.7 %reduce-scatter.57.cloned.1.call-done = f32[96,2304]{1,0:T(8,128)} async-done(((f32[768,2304]{1,0:T(8,128)}), f32[96,2304]{1,0:T(8,128)}) %reduce-scatter.57.cloned.1.call-update) | async-done | bytes 884752 | tf_op jit(solution)/shard_map/cond/branch_1_fun/reduce_scatter | solution.py:293
  3963.4 51.1 %all-reduce.59 = (bf16[2,96]{1,0:T(2,128)(2,1)S(1)}, bf16[2,96]{1,0:T(2,128)(2,1)S(1)}, bf16[2,192]{1,0:T(2,128)(2,1)S(1)}, bf16[2,96]{1,0:T(2,128)(2,1)S(1)}, b...) all-reduce(bf16[2,96]{1,0:T(2,128)(2,1)S(1)} %dynamic_update_slice., ...), channel_id=1, replica_groups=mesh['dp'=8,'section'=4] {'section'}, use_global_device_ids=true, to_apply=%region_248.249 | all-reduce | flops 2304 | bytes 9216 | tf_op jit(solution)/shard_map/psum | solution.py:393
  4019.1 38.3 all-reduce.63.cloned.1.call-done
  (1655 shorter events, 2059.3 us)
Async XLA Ops:
  8.1 52.5 %all-gather.23.cloned.1.call-start = ((), (), s32[]{:S(2)}) async-start(), calls=%async_computation.25 | async-start | bytes 1327104 | tf_op jit(solution)/shard_map/cond/branch_1_fun/all_gather | solution.py:271
  9.7 129.5 %all-gather.21.cloned.1.call-start = ((), (), s32[]{:S(2)}) async-start(), calls=%async_computation.24 | async-start | bytes 3981312 | tf_op jit(solution)/shard_map/cond/branch_1_fun/all_gather | solution.py:269
  144.6 121.8 %copy-start.89 = (bf16[1536]{0:T(1024)(128)(2,1)}, bf16[1536]{0:T(1024)(128)(2,1)S(1)}, u32[]{:S(2)}) copy-start(bf16[1536]{0:T(1024)(128)(2,1)S(1)} %get-tuple-element.3004) | copy-start | bytes 9220
  144.6 121.8 %copy-start.149 = (bf16[768]{0:T(1024)(128)(2,1)}, bf16[768]{0:T(1024)(128)(2,1)S(1)}, u32[]{:S(2)}) copy-start(bf16[768]{0:T(1024)(128)(2,1)S(1)} %get-tuple-element.3002) | copy-start | bytes 4612
  144.6 121.8 %copy-start.158 = (bf16[768]{0:T(1024)(128)(2,1)}, bf16[768]{0:T(1024)(128)(2,1)S(1)}, u32[]{:S(2)}) copy-start(bf16[768]{0:T(1024)(128)(2,1)S(1)} %get-tuple-element.3001) | copy-start | bytes 4612
  258.3 4.6 collective-permute-start
  380.1 4.6 collective-permute-start.1
  502.3 4.6 collective-permute-start.2
  621.7 9.3 collective-permute-start.3
  679.4 72.4 %copy-start.386 = (s32[2]{0:T(128)S(1)}, s32[2]{0:T(128)}, u32[]{:S(2)}) copy-start(s32[2]{0:T(128)} %iota.86) | copy-start | bytes 28
  969.3 5.6 collective-permute-start.4
  984.0 19.8 copy-start.20
  1020.2 85.2 %copy-start.387 = (s32[2]{0:T(128)S(1)}, s32[2]{0:T(128)}, u32[]{:S(2)}) copy-start(s32[2]{0:T(128)} %iota.88) | copy-start | bytes 28
  1323.1 5.8 collective-permute-start.5
  1338.0 19.9 copy-start.17
  1374.2 86.2 %copy-start.388 = (s32[2]{0:T(128)S(1)}, s32[2]{0:T(128)}, u32[]{:S(2)}) copy-start(s32[2]{0:T(128)} %iota.90) | copy-start | bytes 28
  1678.9 5.6 collective-permute-start.6
  1694.3 20.9 copy-start.14
  1695.5 19.7 copy-start.235
  1731.6 85.6 %copy-start.389 = (s32[2]{0:T(128)S(1)}, s32[2]{0:T(128)}, u32[]{:S(2)}) copy-start(s32[2]{0:T(128)} %iota.92) | copy-start | bytes 28
  2035.0 1308.0 %collective-permute-start.7 = (bf16[1,1024,768]{2,1,0:T(8,128)(2,1)}, bf16[1,1024,768]{2,1,0:T(8,128)(2,1)}, u32[]{:S(2)}, u32[]{:S(2)}) collective-permute-start(bf16[1,1024,768]{2,1,0:T(8,128)(2,1)} %bitcast.210), channel_id=1, source_target_pairs={{1,0},{2,1},{3,2},{5,4},{6,5},{7,6},{9,8},{10,9},{11,10},{13,12},{... | collective-permute-start | bytes 4718600 | tf_op jit(solution)/shard_map/ppermute | solution.py:21
  2150.7 1796.8 %all-to-all-start = ((bf16[2,1,1024,768]{3,0,1,2:T(2,128)(2,1)}), bf16[2,1,1024,768]{3,0,1,2:T(2,128)(2,1)}, u32[]{:S(2)}, u32[]{:S(2)}) async-start(bf16[2,1,1024,768]{3,0,1,2:T(2,128)(2,1)} %copy.394), calls=%async_computation.20 | async-start | bytes 6291456 | tf_op jit(solution)/shard_map/all_to_all | solution.py:407
  2264.7 807.8 %copy-start.143 = (f32[768]{0:T(1024)}, f32[768]{0:T(1024)S(1)}, u32[]{:S(2)}) copy-start(f32[768]{0:T(1024)S(1)} %broadcast_in_dim.714) | copy-start | bytes 9220
  2264.7 807.8 %copy-start.145 = (f32[3072]{0:T(1024)}, f32[3072]{0:T(1024)S(1)}, u32[]{:S(2)}) copy-start(f32[3072]{0:T(1024)S(1)} %broadcast_in_dim.716) | copy-start | bytes 36868
  2273.7 798.8 %copy-start.147 = (f32[1536]{0:T(1024)}, f32[1536]{0:T(1024)S(1)}, u32[]{:S(2)}) copy-start(f32[1536]{0:T(1024)S(1)} %broadcast_in_dim.719) | copy-start | bytes 18436
  2273.9 798.7 %copy-start.11 = (f32[768,768]{1,0:T(8,128)}, f32[768,768]{1,0:T(8,128)S(1)}, u32[]{:S(2)}) copy-start(f32[768,768]{1,0:T(8,128)S(1)} %broadcast_in_dim.720) | copy-start | bytes 7077892
  2277.5 262.9 %copy-start.222 = (f32[1536]{0:T(1024)S(1)}, f32[1536]{0:T(1024)}, u32[]{:S(2)}) copy-start(f32[1536]{0:T(1024)} %get-tuple-element.3058) | copy-start | bytes 18436
  2277.6 262.9 %copy-start.226 = (f32[768]{0:T(1024)S(1)}, f32[768]{0:T(1024)}, u32[]{:S(2)}) copy-start(f32[768]{0:T(1024)} %get-tuple-element.3054) | copy-start | bytes 9220
  2277.6 262.9 %copy-start.250 = (f32[768]{0:T(1024)S(1)}, f32[768]{0:T(1024)}, u32[]{:S(2)}) copy-start(f32[768]{0:T(1024)} %get-tuple-element.3060) | copy-start | bytes 9220
  2277.6 262.9 %copy-start.251 = (f32[768]{0:T(1024)S(1)}, f32[768]{0:T(1024)}, u32[]{:S(2)}) copy-start(f32[768]{0:T(1024)} %get-tuple-element.3056) | copy-start | bytes 9220
  2277.6 262.9 %copy-start.252 = (f32[768]{0:T(1024)S(1)}, f32[768]{0:T(1024)}, u32[]{:S(2)}) copy-start(f32[768]{0:T(1024)} %get-tuple-element.3055) | copy-start | bytes 9220
  2277.6 262.9 %copy-start.270 = (f32[3072]{0:T(1024)S(1)}, f32[3072]{0:T(1024)}, u32[]{:S(2)}) copy-start(f32[3072]{0:T(1024)} %get-tuple-element.3052) | copy-start | bytes 36868
  2277.6 262.9 %copy-start.287 = (f32[768]{0:T(1024)S(1)}, f32[768]{0:T(1024)}, u32[]{:S(2)}) copy-start(f32[768]{0:T(1024)} %get-tuple-element.3049) | copy-start | bytes 9220
  2277.6 262.9 %copy-start.288 = (f32[768]{0:T(1024)S(1)}, f32[768]{0:T(1024)}, u32[]{:S(2)}) copy-start(f32[768]{0:T(1024)} %get-tuple-element.3050) | copy-start | bytes 9220
  2277.6 107.0 %reduce-scatter.27.cloned.1.call-start = ((), (), s32[]{:S(2)}) async-start(), calls=%async_computation.29 | async-start | bytes 2654208 | tf_op jit(solution)/shard_map/cond/branch_1_fun/reduce_scatter | solution.py:295
  2279.4 258.0 %reduce-scatter.25.cloned.1.call-start = ((), (), s32[]{:S(2)}) async-start(), calls=%async_computation.28 | async-start | bytes 7962624 | tf_op jit(solution)/shard_map/cond/branch_1_fun/reduce_scatter | solution.py:293
  2540.5 266.2 %copy-start.223 = (f32[1536]{0:T(1024)S(1)}, f32[1536]{0:T(1024)}, u32[]{:S(2)}) copy-start(f32[1536]{0:T(1024)} %get-tuple-element.3071) | copy-start | bytes 18436
  2540.6 266.2 %copy-start.227 = (f32[768]{0:T(1024)S(1)}, f32[768]{0:T(1024)}, u32[]{:S(2)}) copy-start(f32[768]{0:T(1024)} %get-tuple-element.3067) | copy-start | bytes 9220
  2540.6 266.2 %copy-start.253 = (f32[768]{0:T(1024)S(1)}, f32[768]{0:T(1024)}, u32[]{:S(2)}) copy-start(f32[768]{0:T(1024)} %get-tuple-element.3073) | copy-start | bytes 9220
  2540.6 266.2 %copy-start.254 = (f32[768]{0:T(1024)S(1)}, f32[768]{0:T(1024)}, u32[]{:S(2)}) copy-start(f32[768]{0:T(1024)} %get-tuple-element.3069) | copy-start | bytes 9220
  2540.6 266.2 %copy-start.255 = (f32[768]{0:T(1024)S(1)}, f32[768]{0:T(1024)}, u32[]{:S(2)}) copy-start(f32[768]{0:T(1024)} %get-tuple-element.3068) | copy-start | bytes 9220
  2540.6 266.2 %copy-start.271 = (f32[3072]{0:T(1024)S(1)}, f32[3072]{0:T(1024)}, u32[]{:S(2)}) copy-start(f32[3072]{0:T(1024)} %get-tuple-element.3065) | copy-start | bytes 36868
  2540.6 266.2 %copy-start.289 = (f32[768]{0:T(1024)S(1)}, f32[768]{0:T(1024)}, u32[]{:S(2)}) copy-start(f32[768]{0:T(1024)} %get-tuple-element.3062) | copy-start | bytes 9220
  2540.6 266.2 %copy-start.290 = (f32[768]{0:T(1024)S(1)}, f32[768]{0:T(1024)}, u32[]{:S(2)}) copy-start(f32[768]{0:T(1024)} %get-tuple-element.3063) | copy-start | bytes 9220
  2540.7 110.0 %reduce-scatter.35.cloned.1.call-start = ((), (), s32[]{:S(2)}) async-start(), calls=%async_computation.33 | async-start | bytes 2654208 | tf_op jit(solution)/shard_map/cond/branch_1_fun/reduce_scatter | solution.py:295
  2542.5 261.4 %reduce-scatter.33.cloned.1.call-start = ((), (), s32[]{:S(2)}) async-start(), calls=%async_computation.32 | async-start | bytes 7962624 | tf_op jit(solution)/shard_map/cond/branch_1_fun/reduce_scatter | solution.py:293
  2806.8 265.6 %copy-start.224 = (f32[1536]{0:T(1024)S(1)}, f32[1536]{0:T(1024)}, u32[]{:S(2)}) copy-start(f32[1536]{0:T(1024)} %get-tuple-element.3084) | copy-start | bytes 18436
  2806.8 265.6 %copy-start.228 = (f32[768]{0:T(1024)S(1)}, f32[768]{0:T(1024)}, u32[]{:S(2)}) copy-start(f32[768]{0:T(1024)} %get-tuple-element.3080) | copy-start | bytes 9220
  2806.8 265.6 %copy-start.256 = (f32[768]{0:T(1024)S(1)}, f32[768]{0:T(1024)}, u32[]{:S(2)}) copy-start(f32[768]{0:T(1024)} %get-tuple-element.3086) | copy-start | bytes 9220
  2806.8 265.6 %copy-start.257 = (f32[768]{0:T(1024)S(1)}, f32[768]{0:T(1024)}, u32[]{:S(2)}) copy-start(f32[768]{0:T(1024)} %get-tuple-element.3082) | copy-start | bytes 9220
  2806.8 265.6 %copy-start.258 = (f32[768]{0:T(1024)S(1)}, f32[768]{0:T(1024)}, u32[]{:S(2)}) copy-start(f32[768]{0:T(1024)} %get-tuple-element.3081) | copy-start | bytes 9220
  2806.9 265.6 %copy-start.272 = (f32[3072]{0:T(1024)S(1)}, f32[3072]{0:T(1024)}, u32[]{:S(2)}) copy-start(f32[3072]{0:T(1024)} %get-tuple-element.3078) | copy-start | bytes 36868
  2806.9 265.6 %copy-start.291 = (f32[768]{0:T(1024)S(1)}, f32[768]{0:T(1024)}, u32[]{:S(2)}) copy-start(f32[768]{0:T(1024)} %get-tuple-element.3075) | copy-start | bytes 9220
  2806.9 265.6 %copy-start.292 = (f32[768]{0:T(1024)S(1)}, f32[768]{0:T(1024)}, u32[]{:S(2)}) copy-start(f32[768]{0:T(1024)} %get-tuple-element.3076) | copy-start | bytes 9220
  2806.9 109.9 %reduce-scatter.43.cloned.1.call-start = ((), (), s32[]{:S(2)}) async-start(), calls=%async_computation.37 | async-start | bytes 2654208 | tf_op jit(solution)/shard_map/cond/branch_1_fun/reduce_scatter | solution.py:295
  2808.7 261.0 %reduce-scatter.41.cloned.1.call-start = ((), (), s32[]{:S(2)}) async-start(), calls=%async_computation.36 | async-start | bytes 7962624 | tf_op jit(solution)/shard_map/cond/branch_1_fun/reduce_scatter | solution.py:293
  3073.0 110.1 %reduce-scatter.51.cloned.1.call-start = ((), (), s32[]{:S(2)}) async-start(), calls=%async_computation.41 | async-start | bytes 2654208 | tf_op jit(solution)/shard_map/cond/branch_1_fun/reduce_scatter | solution.py:295
  3076.4 259.9 %reduce-scatter.49.cloned.1.call-start = ((), (), s32[]{:S(2)}) async-start(), calls=%async_computation.40 | async-start | bytes 7962624 | tf_op jit(solution)/shard_map/cond/branch_1_fun/reduce_scatter | solution.py:293
  3383.5 74.1 %copy-start.390 = (s32[2]{0:T(128)S(1)}, s32[2]{0:T(128)}, u32[]{:S(2)}) copy-start(s32[2]{0:T(128)} %iota.94) | copy-start | bytes 28 | tf_op jit(solution)/shard_map/cond
  3681.2 258.6 %copy-start.127 = (f32[96,3072]{1,0:T(8,128)S(1)}, f32[96,3072]{1,0:T(8,128)}, u32[]{:S(2)}) copy-start(f32[96,3072]{1,0:T(8,128)} %get-tuple-element.3136) | copy-start | bytes 3538948
  3681.2 102.4 %reduce-scatter.59.cloned.1.call-start = ((), (), s32[]{:S(2)}) async-start(), calls=%async_computation.45 | async-start | bytes 2654208 | tf_op jit(solution)/shard_map/cond/branch_1_fun/reduce_scatter | solution.py:295
  3684.8 251.6 %reduce-scatter.57.cloned.1.call-start = ((), (), s32[]{:S(2)}) async-start(), calls=%async_computation.44 | async-start | bytes 7962624 | tf_op jit(solution)/shard_map/cond/branch_1_fun/reduce_scatter | solution.py:293
  3947.4 117.7 %all-to-all-start.1 = ((bf16[2,1,1024,768]{3,0,1,2:T(2,128)(2,1)}), bf16[2,1,1024,768]{3,0,1,2:T(2,128)(2,1)S(1)}, u32[]{:S(2)}, u32[]{:S(2)}) async-start(bf16[2,1,1024,768]{3,0,1,2:T(2,128)(2,1)} %copy.396), calls=%async_computation.21 | async-start | bytes 6291456 | tf_op jit(solution)/shard_map/all_to_all | solution.py:408
  3952.9 104.4 %all-reduce.63.cloned.1.call-start = ((), (), s32[]{:S(2)}) async-start(), calls=%async_computation.46 | async-start | bytes 7077888 | tf_op jit(solution)/shard_map/psum | solution.py:395
  (384 other events, 1991.0 us)
Sparse Core Ops, SparseCore 0:
  11.7 48.8 all-gather.22
  63.4 75.8 all-gather.20
  2282.0 102.6 reduce-scatter.26
  2388.2 149.1 reduce-scatter.24
  2545.7 104.9 reduce-scatter.34
  2654.6 149.1 reduce-scatter.32
  2811.8 104.9 reduce-scatter.42
  2920.5 149.1 reduce-scatter.40
  3078.3 104.7 reduce-scatter.50
  3187.1 149.1 reduce-scatter.48
  3686.1 97.4 reduce-scatter.58
  3787.1 149.1 reduce-scatter.56
Sparse Core Ops, SparseCore 1:
  3959.1 98.2 all-reduce.62
where the time goes:
time: 4090 us; the launch traced here: 4070 us
  waiting for transfers between devices  1200 us (29%)
  matrix products  1190 us (29%)
  other arithmetic  701 us (17%)
  local copies, waits for them, and re-layouts  389 us (10%)
  blocking collectives  273 us (7%)
  loops' own time  166 us (4%)
  starting transfers between devices  140 us (3%)
    reduce_scatter x5, waiting for transfers between devices, reduce_attn(): lax.psum_scatter(attn_terms[2], 'dp', scatter_dimension=0, tiled=True)  765 us
    dot_general x30, matrix products, block_scores(): jnp.einsum('cqhd,ckhd->chqk', query_part, key_heads, preferred_element_ty...  308 us
    reduce_scatter x5, waiting for transfers between devices, reduce_attn(): lax.psum_scatter(attn_terms[4], 'dp', scatter_dimension=0, tiled=True)  295 us
    reduce_sum x20, other arithmetic, one_block(): jnp.sum(jnp.exp(scores - row_max), axis=-1, keepdims=True)  228 us
    dot_general x20, matrix products, one_block(): jnp.einsum('chqk,ckhd->cqhd', probs_low, value_heads, preferred_element_t...  217 us
    convert_element_type x10, other arithmetic, one_block(): grad_scores = (probs_full * (grad_probs - inner)).astype(jnp.bfloat16)  214 us
    cond x5, blocking collectives  182 us
    dot_general x10, matrix products, one_block(): jnp.einsum('cqhd,ckhd->chqk', grad_part, value_heads, preferred_element_t...  175 us
  transfers between devices with their start and end apart: 23, of which 19 were waited for; matrix products, arithmetic and copies ran while one was open for 13% of the time, Pallas kernels for 0%

commit v1 on v0

v1 whole, which is shorter than its diff:
```python
from functools import partial
import math

import jax
import jax.numpy as jnp
from jax import lax
from jax.experimental import pallas as pl
from jax.experimental.pallas import tpu as pltpu
from jax.sharding import PartitionSpec as P

HEAD = 64
PAIR = 2 * HEAD
NORM_EPS = 1e-05
MASK_FLOOR = -1e30
F32 = jnp.float32
BF16 = jnp.bfloat16


def nt_dot(left, right):
    return lax.dot_general(left, right, (((1,), (1,)), ((), ())), preferred_element_type=F32)


def nn_dot(left, right):
    return jnp.dot(left, right, preferred_element_type=F32)


def tn_dot(left, right):
    return lax.dot_general(left, right, (((0,), (0,)), ((), ())), preferred_element_type=F32)


def head_lanes(block, head):
    lane = lax.broadcasted_iota(jnp.int32, block.shape, 1)
    keep = (lane < HEAD) if head == 0 else (lane >= HEAD)
    return jnp.where(keep, block, jnp.zeros_like(block))


def attend_kernel(lens_ref, q_ref, ko_ref, kp_ref, vo_ref, vp_ref, o_ref, prob_ref):
    rows = q_ref.shape[0]
    score_scale = 1.0 / math.sqrt(HEAD)
    query_pair = q_ref[...] * jnp.asarray(score_scale, BF16)
    value_t = [vo_ref[...].T, vp_ref[...].T]
    mixed = []
    for head in range(2):
        query = head_lanes(query_pair, head)
        scores = []
        for part, key_ref in enumerate((ko_ref, kp_ref)):
            part_scores = nt_dot(key_ref[...], query)
            key_row = lax.broadcasted_iota(jnp.int32, part_scores.shape, 0)
            scores.append(jnp.where(key_row < lens_ref[part], part_scores, MASK_FLOOR))
        row_max = jnp.maximum(
            jnp.max(scores[0], axis=0, keepdims=True), jnp.max(scores[1], axis=0, keepdims=True)
        )
        raised = [jnp.exp(item - row_max) for item in scores]
        total = jnp.sum(raised[0], axis=0, keepdims=True) + jnp.sum(
            raised[1], axis=0, keepdims=True
        )
        inverse = 1.0 / total
        head_out = jnp.zeros((HEAD, rows), F32)
        for part in range(2):
            prob = (raised[part] * inverse).astype(BF16)
            prob_ref[head, part * rows : (part + 1) * rows, :] = prob
            head_out = head_out + nn_dot(
                value_t[part][head * HEAD : (head + 1) * HEAD, :], prob
            )
        mixed.append(head_out)
    o_ref[...] = jnp.concatenate(mixed, axis=0).T.astype(BF16)


def attend(queries, key_own, key_peer, value_own, value_peer, lens):
    rows, width = queries.shape
    pairs = width // PAIR
    block = pl.BlockSpec((rows, PAIR), lambda p, lens: (0, p))
    return pl.pallas_call(
        attend_kernel,
        grid_spec=pltpu.PrefetchScalarGridSpec(
            num_scalar_prefetch=1,
            grid=(pairs,),
            in_specs=[block] * 5,
            out_specs=[
                block,
                pl.BlockSpec((2, 2 * rows, rows), lambda p, lens: (p, 0, 0)),
            ],
        ),
        out_shape=[
            jax.ShapeDtypeStruct((rows, width), BF16),
            jax.ShapeDtypeStruct((2 * pairs, 2 * rows, rows), BF16),
        ],
        compiler_params=pltpu.CompilerParams(vmem_limit_bytes=48 << 20),
        cost_estimate=pl.CostEstimate(
            flops=2 * 2 * rows * 2 * rows * width * 4,
            transcendentals=2 * pairs * 2 * rows * rows,
            bytes_accessed=2 * pairs * 2 * rows * rows * 2 + 6 * rows * width * 2,
        ),
    )(lens, queries, key_own, key_peer, value_own, value_peer)


def attend_back_kernel(
    q_ref, ko_ref, kp_ref, vo_ref, vp_ref, o_ref, go_ref, prob_ref,
    gq_ref, gko_ref, gkp_ref, gvo_ref, gvp_ref,
):
    rows = q_ref.shape[0]
    score_scale = 1.0 / math.sqrt(HEAD)
    query_pair = q_ref[...] * jnp.asarray(score_scale, BF16)
    grad_pair = go_ref[...]
    inner = (o_ref[...].astype(F32) * grad_pair.astype(F32)).T
    key_refs = (ko_ref, kp_ref)
    value_refs = (vo_ref, vp_ref)
    key_t = [ref[...].T for ref in key_refs]
    grad_key = [None, None]
    grad_value = [None, None]
    grad_query = []
    for head in range(2):
        query = head_lanes(query_pair, head)
        grad_out = head_lanes(grad_pair, head)
        inner_row = jnp.sum(inner[head * HEAD : (head + 1) * HEAD, :], axis=0, keepdims=True)
        head_query = jnp.zeros((HEAD, rows), F32)
        for part in range(2):
            prob = prob_ref[head, part * rows : (part + 1) * rows, :]
            grad_prob = nt_dot(value_refs[part][...], grad_out)
            grad_score = (prob.astype(F32) * (grad_prob - inner_row)).astype(BF16)
            value_term = nn_dot(prob, grad_out)
            key_term = nn_dot(grad_score, query)
            grad_value[part] = value_term if head == 0 else grad_value[part] + value_term
            grad_key[part] = key_term if head == 0 else grad_key[part] + key_term
            head_query = head_query + nn_dot(
                key_t[part][head * HEAD : (head + 1) * HEAD, :], grad_score
            )
        grad_query.append(head_query * score_scale)
    gq_ref[...] = jnp.concatenate(grad_query, axis=0).T.astype(BF16)
    gko_ref[...] = grad_key[0]
    gkp_ref[...] = grad_key[1].astype(BF16)
    gvo_ref[...] = grad_value[0]
    gvp_ref[...] = grad_value[1].astype(BF16)


def attend_back(queries, key_own, key_peer, value_own, value_peer, mixed, grad_mixed, probs):
    rows, width = queries.shape
    pairs = width // PAIR
    block = pl.BlockSpec((rows, PAIR), lambda p: (0, p))
    low = jax.ShapeDtypeStruct((rows, width), BF16)
    full = jax.ShapeDtypeStruct((rows, width), F32)
    return pl.pallas_call(
        attend_back_kernel,
        grid=(pairs,),
        in_specs=[block] * 7 + [pl.BlockSpec((2, 2 * rows, rows), lambda p: (p, 0, 0))],
        out_specs=[block] * 5,
        out_shape=[low, full, low, full, low],
        compiler_params=pltpu.CompilerParams(vmem_limit_bytes=48 << 20),
        cost_estimate=pl.CostEstimate(
            flops=2 * 2 * rows * 2 * rows * width * 8,
            transcendentals=0,
            bytes_accessed=2 * pairs * 2 * rows * rows * 2 + 14 * rows * width * 2,
        ),
    )(queries, key_own, key_peer, value_own, value_peer, mixed, grad_mixed, probs)


def norm_stats(stream):
    center = stream - jnp.mean(stream, axis=-1, keepdims=True)
    spread = jnp.mean(center * center, axis=-1, keepdims=True)
    return center, lax.rsqrt(spread + NORM_EPS)


def norm_rows(stream_low, gain, shift):
    center, root = norm_stats(stream_low.astype(F32))
    return (center * root * gain.astype(F32) + shift.astype(F32)).astype(BF16)


def norm_back(stream_low, gain, grad_normed, grad_low):
    center, root = norm_stats(stream_low.astype(F32))
    unit = center * root
    grad_gain = jnp.sum(grad_normed * unit, axis=0)
    grad_shift = jnp.sum(grad_normed, axis=0)
    grad_unit = grad_normed * gain.astype(F32)
    grad_stream = root * (
        grad_unit
        - jnp.mean(grad_unit, axis=-1, keepdims=True)
        - unit * jnp.mean(grad_unit * unit, axis=-1, keepdims=True)
    )
    return (grad_low.astype(F32) + grad_stream).astype(BF16), grad_gain, grad_shift


def gelu_value(up_proj):
    return 0.5 * up_proj * (1.0 + lax.erf(up_proj * math.sqrt(0.5)))


def gelu_slope(up_proj):
    bell = jnp.exp(-0.5 * up_proj * up_proj) * (1.0 / math.sqrt(2.0 * math.pi))
    return 0.5 * (1.0 + lax.erf(up_proj * math.sqrt(0.5))) + up_proj * bell


def local(
    tokens, lengths, cotangent, attn_gain, attn_shift, qkv_weight, qv_bias, out_weight, out_bias,
    ffn_gain, ffn_shift, up_weight, up_bias, down_weight, down_bias,
):
    layers, _, width3 = qkv_weight.shape
    width = width3 // 3
    micro_count, cell_count, seq_len, _ = tokens.shape
    section_id = lax.axis_index("section")
    section_count = lax.axis_size("section")
    share = section_count // micro_count
    assert cell_count == 1 and share == 2
    cell = section_id // share
    half = section_id % share
    rows = seq_len // share
    swap = [(i, i ^ 1) for i in range(section_count)]

    def to_peer(block):
        return lax.ppermute(block, "section", swap)

    def mine(whole):
        return lax.dynamic_slice(
            whole, (cell, 0, half * rows, 0), (1, 1, rows, width)
        ).reshape(rows, width)

    stream = mine(tokens)
    grad = mine(cotangent)
    length = lax.dynamic_slice(lengths, (cell, 0), (1, 1)).reshape(())
    lens = jnp.stack([length - half * rows, length - (1 - half) * rows])

    def whole(shard):
        return lax.all_gather(shard, "dp", axis=0, tiled=True)

    vec = [
        [whole(item[l]) for item in (attn_gain, attn_shift, qv_bias, out_bias, ffn_gain, ffn_shift, up_bias, down_bias)]
        for l in range(layers)
    ]
    mats = [[whole(item[l]) for item in (qkv_weight, out_weight, up_weight, down_weight)] for l in range(layers)]

    saved = []
    for l in range(layers):
        a_gain, a_shift, qv_b, out_b, f_gain, f_shift, up_b, down_b = vec[l]
        qkv_w, out_w, up_w, down_w = mats[l]
        attn_in = stream
        normed = norm_rows(stream, a_gain, a_shift)
        qb = jnp.concatenate([qv_b[:width], jnp.zeros((width,), BF16), qv_b[width:]]).astype(F32)
        proj = (nn_dot(normed, qkv_w) + qb).astype(BF16)
        queries, key_own, value_own = proj[:, :width], proj[:, width : 2 * width], proj[:, 2 * width :]
        key_peer, value_peer = to_peer(key_own), to_peer(value_own)
        mixed, probs = attend(queries, key_own, key_peer, value_own, value_peer, lens)
        stream = (attn_in.astype(F32) + nn_dot(mixed, out_w) + out_b.astype(F32)).astype(BF16)
        ffn_in = stream
        normed2 = norm_rows(stream, f_gain, f_shift)
        up_proj = nn_dot(normed2, up_w) + up_b.astype(F32)
        hidden = gelu_value(up_proj).astype(BF16)
        stream = (ffn_in.astype(F32) + nn_dot(hidden, down_w) + down_b.astype(F32)).astype(BF16)
        saved.append(
            (attn_in, normed, queries, key_own, key_peer, value_own, value_peer, mixed, probs,
             ffn_in, normed2, up_proj, hidden)
        )

    def redistribute(block):
        quarter = rows // 2
        route_a = [(2 * c + h, 2 * h + c) for c in range(2) for h in range(2)]
        route_b = [(2 * c + h, 2 * h + 1 - c) for c in range(2) for h in range(2)]
        low_half, high_half = block[:quarter], block[quarter:]
        first = cell == 0
        send_a = jnp.where(first, low_half, high_half)
        send_b = jnp.where(first, high_half, low_half)
        got_a = lax.ppermute(send_a, "section", route_a)
        got_b = lax.ppermute(send_b, "section", route_b)
        even = section_id % 2 == 0
        return jnp.stack([jnp.where(even, got_a, got_b), jnp.where(even, got_b, got_a)])[:, None]

    encoded = redistribute(stream)

    def scatter(term):
        shard = lax.psum_scatter(term.astype(BF16), "dp", scatter_dimension=0, tiled=True)
        return lax.psum(shard, "section").astype(F32)

    grads = [None] * layers
    for l in reversed(range(layers)):
        a_gain, a_shift, qv_b, out_b, f_gain, f_shift, up_b, down_b = vec[l]
        qkv_w, out_w, up_w, down_w = mats[l]
        (attn_in, normed, queries, key_own, key_peer, value_own, value_peer, mixed, probs,
         ffn_in, normed2, up_proj, hidden) = saved[l]
        g_down_b = jnp.sum(grad.astype(F32), axis=0)
        g_down = tn_dot(hidden, grad)
        grad_up = (nt_dot(grad, down_w) * gelu_slope(up_proj)).astype(BF16)
        g_up_b = jnp.sum(grad_up.astype(F32), axis=0)
        g_up = tn_dot(normed2, grad_up)
        grad, g_f_gain, g_f_shift = norm_back(ffn_in, f_gain, nt_dot(grad_up, up_w), grad)
        g_out_b = jnp.sum(grad.astype(F32), axis=0)
        g_out = tn_dot(mixed, grad)
        grad_mixed = nt_dot(grad, out_w).astype(BF16)
        grad_q, gk_own, gk_peer, gv_own, gv_peer = attend_back(
            queries, key_own, key_peer, value_own, value_peer, mixed, grad_mixed, probs
        )
        grad_k = (gk_own + to_peer(gk_peer).astype(F32)).astype(BF16)
        grad_v = (gv_own + to_peer(gv_peer).astype(F32)).astype(BF16)
        g_qv_b = jnp.concatenate(
            [jnp.sum(grad_q.astype(F32), axis=0), jnp.sum(grad_v.astype(F32), axis=0)]
        )
        grad_proj = jnp.concatenate([grad_q, grad_k, grad_v], axis=1)
        g_qkv = tn_dot(normed, grad_proj)
        grad, g_a_gain, g_a_shift = norm_back(attn_in, a_gain, nt_dot(grad_proj, qkv_w), grad)
        grads[l] = [
            scatter(item)
            for item in (g_a_gain, g_a_shift, g_qkv, g_qv_b, g_out, g_out_b, g_f_gain, g_f_shift,
                         g_up, g_up_b, g_down, g_down_b)
        ]
    grad_tokens = redistribute(grad)
    return (encoded, grad_tokens) + tuple(jnp.stack(pair) for pair in zip(*grads))


def solution(mesh):
    flat, rows4 = P(None, "dp"), P(None, "dp", None, None)
    mat, spread = P(None, "dp", None), P(None, "dp", "section", None)
    in_specs = (
        rows4, flat, rows4, flat, flat, mat, flat, mat, flat, flat, flat, mat, flat, mat, flat,
    )
    out_specs = (
        spread, spread, flat, flat, mat, flat, mat, flat, flat, flat, mat, flat, mat, flat,
    )
    return jax.shard_map(local, mesh=mesh, in_specs=in_specs, out_specs=out_specs, check_vma=False)
```

time: 4090 us -> 1380 us (0.34)
  matrix products: 1190 us -> 117 us
  other arithmetic: 701 us -> 28 us
  local copies, waits for them, and re-layouts: 389 us -> 27.5 us
  waiting for transfers between devices: 1200 us -> 959 us
  loops' own time: 166 us -> 0 us
  blocking collectives: 273 us -> 139 us
  starting transfers between devices: 140 us -> 8.8 us
  Pallas kernels: 0 us -> 68.9 us
    dot_general x125 -> x24, matrix products: 1190 us -> 117 us  [the longest x8 41.4 us: nn_dot(): return jnp.dot(left, right, preferred_element_type=F32)]
    reduce_scatter x10 -> x8, waiting for transfers between devices: 1060 us -> 537 us  [scatter(): lax.psum_scatter(term.astype(BF16), 'dp', scatter_dimension=0, tiled=True)]
    all_gather x2 -> x8, waiting for transfers between devices: 82.6 us -> 357 us  [whole(): return lax.all_gather(shard, 'dp', axis=0, tiled=True)]
    reduce_sum x55 -> x13, other arithmetic: 282 us -> 9.92 us  [the longest x2 3.3 us: local(): jnp.sum(grad_v.astype(F32), axis=0)]
    convert_element_type x62 -> x18, other arithmetic: 265 us -> 4.55 us  [the longest x1 2.43 us: norm_back(): (grad_low.astype(F32) + grad_stream).astype(BF16)]
    cond x5 -> x0, blocking collectives: 182 us -> none
    all_to_all x2 -> x0, starting transfers between devices: 119 us -> none  [the longest x1 114 us: local(): lax.all_to_all(out_store, 'section', split_axis=2, concat_axis=0, tiled=T...]
    another operation x23 -> x0, loops' own time: 117 us -> none  [the longest x10 79.7 us: attend(): block_outs, log_totals = lax.map(one_block, jnp.arange(block_count))]
  transfers between devices with their start and end apart: 23 -> 29, of which waited for: 19 -> 15; matrix products, arithmetic and copies ran while one was open for 13% -> 10% of each run, Pallas kernels for 0% -> 4%
where the time goes in v1:
time: 1380 us; the launch traced here: 1370 us
  waiting for transfers between devices  959 us (69%)
  blocking collectives  139 us (10%)
  matrix products  117 us (8%)
  Pallas kernels  68.9 us (5%)
  other arithmetic  28 us (2%)
  local copies, waits for them, and re-layouts  27.5 us (2%)
  between operations  20.2 us (1%)
    reduce_scatter x8, waiting for transfers between devices, scatter(): lax.psum_scatter(term.astype(BF16), 'dp', scatter_dimension=0, tiled=True)  537 us
    all_gather x8, waiting for transfers between devices, whole(): return lax.all_gather(shard, 'dp', axis=0, tiled=True)  357 us
    unnamed x2, blocking collectives  74.7 us
    psum x1, waiting for transfers between devices, scatter(): return lax.psum(shard, 'section').astype(F32)  60.3 us
    all_gather x2, blocking collectives, whole(): return lax.all_gather(shard, 'dp', axis=0, tiled=True)  52.6 us
    dot_general x8, matrix products, nn_dot(): return jnp.dot(left, right, preferred_element_type=F32)  41.4 us
    dot_general x8, matrix products, tn_dot(): lax.dot_general(left, right, (((0,), (0,)), ((), ())), preferred_element_...  41 us
    pallas_call x2, Pallas kernels, attend_back(): pl.pallas_call(attend_back_kernel, grid=(pairs,), in_specs=[block] * 7 +...  35.4 us
  transfers between devices with their start and end apart: 29, of which 15 were waited for; matrix products, arithmetic and copies ran while one was open for 10% of the time, Pallas kernels for 4%

profile of v1, /device:TPU:0, one launch (start us, length us, event | category | flops | bytes accessed | tf_op | source)
XLA Modules:
  0.0 1368.3 jit_solution(12723560706781215240)
XLA Ops:
  7.3 2.2 fusion.146
  10.4 1.1 fusion.145
  11.6 2.5 fusion.144
  21.6 39.7 %all-reduce.31 = (bf16[1536]{0:T(1024)(128)(2,1)S(1)}, bf16[768]{0:T(1024)(128)(2,1)S(1)}, bf16[768]{0:T(1024)(128)(2,1)S(1)}, bf16[768]{0:T(1024)(128)(2,1)S(1)...) all-reduce(bf16[1536]{0:T(1024)(128)(2,1)S(1)} %dynamic-update-slic, ...), channel_id=5, replica_groups=mesh['dp'=8,'section'=4] {'dp'}, use_global_device_ids=true, to_apply=%add.2 | all-reduce | flops 11520 | bytes 46080
  62.0 17.4 %all-gather.33.cloned.1.call-done = bf16[1,768,2304]{2,1,0:T(8,128)(2,1)} async-done(((bf16[1,96,2304]{2,1,0:T(8,128)(2,1)}), bf16[1,768,2304]{2,1,0:T(8,128)(2,1)}) %all-gather.33.cloned.1.call-update) | async-done | bytes 3538960 | tf_op jit(solution)/shard_map/all_gather | solution.py:221
  79.4 4.2 fusion.26
  86.4 26.2 %all-gather.9 = bf16[1,3072]{1,0:T(2,128)(2,1)S(1)} all-gather(bf16[1,384]{1,0:T(2,128)(2,1)S(1)} %get-tuple-element.181), channel_id=11, replica_groups=mesh['dp'=8,'section'=4] {'dp'}, dimensions={1}, use_global_device_ids=true | all-gather | bytes 6912 | tf_op jit(solution)/shard_map/all_gather | solution.py:221
  112.7 17.0 %shard_map.254 = (bf16[512,768]{1,0:T(8,128)(2,1)S(1)}, bf16[12,1024,512]{2,1,0:T(8,128)(2,1)}) custom-call(s32[2]{0:T(128)S(1)} %pad_add_fusion.lens_ref, bf16[512,768]{1,0:T(8,128)(2,1)S(1)} %get-tuple-element.161.q_ref, bf16[512,768]{1,0:T(8,128)(2,1)S(1)} %get-tuple-element.160.ko_ref, bf16[512,768]{1,0:T(8,128)(2,1)S(1)} %collective-permute-done.kp_ref, ...), custom_call_target="tpu_custom_call" | custom-call | flops 6442450944 | bytes 17301504 | tf_op jit(solution)/shard_map/pallas_call | solution.py:73
  130.6 2.8 convert_reduce_fusion.2
  133.8 69.6 %all-gather.37.cloned.1.call-done = bf16[1,768,3072]{2,1,0:T(8,128)(2,1)} async-done(((bf16[1,96,3072]{2,1,0:T(8,128)(2,1)}), bf16[1,768,3072]{2,1,0:T(8,128)(2,1)}) %all-gather.37.cloned.1.call-update) | async-done | bytes 4718608 | tf_op jit(solution)/shard_map/all_gather | solution.py:221
  203.4 8.2 multiply_convert_fusion.1
  211.5 72.5 %all-gather.39.cloned.1.call-done = bf16[1,3072,768]{2,1,0:T(8,128)(2,1)} async-done(((bf16[1,384,768]{2,1,0:T(8,128)(2,1)}), bf16[1,3072,768]{2,1,0:T(8,128)(2,1)}) %all-gather.39.cloned.1.call-update) | async-done | bytes 4718608 | tf_op jit(solution)/shard_map/all_gather | solution.py:221
  284.0 6.0 convert_reduce_fusion.1
  291.3 58.7 %all-gather.41.cloned.1.call-done = bf16[1,768,2304]{2,1,0:T(8,128)(2,1)} async-done(((bf16[1,96,2304]{2,1,0:T(8,128)(2,1)}), bf16[1,768,2304]{2,1,0:T(8,128)(2,1)}) %all-gather.41.cloned.1.call-update) | async-done | bytes 3538960 | tf_op jit(solution)/shard_map/all_gather | solution.py:221
  350.0 4.4 fusion.27
  355.2 26.4 %all-gather.21 = bf16[1,3072]{1,0:T(2,128)(2,1)S(1)} all-gather(bf16[1,384]{1,0:T(2,128)(2,1)S(1)} %get-tuple-element.180), channel_id=23, replica_groups=mesh['dp'=8,'section'=4] {'dp'}, dimensions={1}, use_global_device_ids=true | all-gather | bytes 6912 | tf_op jit(solution)/shard_map/all_gather | solution.py:221
  381.6 16.5 %shard_map.255 = (bf16[512,768]{1,0:T(8,128)(2,1)S(1)}, bf16[12,1024,512]{2,1,0:T(8,128)(2,1)}) custom-call(s32[2]{0:T(128)S(1)} %pad_add_fusion.lens_ref, bf16[512,768]{1,0:T(8,128)(2,1)S(1)} %get-tuple-element.158.q_ref, bf16[512,768]{1,0:T(8,128)(2,1)S(1)} %get-tuple-element.157.ko_ref, bf16[512,768]{1,0:T(8,128)(2,1)S(1)} %collective-permute-done.2.kp_ref, ...), custom_call_target="tpu_custom_call" | custom-call | flops 6442450944 | bytes 17301504 | tf_op jit(solution)/shard_map/pallas_call | solution.py:73
  402.7 2.6 convert_reduce_fusion
  406.6 66.5 %all-gather.45.cloned.1.call-done = bf16[1,768,3072]{2,1,0:T(8,128)(2,1)} async-done(((bf16[1,96,3072]{2,1,0:T(8,128)(2,1)}), bf16[1,768,3072]{2,1,0:T(8,128)(2,1)}) %all-gather.45.cloned.1.call-update) | async-done | bytes 4718608 | tf_op jit(solution)/shard_map/all_gather | solution.py:221
  473.1 8.3 multiply_convert_fusion
  481.4 72.0 %all-gather.47.cloned.1.call-done = bf16[1,3072,768]{2,1,0:T(8,128)(2,1)} async-done(((bf16[1,384,768]{2,1,0:T(8,128)(2,1)}), bf16[1,3072,768]{2,1,0:T(8,128)(2,1)}) %all-gather.47.cloned.1.call-update) | async-done | bytes 4718608 | tf_op jit(solution)/shard_map/all_gather | solution.py:221
  553.4 7.5 fusion.150
  560.8 3.0 fusion.67
  563.9 2.0 fusion.138
  565.9 1.7 convolution_convert_fusion.9.go_ref
  568.1 17.7 %shard_map.256 = (bf16[512,768]{1,0:T(8,128)(2,1)S(1)}, f32[512,768]{1,0:T(8,128)}, bf16[512,768]{1,0:T(8,128)(2,1)}, f32[512,768]{1,0:T(8,128)}, bf16[512,768]{1,0:T(8,128)(2,1)}) custom-call(bf16[512,768]{1,0:T(8,128)(2,1)S(1)} %copy-done.5, bf16[512,768]{1,0:T(8,128)(2,1)S(1)} %copy-done.3, bf16[512,768]{1,0:T(8,128)(2,1)S(1)} %copy-done.13, ...), custom_call_target="tpu_custom_call" | custom-call | flops 12884901888 | bytes 23592960 | tf_op jit(solution)/shard_map/pallas_call | solution.py:142
  587.2 1.8 convolution_convert_fusion.6
  589.1 1.0 collective-permute-done.6
  590.1 1.9 add_convert_fusion.3
  593.0 1.5 fusion.141
  594.6 5.4 fusion.76
  600.9 4.6 fusion.151
  605.5 3.0 fusion.85
  610.2 1.8 convolution_convert_fusion.7
  612.4 5.6 convolution_convert_fusion.4
  618.0 3.3 convolution_convert_fusion.8.go_ref
  621.3 17.6 %shard_map.257 = (bf16[512,768]{1,0:T(8,128)(2,1)S(1)}, f32[512,768]{1,0:T(8,128)}, bf16[512,768]{1,0:T(8,128)(2,1)S(1)}, f32[512,768]{1,0:T(8,128)}, bf16[512,768]{1,0:T(8,128)(2,1)S(1)}) custom-call(bf16[512,768]{1,0:T(8,128)(2,1)S(1)} %get-tuple-element.161.q_ref, bf16[512,768]{1,0:T(8,128)(2,1)S(1)} %get-tuple-element.160.ko_ref, ...), custom_call_target="tpu_custom_call" | custom-call | flops 12884901888 | bytes 23592960 | tf_op jit(solution)/shard_map/pallas_call | solution.py:142
  639.5 1.8 collective-permute-done.9
  641.3 1.8 fusion.140
  644.2 5.1 convolution_convert_fusion.5
  649.4 1.1 copy-done.23
  650.5 6.5 convolution_convert_fusion.2
  657.0 6.9 convolution_convert_fusion
  665.1 6.5 convolution_convert_fusion.3
  671.7 1.1 copy-done.30
  672.7 6.7 convolution_convert_fusion.1
  681.8 1.3 dynamic-slice_reduce_fusion
  683.5 6.1 fusion.94
  689.6 35.0 %all-reduce.30 = (bf16[768]{0:T(1024)(128)(2,1)S(1)}, bf16[768]{0:T(1024)(128)(2,1)S(1)}, bf16[768]{0:T(1024)(128)(2,1)S(1)}, bf16[768]{0:T(1024)(128)(2,1)S(1)}...) all-reduce(bf16[768]{0:T(1024)(128)(2,1)S(1)} %dynamic-update-slice, ...), channel_id=25, replica_groups=mesh['dp'=8,'section'=4] {'dp'}, use_global_device_ids=true, to_apply=%add.13 | all-reduce | flops 19200 | bytes 76800
  725.0 2.4 fusion.93
  728.2 2.8 collective-permute-start.11
  731.0 5.0 fusion.103
  736.7 1.3 collective-permute-start.5
  738.9 60.8 %reduce-scatter.11.cloned.1.call-done = bf16[96,2304]{1,0:T(8,128)(2,1)} async-done(((bf16[768,2304]{1,0:T(8,128)(2,1)}), bf16[96,2304]{1,0:T(8,128)(2,1)}) %reduce-scatter.11.cloned.1.call-update) | async-done | bytes 442384 | tf_op jit(solution)/shard_map/reduce_scatter | solution.py:267
  799.7 82.2 %reduce-scatter.9.cloned.1.call-done = bf16[96,2304]{1,0:T(8,128)(2,1)} async-done(((bf16[768,2304]{1,0:T(8,128)(2,1)}), bf16[96,2304]{1,0:T(8,128)(2,1)}) %reduce-scatter.9.cloned.1.call-update) | async-done | bytes 442384 | tf_op jit(solution)/shard_map/reduce_scatter | solution.py:267
  881.9 98.5 %reduce-scatter.19.cloned.1.call-done = bf16[96,3072]{1,0:T(8,128)(2,1)} async-done(((bf16[768,3072]{1,0:T(8,128)(2,1)}), bf16[96,3072]{1,0:T(8,128)(2,1)}) %reduce-scatter.19.cloned.1.call-update) | async-done | bytes 589840 | tf_op jit(solution)/shard_map/reduce_scatter | solution.py:267
  980.4 98.6 %reduce-scatter.23.cloned.1.call-done = bf16[384,768]{1,0:T(8,128)(2,1)} async-done(((bf16[3072,768]{1,0:T(8,128)(2,1)}), bf16[384,768]{1,0:T(8,128)(2,1)}) %reduce-scatter.23.cloned.1.call-update) | async-done | bytes 589840 | tf_op jit(solution)/shard_map/reduce_scatter | solution.py:267
  1078.9 98.5 %reduce-scatter.17.cloned.1.call-done = bf16[96,3072]{1,0:T(8,128)(2,1)} async-done(((bf16[768,3072]{1,0:T(8,128)(2,1)}), bf16[96,3072]{1,0:T(8,128)(2,1)}) %reduce-scatter.17.cloned.1.call-update) | async-done | bytes 589840 | tf_op jit(solution)/shard_map/reduce_scatter | solution.py:267
  1177.5 98.5 %reduce-scatter.21.cloned.1.call-done = bf16[384,768]{1,0:T(8,128)(2,1)} async-done(((bf16[3072,768]{1,0:T(8,128)(2,1)}), bf16[384,768]{1,0:T(8,128)(2,1)}) %reduce-scatter.21.cloned.1.call-update) | async-done | bytes 589840 | tf_op jit(solution)/shard_map/reduce_scatter | solution.py:267
  1276.1 11.6 all-reduce.32
  1294.4 60.3 %all-reduce.36.cloned.1.call-done = (bf16[1,96,2304]{2,1,0:T(8,128)(2,1)}, bf16[1,96,2304]{2,1,0:T(8,128)(2,1)}, bf16[1,96,768]{2,1,0:T(8,128)(2,1)}, bf16[1,96,...) async-done(((bf16[1,96,2304]{2,1,0:T(8,128)(2,1)}, ...) | async-done | bytes 3538960 | tf_op jit(solution)/shard_map/psum | solution.py:268
  1354.7 2.9 maximum_convert_fusion.1
  1357.6 1.6 maximum_convert_fusion
  1360.0 1.3 maximum_convert_fusion.2
  (323 shorter events, 37.7 us)
Async XLA Ops:
  7.2 77.3 %copy-start = (s32[2,1]{0,1:T(1,128)S(1)}, s32[2,1]{0,1:T(1,128)}, u32[]{:S(2)}) copy-start(s32[2,1]{0,1:T(1,128)} %param.16) | copy-start | bytes 28
  7.2 3.2 copy-start.36
  7.2 72.2 %all-gather.33.cloned.1.call-start = ((), (), s32[]{:S(2)}) async-start(), calls=%async_computation.16 | async-start | bytes 3981312 | tf_op jit(solution)/shard_map/all_gather | solution.py:221
  9.5 121.1 %all-gather.35.cloned.1.call-start = ((), (), s32[]{:S(2)}) async-start(), calls=%async_computation.17 | async-start | bytes 1327104 | tf_op jit(solution)/shard_map/all_gather | solution.py:221
  10.3 193.1 %all-gather.37.cloned.1.call-start = ((), (), s32[]{:S(2)}) async-start(), calls=%async_computation.18 | async-start | bytes 5308416 | tf_op jit(solution)/shard_map/all_gather | solution.py:221
  11.5 4.7 copy-start.51
  11.5 6.5 copy-start.52
  11.5 6.8 copy-start.53
  11.5 7.0 copy-start.54
  11.5 7.3 copy-start.55
  11.5 7.5 copy-start.56
  11.6 8.4 copy-start.57
  11.6 9.5 copy-start.50
  11.6 272.5 %all-gather.39.cloned.1.call-start = ((), (), s32[]{:S(2)}) async-start(), calls=%async_computation.19 | async-start | bytes 5308416 | tf_op jit(solution)/shard_map/all_gather | solution.py:221
  11.6 49.7 %copy-start.33 = (bf16[2,1,1024,768]{3,2,1,0:T(8,128)(2,1)S(1)}, bf16[2,1,1024,768]{3,2,1,0:T(8,128)(2,1)}, u32[]{:S(2)}) copy-start(bf16[2,1,1024,768]{3,2,1,0:T(8,128)(2,1)} %param.15) | copy-start | bytes 9437188
  14.2 335.9 %all-gather.41.cloned.1.call-start = ((), (), s32[]{:S(2)}) async-start(), calls=%async_computation.20 | async-start | bytes 3981312 | tf_op jit(solution)/shard_map/all_gather | solution.py:221
  14.7 387.9 %all-gather.43.cloned.1.call-start = ((), (), s32[]{:S(2)}) async-start(), calls=%async_computation.21 | async-start | bytes 1327104 | tf_op jit(solution)/shard_map/all_gather | solution.py:221
  15.3 457.8 %all-gather.45.cloned.1.call-start = ((), (), s32[]{:S(2)}) async-start(), calls=%async_computation.22 | async-start | bytes 5308416 | tf_op jit(solution)/shard_map/all_gather | solution.py:221
  16.1 537.3 %all-gather.47.cloned.1.call-start = ((), (), s32[]{:S(2)}) async-start(), calls=%async_computation.23 | async-start | bytes 5308416 | tf_op jit(solution)/shard_map/all_gather | solution.py:221
  83.8 28.9 %collective-permute-start = (bf16[512,768]{1,0:T(8,128)(2,1)S(1)}, bf16[512,768]{1,0:T(8,128)(2,1)S(1)}, u32[]{:S(2)}, u32[]{:S(2)}) collective-permute-start(bf16[512,768]{1,0:T(8,128)(2,1)S(1)} %get-tuple-element.160.ko_ref), channel_id=1, source_target_pairs={{0,1},{1,0},{2,3},{3,2},{4,5},{5,4},{6,7},{7,6},{8,9},{9,8},{10,11... | collective-permute-start | bytes 2359304 | tf_op jit(solution)/shard_map/ppermute | solution.py:208
  83.9 28.9 %collective-permute-start.1 = (bf16[512,768]{1,0:T(8,128)(2,1)S(1)}, bf16[512,768]{1,0:T(8,128)(2,1)}, u32[]{:S(2)}, u32[]{:S(2)}) collective-permute-start(bf16[512,768]{1,0:T(8,128)(2,1)S(1)} %get-tuple-element.159.vo_ref), channel_id=1, source_target_pairs={{0,1},{1,0},{2,3},{3,2},{4,5},{5,4},{6,7},{7,6},{8,9},{9,8},{10,11... | collective-permute-start | bytes 2359304 | tf_op jit(solution)/shard_map/ppermute | solution.py:208
  84.4 654.5 %reduce-scatter.15.cloned.1.call-start = ((), (), s32[]{:S(2)}) async-start(), calls=%async_computation.11 | async-start | bytes 1327104 | tf_op jit(solution)/shard_map/reduce_scatter | solution.py:267
  112.7 17.0 %copy-start.10 = (bf16[512,768]{1,0:T(8,128)(2,1)}, bf16[512,768]{1,0:T(8,128)(2,1)S(1)}, u32[]{:S(2)}) copy-start(bf16[512,768]{1,0:T(8,128)(2,1)S(1)} %collective-permute-done.kp_ref) | copy-start | bytes 2359300
  133.4 150.6 %copy-start.24 = (bf16[512,768]{1,0:T(8,128)(2,1)}, bf16[512,768]{1,0:T(8,128)(2,1)S(1)}, u32[]{:S(2)}) copy-start(bf16[512,768]{1,0:T(8,128)(2,1)S(1)} %get-tuple-element.197) | copy-start | bytes 2359300
  354.6 27.0 %collective-permute-start.2 = (bf16[512,768]{1,0:T(8,128)(2,1)S(1)}, bf16[512,768]{1,0:T(8,128)(2,1)S(1)}, u32[]{:S(2)}, u32[]{:S(2)}) collective-permute-start(bf16[512,768]{1,0:T(8,128)(2,1)S(1)} %get-tuple-element.157.ko_ref), channel_id=1, source_target_pairs={{0,1},{1,0},{2,3},{3,2},{4,5},{5,4},{6,7},{7,6},{8,9},{9,8},{10,11... | collective-permute-start | bytes 2359304 | tf_op jit(solution)/shard_map/ppermute | solution.py:208
  354.6 27.0 %collective-permute-start.3 = (bf16[512,768]{1,0:T(8,128)(2,1)S(1)}, bf16[512,768]{1,0:T(8,128)(2,1)S(1)}, u32[]{:S(2)}, u32[]{:S(2)}) collective-permute-start(bf16[512,768]{1,0:T(8,128)(2,1)S(1)} %get-tuple-element.156.vo_ref), channel_id=1, source_target_pairs={{0,1},{1,0},{2,3},{3,2},{4,5},{5,4},{6,7},{7,6},{8,9},{9,8},{10,11... | collective-permute-start | bytes 2359304 | tf_op jit(solution)/shard_map/ppermute | solution.py:208
  553.3 7.5 copy-start.22
  553.3 7.5 copy-start.59
  560.8 3.1 copy-start.62
  565.9 21.4 %copy-start.31 = (bf16[512,768]{1,0:T(8,128)(2,1)}, bf16[512,768]{1,0:T(8,128)(2,1)S(1)}, u32[]{:S(2)}) copy-start(bf16[512,768]{1,0:T(8,128)(2,1)S(1)} %get-tuple-element.151) | copy-start | bytes 2359300
  568.1 19.2 %copy-start.18 = (bf16[512,768]{1,0:T(8,128)(2,1)S(1)}, bf16[512,768]{1,0:T(8,128)(2,1)}, u32[]{:S(2)}) copy-start(bf16[512,768]{1,0:T(8,128)(2,1)} %copy-done.17) | copy-start | bytes 2359300
  586.7 3.4 collective-permute-start.6
  586.7 5.3 collective-permute-start.7
  589.1 149.8 %reduce-scatter.13.cloned.1.call-start = ((), (), s32[]{:S(2)}) async-start(), calls=%async_computation.10 | async-start | bytes 1327104 | tf_op jit(solution)/shard_map/reduce_scatter | solution.py:267
  593.0 7.8 slice-start.2
  593.0 7.8 slice-start.4
  594.5 5.5 copy-start.40
  594.6 5.5 copy-start.32
  594.6 6.2 slice-start.3
  594.6 6.2 slice-start.5
  600.0 5.5 slice-start
  600.8 7.8 copy-start.29
  600.9 4.7 copy-start.25
  600.9 4.7 slice-start.1
  605.5 3.1 copy-start.63
  612.1 187.6 %reduce-scatter.11.cloned.1.call-start = ((), (), s32[]{:S(2)}) async-start(), calls=%async_computation.9 | async-start | bytes 3981312 | tf_op jit(solution)/shard_map/reduce_scatter | solution.py:267
  618.0 263.9 %reduce-scatter.9.cloned.1.call-start = ((), (), s32[]{:S(2)}) async-start(), calls=%async_computation.8 | async-start | bytes 3981312 | tf_op jit(solution)/shard_map/reduce_scatter | solution.py:267
  618.0 3.3 copy-start.11
  639.0 4.4 copy-start.8
  639.0 2.3 collective-permute-start.9
  639.1 3.9 collective-permute-start.8
  649.4 331.0 %reduce-scatter.19.cloned.1.call-start = ((), (), s32[]{:S(2)}) async-start(), calls=%async_computation.13 | async-start | bytes 5308416 | tf_op jit(solution)/shard_map/reduce_scatter | solution.py:267
  657.0 422.0 %reduce-scatter.23.cloned.1.call-start = ((), (), s32[]{:S(2)}) async-start(), calls=%async_computation.15 | async-start | bytes 5308416 | tf_op jit(solution)/shard_map/reduce_scatter | solution.py:267
  664.0 513.5 %reduce-scatter.17.cloned.1.call-start = ((), (), s32[]{:S(2)}) async-start(), calls=%async_computation.12 | async-start | bytes 5308416 | tf_op jit(solution)/shard_map/reduce_scatter | solution.py:267
  671.6 604.4 %reduce-scatter.21.cloned.1.call-start = ((), (), s32[]{:S(2)}) async-start(), calls=%async_computation.14 | async-start | bytes 5308416 | tf_op jit(solution)/shard_map/reduce_scatter | solution.py:267
  679.5 3.8 copy-start.9
  679.5 675.2 %all-reduce.36.cloned.1.call-start = ((), (), s32[]{:S(2)}) async-start(), calls=%async_computation.24 | async-start | bytes 7077888 | tf_op jit(solution)/shard_map/psum | solution.py:268
  683.5 41.5 %copy-start.20 = (bf16[512,768]{1,0:T(8,128)(2,1)S(1)}, bf16[512,768]{1,0:T(8,128)(2,1)}, u32[]{:S(2)}) copy-start(bf16[512,768]{1,0:T(8,128)(2,1)} %copy-done.19) | copy-start | bytes 2359300
  725.0 6.0 copy-start.61
  727.5 564.8 %collective-permute-start.10 = (bf16[256,768]{1,0:T(8,128)(2,1)S(1)}, bf16[256,768]{1,0:T(8,128)(2,1)S(1)}, u32[]{:S(2)}, u32[]{:S(2)}) collective-permute-start(bf16[256,768]{1,0:T(8,128)(2,1)S(1)} %get-tuple-element.170), channel_id=1, source_target_pairs={{0,0},{1,2},{2,1},{3,3},{4,4},{5,6},{6,5},{7,7},{8,8},{9,10},{10,9... | collective-permute-start | bytes 1179656 | tf_op jit(solution)/shard_map/ppermute | solution.py:259
  728.2 564.2 %collective-permute-start.11 = (bf16[256,768]{1,0:T(8,128)(2,1)S(1)}, bf16[256,768]{1,0:T(8,128)(2,1)S(1)}, u32[]{:S(2)}, u32[]{:S(2)}) collective-permute-start(bf16[256,768]{1,0:T(8,128)(2,1)S(1)} %get-tuple-element.171), channel_id=1, source_target_pairs={{0,1},{1,3},{2,0},{3,2},{4,5},{5,7},{6,4},{7,6},{8,9},{9,11},{10,8... | collective-permute-start | bytes 1179656 | tf_op jit(solution)/shard_map/ppermute | solution.py:260
  736.0 557.3 %collective-permute-start.4 = (bf16[256,768]{1,0:T(8,128)(2,1)S(1)}, bf16[256,768]{1,0:T(8,128)(2,1)S(1)}, u32[]{:S(2)}, u32[]{:S(2)}) collective-permute-start(bf16[256,768]{1,0:T(8,128)(2,1)S(1)} %get-tuple-element.174), channel_id=1, source_target_pairs={{0,0},{1,2},{2,1},{3,3},{4,4},{5,6},{6,5},{7,7},{8,8},{9,10},{10,9... | collective-permute-start | bytes 1179656 | tf_op jit(solution)/shard_map/ppermute | solution.py:259
  736.7 556.6 %collective-permute-start.5 = (bf16[256,768]{1,0:T(8,128)(2,1)S(1)}, bf16[256,768]{1,0:T(8,128)(2,1)S(1)}, u32[]{:S(2)}, u32[]{:S(2)}) collective-permute-start(bf16[256,768]{1,0:T(8,128)(2,1)S(1)} %get-tuple-element.175), channel_id=1, source_target_pairs={{0,1},{1,3},{2,0},{3,2},{4,5},{5,7},{6,4},{7,6},{8,9},{9,11},{10,8... | collective-permute-start | bytes 1179656 | tf_op jit(solution)/shard_map/ppermute | solution.py:260
  1354.7 2.9 copy-start.43
  (35 other events, 55.2 us)
Sparse Core Ops, SparseCore 0:
  10.8 68.5 all-gather.32
  82.2 39.6 all-gather.34
  124.7 78.6 all-gather.36
  206.0 78.0 all-gather.38
  286.6 63.3 all-gather.40
  352.0 39.6 all-gather.42
  394.5 78.5 all-gather.44
  475.3 78.0 all-gather.46
  589.2 62.1 reduce-scatter.14
  654.6 63.0 reduce-scatter.12
  721.4 78.2 reduce-scatter.10
  803.2 78.6 reduce-scatter.8
  885.6 94.7 reduce-scatter.18
  983.9 95.0 reduce-scatter.22
  1082.4 94.9 reduce-scatter.16
  1181.0 94.9 reduce-scatter.20
  1278.7 75.9 all-reduce.35

commit v2 on v1

v2 whole, which is shorter than its diff:
```python
from functools import partial
import math

import jax
import jax.numpy as jnp
from jax import lax
from jax.experimental import pallas as pl
from jax.experimental.pallas import tpu as pltpu
from jax.sharding import PartitionSpec as P

HEAD = 64
PAIR = 2 * HEAD
NORM_EPS = 1e-05
MASK_FLOOR = -1e30
F32 = jnp.float32
BF16 = jnp.bfloat16
VMEM_ROOM = 56 << 20
WHOLE = pl.BlockSpec(memory_space=pltpu.VMEM)
PLACED = pl.BlockSpec(memory_space=pl.ANY)


def nt_dot(left, right):
    return lax.dot_general(left, right, (((1,), (1,)), ((), ())), preferred_element_type=F32)


def nn_dot(left, right):
    return jnp.dot(left, right, preferred_element_type=F32)


def tn_dot(left, right):
    return lax.dot_general(left, right, (((0,), (0,)), ((), ())), preferred_element_type=F32)


def lasting(micros):
    return pl.CostEstimate(flops=micros << 28, transcendentals=0, bytes_accessed=1 << 16)


def struct(shape, kind):
    return jax.ShapeDtypeStruct(shape, kind)


def call(body, outs, operands, placed=(), scratch=(), micros=2, out_placed=()):
    return pl.pallas_call(
        body,
        in_specs=[PLACED if n in placed else WHOLE for n in range(len(operands))],
        out_specs=[PLACED if n in out_placed else WHOLE for n in range(len(outs))],
        out_shape=outs,
        scratch_shapes=list(scratch),
        compiler_params=pltpu.CompilerParams(vmem_limit_bytes=VMEM_ROOM),
        cost_estimate=lasting(micros),
    )(*operands)


def start_copy(src, dst, sem):
    copy = pltpu.make_async_copy(src, dst, sem)
    copy.start()
    return copy


def head_lanes(block, head):
    lane = lax.broadcasted_iota(jnp.int32, block.shape, 1)
    keep = (lane < HEAD) if head == 0 else (lane >= HEAD)
    return jnp.where(keep, block, jnp.zeros_like(block))


def attend_kernel(lens_ref, q_ref, ko_ref, kp_ref, vo_ref, vp_ref, o_ref, raised_ref, scale_ref):
    rows = q_ref.shape[0]
    score_scale = 1.0 / math.sqrt(HEAD)
    query_pair = q_ref[...] * jnp.asarray(score_scale, BF16)
    value_t = [vo_ref[...].T, vp_ref[...].T]
    mixed, scales = [], []
    for head in range(2):
        query = head_lanes(query_pair, head)
        scores = []
        for part, key_ref in enumerate((ko_ref, kp_ref)):
            part_scores = nt_dot(key_ref[...], query)
            key_row = lax.broadcasted_iota(jnp.int32, part_scores.shape, 0)
            scores.append(jnp.where(key_row < lens_ref[part], part_scores, MASK_FLOOR))
        row_max = jnp.maximum(
            jnp.max(scores[0], axis=0, keepdims=True), jnp.max(scores[1], axis=0, keepdims=True)
        )
        total = jnp.zeros((1, rows), F32)
        head_out = jnp.zeros((HEAD, rows), F32)
        for part in range(2):
            raised = jnp.exp(scores[part] - row_max)
            total = total + jnp.sum(raised, axis=0, keepdims=True)
            low = raised.astype(BF16)
            raised_ref[head, part * rows : (part + 1) * rows, :] = low
            head_out = head_out + nn_dot(value_t[part][head * HEAD : (head + 1) * HEAD, :], low)
        inverse = 1.0 / total
        mixed.append(head_out * inverse)
        scales.append(jnp.broadcast_to(inverse, (HEAD, rows)))
    o_ref[...] = jnp.concatenate(mixed, axis=0).T.astype(BF16)
    scale_ref[...] = jnp.concatenate(scales, axis=0).T


def attend(queries, own, peer, lens):
    rows, width = queries.shape
    pairs = width // PAIR
    block = pl.BlockSpec((rows, PAIR), lambda p, lens: (0, p))
    key = pl.BlockSpec((None, rows, PAIR), lambda p, lens: (0, 0, p))
    value = pl.BlockSpec((None, rows, PAIR), lambda p, lens: (1, 0, p))
    return pl.pallas_call(
        attend_kernel,
        grid_spec=pltpu.PrefetchScalarGridSpec(
            num_scalar_prefetch=1,
            grid=(pairs,),
            in_specs=[block, key, key, value, value],
            out_specs=[
                block, pl.BlockSpec((2, 2 * rows, rows), lambda p, lens: (p, 0, 0)), block,
            ],
        ),
        out_shape=[
            struct((rows, width), BF16), struct((2 * pairs, 2 * rows, rows), BF16),
            struct((rows, width), F32),
        ],
        compiler_params=pltpu.CompilerParams(vmem_limit_bytes=48 << 20),
        cost_estimate=lasting(16),
    )(lens, queries, own, peer, own, peer)


def attend_back_kernel(
    q_ref, ko_ref, kp_ref, vo_ref, vp_ref, o_ref, go_ref, raised_ref, scale_ref,
    gq_ref, own_ref, peer_ref,
):
    rows = q_ref.shape[0]
    score_scale = 1.0 / math.sqrt(HEAD)
    query_pair = q_ref[...] * jnp.asarray(score_scale, BF16)
    query_t = query_pair.T
    grad_pair = (go_ref[...].astype(F32) * scale_ref[...]).astype(BF16)
    grad_t = grad_pair.T
    inner = (o_ref[...].astype(F32) * grad_pair.astype(F32)).T
    value_refs = (vo_ref, vp_ref)
    key_t = [ko_ref[...].T, kp_ref[...].T]
    grad_key = [[], []]
    grad_value = [[], []]
    grad_query = []
    for head in range(2):
        lanes = slice(head * HEAD, (head + 1) * HEAD)
        grad_out = head_lanes(grad_pair, head)
        inner_row = jnp.sum(inner[lanes, :], axis=0, keepdims=True)
        head_query = jnp.zeros((HEAD, rows), F32)
        for part in range(2):
            raised = raised_ref[head, part * rows : (part + 1) * rows, :]
            grad_prob = nt_dot(value_refs[part][...], grad_out)
            grad_score = (raised.astype(F32) * (grad_prob - inner_row)).astype(BF16)
            grad_value[part].append(nt_dot(grad_t[lanes, :], raised))
            grad_key[part].append(nt_dot(query_t[lanes, :], grad_score))
            head_query = head_query + nn_dot(key_t[part][lanes, :], grad_score)
        grad_query.append(head_query * score_scale)
    gq_ref[...] = jnp.concatenate(grad_query, axis=0).T.astype(BF16)
    for n, grads in enumerate((grad_key, grad_value)):
        own_ref[n] = jnp.concatenate(grads[0], axis=0).T
        peer_ref[n] = jnp.concatenate(grads[1], axis=0).T.astype(BF16)


def attend_back(queries, own, peer, mixed, grad_mixed, raised, scale):
    rows, width = queries.shape
    pairs = width // PAIR
    block = pl.BlockSpec((rows, PAIR), lambda p: (0, p))
    key = pl.BlockSpec((None, rows, PAIR), lambda p: (0, 0, p))
    value = pl.BlockSpec((None, rows, PAIR), lambda p: (1, 0, p))
    both = pl.BlockSpec((2, rows, PAIR), lambda p: (0, 0, p))
    low, full = struct((rows, width), BF16), struct((2, rows, width), F32)
    sent = struct((2, rows, width), BF16)
    return pl.pallas_call(
        attend_back_kernel,
        grid=(pairs,),
        in_specs=[
            block, key, key, value, value, block, block,
            pl.BlockSpec((2, 2 * rows, rows), lambda p: (p, 0, 0)), block,
        ],
        out_specs=[block, both, both],
        out_shape=[low, full, sent],
        compiler_params=pltpu.CompilerParams(vmem_limit_bytes=48 << 20),
        cost_estimate=lasting(16),
    )(queries, own, peer, own, peer, mixed, grad_mixed, raised, scale)


def norm_unit(stream):
    center = stream - jnp.mean(stream, axis=-1, keepdims=True)
    spread = jnp.mean(center * center, axis=-1, keepdims=True)
    root = lax.rsqrt(spread + NORM_EPS)
    return center * root, root


def norm_back(stream, gain, grad_normed, grad_low):
    unit, root = norm_unit(stream)
    grad_gain = jnp.sum(grad_normed * unit, axis=0, keepdims=True)
    grad_shift = jnp.sum(grad_normed, axis=0, keepdims=True)
    grad_unit = grad_normed * gain
    grad_stream = root * (
        grad_unit
        - jnp.mean(grad_unit, axis=-1, keepdims=True)
        - unit * jnp.mean(grad_unit * unit, axis=-1, keepdims=True)
    )
    return (grad_low.astype(F32) + grad_stream).astype(BF16), grad_gain, grad_shift


def block_ref(refs, n, which):
    if len(refs) == 2:
        return refs[n % 2].at[which, n // 2]
    return refs[0].at[:, jnp.bitwise_xor(lax.axis_index("section"), n), which]


def start_section(refs, which, wanted, dst_refs, sems):
    here = lax.axis_index("section")
    waits = []
    for slot, block in enumerate(wanted):
        if len(refs) == 1:
            waits.append(start_copy(refs[0].at[:, block, which], dst_refs.at[slot], sems.at[slot]))
            continue
        place = jnp.bitwise_xor(here, block)
        for n in range(4):
            @pl.when(place == n)
            def _():
                start_copy(block_ref(refs, n, which), dst_refs.at[slot], sems.at[slot])
        waits.append(
            pltpu.make_async_copy(block_ref(refs, 0, which), dst_refs.at[slot], sems.at[slot])
        )
    return waits


def block_shape(blocks):
    shape = blocks[0].shape
    return shape[-3:] if len(blocks) == 2 else shape[:1] + shape[-2:]


def square(block):
    return block.reshape(block.shape[-3] * block.shape[-2], block.shape[-1])


def qkv_kernel(which, count, h_ref, vec_ref, *refs):
    blocks = refs[:count]
    a_hbm, q_hbm, kv_hbm, mat, a_ref, q_ref, kv_ref, sems, outs = refs[count:]
    waits = start_section(blocks, which, (1, 2, 0), mat, sems)
    unit, _ = norm_unit(h_ref[...].astype(F32))
    normed = (unit * vec_ref[0:1, :] + vec_ref[1:2, :]).astype(BF16)
    a_ref[...] = normed
    copies = [start_copy(a_ref, a_hbm, outs.at[0])]
    waits[0].wait()
    kv_ref[0] = nn_dot(normed, square(mat[0])).astype(BF16)
    copies.append(start_copy(kv_ref.at[0], kv_hbm.at[0], outs.at[1]))
    waits[1].wait()
    kv_ref[1] = (nn_dot(normed, square(mat[1])) + vec_ref[3:4, :]).astype(BF16)
    copies.append(start_copy(kv_ref.at[1], kv_hbm.at[1], outs.at[2]))
    waits[2].wait()
    q_ref[...] = (nn_dot(normed, square(mat[2])) + vec_ref[2:3, :]).astype(BF16)
    copies.append(start_copy(q_ref, q_hbm, outs.at[3]))
    for item in copies:
        item.wait()


def qkv_part(stream, vec, attn):
    rows, width = stream.shape
    blocks, which = attn
    low, both = struct((rows, width), BF16), struct((2, rows, width), BF16)
    return call(
        partial(qkv_kernel, which, len(blocks)), [low, low, both], (stream, vec, *blocks), (2, 3),
        (
            pltpu.VMEM((3,) + block_shape(blocks), BF16), pltpu.VMEM(low.shape, BF16),
            pltpu.VMEM(low.shape, BF16), pltpu.VMEM(both.shape, BF16),
            pltpu.SemaphoreType.DMA((3,)), pltpu.SemaphoreType.DMA((4,)),
        ), micros=5, out_placed=(0, 1, 2),
    )


def out_kernel(which, count, h_ref, o_ref, vec_ref, *refs):
    y_ref, mat, sems = refs[count:]
    start_section(refs[:count], which, (3,), mat, sems)[0].wait()
    y_ref[...] = (
        h_ref[...].astype(F32) + nn_dot(o_ref[...], square(mat[0])) + vec_ref[4:5, :]
    ).astype(BF16)


def out_part(stream, mixed, vec, attn):
    rows, width = stream.shape
    blocks, which = attn
    return call(
        partial(out_kernel, which, len(blocks)), [struct((rows, width), BF16)],
        (stream, mixed, vec, *blocks), (3, 4),
        (pltpu.VMEM((1,) + block_shape(blocks), BF16), pltpu.SemaphoreType.DMA((1,))), micros=4,
    )[0]


def up_kernel(which, count, h_ref, vec_ref, *refs):
    a_ref, g_hbm, slope_hbm, mat, g_ref, slope_ref, sems, outs = refs[count:]
    here = lax.axis_index("section")
    waits = [
        start_copy(block_ref(refs[:count], n, which), mat.at[n], sems.at[n]) for n in range(4)
    ]
    unit, _ = norm_unit(h_ref[...].astype(F32))
    normed = (unit * vec_ref[5:6, :] + vec_ref[6:7, :]).astype(BF16)
    a_ref[...] = normed
    copies = []
    for n in range(4):
        waits[n].wait()
        bias = vec_ref[pl.ds(7 + jnp.bitwise_xor(here, n), 1), :]
        up_proj = nn_dot(normed, square(mat[n])) + bias
        below = 0.5 * (1.0 + lax.erf(up_proj * math.sqrt(0.5)))
        bell = jnp.exp(-0.5 * up_proj * up_proj) * (1.0 / math.sqrt(2.0 * math.pi))
        g_ref[n] = (up_proj * below).astype(BF16)
        slope_ref[n] = (below + up_proj * bell).astype(BF16)
        copies.append(start_copy(g_ref.at[n], g_hbm.at[n], outs.at[0, n]))
        copies.append(start_copy(slope_ref.at[n], slope_hbm.at[n], outs.at[1, n]))
    for item in copies:
        item.wait()


def up_part(stream, vec, ups):
    rows, width = stream.shape
    wide = struct((4, rows, width), BF16)
    blocks, which = ups
    return call(
        partial(up_kernel, which, len(blocks)), [struct((rows, width), BF16), wide, wide],
        (stream, vec, *blocks), (2, 3),
        (
            pltpu.VMEM((4,) + block_shape(blocks), BF16), pltpu.VMEM(wide.shape, BF16),
            pltpu.VMEM(wide.shape, BF16), pltpu.SemaphoreType.DMA((4,)),
            pltpu.SemaphoreType.DMA((2, 4)),
        ), micros=9, out_placed=(1, 2),
    )


def start_down(refs, which, n, mat, sems):
    here = lax.axis_index("section")
    size = mat.shape[1] // 8
    waits = []
    for side in range(2):
        owner = 2 * jnp.bitwise_xor(here, n) + side
        for k in range(4):
            if len(refs) == 1:
                src, start = refs[0].at[owner, k, which], (side * 4 + k) * size
            else:
                src = block_ref(refs, k, which).at[owner]
                start = side * 4 * size + jnp.bitwise_xor(here, k) * size
            waits.append(
                start_copy(
                    src, mat.at[n, pl.ds(pl.multiple_of(start, size), size)],
                    sems.at[n, 2 * k + side],
                )
            )
    return waits


def down_kernel(which, count, h_ref, g_hbm, vec_ref, *refs):
    y_ref, mat, g_ref, sems, g_sems = refs[count:]
    waits = []
    for n in range(4):
        found = start_down(refs[:count], which, n, mat, sems)
        waits.append(found + [start_copy(g_hbm.at[n], g_ref.at[n], g_sems.at[n])])
    total = h_ref[...].astype(F32) + vec_ref[11:12, :]
    for n in range(4):
        for item in waits[n]:
            item.wait()
        total = total + nn_dot(g_ref[n], mat[n])
    y_ref[...] = total.astype(BF16)


def down_part(stream, hidden, vec, downs):
    rows, width = stream.shape
    blocks, which = downs
    return call(
        partial(down_kernel, which, len(blocks)), [struct((rows, width), BF16)],
        (stream, hidden, vec, *blocks), (1, 3, 4),
        (
            pltpu.VMEM((4, width, width), BF16), pltpu.VMEM((4, rows, width), BF16),
            pltpu.SemaphoreType.DMA((4, 8)), pltpu.SemaphoreType.DMA((4,)),
        ), micros=6,
    )[0]


def ffn_back_kernel(
    places, counts, gy_ref, h_ref, a_ref, g_hbm, slope_hbm, vec_ref, *refs
):
    (up_at, down_at, attn_at), (up_count, down_count, attn_count) = places, counts
    up_refs, refs = refs[:up_count], refs[up_count:]
    down_refs, refs = refs[:down_count], refs[down_count:]
    attn_refs, refs = refs[:attn_count], refs[attn_count:]
    (
        gh_ref, go_ref, keep_hbm, send_hbm, vg_ref,
        g_ref, slope_ref, mat, up_mat, out_mat, up_grad, down_grad,
        in_sems, sems, out_sems, up_sems, down_sems,
    ) = refs
    here = lax.axis_index("section")
    size, width = keep_hbm.shape[-2:]
    waits = []
    for n in range(4):
        found = start_down(down_refs, down_at, n, mat, sems)
        found.append(start_copy(slope_hbm.at[n], slope_ref.at[n], in_sems.at[0, n]))
        found.append(start_copy(g_hbm.at[n], g_ref.at[n], in_sems.at[1, n]))
        found.append(
            start_copy(block_ref(up_refs, n, up_at), up_mat.at[n], in_sems.at[2, n])
        )
        waits.append(found)
    out_wait = start_section(attn_refs, attn_at, (3,), out_mat, out_sems)[0]
    grad = gy_ref[...]
    normed = a_ref[...]
    vg_ref[...] = jnp.zeros_like(vg_ref)
    vg_ref[6:7, :] = jnp.sum(grad.astype(F32), axis=0, keepdims=True)
    grad_normed = None
    copies = []
    for n in range(4):
        for item in waits[n]:
            item.wait()
        block = jnp.bitwise_xor(here, n)
        grad_up = nt_dot(grad, mat[n]) * slope_ref[n].astype(F32)
        grad_up = grad_up.astype(BF16)
        vg_ref[pl.ds(2 + block, 1), :] = jnp.sum(grad_up.astype(F32), axis=0, keepdims=True)
        up_grad[n] = tn_dot(normed, grad_up).astype(BF16).reshape(8, size, width)
        out = keep_hbm if n in (0, 2) else send_hbm
        copies.append(start_copy(up_grad.at[n], out.at[n // 2, 0], up_sems.at[n]))
        down_grad[n] = tn_dot(g_ref[n], grad).astype(BF16).reshape(8, size, width)
        for j in range(4):
            place = jnp.bitwise_xor(here, j)
            for side in range(2):
                src, sem = down_grad.at[n, 4 * side + j], down_sems.at[n, 4 * side + j]

                @pl.when(place % 2 == 0)
                def _():
                    start_copy(src, keep_hbm.at[place // 2, 1, 2 * block + side], sem)

                @pl.when(place % 2 == 1)
                def _():
                    start_copy(src, send_hbm.at[place // 2, 1, 2 * block + side], sem)

                copies.append(pltpu.make_async_copy(src, keep_hbm.at[0, 1, 0], sem))
        term = nt_dot(grad_up, square(up_mat[n]))
        grad_normed = term if n == 0 else grad_normed + term
    grad_in, grad_gain, grad_shift = norm_back(
        h_ref[...].astype(F32), vec_ref[5:6, :], grad_normed, grad
    )
    gh_ref[...] = grad_in
    vg_ref[0:1, :] = grad_gain
    vg_ref[1:2, :] = grad_shift
    out_wait.wait()
    go_ref[...] = nt_dot(grad_in, square(out_mat[0])).astype(BF16)
    for item in copies:
        item.wait()


def ffn_back(grad, stream, normed, hidden, slope, vec, ups, downs, attn):
    rows, width = grad.shape
    sets = (ups, downs, attn)
    counts, places = tuple(len(item[0]) for item in sets), tuple(item[1] for item in sets)
    blocks = [ref for item in sets for ref in item[0]]
    block = block_shape(ups[0])
    part = struct((2, 2) + block, BF16)
    low = struct((rows, width), BF16)
    dma = pltpu.SemaphoreType.DMA
    return call(
        partial(ffn_back_kernel, places, counts),
        [low, low, part, part, struct((8, width), F32)],
        (grad, stream, normed, hidden, slope, vec, *blocks),
        (3, 4, *range(6, 6 + len(blocks))),
        (
            pltpu.VMEM((4, rows, width), BF16), pltpu.VMEM((4, rows, width), BF16),
            pltpu.VMEM((4, width, width), BF16), pltpu.VMEM((4,) + block, BF16),
            pltpu.VMEM((1,) + block, BF16), pltpu.VMEM((4,) + block, BF16),
            pltpu.VMEM((4,) + block, BF16), dma((3, 4)), dma((4, 8)), dma((1,)), dma((4,)),
            dma((4, 8)),
        ), micros=20, out_placed=(2, 3),
    )


def qkv_back_kernel(
    which, count, gy_ref, h_ref, a_ref, o_ref, gq_ref, own_hbm, got_ref, vec_ref, *refs
):
    gh_ref, keep_hbm, send_hbm, vg_ref, mat, own_ref, term, sems, own_sems, out_sems = refs[count:]
    waits = start_section(refs[:count], which, (0, 1, 2), mat, sems)
    own_waits = [start_copy(own_hbm.at[n], own_ref.at[n], own_sems.at[n]) for n in range(2)]
    here = lax.axis_index("section")
    grad = gy_ref[...]
    normed = a_ref[...]
    vg_ref[...] = jnp.zeros_like(vg_ref)
    copies = []

    def give(block, left, right):
        term[block] = tn_dot(left, right).astype(BF16).reshape(term.shape[1:])
        place = jnp.bitwise_xor(here, block)

        @pl.when(place % 2 == 0)
        def _():
            start_copy(term.at[block], keep_hbm.at[place // 2, 0], out_sems.at[block])

        @pl.when(place % 2 == 1)
        def _():
            start_copy(term.at[block], send_hbm.at[place // 2, 0], out_sems.at[block])

        copies.append(pltpu.make_async_copy(term.at[block], keep_hbm.at[0, 0], out_sems.at[block]))

    vg_ref[4:5, :] = jnp.sum(grad.astype(F32), axis=0, keepdims=True)
    give(3, o_ref[...], grad)
    grad_q = gq_ref[...]
    vg_ref[2:3, :] = jnp.sum(grad_q.astype(F32), axis=0, keepdims=True)
    give(0, normed, grad_q)
    own_waits[0].wait()
    grad_k = (own_ref[0] + got_ref[0].astype(F32)).astype(BF16)
    give(1, normed, grad_k)
    own_waits[1].wait()
    grad_v = (own_ref[1] + got_ref[1].astype(F32)).astype(BF16)
    vg_ref[3:4, :] = jnp.sum(grad_v.astype(F32), axis=0, keepdims=True)
    give(2, normed, grad_v)
    for item in waits:
        item.wait()
    grad_normed = (
        nt_dot(grad_q, square(mat[0])) + nt_dot(grad_k, square(mat[1])) + nt_dot(grad_v, square(mat[2]))
    )
    gh_ref[...], grad_gain, grad_shift = norm_back(
        h_ref[...].astype(F32), vec_ref[0:1, :], grad_normed, grad
    )
    vg_ref[0:1, :] = grad_gain
    vg_ref[1:2, :] = grad_shift
    for item in copies:
        item.wait()


def qkv_back(grad, stream, normed, mixed, parts, vec, attn):
    rows, width = grad.shape
    blocks, which = attn
    block = block_shape(blocks)
    part = struct((2, 1) + block, BF16)
    dma = pltpu.SemaphoreType.DMA
    return call(
        partial(qkv_back_kernel, which, len(blocks)),
        [struct((rows, width), BF16), part, part, struct((8, width), F32)],
        (grad, stream, normed, mixed, *parts, vec, *blocks),
        (5, *range(8, 8 + len(blocks))),
        (
            pltpu.VMEM((3,) + block, BF16), pltpu.VMEM((2, rows, width), F32),
            pltpu.VMEM((4,) + block, BF16), dma((3,)), dma((2,)), dma((4,)),
        ), micros=10, out_placed=(1, 2),
    )


def over(block, axis, move):
    count = lax.axis_size(axis)
    return lax.ppermute(block, axis, [(i, move(i)) for i in range(count)])


def to_core(block):
    return over(block, "section", lambda i: i ^ 1)


def to_x(block):
    return over(block, "section", lambda i: i ^ 2)


def to_y(block):
    return over(block, "dp", lambda i: i ^ 1)


def to_z(block, steps):
    return over(block, "dp", lambda i: (i + 2 * steps) % 8)


ALONG = [[0, 2, 4, 6], [1, 3, 5, 7]]


def gather_along(block):
    return lax.all_gather(block, "dp", axis=0, axis_index_groups=ALONG)


def all_z(block):
    return tuple(to_z(block, k) for k in (1, 2, 3))


class Line:
    def __init__(self, start):
        self.token = start

    def fence(self, arrays):
        *arrays, self.token = lax.optimization_barrier(tuple(arrays) + (self.token,))
        return arrays

    def run(self, body, *operands):
        flat, shape = jax.tree.flatten(operands)
        arrays = self.fence([item for item in flat if not isinstance(item, int)])
        flat = [item if isinstance(item, int) else arrays.pop(0) for item in flat]
        flat, shape = jax.tree.flatten(body(*jax.tree.unflatten(shape, flat)))
        return jax.tree.unflatten(shape, self.fence(flat))


def pick_kernel(
    qkv_ref, out_ref, up_ref, down_ref, again, ashift, qvb, outb, fgain, fshift, upb, downb,
    a1, f1, rest, ride,
):
    size, width = f1.shape[1:]
    here = lax.axis_index("section")
    group = lax.axis_index("dp")
    ride[...] = jnp.zeros_like(ride)
    for i in range(8):
        @pl.when(group == i)
        def _():
            for l in range(2):
                def put(row, start, ref):
                    wide = ref.shape[1]
                    at = slice(start % width, start % width + wide)
                    ride[16 * l + row : 16 * l + row + 1, at] = ref[l : l + 1, :].astype(F32)

                put(0, size * i, again)
                put(1, size * i, ashift)
                put(2 + 2 * size * i // width, 2 * size * i, qvb)
                put(4, size * i, outb)
                put(5, size * i, fgain)
                put(6, size * i, fshift)
                put(7 + 4 * size * i // width, 4 * size * i, upb)
                put(11, size * i, downb)

    a1[size:] = ride[...].astype(BF16)
    for m in range(4):
        @pl.when(here == m)
        def _():
            for l in range(2):
                attn = qkv_ref[l, :, m * width : (m + 1) * width] if m < 3 else out_ref[l]
                ffn = f1 if l == 0 else rest
                ffn[0] = up_ref[l, :, m * width : (m + 1) * width]
                ffn[1] = down_ref[l, m * size : (m + 1) * size]
                if l == 0:
                    a1[:size] = attn
                else:
                    rest[2] = attn


def pick_blocks(*operands):
    size = operands[0].shape[1]
    width = operands[1].shape[2]
    return call(
        pick_kernel,
        [
            struct((size + 32, width), BF16), struct((2, size, width), BF16),
            struct((3, size, width), BF16),
        ],
        operands, (), (pltpu.VMEM((32, width), F32),), micros=4,
    )


def split_kernel(near_ref, *out_refs):
    at = 0
    for left_ref, right_ref in zip(out_refs[::2], out_refs[1::2]):
        count, wide = left_ref.shape[1], left_ref.shape[-1]
        left_ref[...] = near_ref[:, at : at + count, :, :wide]
        right_ref[...] = near_ref[:, at : at + count, :, wide:]
        at += count


def split_near(near, counts):
    size, width = near.shape[2:]
    outs = []
    for count in counts:
        outs += [struct((4, count, size, width // 2), BF16)] * 2
    return call(split_kernel, outs, (near,))


def middle_kernel(left_ref, left_got, right_ref, right_got, x_ref, y_ref):
    side = lax.axis_index("dp") % 2
    for along in range(4):
        x_ref[2 * along + side] = left_ref[along]
        x_ref[2 * along + 1 - side] = left_got[along]
    y_ref[0] = right_ref[...]
    y_ref[1] = right_got[...]


def middle(left, left_got, right, right_got):
    part = left.shape[1:]
    return call(
        middle_kernel, [struct((8,) + part, BF16), struct((2, 4) + part, BF16)],
        (left, left_got, right, right_got), micros=60,
    )


def whole_kernel(x_ref, x_got, y_ref, y_got, out_ref, *ride_refs):
    side = lax.axis_index("dp") % 2
    count, size, wide = out_ref.shape[0], out_ref.shape[3], x_ref.shape[3]
    for c in range(count):
        for n, ref in enumerate((x_ref, x_got)):
            out_ref[c, n, :, :, :wide] = ref[:, c, :size]
            for along in range(4):
                out_ref[c, n, 2 * along + side, :, wide:] = y_ref[n, along, c, :size]
                out_ref[c, n, 2 * along + 1 - side, :, wide:] = y_got[n, along, c, :size]
    if ride_refs:
        vec_ref = ride_refs[0]
        left = jnp.sum(x_ref[:, 0, size:].astype(F32), axis=0)
        right = jnp.sum(y_ref[0, :, 0, size:].astype(F32), axis=0)
        right = right + jnp.sum(y_got[0, :, 0, size:].astype(F32), axis=0)
        for l in range(2):
            vec_ref[l, :, :wide] = left[16 * l : 16 * l + 16]
            vec_ref[l, :, wide:] = right[16 * l : 16 * l + 16]


def whole_blocks(x_send, x_got, y_send, y_got, size):
    _, count, full, wide = x_send.shape
    outs = [struct((count, 2, 8, size, 2 * wide), BF16)]
    if full > size:
        outs.append(struct((2, 16, 2 * wide), F32))
    return call(whole_kernel, outs, (x_send, x_got, y_send, y_got))


class Gather:
    def __init__(self, line, left, right, size):
        self.line, self.left, self.right, self.size = line, left, right, size
        self.left_got, self.right_got = to_y(left), to_x(right)

    def middle(self):
        self.x_send, self.y_send = self.line.run(
            middle, self.left, self.left_got, self.right, self.right_got
        )
        self.x_got, self.y_got = to_x(self.x_send), to_y(self.y_send)

    def whole(self):
        found = self.line.run(
            lambda *items: whole_blocks(*items, self.size),
            self.x_send, self.x_got, self.y_send, self.y_got,
        )
        self.pair = (found[0], to_core(found[0]))
        return found[1:]


def first_kernel(keep_ref, got_ref, x_ref, y_ref, left_ref, right_ref):
    wide = x_ref.shape[-1]
    side = lax.axis_index("dp") % 2
    for c in range(keep_ref.shape[1]):
        for n, ref in enumerate((left_ref, x_ref)):
            ref[c] = (
                keep_ref[n, c, :, :, :wide].astype(F32) + got_ref[n, c, :, :, :wide].astype(F32)
            ).astype(BF16)
        for n in range(2):
            for along in range(4):
                for ref, pick in ((right_ref, side), (y_ref, 1 - side)):
                    at = 2 * along + pick
                    ref[n, c, along] = (
                        keep_ref[n, c, at, :, wide:].astype(F32)
                        + got_ref[n, c, at, :, wide:].astype(F32)
                    ).astype(BF16)


def add_first(keep, got):
    _, count, _, size, width = keep.shape
    x_part = struct((count, 8, size, width // 2), BF16)
    y_part = struct((2, count, 4, size, width // 2), BF16)
    return call(first_kernel, [x_part, y_part, x_part, y_part], (keep, got), micros=5)


def both_kernel(keep_ref, got_ref, out_ref):
    out_ref[0] = (
        keep_ref[:, :, 0].astype(F32) + got_ref[:, :, 0].astype(F32)
    ).astype(BF16)


def add_both(keep, got):
    _, count, parts, size, width = keep.shape
    spec = pl.BlockSpec((2, count, 1, size, width), lambda i: (0, 0, i, 0, 0))
    return pl.pallas_call(
        both_kernel,
        grid=(parts,),
        in_specs=[spec, spec],
        out_specs=pl.BlockSpec((1, 2, count, size, width), lambda i: (i, 0, 0, 0, 0)),
        out_shape=struct((parts, 2, count, size, width), BF16),
        compiler_params=pltpu.CompilerParams(vmem_limit_bytes=VMEM_ROOM),
        cost_estimate=lasting(60),
    )(keep, got)


def scatter_both(block):
    return lax.psum_scatter(block, "dp", scatter_dimension=0, tiled=True)[0]


def second_kernel(left_ref, x_got, right_ref, y_got, y_ref, x_ref, near_ref, rest_ref):
    side = lax.axis_index("dp") % 2
    for c in range(left_ref.shape[0]):
        for along in range(4):
            for ref, pick in ((near_ref, side), (y_ref, 1 - side)):
                at = 2 * along + pick
                ref[c, along] = (
                    left_ref[c, at].astype(F32) + x_got[c, at].astype(F32)
                ).astype(BF16)
        for n, ref in enumerate((rest_ref, x_ref)):
            ref[c] = (right_ref[n, c].astype(F32) + y_got[n, c].astype(F32)).astype(BF16)


def add_second(left, x_got, right, y_got):
    part = struct(right.shape[1:], BF16)
    return call(second_kernel, [part] * 4, (left, x_got, right, y_got), micros=120)


def third_kernel(near_ref, y_got, rest_ref, x_got, out_ref):
    wide = near_ref.shape[-1]
    for c in range(near_ref.shape[0]):
        for along in range(4):
            out_ref[along, c, :, :wide] = (
                near_ref[c, along].astype(F32) + y_got[c, along].astype(F32)
            ).astype(BF16)
            out_ref[along, c, :, wide:] = (
                rest_ref[c, along].astype(F32) + x_got[c, along].astype(F32)
            ).astype(BF16)


def add_third(near, y_got, rest, x_got):
    count, _, size, wide = near.shape
    return call(
        third_kernel, [struct((4, count, size, 2 * wide), BF16)], (near, y_got, rest, x_got),
        micros=60,
    )[0]


def split_kernel_back(near_ref, y_got, rest_ref, x_got, o0, o1, o2, o3):
    along = lax.axis_index("dp") // 2
    wide = near_ref.shape[-1]
    for c in range(near_ref.shape[0]):
        for k, ref in enumerate((o0, o1, o2, o3)):
            pick = lax.rem(along + k, 4)
            ref[c, :, :wide] = (
                near_ref[c, pick].astype(F32) + y_got[c, pick].astype(F32)
            ).astype(BF16)
            ref[c, :, wide:] = (
                rest_ref[c, pick].astype(F32) + x_got[c, pick].astype(F32)
            ).astype(BF16)


def add_third_split(near, y_got, rest, x_got):
    count, _, size, wide = near.shape
    part = struct((count, size, 2 * wide), BF16)
    return call(split_kernel_back, [part] * 4, (near, y_got, rest, x_got), micros=60)


def last_kernel(o0, o1, o2, o3, out_ref):
    out_ref[...] = (
        o0[...].astype(F32) + o1[...].astype(F32) + o2[...].astype(F32) + o3[...].astype(F32)
    ).astype(BF16)


def add_last(*parts):
    return call(last_kernel, [struct(parts[0].shape, BF16)], parts)[0]


def across(own):
    far = to_x(own)
    return own, to_core(own), far, to_core(far)


class Reduce:
    def __init__(self, line, x_send, y_send, left, right):
        self.line, self.left, self.right = line, left, right
        self.x_got, self.y_got = to_x(x_send), to_y(y_send)

    def second(self):
        y_send, x_send, self.near, self.rest = self.line.run(
            add_second, self.left, self.x_got, self.right, self.y_got
        )
        self.y_got, self.x_got = to_y(y_send), to_x(x_send)

    def third(self):
        whole = self.line.run(add_third, self.near, self.y_got, self.rest, self.x_got)
        self.shard = lax.psum_scatter(
            whole, "dp", scatter_dimension=0, tiled=True, axis_index_groups=ALONG
        )[0]

    def third_split(self):
        self.parts = self.line.run(
            add_third_split, self.near, self.y_got, self.rest, self.x_got
        )
        self.z_got = [to_z(self.parts[k], k) for k in (1, 2, 3)]

    def last(self):
        self.shard = self.line.run(add_last, self.parts[0], *self.z_got)


def finish_kernel(*refs):
    attn, ffn, (rest_ref, qkv_ref, out_ref, up_ref, down_ref) = refs[:4], refs[4:8], refs[8:]
    here = lax.axis_index("section")
    size, width = rest_ref.shape[-2:]

    def put(l, b, found):
        if b < 3:
            qkv_ref[l, :, b * width : (b + 1) * width] = found.astype(F32)
        else:
            out_ref[l] = found.astype(F32)

    def put_ffn(l, b, ups, downs):
        up_ref[l, :, b * width : (b + 1) * width] = ups.astype(F32)
        down_ref[l, b * size : (b + 1) * size] = downs.astype(F32)

    for m in range(4):
        @pl.when(here == m)
        def _():
            for b in range(4):
                put(0, b, attn[m ^ b][0])
                put_ffn(0, b, ffn[m ^ b][0], ffn[m ^ b][1])

    for b in range(4):
        put(1, b, rest_ref[b, 2])
        put_ffn(1, b, rest_ref[b, 0], rest_ref[b, 1])


def finish(*held):
    _, size, width = held[0].shape
    return call(
        finish_kernel,
        [
            struct((2, size, 3 * width), F32), struct((2, size, width), F32),
            struct((2, size, 4 * width), F32), struct((2, 4 * size, width), F32),
        ],
        held, micros=5,
    )


def pick_row(stacked, index):
    return lax.dynamic_index_in_dim(stacked, index, 0, keepdims=False)


def local(
    tokens, lengths, cotangent, attn_gain, attn_shift, qkv_weight, qv_bias, out_weight, out_bias,
    ffn_gain, ffn_shift, up_weight, up_bias, down_weight, down_bias,
):
    layers, size, width3 = qkv_weight.shape
    width = width3 // 3
    eighth = width // 8
    micro_count, cell_count, seq_len, _ = tokens.shape
    section_id = lax.axis_index("section")
    section_count = lax.axis_size("section")
    group = lax.axis_size("dp")
    dp_id = lax.axis_index("dp")
    share = section_count // micro_count
    assert cell_count == 1 and share == 2 and section_count == 4 and layers == 2
    cell = section_id // share
    half = section_id % share
    rows = seq_len // share
    direct = group == 8
    line = Line(jnp.zeros((1, 1), F32))

    def mine(stacked):
        return lax.dynamic_slice(
            stacked, (cell, 0, half * rows, 0), (1, 1, rows, width)
        ).reshape(rows, width)

    stream = mine(tokens)
    length = lax.dynamic_slice(lengths, (cell, 0), (1, 1)).reshape(())
    lens = jnp.stack([length - half * rows, length - (1 - half) * rows])

    def attn_first(l, vec, blocks):
        normed, queries, own = line.run(qkv_part, stream, vec, blocks)
        return normed, queries, own, to_core(own)

    if direct:
        a1_block, f1_block, rest_block = line.run(
            pick_blocks, qkv_weight, out_weight, up_weight, down_weight,
            attn_gain, attn_shift, qv_bias, out_bias, ffn_gain, ffn_shift, up_bias, down_bias,
        )
        a1_near = gather_along(a1_block[None])
        f1_near = gather_along(f1_block)
        rest = lax.all_gather(rest_block, ("dp", "section"), axis=0, tiled=False)
        rest = rest.reshape(8, 4, 3, size, width)
        a1 = Gather(line, *line.run(lambda near: split_near(near, (1,)), a1_near), size)
        a1.middle()
        u1_d1 = line.run(lambda near: split_near(near, (1, 1)), f1_near)
        u1 = Gather(line, *u1_d1[:2], size)
        d1 = Gather(line, *u1_d1[2:], size)
        vecs = a1.whole()[0]
        vec1, vec2 = vecs[0], vecs[1]
        attn1 = (a1.pair, 0)
    else:
        def gather(block, axis):
            return lax.all_gather(block, "dp", axis=axis, tiled=True)

        def relative(blocks):
            found = [pick_row(blocks, section_id ^ n) for n in range(4)]
            return jnp.stack([found[0], found[2]])[None], jnp.stack([found[1], found[3]])[None]

        def attn_blocks(l):
            whole = gather(jnp.concatenate([qkv_weight[l], out_weight[l]], axis=1), 0)
            return relative(whole.reshape(8, eighth, 4, width).transpose(2, 0, 1, 3))

        def up_blocks(l):
            return relative(gather(up_weight[l], 0).reshape(8, eighth, 4, width).transpose(2, 0, 1, 3))

        def down_blocks(l):
            return relative(gather(down_weight[l], 0).reshape(8, 4, eighth, width).transpose(1, 0, 2, 3))

        def spread_vectors():
            def at(block, row_count):
                empty = jnp.zeros((layers, row_count, width), BF16)
                flat = block.shape[-1] * dp_id
                return lax.dynamic_update_slice(empty, block, (0, flat // width, flat % width))

            six = jnp.stack([attn_gain, attn_shift, out_bias, ffn_gain, ffn_shift, down_bias], axis=1)
            six = lax.dynamic_update_slice(
                jnp.zeros((layers, 6, width), BF16), six, (0, 0, dp_id * size)
            )
            qv = at(qv_bias[:, None], 2)
            ups = at(up_bias[:, None], 4)
            return jnp.concatenate(
                [six[:, :2], qv, six[:, 2:5], ups, six[:, 5:], jnp.zeros((layers, 4, width), BF16)],
                axis=1,
            )

        vecs = lax.psum(spread_vectors().astype(F32), "dp")
        vec1, vec2 = vecs[0], vecs[1]
        attn1, ups1, downs1 = [(blocks(0), 0) for blocks in (attn_blocks, up_blocks, down_blocks)]
        attn2, ups2, downs2 = [(blocks(1), 0) for blocks in (attn_blocks, up_blocks, down_blocks)]

    def redistribute_start(block):
        quarter = rows // 2
        route_a = [(2 * c + h, 2 * h + c) for c in range(2) for h in range(2)]
        route_b = [(2 * c + h, 2 * h + 1 - c) for c in range(2) for h in range(2)]
        low_half, high_half = block[:quarter], block[quarter:]
        first = cell == 0
        send_a, send_b = line.run(
            lambda low, high: (jnp.where(first, low, high), jnp.where(first, high, low)),
            low_half, high_half,
        )
        return lax.ppermute(send_a, "section", route_a), lax.ppermute(send_b, "section", route_b)

    def redistribute_end(got_a, got_b):
        even = section_id % 2 == 0
        return line.run(
            lambda a, b: jnp.stack([jnp.where(even, a, b), jnp.where(even, b, a)])[:, None],
            got_a, got_b,
        )

    attn_in1 = stream
    normed1, queries1, own1 = line.run(qkv_part, stream, vec1, attn1)
    peer1 = to_core(own1)
    if direct:
        u1.middle()
        d1.middle()
    mixed1, raised1, scale1 = line.run(attend, queries1, own1, peer1, lens)
    if direct:
        u1.whole()
        ups1 = (u1.pair, 0)
    ffn_in1 = line.run(out_part, attn_in1, mixed1, vec1, attn1)
    if direct:
        d1.whole()
        downs1 = (d1.pair, 0)
    normed2_1, hidden1, slope1 = line.run(up_part, ffn_in1, vec1, ups1)
    stream = line.run(down_part, ffn_in1, hidden1, vec1, downs1)
    attn_in2 = stream
    if direct:
        ups2, downs2, attn2 = ((rest,), 0), ((rest,), 1), ((rest,), 2)
    normed2, queries2, own2 = line.run(qkv_part, stream, vec2, attn2)
    peer2 = to_core(own2)
    mixed2, raised2, scale2 = line.run(attend, queries2, own2, peer2, lens)
    ffn_in2 = line.run(out_part, attn_in2, mixed2, vec2, attn2)
    normed2_2, hidden2, slope2 = line.run(up_part, ffn_in2, vec2, ups2)
    stream = line.run(down_part, ffn_in2, hidden2, vec2, downs2)

    encoded_got = redistribute_start(stream)
    grad = mine(cotangent)
    grad, grad_mixed, f2_keep, f2_send, f2_vec = line.run(
        ffn_back, grad, ffn_in2, normed2_2, hidden2, slope2, vec2, ups2, downs2, attn2
    )
    encoded = redistribute_end(*encoded_got)
    if direct:
        f2_got = to_core(f2_send)
    grad_q, kv_own, kv_peer = line.run(
        attend_back, queries2, own2, peer2, mixed2, grad_mixed, raised2, scale2
    )
    kv_got = to_core(kv_peer)
    if direct:
        f2_part = scatter_both(line.run(add_both, f2_keep, f2_got))
    grad, a2_keep, a2_send, a2_vec = line.run(
        qkv_back, grad, attn_in2, normed2, mixed2, (grad_q, kv_own, kv_got), vec2, attn2
    )
    if direct:
        a2_got = to_core(a2_send)
    grad, grad_mixed, f1_keep, f1_send, f1_vec = line.run(
        ffn_back, grad, ffn_in1, normed2_1, hidden1, slope1, vec1, ups1, downs1, attn1
    )
    if direct:
        f1_got = to_core(f1_send)
        a2r = Reduce(line, *line.run(add_first, a2_keep, a2_got))
    grad_q, kv_own, kv_peer = line.run(
        attend_back, queries1, own1, peer1, mixed1, grad_mixed, raised1, scale1
    )
    kv_got = to_core(kv_peer)
    if direct:
        a2r.second()
        f1r = Reduce(line, *line.run(add_first, f1_keep, f1_got))
    grad, a1_keep, a1_send, a1_vec = line.run(
        qkv_back, grad, attn_in1, normed1, mixed1, (grad_q, kv_own, kv_got), vec1, attn1
    )
    if direct:
        a1_got = to_core(a1_send)
        f1r.second()
        a2r.third()
        vec_grads = line.run(
            lambda a, b, c, d: jnp.stack([jnp.concatenate([a, b]), jnp.concatenate([c, d])]),
            a1_vec, f1_vec, a2_vec, f2_vec,
        )
        vec_all = lax.all_gather(vec_grads, ("dp", "section"), axis=0, tiled=False)
        a1r = Reduce(line, *line.run(add_first, a1_keep, a1_got))
        f1r.third_split()
        a1r.second()
        f1r.last()
        f1_held = across(f1r.shard)
        a1r.third_split()
        tokens_got = redistribute_start(grad)
        f2_far = to_x(f2_part[1])
        rest_own = line.run(
            lambda near, far, attn: jnp.concatenate([near[0] + far, attn]), f2_part, f2_far, a2r.shard
        )
        rest_held = lax.all_gather(rest_own, "section", axis=0)
        a1r.last()
        a1_held = across(a1r.shard)
        grad_tokens = redistribute_end(*tokens_got)
        total = line.run(lambda a: jnp.sum(a, axis=0), vec_all)
        g_qkv, g_out, g_up, g_down = line.run(finish, *a1_held, *f1_held, rest_held)
    else:
        grad_tokens = redistribute_end(*redistribute_start(grad))
        vec_grads = jnp.stack(
            [jnp.concatenate([a1_vec, f1_vec]), jnp.concatenate([a2_vec, f2_vec])]
        )

        def canonical(keep, send):
            blocks = jnp.stack([keep[0], send[0], keep[1], send[1]])
            return jnp.stack([pick_row(blocks, section_id ^ n) for n in range(4)])

        def scatter(whole):
            part = lax.psum_scatter(whole, "dp", scatter_dimension=0, tiled=True)
            return lax.psum(part, "section").astype(F32)

        def wide(blocks):
            return blocks.transpose(1, 2, 0, 3).reshape(width, 4 * width)

        both = [
            (canonical(a1_keep, a1_send), canonical(f1_keep, f1_send)),
            (canonical(a2_keep, a2_send), canonical(f2_keep, f2_send)),
        ]
        attn_all = jnp.stack([scatter(wide(attn[:, 0])) for attn, _ in both])
        g_qkv, g_out = attn_all[:, :, :width3], attn_all[:, :, width3:]
        g_up = jnp.stack([scatter(wide(ffn[:, 0])) for _, ffn in both])
        g_down = jnp.stack(
            [scatter(ffn[:, 1].transpose(1, 0, 2, 3).reshape(4 * width, width)) for _, ffn in both]
        )
        total = lax.psum(vec_grads, ("dp", "section"))

    total = total + line.token
    my_vec = lax.dynamic_slice_in_dim(total, dp_id * size, size, 2)
    qv = lax.dynamic_slice_in_dim(total[:, 2:4].reshape(layers, 2 * width), dp_id * 2 * size, 2 * size, 1)
    ups = lax.dynamic_slice_in_dim(total[:, 10:14].reshape(layers, 4 * width), dp_id * 4 * size, 4 * size, 1)
    return (
        encoded, grad_tokens, my_vec[:, 0], my_vec[:, 1], g_qkv, qv, g_out, my_vec[:, 4],
        my_vec[:, 8], my_vec[:, 9], g_up, ups, g_down, my_vec[:, 14],
    )


def solution(mesh):
    flat, rows4 = P(None, "dp"), P(None, "dp", None, None)
    mat, spread = P(None, "dp", None), P(None, "dp", "section", None)
    in_specs = (
        rows4, flat, rows4, flat, flat, mat, flat, mat, flat, flat, flat, mat, flat, mat, flat,
    )
    out_specs = (
        spread, spread, flat, flat, mat, flat, mat, flat, flat, flat, mat, flat, mat, flat,
    )
    return jax.shard_map(local, mesh=mesh, in_specs=in_specs, out_specs=out_specs, check_vma=False)
```

time: 1380 us -> 608 us (0.44)
  waiting for transfers between devices: 959 us -> 187 us
  Pallas kernels: 68.9 us -> 265 us
  matrix products: 117 us -> 0 us
  blocking collectives: 139 us -> 28.9 us
  starting transfers between devices: 8.8 us -> 57 us
  other arithmetic: 28 us -> 8.51 us
    reduce_scatter x8 -> x2, waiting for transfers between devices: 537 us -> 14 us  [the longest x1 14 us: third(): lax.psum_scatter(whole, 'dp', scatter_dimension=0, tiled=True, axis_index...]
    all_gather x8 -> x4, waiting for transfers between devices: 357 us -> 52.3 us  [the longest x1 35.5 us: local(): vec_all = lax.all_gather(vec_grads, ('dp', 'section'), axis=0, tiled=False)]
    pallas_call x2 -> x36, Pallas kernels: 35.4 us -> 231 us  [the longest x33 186 us: call(): pl.pallas_call(body, in_specs=[PLACED if n in placed else WHOLE for n in...]
    dot_general x24 -> x0, matrix products: 117 us -> none  [the longest x8 41.4 us: nn_dot(): return jnp.dot(left, right, preferred_element_type=F32)]
    ppermute x12 -> x52, waiting for transfers between devices: 2.77 us -> 120 us  [the longest x48 110 us: over(): return lax.ppermute(block, axis, [(i, move(i)) for i in range(count)])]
    unnamed x2 -> x0, blocking collectives: 74.7 us -> none
    psum x1 -> x0, waiting for transfers between devices: 60.3 us -> none  [scatter(): return lax.psum(shard, 'section').astype(F32)]
    ppermute x12 -> x52, starting transfers between devices: 7.64 us -> 56.7 us  [the longest x48 48.7 us: over(): return lax.ppermute(block, axis, [(i, move(i)) for i in range(count)])]
  transfers between devices with their start and end apart: 29 -> 58, of which waited for: 15 -> 22; matrix products, arithmetic and copies ran while one was open for 10% -> 2% of each run, Pallas kernels for 4% -> 30%
where the time goes in v2:
time: 608 us; the launch traced here: 601 us
  Pallas kernels  265 us (44%)
  waiting for transfers between devices  187 us (31%)
  starting transfers between devices  57 us (9%)
  local copies, waits for them, and re-layouts  37.6 us (6%)
  blocking collectives  28.9 us (5%)
  between operations  16.3 us (3%)
  other arithmetic  8.51 us (1%)
    pallas_call x33, Pallas kernels, call(): pl.pallas_call(body, in_specs=[PLACED if n in placed else WHOLE for n in...  186 us
    ppermute x48, waiting for transfers between devices, over(): return lax.ppermute(block, axis, [(i, move(i)) for i in range(count)])  110 us
    ppermute x48, starting transfers between devices, over(): return lax.ppermute(block, axis, [(i, move(i)) for i in range(count)])  48.7 us
    pallas_call x2, Pallas kernels, attend_back(): pl.pallas_call(attend_back_kernel, grid=(pairs,), in_specs=[block, key, k...  36 us
    all_gather x1, waiting for transfers between devices, local(): vec_all = lax.all_gather(vec_grads, ('dp', 'section'), axis=0, tiled=False)  35.5 us
    pallas_call x2, Pallas kernels, attend(): pl.pallas_call(attend_kernel, grid_spec=pltpu.PrefetchScalarGridSpec(num_...  34.6 us
    all_gather x1, blocking collectives, gather_along(): return lax.all_gather(block, 'dp', axis=0, axis_index_groups=ALONG)  28.9 us
    unnamed x136, local copies, waits for them, and re-layouts  28.3 us
  transfers between devices with their start and end apart: 58, of which 22 were waited for; matrix products, arithmetic and copies ran while one was open for 2% of the time, Pallas kernels for 30%

profile of v2, /device:TPU:0, one launch (start us, length us, event | category | flops | bytes accessed | tf_op | source)
XLA Modules:
  0.0 600.5 jit_solution(14469050667218569649)
XLA Ops:
  7.2 3.2 shard_map.254
  11.3 28.9 %all-gather = bf16[512,768]{1,0:T(8,128)(2,1)} all-gather(bf16[128,768]{1,0:T(8,128)(2,1)} %get-tuple-element.526), channel_id=2, replica_groups={{0,8,16,24},{4,12,20,28},{1,9,17,25},{5,13,21,29},{2,10,18,26},{6,14,22..., dimensions={0}, use_global_device_ids=true | all-gather | bytes 983040 | tf_op jit(solution)/shard_map/all_gather | solution.py:561
  45.1 5.1 collective-permute-done.left_got
  52.4 2.6 shard_map.256
  57.2 2.3 shard_map.257
  59.5 13.6 %collective-permute-done.2.x_got = bf16[8,1,128,384]{3,2,1,0:T(8,128)(2,1)} collective-permute-done((bf16[8,1,128,384]{3,2,1,0:T(8,128)(2,1)}, bf16[8,1,128,384]{3,2,1,0:T(8,128)(2,1)}, u32[]{:S(2)}, u32[]{:S(2)}) %collective-permute-start.2) | collective-permute-done | bytes 786464 | tf_op jit(solution)/shard_map/ppermute | solution.py:538
  74.4 3.5 shard_map.258
  86.3 6.1 %shard_map.259 = (bf16[512,768]{1,0:T(8,128)(2,1)}, bf16[512,768]{1,0:T(8,128)(2,1)}, bf16[2,512,768]{2,1,0:T(8,128)(2,1)}) custom-call(bf16[512,768]{1,0:T(8,128)(2,1)} %dynamic-slice_bitcast_fusion.1.h_ref, f32[16,768]{1,0:T(8,128)} %get-tuple-element.845.vec_ref, bf16[1,2,8,96,768]{4,3,2,1,0:T(8,128)(2,1)} %get-tuple-element.846.refs_0_.refs_4_, ...), custom_call_target="tpu_custom_call" | custom-call | flops 1342177280 | bytes 65536 | tf_op jit(solution)/shard_map/pallas_call | solution.py:43
  92.4 10.4 %collective-permute-done.8.left_got = bf16[4,1,96,384]{3,2,1,0:T(8,128)(2,1)S(1)} collective-permute-done((bf16[4,1,96,384]{3,2,1,0:T(8,128)(2,1)}, bf16[4,1,96,384]{3,2,1,0:T(8,128)(2,1)S(1)}, u32[]{:S(2)}, u32[]{:S(2)}) %collective-permute-start.8) | collective-permute-done | bytes 294944 | tf_op jit(solution)/shard_map/ppermute | solution.py:538
  102.8 7.2 %collective-permute-done.9.right_got = bf16[4,1,96,384]{3,2,1,0:T(8,128)(2,1)S(1)} collective-permute-done((bf16[4,1,96,384]{3,2,1,0:T(8,128)(2,1)}, bf16[4,1,96,384]{3,2,1,0:T(8,128)(2,1)S(1)}, u32[]{:S(2)}, u32[]{:S(2)}) %collective-permute-start.9) | collective-permute-done | bytes 294944 | tf_op jit(solution)/shard_map/ppermute | solution.py:538
  110.7 2.4 shard_map.260
  114.1 2.3 shard_map.261
  120.9 17.2 %shard_map.262 = (bf16[512,768]{1,0:T(8,128)(2,1)S(1)}, bf16[12,1024,512]{2,1,0:T(8,128)(2,1)}, f32[512,768]{1,0:T(8,128)S(1)}) custom-call(s32[2]{0:T(128)S(1)} %pad_add_fusion.lens_ref, bf16[512,768]{1,0:T(8,128)(2,1)S(1)} %copy-done.10, bf16[2,512,768]{2,1,0:T(8,128)(2,1)S(1)} %copy-done.6, bf16[2,512,768]{2,1,0:T(8,128)(2,1)} %copy-done.18, ...), custom_call_target="tpu_custom_call" | custom-call | flops 4294967296 | bytes 65536 | tf_op jit(solution)/shard_map/pallas_call | solution.py:103
  141.8 3.2 shard_map.263.refs_0_
  145.1 4.3 shard_map.264.h_ref
  149.4 5.5 collective-permute-done.13.x_got
  156.2 3.3 shard_map.265.refs_0_.refs_2_
  160.9 9.4 %shard_map.266 = (bf16[512,768]{1,0:T(8,128)(2,1)}, bf16[4,512,768]{2,1,0:T(8,128)(2,1)}, bf16[4,512,768]{2,1,0:T(8,128)(2,1)}) custom-call(bf16[512,768]{1,0:T(8,128)(2,1)} %shard_map.264.h_ref, f32[16,768]{1,0:T(8,128)} %get-tuple-element.845.vec_ref, bf16[1,2,8,96,768]{4,3,2,1,0:T(8,128)(2,1)} %shard_map.263.refs_0_, bf16[1,2,8,96,768]{4,3,2,1,0:T(8,128)(2,1)} %copy-done.20), custom_call_target="tpu_custom_call" | custom-call | flops 2415919104 | bytes 65536 | tf_op jit(solution)/shard_map/pallas_call | solution.py:43
  171.7 9.2 %shard_map.267.h_ref = bf16[512,768]{1,0:T(8,128)(2,1)} custom-call(bf16[512,768]{1,0:T(8,128)(2,1)} %shard_map.264.h_ref, bf16[4,512,768]{2,1,0:T(8,128)(2,1)} %get-tuple-element.768.g_hbm, f32[16,768]{1,0:T(8,128)} %get-tuple-element.845.vec_ref, bf16[1,2,8,96,768]{4,3,2,1,0:T(8,128)(2,1)} %shard_map.265.refs_0_.refs_2_, bf16[1,2,8,96,768]{4,3,2,1,0:T(8,128)(2,1)} %copy-done.17), custom_call_target="tpu_custom_call" | custom-call | flops 1610612736 | bytes 65536 | tf_op jit(solution)/shard_map/pallas_call | solution.py:43
  180.9 6.1 %shard_map.268 = (bf16[512,768]{1,0:T(8,128)(2,1)}, bf16[512,768]{1,0:T(8,128)(2,1)}, bf16[2,512,768]{2,1,0:T(8,128)(2,1)}) custom-call(bf16[512,768]{1,0:T(8,128)(2,1)} %shard_map.267.h_ref, f32[16,768]{1,0:T(8,128)} %get-tuple-element.754.vec_ref, bf16[8,4,3,96,768]{4,3,2,1,0:T(8,128)(2,1)} %bitcast.53), custom_call_target="tpu_custom_call" | custom-call | flops 1342177280 | bytes 65536 | tf_op jit(solution)/shard_map/pallas_call | solution.py:43
  187.6 2.1 dynamic-slice_bitcast_fusion.gy_ref
  194.6 17.4 %shard_map.269 = (bf16[512,768]{1,0:T(8,128)(2,1)S(1)}, bf16[12,1024,512]{2,1,0:T(8,128)(2,1)}, f32[512,768]{1,0:T(8,128)S(1)}) custom-call(s32[2]{0:T(128)S(1)} %pad_add_fusion.lens_ref, bf16[512,768]{1,0:T(8,128)(2,1)S(1)} %copy-done.11, bf16[2,512,768]{2,1,0:T(8,128)(2,1)S(1)} %copy-done.7, bf16[2,512,768]{2,1,0:T(8,128)(2,1)} %copy-done.19, ...), custom_call_target="tpu_custom_call" | custom-call | flops 4294967296 | bytes 65536 | tf_op jit(solution)/shard_map/pallas_call | solution.py:103
  214.1 4.3 shard_map.270.h_ref
  218.4 9.4 %shard_map.271 = (bf16[512,768]{1,0:T(8,128)(2,1)}, bf16[4,512,768]{2,1,0:T(8,128)(2,1)}, bf16[4,512,768]{2,1,0:T(8,128)(2,1)}) custom-call(bf16[512,768]{1,0:T(8,128)(2,1)} %shard_map.270.h_ref, f32[16,768]{1,0:T(8,128)} %get-tuple-element.754.vec_ref, bf16[8,4,3,96,768]{4,3,2,1,0:T(8,128)(2,1)} %bitcast.55), custom_call_target="tpu_custom_call" | custom-call | flops 2415919104 | bytes 65536 | tf_op jit(solution)/shard_map/pallas_call | solution.py:43
  227.8 8.9 %shard_map.272 = bf16[512,768]{1,0:T(8,128)(2,1)} custom-call(bf16[512,768]{1,0:T(8,128)(2,1)} %shard_map.270.h_ref, bf16[4,512,768]{2,1,0:T(8,128)(2,1)} %get-tuple-element.703.g_hbm, f32[16,768]{1,0:T(8,128)} %get-tuple-element.754.vec_ref, bf16[8,4,3,96,768]{4,3,2,1,0:T(8,128)(2,1)} %bitcast.56), custom_call_target="tpu_custom_call" | custom-call | flops 1610612736 | bytes 65536 | tf_op jit(solution)/shard_map/pallas_call | solution.py:43
  238.7 20.1 %shard_map.273 = (bf16[512,768]{1,0:T(8,128)(2,1)}, bf16[512,768]{1,0:T(8,128)(2,1)}, bf16[2,2,8,96,768]{4,3,2,1,0:T(8,128)(2,1)}, bf16[2,2,8,96,768]{4,3,2,1,0:T(8,128)(2,1)}, f32[8,768]{1,0:T(8,128)}) custom-call(bf16[512,768]{1,0:T(8,128)(2,1)} %dynamic-slice_bitcast_fusion.gy_ref, bf16[512,768]{1,0:T(8,128)(2,1)} %shard_map.270.h_ref, ...), custom_call_target="tpu_custom_call" | custom-call | flops 5368709120 | bytes 65536 | tf_op jit(solution)/shard_map/pallas_call | solution.py:43
  259.3 4.6 collective-permute-start.17
  263.9 9.5 %collective-permute-done.18 = bf16[256,768]{1,0:T(8,128)(2,1)} collective-permute-done((bf16[256,768]{1,0:T(8,128)(2,1)S(1)}, bf16[256,768]{1,0:T(8,128)(2,1)}, u32[]{:S(2)}, u32[]{:S(2)}) %collective-permute-start.18) | collective-permute-done | bytes 393248 | tf_op jit(solution)/shard_map/ppermute | solution.py:1011
  275.5 17.8 %shard_map.274 = (bf16[512,768]{1,0:T(8,128)(2,1)S(1)}, f32[2,512,768]{2,1,0:T(8,128)}, bf16[2,512,768]{2,1,0:T(8,128)(2,1)}) custom-call(bf16[512,768]{1,0:T(8,128)(2,1)S(1)} %copy-done.12, bf16[2,512,768]{2,1,0:T(8,128)(2,1)} %get-tuple-element.727.ko_ref.vo_ref, bf16[2,512,768]{2,1,0:T(8,128)(2,1)} %copy-done.19, ...), custom_call_target="tpu_custom_call" | custom-call | flops 4294967296 | bytes 65536 | tf_op jit(solution)/shard_map/pallas_call | solution.py:166
  294.2 8.6 %shard_map.275 = bf16[8,2,2,96,768]{4,3,2,1,0:T(8,128)(2,1)} custom-call(bf16[2,2,8,96,768]{4,3,2,1,0:T(8,128)(2,1)} %get-tuple-element.743.keep_ref, bf16[2,2,8,96,768]{4,3,2,1,0:T(8,128)(2,1)} %collective-permute-done.20.got_ref), custom_call_target="tpu_custom_call" | custom-call | flops 16106127360 | bytes 65536 | tf_op jit(solution)/shard_map/pallas_call | solution.py:753
  304.0 10.9 %shard_map.276 = (bf16[512,768]{1,0:T(8,128)(2,1)}, bf16[2,1,8,96,768]{4,3,2,1,0:T(8,128)(2,1)}, bf16[2,1,8,96,768]{4,3,2,1,0:T(8,128)(2,1)}, f32[8,768]{1,0:T(8,128)}) custom-call(bf16[512,768]{1,0:T(8,128)(2,1)} %get-tuple-element.747.gy_ref, bf16[512,768]{1,0:T(8,128)(2,1)} %shard_map.267.h_ref, bf16[512,768]{1,0:T(8,128)(2,1)} %get-tuple-element.749.a_ref, ...), custom_call_target="tpu_custom_call" | custom-call | flops 2684354560 | bytes 65536 | tf_op jit(solution)/shard_map/pallas_call | solution.py:43
  315.5 19.2 %shard_map.277 = (bf16[512,768]{1,0:T(8,128)(2,1)}, bf16[512,768]{1,0:T(8,128)(2,1)}, bf16[2,2,8,96,768]{4,3,2,1,0:T(8,128)(2,1)}, bf16[2,2,8,96,768]{4,3,2,1,0:T(8,128)(2,1)}, f32[8,768]{1,0:T(8,128)}) custom-call(bf16[512,768]{1,0:T(8,128)(2,1)} %get-tuple-element.765.gy_ref, bf16[512,768]{1,0:T(8,128)(2,1)} %shard_map.264.h_ref, ...), custom_call_target="tpu_custom_call" | custom-call | flops 5368709120 | bytes 65536 | tf_op jit(solution)/shard_map/pallas_call | solution.py:43
  336.2 4.0 shard_map.278
  341.9 18.1 %shard_map.279 = (bf16[512,768]{1,0:T(8,128)(2,1)S(1)}, f32[2,512,768]{2,1,0:T(8,128)}, bf16[2,512,768]{2,1,0:T(8,128)(2,1)S(1)}) custom-call(bf16[512,768]{1,0:T(8,128)(2,1)S(1)} %copy-done.10, bf16[2,512,768]{2,1,0:T(8,128)(2,1)} %get-tuple-element.800.ko_ref.vo_ref, bf16[2,512,768]{2,1,0:T(8,128)(2,1)} %copy-done.18, ...), custom_call_target="tpu_custom_call" | custom-call | flops 4294967296 | bytes 65536 | tf_op jit(solution)/shard_map/pallas_call | solution.py:166
  360.1 2.9 shard_map.280
  363.1 6.6 %shard_map.281 = (bf16[2,8,96,384]{3,2,1,0:T(8,128)(2,1)}, bf16[2,2,4,96,384]{4,3,2,1,0:T(8,128)(2,1)}, bf16[2,8,96,384]{3,2,1,0:T(8,128)(2,1)}, bf16[2,2,4,96,384]{4,3,2,1,0:T(8,128)(2,1)}) custom-call(bf16[2,2,8,96,768]{4,3,2,1,0:T(8,128)(2,1)} %get-tuple-element.830.keep_ref, bf16[2,2,8,96,768]{4,3,2,1,0:T(8,128)(2,1)} %collective-permute-done.23.got_ref), custom_call_target="tpu_custom_call" | custom-call | flops 1342177280 | bytes 65536 | tf_op jit(solution)/shard_map/pallas_call | solution.py:43
  374.9 12.7 %shard_map.282 = (bf16[512,768]{1,0:T(8,128)(2,1)}, bf16[2,1,8,96,768]{4,3,2,1,0:T(8,128)(2,1)}, bf16[2,1,8,96,768]{4,3,2,1,0:T(8,128)(2,1)}, f32[8,768]{1,0:T(8,128)}) custom-call(bf16[512,768]{1,0:T(8,128)(2,1)} %get-tuple-element.838.gy_ref, bf16[512,768]{1,0:T(8,128)(2,1)} %dynamic-slice_bitcast_fusion.1.h_ref, ...), custom_call_target="tpu_custom_call" | custom-call | flops 2684354560 | bytes 65536 | tf_op jit(solution)/shard_map/pallas_call | solution.py:43
  387.6 11.1 %collective-permute-done.29.x_got = bf16[2,8,96,384]{3,2,1,0:T(8,128)(2,1)S(1)} collective-permute-done((bf16[2,8,96,384]{3,2,1,0:T(8,128)(2,1)}, bf16[2,8,96,384]{3,2,1,0:T(8,128)(2,1)S(1)}, u32[]{:S(2)}, u32[]{:S(2)}) %collective-permute-start.29) | collective-permute-done | bytes 1179680 | tf_op jit(solution)/shard_map/ppermute | solution.py:538
  398.7 13.9 %collective-permute-done.30.y_got = bf16[2,2,4,96,384]{4,3,2,1,0:T(8,128)(2,1)} collective-permute-done((bf16[2,2,4,96,384]{4,3,2,1,0:T(8,128)(2,1)}, bf16[2,2,4,96,384]{4,3,2,1,0:T(8,128)(2,1)}, u32[]{:S(2)}, u32[]{:S(2)}) %collective-permute-start.30) | collective-permute-done | bytes 1179680 | tf_op jit(solution)/shard_map/ppermute | solution.py:538
  412.6 4.1 shard_map.283
  416.8 6.6 %collective-permute-done.27.y_got = bf16[1,4,96,384]{3,2,1,0:T(8,128)(2,1)} collective-permute-done((bf16[1,4,96,384]{3,2,1,0:T(8,128)(2,1)S(1)}, bf16[1,4,96,384]{3,2,1,0:T(8,128)(2,1)}, u32[]{:S(2)}, u32[]{:S(2)}) %collective-permute-start.27) | collective-permute-done | bytes 294944 | tf_op jit(solution)/shard_map/ppermute | solution.py:538
  423.4 2.2 shard_map.284
  429.3 3.9 shard_map.285
  435.9 8.9 %collective-permute-done.33.y_got = bf16[2,4,96,384]{3,2,1,0:T(8,128)(2,1)} collective-permute-done((bf16[2,4,96,384]{3,2,1,0:T(8,128)(2,1)}, bf16[2,4,96,384]{3,2,1,0:T(8,128)(2,1)}, u32[]{:S(2)}, u32[]{:S(2)}) %collective-permute-start.33) | collective-permute-done | bytes 589856 | tf_op jit(solution)/shard_map/ppermute | solution.py:538
  444.8 2.8 shard_map.286
  447.6 3.5 collective-permute-start.37
  451.1 6.8 %collective-permute-start.38 = (bf16[2,96,768]{2,1,0:T(8,128)(2,1)}, bf16[2,96,768]{2,1,0:T(8,128)(2,1)S(1)}, u32[]{:S(2)}, u32[]{:S(2)}) collective-permute-start(bf16[2,96,768]{2,1,0:T(8,128)(2,1)} %get-tuple-element.932), channel_id=1, source_target_pairs={{0,16},{4,20},{8,24},{12,28},{16,0},{20,4},{24,8},{28,12},{1,17},{... | collective-permute-start | bytes 884744 | tf_op jit(solution)/shard_map/ppermute | solution.py:538
  460.4 2.8 shard_map.287
  463.2 2.4 collective-permute-start.35
  465.6 2.6 collective-permute-start.36
  468.2 3.6 collective-permute-done.37.o1
  471.8 8.3 %collective-permute-done.38.o2 = bf16[2,96,768]{2,1,0:T(8,128)(2,1)S(1)} collective-permute-done((bf16[2,96,768]{2,1,0:T(8,128)(2,1)}, bf16[2,96,768]{2,1,0:T(8,128)(2,1)S(1)}, u32[]{:S(2)}, u32[]{:S(2)}) %collective-permute-start.38) | collective-permute-done | bytes 294944 | tf_op jit(solution)/shard_map/ppermute | solution.py:538
  481.6 2.1 shard_map.288.refs_4_
  486.5 2.1 shard_map.289
  488.6 14.0 %reduce-scatter.5.cloned.1.call-done = bf16[1,1,96,768]{3,2,1,0:T(8,128)(2,1)} async-done(((bf16[4,1,96,768]{3,2,1,0:T(8,128)(2,1)}), bf16[1,1,96,768]{3,2,1,0:T(8,128)(2,1)}) %reduce-scatter.5.cloned.1.call-update) | async-done | bytes 147472 | tf_op jit(solution)/shard_map/reduce_scatter | solution.py:854
  505.2 2.7 collective-permute-start.41
  509.2 2.5 collective-permute-start.44
  512.9 6.5 %collective-permute-done.43.o2 = bf16[1,96,768]{2,1,0:T(8,128)(2,1)S(1)} collective-permute-done((bf16[1,96,768]{2,1,0:T(8,128)(2,1)S(1)}, bf16[1,96,768]{2,1,0:T(8,128)(2,1)S(1)}, u32[]{:S(2)}, u32[]{:S(2)}) %collective-permute-start.43) | collective-permute-done | bytes 147488 | tf_op jit(solution)/shard_map/ppermute | solution.py:538
  523.1 2.2 collective-permute-done.50.refs_6_
  525.8 2.2 collective-permute-done.47.refs_2_
  529.0 35.5 %all-gather.14.cloned.1.call-done = f32[64,16,768]{2,1,0:T(8,128)} async-done(((f32[2,16,768]{2,1,0:T(8,128)}), f32[64,16,768]{2,1,0:T(8,128)}) %all-gather.14.cloned.1.call-update) | async-done | bytes 3145744 | tf_op jit(solution)/shard_map/all_gather | solution.py:1089
  564.4 2.0 reduce_sum.9
  569.3 16.8 %all-gather.16.cloned.1.call-done = bf16[12,96,768]{2,1,0:T(8,128)(2,1)} async-done(((bf16[3,96,768]{2,1,0:T(8,128)(2,1)}), bf16[12,96,768]{2,1,0:T(8,128)(2,1)}) %all-gather.16.cloned.1.call-update) | async-done | bytes 1769488 | tf_op jit(solution)/shard_map/all_gather | solution.py:1101
  586.0 5.4 shard_map.291
  (256 shorter events, 83.8 us)
Async XLA Ops:
  7.2 72.7 %copy-start = (bf16[2,1,1024,768]{3,2,1,0:T(8,128)(2,1)S(1)}, bf16[2,1,1024,768]{3,2,1,0:T(8,128)(2,1)}, u32[]{:S(2)}) copy-start(bf16[2,1,1024,768]{3,2,1,0:T(8,128)(2,1)} %param.15) | copy-start | bytes 9437188
  7.2 50.0 %all-gather.10.cloned.1.call-start = ((), (), s32[]{:S(2)}) async-start(), calls=%async_computation.4 | async-start | bytes 1474560 | tf_op jit(solution)/shard_map/all_gather | solution.py:561
  10.5 170.4 %all-gather.12.cloned.1.call-start = ((), (), s32[]{:S(2)}) async-start(), calls=%async_computation.5 | async-start | bytes 14598144 | tf_op jit(solution)/shard_map/all_gather | solution.py:951
  11.2 472.4 %reduce-scatter.3.cloned.1.call-start = ((), (), s32[]{:S(2)}) async-start(), calls=%async_computation.2 | async-start | bytes 5308416 | tf_op jit(solution)/shard_map/reduce_scatter | solution.py:765
  42.2 8.0 %collective-permute-start = (bf16[4,1,128,384]{3,2,1,0:T(8,128)(2,1)}, bf16[4,1,128,384]{3,2,1,0:T(8,128)(2,1)S(1)}, u32[]{:S(2)}, u32[]{:S(2)}) collective-permute-start(bf16[4,1,128,384]{3,2,1,0:T(8,128)(2,1)} %get-tuple-element.535.left_ref), channel_id=1, source_target_pairs={{0,4},{4,0},{8,12},{12,8},{16,20},{20,16},{24,28},{28,24},{1,5},{5... | collective-permute-start | bytes 1179656 | tf_op jit(solution)/shard_map/ppermute | solution.py:538
  43.7 8.0 %collective-permute-start.1 = (bf16[4,1,128,384]{3,2,1,0:T(8,128)(2,1)}, bf16[4,1,128,384]{3,2,1,0:T(8,128)(2,1)S(1)}, u32[]{:S(2)}, u32[]{:S(2)}) collective-permute-start(bf16[4,1,128,384]{3,2,1,0:T(8,128)(2,1)} %get-tuple-element.537.right_ref), channel_id=1, source_target_pairs={{0,2},{1,3},{2,0},{3,1},{4,6},{5,7},{6,4},{7,5},{8,10},{9,11},{10,... | collective-permute-start | bytes 1179656 | tf_op jit(solution)/shard_map/ppermute | solution.py:538
  55.0 18.1 %collective-permute-start.2 = (bf16[8,1,128,384]{3,2,1,0:T(8,128)(2,1)}, bf16[8,1,128,384]{3,2,1,0:T(8,128)(2,1)}, u32[]{:S(2)}, u32[]{:S(2)}) collective-permute-start(bf16[8,1,128,384]{3,2,1,0:T(8,128)(2,1)} %get-tuple-element.553.x_ref), channel_id=1, source_target_pairs={{0,2},{1,3},{2,0},{3,1},{4,6},{5,7},{6,4},{7,5},{8,10},{9,11},{10,... | collective-permute-start | bytes 2359304 | tf_op jit(solution)/shard_map/ppermute | solution.py:538
  56.4 17.9 %collective-permute-start.3 = (bf16[2,4,1,128,384]{4,3,2,1,0:T(8,128)(2,1)}, bf16[2,4,1,128,384]{4,3,2,1,0:T(8,128)(2,1)}, u32[]{:S(2)}, u32[]{:S(2)}) collective-permute-start(bf16[2,4,1,128,384]{4,3,2,1,0:T(8,128)(2,1)} %get-tuple-element.555.y_ref), channel_id=1, source_target_pairs={{0,4},{4,0},{8,12},{12,8},{16,20},{20,16},{24,28},{28,24},{1,5},{5... | collective-permute-start | bytes 2359304 | tf_op jit(solution)/shard_map/ppermute | solution.py:538
  57.2 20.7 %copy-start.65 = (s32[2,1]{0,1:T(1,128)S(1)}, s32[2,1]{0,1:T(1,128)}, u32[]{:S(2)}) copy-start(s32[2,1]{0,1:T(1,128)} %param.16) | copy-start | bytes 28
  59.5 21.3 %copy-start.41 = (bf16[4,1,96,384]{3,2,1,0:T(8,128)(2,1)S(1)}, bf16[4,1,96,384]{3,2,1,0:T(8,128)(2,1)}, u32[]{:S(2)}) copy-start(bf16[4,1,96,384]{3,2,1,0:T(8,128)(2,1)} %get-tuple-element.586.left_ref) | copy-start | bytes 884740
  77.9 8.4 %collective-permute-start.4 = (bf16[1,2,8,96,768]{4,3,2,1,0:T(8,128)(2,1)}, bf16[1,2,8,96,768]{4,3,2,1,0:T(8,128)(2,1)}, u32[]{:S(2)}, u32[]{:S(2)}) collective-permute-start(bf16[1,2,8,96,768]{4,3,2,1,0:T(8,128)(2,1)} %get-tuple-element.846.refs_0_.refs_4_), channel_id=1, source_target_pairs={{0,1},{1,0},{2,3},{3,2},{4,5},{5,4},{6,7},{7,6},{8,9},{9,8},{10,11... | collective-permute-start | bytes 7077896 | tf_op jit(solution)/shard_map/ppermute | solution.py:538
  80.8 32.4 %collective-permute-start.6 = (bf16[4,1,96,384]{3,2,1,0:T(8,128)(2,1)S(1)}, bf16[4,1,96,384]{3,2,1,0:T(8,128)(2,1)S(1)}, u32[]{:S(2)}, u32[]{:S(2)}) collective-permute-start(bf16[4,1,96,384]{3,2,1,0:T(8,128)(2,1)S(1)} %copy-done.41), channel_id=1, source_target_pairs={{0,4},{4,0},{8,12},{12,8},{16,20},{20,16},{24,28},{28,24},{1,5},{5... | collective-permute-start | bytes 884744 | tf_op jit(solution)/shard_map/ppermute | solution.py:538
  81.8 31.4 %collective-permute-start.7 = (bf16[4,1,96,384]{3,2,1,0:T(8,128)(2,1)}, bf16[4,1,96,384]{3,2,1,0:T(8,128)(2,1)S(1)}, u32[]{:S(2)}, u32[]{:S(2)}) collective-permute-start(bf16[4,1,96,384]{3,2,1,0:T(8,128)(2,1)} %get-tuple-element.588.right_ref), channel_id=1, source_target_pairs={{0,2},{1,3},{2,0},{3,1},{4,6},{5,7},{6,4},{7,5},{8,10},{9,11},{10,... | collective-permute-start | bytes 884744 | tf_op jit(solution)/shard_map/ppermute | solution.py:538
  82.3 20.5 %collective-permute-start.8 = (bf16[4,1,96,384]{3,2,1,0:T(8,128)(2,1)}, bf16[4,1,96,384]{3,2,1,0:T(8,128)(2,1)S(1)}, u32[]{:S(2)}, u32[]{:S(2)}) collective-permute-start(bf16[4,1,96,384]{3,2,1,0:T(8,128)(2,1)} %get-tuple-element.578.left_ref), channel_id=1, source_target_pairs={{0,4},{4,0},{8,12},{12,8},{16,20},{20,16},{24,28},{28,24},{1,5},{5... | collective-permute-start | bytes 884744 | tf_op jit(solution)/shard_map/ppermute | solution.py:538
  83.3 26.7 %collective-permute-start.9 = (bf16[4,1,96,384]{3,2,1,0:T(8,128)(2,1)}, bf16[4,1,96,384]{3,2,1,0:T(8,128)(2,1)S(1)}, u32[]{:S(2)}, u32[]{:S(2)}) collective-permute-start(bf16[4,1,96,384]{3,2,1,0:T(8,128)(2,1)} %get-tuple-element.580.right_ref), channel_id=1, source_target_pairs={{0,2},{1,3},{2,0},{3,1},{4,6},{5,7},{6,4},{7,5},{8,10},{9,11},{10,... | collective-permute-start | bytes 884744 | tf_op jit(solution)/shard_map/ppermute | solution.py:538
  92.4 27.3 %collective-permute-start.5 = (bf16[2,512,768]{2,1,0:T(8,128)(2,1)}, bf16[2,512,768]{2,1,0:T(8,128)(2,1)S(1)}, u32[]{:S(2)}, u32[]{:S(2)}) collective-permute-start(bf16[2,512,768]{2,1,0:T(8,128)(2,1)} %get-tuple-element.800.ko_ref.vo_ref), channel_id=1, source_target_pairs={{0,1},{1,0},{2,3},{3,2},{4,5},{5,4},{6,7},{7,6},{8,9},{9,8},{10,11... | collective-permute-start | bytes 4718600 | tf_op jit(solution)/shard_map/ppermute | solution.py:538
  113.2 27.0 %collective-permute-start.10 = (bf16[8,1,96,384]{3,2,1,0:T(8,128)(2,1)}, bf16[8,1,96,384]{3,2,1,0:T(8,128)(2,1)S(1)}, u32[]{:S(2)}, u32[]{:S(2)}) collective-permute-start(bf16[8,1,96,384]{3,2,1,0:T(8,128)(2,1)} %get-tuple-element.606.x_ref), channel_id=1, source_target_pairs={{0,2},{1,3},{2,0},{3,1},{4,6},{5,7},{6,4},{7,5},{8,10},{9,11},{10,... | collective-permute-start | bytes 1769480 | tf_op jit(solution)/shard_map/ppermute | solution.py:538
  113.8 26.3 %collective-permute-start.11 = (bf16[2,4,1,96,384]{4,3,2,1,0:T(8,128)(2,1)}, bf16[2,4,1,96,384]{4,3,2,1,0:T(8,128)(2,1)S(1)}, u32[]{:S(2)}, u32[]{:S(2)}) collective-permute-start(bf16[2,4,1,96,384]{4,3,2,1,0:T(8,128)(2,1)} %get-tuple-element.608.y_ref), channel_id=1, source_target_pairs={{0,4},{4,0},{8,12},{12,8},{16,20},{20,16},{24,28},{28,24},{1,5},{5... | collective-permute-start | bytes 1769480 | tf_op jit(solution)/shard_map/ppermute | solution.py:538
  116.4 38.4 %collective-permute-start.13 = (bf16[8,1,96,384]{3,2,1,0:T(8,128)(2,1)}, bf16[8,1,96,384]{3,2,1,0:T(8,128)(2,1)S(1)}, u32[]{:S(2)}, u32[]{:S(2)}) collective-permute-start(bf16[8,1,96,384]{3,2,1,0:T(8,128)(2,1)} %get-tuple-element.623.x_ref), channel_id=1, source_target_pairs={{0,2},{1,3},{2,0},{3,1},{4,6},{5,7},{6,4},{7,5},{8,10},{9,11},{10,... | collective-permute-start | bytes 1769480 | tf_op jit(solution)/shard_map/ppermute | solution.py:538
  118.0 38.2 %collective-permute-start.14 = (bf16[2,4,1,96,384]{4,3,2,1,0:T(8,128)(2,1)}, bf16[2,4,1,96,384]{4,3,2,1,0:T(8,128)(2,1)}, u32[]{:S(2)}, u32[]{:S(2)}) collective-permute-start(bf16[2,4,1,96,384]{4,3,2,1,0:T(8,128)(2,1)} %get-tuple-element.625.y_ref), channel_id=1, source_target_pairs={{0,4},{4,0},{8,12},{12,8},{16,20},{20,16},{24,28},{28,24},{1,5},{5... | collective-permute-start | bytes 1769480 | tf_op jit(solution)/shard_map/ppermute | solution.py:538
  145.1 14.4 %collective-permute-start.12 = (bf16[1,2,8,96,768]{4,3,2,1,0:T(8,128)(2,1)}, bf16[1,2,8,96,768]{4,3,2,1,0:T(8,128)(2,1)S(1)}, u32[]{:S(2)}, u32[]{:S(2)}) collective-permute-start(bf16[1,2,8,96,768]{4,3,2,1,0:T(8,128)(2,1)} %shard_map.263.refs_0_), channel_id=1, source_target_pairs={{0,1},{1,0},{2,3},{3,2},{4,5},{5,4},{6,7},{7,6},{8,9},{9,8},{10,11... | collective-permute-start | bytes 7077896 | tf_op jit(solution)/shard_map/ppermute | solution.py:538
  159.5 10.9 %collective-permute-start.15 = (bf16[1,2,8,96,768]{4,3,2,1,0:T(8,128)(2,1)}, bf16[1,2,8,96,768]{4,3,2,1,0:T(8,128)(2,1)S(1)}, u32[]{:S(2)}, u32[]{:S(2)}) collective-permute-start(bf16[1,2,8,96,768]{4,3,2,1,0:T(8,128)(2,1)} %shard_map.265.refs_0_.refs_2_), channel_id=1, source_target_pairs={{0,1},{1,0},{2,3},{3,2},{4,5},{5,4},{6,7},{7,6},{8,9},{9,8},{10,11... | collective-permute-start | bytes 7077896 | tf_op jit(solution)/shard_map/ppermute | solution.py:538
  187.0 3.8 collective-permute-start.16
  258.9 35.4 %collective-permute-start.20 = (bf16[2,2,8,96,768]{4,3,2,1,0:T(8,128)(2,1)}, bf16[2,2,8,96,768]{4,3,2,1,0:T(8,128)(2,1)}, u32[]{:S(2)}, u32[]{:S(2)}) collective-permute-start(bf16[2,2,8,96,768]{4,3,2,1,0:T(8,128)(2,1)} %get-tuple-element.741), channel_id=1, source_target_pairs={{0,1},{1,0},{2,3},{3,2},{4,5},{5,4},{6,7},{7,6},{8,9},{9,8},{10,11... | collective-permute-start | bytes 14155784 | tf_op jit(solution)/shard_map/ppermute | solution.py:538
  259.3 4.6 collective-permute-start.17
  263.9 9.5 %collective-permute-start.18 = (bf16[256,768]{1,0:T(8,128)(2,1)S(1)}, bf16[256,768]{1,0:T(8,128)(2,1)}, u32[]{:S(2)}, u32[]{:S(2)}) collective-permute-start(bf16[256,768]{1,0:T(8,128)(2,1)S(1)} %get-tuple-element.696), channel_id=1, source_target_pairs={{0,1},{1,3},{2,0},{3,2},{4,5},{5,7},{6,4},{7,6},{8,9},{9,11},{10,8... | collective-permute-start | bytes 1179656 | tf_op jit(solution)/shard_map/ppermute | solution.py:1011
  294.2 8.7 %collective-permute-start.19 = (bf16[2,512,768]{2,1,0:T(8,128)(2,1)}, bf16[2,512,768]{2,1,0:T(8,128)(2,1)S(1)}, u32[]{:S(2)}, u32[]{:S(2)}) collective-permute-start(bf16[2,512,768]{2,1,0:T(8,128)(2,1)} %get-tuple-element.739), channel_id=1, source_target_pairs={{0,1},{1,0},{2,3},{3,2},{4,5},{5,4},{6,7},{7,6},{8,9},{9,8},{10,11... | collective-permute-start | bytes 4718600 | tf_op jit(solution)/shard_map/ppermute | solution.py:538
  314.9 19.8 %collective-permute-start.21 = (bf16[2,1,8,96,768]{4,3,2,1,0:T(8,128)(2,1)}, bf16[2,1,8,96,768]{4,3,2,1,0:T(8,128)(2,1)S(1)}, u32[]{:S(2)}, u32[]{:S(2)}) collective-permute-start(bf16[2,1,8,96,768]{4,3,2,1,0:T(8,128)(2,1)} %get-tuple-element.789), channel_id=1, source_target_pairs={{0,1},{1,0},{2,3},{3,2},{4,5},{5,4},{6,7},{7,6},{8,9},{9,8},{10,11... | collective-permute-start | bytes 7077896 | tf_op jit(solution)/shard_map/ppermute | solution.py:538
  334.7 28.4 %collective-permute-start.23 = (bf16[2,2,8,96,768]{4,3,2,1,0:T(8,128)(2,1)}, bf16[2,2,8,96,768]{4,3,2,1,0:T(8,128)(2,1)}, u32[]{:S(2)}, u32[]{:S(2)}) collective-permute-start(bf16[2,2,8,96,768]{4,3,2,1,0:T(8,128)(2,1)} %get-tuple-element.814), channel_id=1, source_target_pairs={{0,1},{1,0},{2,3},{3,2},{4,5},{5,4},{6,7},{7,6},{8,9},{9,8},{10,11... | collective-permute-start | bytes 14155784 | tf_op jit(solution)/shard_map/ppermute | solution.py:538
  340.1 20.0 %collective-permute-start.24 = (bf16[1,8,96,384]{3,2,1,0:T(8,128)(2,1)}, bf16[1,8,96,384]{3,2,1,0:T(8,128)(2,1)}, u32[]{:S(2)}, u32[]{:S(2)}) collective-permute-start(bf16[1,8,96,384]{3,2,1,0:T(8,128)(2,1)} %get-tuple-element.816), channel_id=1, source_target_pairs={{0,2},{1,3},{2,0},{3,1},{4,6},{5,7},{6,4},{7,5},{8,10},{9,11},{10,... | collective-permute-start | bytes 1769480 | tf_op jit(solution)/shard_map/ppermute | solution.py:538
  340.8 19.3 %collective-permute-start.25 = (bf16[2,1,4,96,384]{4,3,2,1,0:T(8,128)(2,1)}, bf16[2,1,4,96,384]{4,3,2,1,0:T(8,128)(2,1)}, u32[]{:S(2)}, u32[]{:S(2)}) collective-permute-start(bf16[2,1,4,96,384]{4,3,2,1,0:T(8,128)(2,1)} %get-tuple-element.818), channel_id=1, source_target_pairs={{0,4},{4,0},{8,12},{12,8},{16,20},{20,16},{24,28},{28,24},{1,5},{5... | collective-permute-start | bytes 1769480 | tf_op jit(solution)/shard_map/ppermute | solution.py:538
  341.8 160.8 %reduce-scatter.5.cloned.1.call-start = ((), (), s32[]{:S(2)}) async-start(), calls=%async_computation.3 | async-start | bytes 737280 | tf_op jit(solution)/shard_map/reduce_scatter | solution.py:854
  360.0 13.7 %collective-permute-start.22 = (bf16[2,512,768]{2,1,0:T(8,128)(2,1)S(1)}, bf16[2,512,768]{2,1,0:T(8,128)(2,1)S(1)}, u32[]{:S(2)}, u32[]{:S(2)}) collective-permute-start(bf16[2,512,768]{2,1,0:T(8,128)(2,1)S(1)} %get-tuple-element.812), channel_id=1, source_target_pairs={{0,1},{1,0},{2,3},{3,2},{4,5},{5,4},{6,7},{7,6},{8,9},{9,8},{10,11... | collective-permute-start | bytes 4718600 | tf_op jit(solution)/shard_map/ppermute | solution.py:538
  369.7 29.0 %collective-permute-start.29 = (bf16[2,8,96,384]{3,2,1,0:T(8,128)(2,1)}, bf16[2,8,96,384]{3,2,1,0:T(8,128)(2,1)S(1)}, u32[]{:S(2)}, u32[]{:S(2)}) collective-permute-start(bf16[2,8,96,384]{3,2,1,0:T(8,128)(2,1)} %get-tuple-element.865), channel_id=1, source_target_pairs={{0,2},{1,3},{2,0},{3,1},{4,6},{5,7},{6,4},{7,5},{8,10},{9,11},{10,... | collective-permute-start | bytes 3538952 | tf_op jit(solution)/shard_map/ppermute | solution.py:538
  370.8 41.8 %collective-permute-start.30 = (bf16[2,2,4,96,384]{4,3,2,1,0:T(8,128)(2,1)}, bf16[2,2,4,96,384]{4,3,2,1,0:T(8,128)(2,1)}, u32[]{:S(2)}, u32[]{:S(2)}) collective-permute-start(bf16[2,2,4,96,384]{4,3,2,1,0:T(8,128)(2,1)} %get-tuple-element.867), channel_id=1, source_target_pairs={{0,4},{4,0},{8,12},{12,8},{16,20},{20,16},{24,28},{28,24},{1,5},{5... | collective-permute-start | bytes 3538952 | tf_op jit(solution)/shard_map/ppermute | solution.py:538
  372.1 51.3 %collective-permute-start.27 = (bf16[1,4,96,384]{3,2,1,0:T(8,128)(2,1)S(1)}, bf16[1,4,96,384]{3,2,1,0:T(8,128)(2,1)}, u32[]{:S(2)}, u32[]{:S(2)}) collective-permute-start(bf16[1,4,96,384]{3,2,1,0:T(8,128)(2,1)S(1)} %copy-done.44), channel_id=1, source_target_pairs={{0,4},{4,0},{8,12},{12,8},{16,20},{20,16},{24,28},{28,24},{1,5},{5... | collective-permute-start | bytes 884744 | tf_op jit(solution)/shard_map/ppermute | solution.py:538
  372.9 50.5 %collective-permute-start.28 = (bf16[1,4,96,384]{3,2,1,0:T(8,128)(2,1)S(1)}, bf16[1,4,96,384]{3,2,1,0:T(8,128)(2,1)}, u32[]{:S(2)}, u32[]{:S(2)}) collective-permute-start(bf16[1,4,96,384]{3,2,1,0:T(8,128)(2,1)S(1)} %copy-done.43), channel_id=1, source_target_pairs={{0,2},{1,3},{2,0},{3,1},{4,6},{5,7},{6,4},{7,5},{8,10},{9,11},{10,... | collective-permute-start | bytes 884744 | tf_op jit(solution)/shard_map/ppermute | solution.py:538
  387.6 40.4 %collective-permute-start.26 = (bf16[2,1,8,96,768]{4,3,2,1,0:T(8,128)(2,1)}, bf16[2,1,8,96,768]{4,3,2,1,0:T(8,128)(2,1)S(1)}, u32[]{:S(2)}, u32[]{:S(2)}) collective-permute-start(bf16[2,1,8,96,768]{4,3,2,1,0:T(8,128)(2,1)} %get-tuple-element.855), channel_id=1, source_target_pairs={{0,1},{1,0},{2,3},{3,2},{4,5},{5,4},{6,7},{7,6},{8,9},{9,8},{10,11... | collective-permute-start | bytes 7077896 | tf_op jit(solution)/shard_map/ppermute | solution.py:538
  425.6 138.8 %all-gather.14.cloned.1.call-start = ((), (), s32[]{:S(2)}) async-start(), calls=%async_computation.6 | async-start | bytes 3244032 | tf_op jit(solution)/shard_map/all_gather | solution.py:1089
  425.7 19.1 %collective-permute-start.33 = (bf16[2,4,96,384]{3,2,1,0:T(8,128)(2,1)}, bf16[2,4,96,384]{3,2,1,0:T(8,128)(2,1)}, u32[]{:S(2)}, u32[]{:S(2)}) collective-permute-start(bf16[2,4,96,384]{3,2,1,0:T(8,128)(2,1)} %get-tuple-element.903), channel_id=1, source_target_pairs={{0,4},{4,0},{8,12},{12,8},{16,20},{20,16},{24,28},{28,24},{1,5},{5... | collective-permute-start | bytes 1769480 | tf_op jit(solution)/shard_map/ppermute | solution.py:538
  427.2 17.6 %collective-permute-start.34 = (bf16[2,4,96,384]{3,2,1,0:T(8,128)(2,1)S(1)}, bf16[2,4,96,384]{3,2,1,0:T(8,128)(2,1)}, u32[]{:S(2)}, u32[]{:S(2)}) collective-permute-start(bf16[2,4,96,384]{3,2,1,0:T(8,128)(2,1)S(1)} %copy-done.35), channel_id=1, source_target_pairs={{0,2},{1,3},{2,0},{3,1},{4,6},{5,7},{6,4},{7,5},{8,10},{9,11},{10,... | collective-permute-start | bytes 1769480 | tf_op jit(solution)/shard_map/ppermute | solution.py:538
  427.9 158.2 %all-gather.16.cloned.1.call-start = ((), (), s32[]{:S(2)}) async-start(), calls=%async_computation.7 | async-start | bytes 2211840 | tf_op jit(solution)/shard_map/all_gather | solution.py:1101
  433.3 25.5 %collective-permute-start.31 = (bf16[1,8,96,384]{3,2,1,0:T(8,128)(2,1)}, bf16[1,8,96,384]{3,2,1,0:T(8,128)(2,1)S(1)}, u32[]{:S(2)}, u32[]{:S(2)}) collective-permute-start(bf16[1,8,96,384]{3,2,1,0:T(8,128)(2,1)} %get-tuple-element.899), channel_id=1, source_target_pairs={{0,2},{1,3},{2,0},{3,1},{4,6},{5,7},{6,4},{7,5},{8,10},{9,11},{10,... | collective-permute-start | bytes 1769480 | tf_op jit(solution)/shard_map/ppermute | solution.py:538
  435.3 23.5 %collective-permute-start.32 = (bf16[2,1,4,96,384]{4,3,2,1,0:T(8,128)(2,1)}, bf16[2,1,4,96,384]{4,3,2,1,0:T(8,128)(2,1)S(1)}, u32[]{:S(2)}, u32[]{:S(2)}) collective-permute-start(bf16[2,1,4,96,384]{4,3,2,1,0:T(8,128)(2,1)} %get-tuple-element.901), channel_id=1, source_target_pairs={{0,4},{4,0},{8,12},{12,8},{16,20},{20,16},{24,28},{28,24},{1,5},{5... | collective-permute-start | bytes 1769480 | tf_op jit(solution)/shard_map/ppermute | solution.py:538
  447.6 24.2 %collective-permute-start.37 = (bf16[2,96,768]{2,1,0:T(8,128)(2,1)}, bf16[2,96,768]{2,1,0:T(8,128)(2,1)S(1)}, u32[]{:S(2)}, u32[]{:S(2)}) collective-permute-start(bf16[2,96,768]{2,1,0:T(8,128)(2,1)} %get-tuple-element.931), channel_id=1, source_target_pairs={{0,8},{4,12},{8,16},{12,20},{16,24},{20,28},{24,0},{28,4},{1,9},{5... | collective-permute-start | bytes 884744 | tf_op jit(solution)/shard_map/ppermute | solution.py:538
  451.1 29.1 %collective-permute-start.38 = (bf16[2,96,768]{2,1,0:T(8,128)(2,1)}, bf16[2,96,768]{2,1,0:T(8,128)(2,1)S(1)}, u32[]{:S(2)}, u32[]{:S(2)}) collective-permute-start(bf16[2,96,768]{2,1,0:T(8,128)(2,1)} %get-tuple-element.932), channel_id=1, source_target_pairs={{0,16},{4,20},{8,24},{12,28},{16,0},{20,4},{24,8},{28,12},{1,17},{... | collective-permute-start | bytes 884744 | tf_op jit(solution)/shard_map/ppermute | solution.py:538
  457.8 22.3 %collective-permute-start.39 = (bf16[2,96,768]{2,1,0:T(8,128)(2,1)}, bf16[2,96,768]{2,1,0:T(8,128)(2,1)S(1)}, u32[]{:S(2)}, u32[]{:S(2)}) collective-permute-start(bf16[2,96,768]{2,1,0:T(8,128)(2,1)} %get-tuple-element.933), channel_id=1, source_target_pairs={{0,24},{4,28},{8,0},{12,4},{16,8},{20,12},{24,16},{28,20},{1,25},{... | collective-permute-start | bytes 884744 | tf_op jit(solution)/shard_map/ppermute | solution.py:538
  463.2 20.5 %collective-permute-start.35 = (bf16[1,4,96,384]{3,2,1,0:T(8,128)(2,1)}, bf16[1,4,96,384]{3,2,1,0:T(8,128)(2,1)S(1)}, u32[]{:S(2)}, u32[]{:S(2)}) collective-permute-start(bf16[1,4,96,384]{3,2,1,0:T(8,128)(2,1)} %get-tuple-element.927), channel_id=1, source_target_pairs={{0,4},{4,0},{8,12},{12,8},{16,20},{20,16},{24,28},{28,24},{1,5},{5... | collective-permute-start | bytes 884744 | tf_op jit(solution)/shard_map/ppermute | solution.py:538
  465.6 18.1 %collective-permute-start.36 = (bf16[1,4,96,384]{3,2,1,0:T(8,128)(2,1)}, bf16[1,4,96,384]{3,2,1,0:T(8,128)(2,1)S(1)}, u32[]{:S(2)}, u32[]{:S(2)}) collective-permute-start(bf16[1,4,96,384]{3,2,1,0:T(8,128)(2,1)} %get-tuple-element.929), channel_id=1, source_target_pairs={{0,2},{1,3},{2,0},{3,1},{4,6},{5,7},{6,4},{7,5},{8,10},{9,11},{10,... | collective-permute-start | bytes 884744 | tf_op jit(solution)/shard_map/ppermute | solution.py:538
  484.9 17.7 %collective-permute-start.45 = (bf16[2,96,768]{2,1,0:T(8,128)(2,1)S(1)}, bf16[2,96,768]{2,1,0:T(8,128)(2,1)S(1)}, u32[]{:S(2)}, u32[]{:S(2)}) collective-permute-start(bf16[2,96,768]{2,1,0:T(8,128)(2,1)S(1)} %slice_bitcast_fusion), channel_id=1, source_target_pairs={{0,2},{1,3},{2,0},{3,1},{4,6},{5,7},{6,4},{7,5},{8,10},{9,11},{10,... | collective-permute-start | bytes 884744 | tf_op jit(solution)/shard_map/ppermute | solution.py:538
  488.6 23.2 %copy-start.40 = (bf16[2,96,768]{2,1,0:T(8,128)(2,1)S(1)}, bf16[2,96,768]{2,1,0:T(8,128)(2,1)}, u32[]{:S(2)}) copy-start(bf16[2,96,768]{2,1,0:T(8,128)(2,1)} %shard_map.288.refs_4_) | copy-start | bytes 884740
  504.4 7.3 %collective-permute-start.42 = (bf16[1,96,768]{2,1,0:T(8,128)(2,1)S(1)}, bf16[1,96,768]{2,1,0:T(8,128)(2,1)S(1)}, u32[]{:S(2)}, u32[]{:S(2)}) collective-permute-start(bf16[1,96,768]{2,1,0:T(8,128)(2,1)S(1)} %copy-done.59), channel_id=1, source_target_pairs={{0,8},{4,12},{8,16},{12,20},{16,24},{20,28},{24,0},{28,4},{1,9},{5... | collective-permute-start | bytes 442376 | tf_op jit(solution)/shard_map/ppermute | solution.py:538
  504.5 20.8 %collective-permute-start.40 = (bf16[256,768]{1,0:T(8,128)(2,1)S(1)}, bf16[256,768]{1,0:T(8,128)(2,1)S(1)}, u32[]{:S(2)}, u32[]{:S(2)}) collective-permute-start(bf16[256,768]{1,0:T(8,128)(2,1)S(1)} %get-tuple-element.954), channel_id=1, source_target_pairs={{0,0},{1,2},{2,1},{3,3},{4,4},{5,6},{6,5},{7,7},{8,8},{9,10},{10,9... | collective-permute-start | bytes 1179656 | tf_op jit(solution)/shard_map/ppermute | solution.py:1011
  505.2 20.6 %collective-permute-start.41 = (bf16[256,768]{1,0:T(8,128)(2,1)S(1)}, bf16[256,768]{1,0:T(8,128)(2,1)S(1)}, u32[]{:S(2)}, u32[]{:S(2)}) collective-permute-start(bf16[256,768]{1,0:T(8,128)(2,1)S(1)} %get-tuple-element.955), channel_id=1, source_target_pairs={{0,1},{1,3},{2,0},{3,2},{4,5},{5,7},{6,4},{7,6},{8,9},{9,11},{10,8... | collective-permute-start | bytes 1179656 | tf_op jit(solution)/shard_map/ppermute | solution.py:1011
  507.9 11.5 %collective-permute-start.43 = (bf16[1,96,768]{2,1,0:T(8,128)(2,1)S(1)}, bf16[1,96,768]{2,1,0:T(8,128)(2,1)S(1)}, u32[]{:S(2)}, u32[]{:S(2)}) collective-permute-start(bf16[1,96,768]{2,1,0:T(8,128)(2,1)S(1)} %copy-done.58), channel_id=1, source_target_pairs={{0,16},{4,20},{8,24},{12,28},{16,0},{20,4},{24,8},{28,12},{1,17},{... | collective-permute-start | bytes 442376 | tf_op jit(solution)/shard_map/ppermute | solution.py:538
  509.2 10.2 %collective-permute-start.44 = (bf16[1,96,768]{2,1,0:T(8,128)(2,1)S(1)}, bf16[1,96,768]{2,1,0:T(8,128)(2,1)S(1)}, u32[]{:S(2)}, u32[]{:S(2)}) collective-permute-start(bf16[1,96,768]{2,1,0:T(8,128)(2,1)S(1)} %copy-done.57), channel_id=1, source_target_pairs={{0,24},{4,28},{8,0},{12,4},{16,8},{20,12},{24,16},{28,20},{1,25},{... | collective-permute-start | bytes 442376 | tf_op jit(solution)/shard_map/ppermute | solution.py:538
  511.8 13.5 %collective-permute-start.50 = (bf16[2,96,768]{2,1,0:T(8,128)(2,1)S(1)}, bf16[2,96,768]{2,1,0:T(8,128)(2,1)S(1)}, u32[]{:S(2)}, u32[]{:S(2)}) collective-permute-start(bf16[2,96,768]{2,1,0:T(8,128)(2,1)S(1)} %copy-done.40), channel_id=1, source_target_pairs={{0,2},{1,3},{2,0},{3,1},{4,6},{5,7},{6,4},{7,5},{8,10},{9,11},{10,... | collective-permute-start | bytes 884744 | tf_op jit(solution)/shard_map/ppermute | solution.py:538
  522.6 5.4 collective-permute-start.47
  523.1 43.4 %collective-permute-start.49 = (bf16[2,96,768]{2,1,0:T(8,128)(2,1)S(1)}, bf16[2,96,768]{2,1,0:T(8,128)(2,1)S(1)}, u32[]{:S(2)}, u32[]{:S(2)}) collective-permute-start(bf16[2,96,768]{2,1,0:T(8,128)(2,1)S(1)} %copy-done.40), channel_id=1, source_target_pairs={{0,1},{1,0},{2,3},{3,2},{4,5},{5,4},{6,7},{7,6},{8,9},{9,8},{10,11... | collective-permute-start | bytes 884744 | tf_op jit(solution)/shard_map/ppermute | solution.py:538
  525.2 41.3 %copy-start.42 = (bf16[2,96,768]{2,1,0:T(8,128)(2,1)}, bf16[2,96,768]{2,1,0:T(8,128)(2,1)S(1)}, u32[]{:S(2)}) copy-start(bf16[2,96,768]{2,1,0:T(8,128)(2,1)S(1)} %collective-permute-done.50.refs_6_) | copy-start | bytes 884740
  525.2 41.3 %collective-permute-start.51 = (bf16[2,96,768]{2,1,0:T(8,128)(2,1)S(1)}, bf16[2,96,768]{2,1,0:T(8,128)(2,1)S(1)}, u32[]{:S(2)}, u32[]{:S(2)}) collective-permute-start(bf16[2,96,768]{2,1,0:T(8,128)(2,1)S(1)} %collective-permute-done.50.refs_6_), channel_id=1, source_target_pairs={{0,1},{1,0},{2,3},{3,2},{4,5},{5,4},{6,7},{7,6},{8,9},{9,8},{10,11... | collective-permute-start | bytes 884744 | tf_op jit(solution)/shard_map/ppermute | solution.py:538
  525.3 42.0 %collective-permute-start.46 = (bf16[1,96,768]{2,1,0:T(8,128)(2,1)}, bf16[1,96,768]{2,1,0:T(8,128)(2,1)S(1)}, u32[]{:S(2)}, u32[]{:S(2)}) collective-permute-start(bf16[1,96,768]{2,1,0:T(8,128)(2,1)} %shard_map.290.refs_0_), channel_id=1, source_target_pairs={{0,1},{1,0},{2,3},{3,2},{4,5},{5,4},{6,7},{7,6},{8,9},{9,8},{10,11... | collective-permute-start | bytes 442376 | tf_op jit(solution)/shard_map/ppermute | solution.py:538
  527.9 38.6 %copy-start.56 = (bf16[1,96,768]{2,1,0:T(8,128)(2,1)}, bf16[1,96,768]{2,1,0:T(8,128)(2,1)S(1)}, u32[]{:S(2)}) copy-start(bf16[1,96,768]{2,1,0:T(8,128)(2,1)S(1)} %collective-permute-done.47.refs_2_) | copy-start | bytes 442372
  527.9 40.0 %collective-permute-start.48 = (bf16[1,96,768]{2,1,0:T(8,128)(2,1)S(1)}, bf16[1,96,768]{2,1,0:T(8,128)(2,1)S(1)}, u32[]{:S(2)}, u32[]{:S(2)}) collective-permute-start(bf16[1,96,768]{2,1,0:T(8,128)(2,1)S(1)} %collective-permute-done.47.refs_2_), channel_id=1, source_target_pairs={{0,1},{1,0},{2,3},{3,2},{4,5},{5,4},{6,7},{7,6},{8,9},{9,8},{10,11... | collective-permute-start | bytes 442376 | tf_op jit(solution)/shard_map/ppermute | solution.py:538
  (60 other events, 319.9 us)
Sparse Core Ops, SparseCore 0:
  10.6 39.8 all-gather.9
  53.4 127.5 all-gather.11
  341.9 136.7 reduce-scatter.2
  480.9 21.6 reduce-scatter.4
  505.3 59.0 all-gather.13
  566.4 19.5 all-gather.15

commit v3 on v2

--- a/solution.py
+++ b/solution.py
@@ -378,7 +378,7 @@
     down_refs, refs = refs[:down_count], refs[down_count:]
     attn_refs, refs = refs[:attn_count], refs[attn_count:]
     (
-        gh_ref, go_ref, keep_hbm, send_hbm, vg_ref,
+        gh_ref, go_ref, keep_hbm, send_up, send_down, vg_ref,
         g_ref, slope_ref, mat, up_mat, out_mat, up_grad, down_grad,
         in_sems, sems, out_sems, up_sems, down_sems,
     ) = refs
@@ -408,8 +408,8 @@
         grad_up = grad_up.astype(BF16)
         vg_ref[pl.ds(2 + block, 1), :] = jnp.sum(grad_up.astype(F32), axis=0, keepdims=True)
         up_grad[n] = tn_dot(normed, grad_up).astype(BF16).reshape(8, size, width)
-        out = keep_hbm if n in (0, 2) else send_hbm
-        copies.append(start_copy(up_grad.at[n], out.at[n // 2, 0], up_sems.at[n]))
+        out = (keep_hbm.at[:, 0], send_up.at[:, 0])[n % 2]
+        copies.append(start_copy(up_grad.at[n], out.at[n // 2], up_sems.at[n]))
         down_grad[n] = tn_dot(g_ref[n], grad).astype(BF16).reshape(8, size, width)
         for j in range(4):
             place = jnp.bitwise_xor(here, j)
@@ -422,7 +422,7 @@
 
                 @pl.when(place % 2 == 1)
                 def _():
-                    start_copy(src, send_hbm.at[place // 2, 1, 2 * block + side], sem)
+                    start_copy(src, send_down.at[place // 2, 0, 2 * block + side], sem)
 
                 copies.append(pltpu.make_async_copy(src, keep_hbm.at[0, 1, 0], sem))
         term = nt_dot(grad_up, square(up_mat[n]))
@@ -445,12 +445,12 @@
     counts, places = tuple(len(item[0]) for item in sets), tuple(item[1] for item in sets)
     blocks = [ref for item in sets for ref in item[0]]
     block = block_shape(ups[0])
-    part = struct((2, 2) + block, BF16)
+    part, half = struct((2, 2) + block, BF16), struct((2, 1) + block, BF16)
     low = struct((rows, width), BF16)
     dma = pltpu.SemaphoreType.DMA
     return call(
         partial(ffn_back_kernel, places, counts),
-        [low, low, part, part, struct((8, width), F32)],
+        [low, low, part, half, half, struct((8, width), F32)],
         (grad, stream, normed, hidden, slope, vec, *blocks),
         (3, 4, *range(6, 6 + len(blocks))),
         (
@@ -459,7 +459,7 @@
             pltpu.VMEM((1,) + block, BF16), pltpu.VMEM((4,) + block, BF16),
             pltpu.VMEM((4,) + block, BF16), dma((3, 4)), dma((4, 8)), dma((1,)), dma((4,)),
             dma((4, 8)),
-        ), micros=20, out_placed=(2, 3),
+        ), micros=20, out_placed=(2, 3, 4),
     )
 
 
@@ -665,7 +665,7 @@
     part = left.shape[1:]
     return call(
         middle_kernel, [struct((8,) + part, BF16), struct((2, 4) + part, BF16)],
-        (left, left_got, right, right_got), micros=60,
+        (left, left_got, right, right_got), micros=120,
     )
 
 
@@ -679,20 +679,19 @@
                 out_ref[c, n, 2 * along + side, :, wide:] = y_ref[n, along, c, :size]
                 out_ref[c, n, 2 * along + 1 - side, :, wide:] = y_got[n, along, c, :size]
     if ride_refs:
-        vec_ref = ride_refs[0]
         left = jnp.sum(x_ref[:, 0, size:].astype(F32), axis=0)
         right = jnp.sum(y_ref[0, :, 0, size:].astype(F32), axis=0)
         right = right + jnp.sum(y_got[0, :, 0, size:].astype(F32), axis=0)
         for l in range(2):
-            vec_ref[l, :, :wide] = left[16 * l : 16 * l + 16]
-            vec_ref[l, :, wide:] = right[16 * l : 16 * l + 16]
+            ride_refs[l][:, :wide] = left[16 * l : 16 * l + 16]
+            ride_refs[l][:, wide:] = right[16 * l : 16 * l + 16]
 
 
 def whole_blocks(x_send, x_got, y_send, y_got, size):
     _, count, full, wide = x_send.shape
     outs = [struct((count, 2, 8, size, 2 * wide), BF16)]
     if full > size:
-        outs.append(struct((2, 16, 2 * wide), F32))
+        outs += [struct((16, 2 * wide), F32)] * 2
     return call(whole_kernel, outs, (x_send, x_got, y_send, y_got))
 
 
@@ -716,13 +715,15 @@
         return found[1:]
 
 
-def first_kernel(keep_ref, got_ref, x_ref, y_ref, left_ref, right_ref):
+def first_kernel(keep_ref, *refs):
+    got_refs, (x_ref, y_ref, left_ref, right_ref) = refs[:-4], refs[-4:]
     wide = x_ref.shape[-1]
     side = lax.axis_index("dp") % 2
     for c in range(keep_ref.shape[1]):
         for n, ref in enumerate((left_ref, x_ref)):
             ref[c] = (
-                keep_ref[n, c, :, :, :wide].astype(F32) + got_ref[n, c, :, :, :wide].astype(F32)
+                keep_ref[n, c, :, :, :wide].astype(F32)
+                + got_refs[c][n, 0, :, :, :wide].astype(F32)
             ).astype(BF16)
         for n in range(2):
             for along in range(4):
@@ -730,35 +731,39 @@
                     at = 2 * along + pick
                     ref[n, c, along] = (
                         keep_ref[n, c, at, :, wide:].astype(F32)
-                        + got_ref[n, c, at, :, wide:].astype(F32)
+                        + got_refs[c][n, 0, at, :, wide:].astype(F32)
                     ).astype(BF16)
 
 
-def add_first(keep, got):
+def add_first(keep, *got):
     _, count, _, size, width = keep.shape
     x_part = struct((count, 8, size, width // 2), BF16)
     y_part = struct((2, count, 4, size, width // 2), BF16)
-    return call(first_kernel, [x_part, y_part, x_part, y_part], (keep, got), micros=5)
-
-
-def both_kernel(keep_ref, got_ref, out_ref):
-    out_ref[0] = (
-        keep_ref[:, :, 0].astype(F32) + got_ref[:, :, 0].astype(F32)
-    ).astype(BF16)
-
-
-def add_both(keep, got):
+    return call(first_kernel, [x_part, y_part, x_part, y_part], (keep, *got), micros=5)
+
+
+def both_kernel(keep_ref, up_ref, down_ref, out_ref):
+    for c, ref in enumerate((up_ref, down_ref)):
+        for n in range(2):
+            out_ref[:, n, c] = (
+                keep_ref[n, c].astype(F32) + ref[n, 0].astype(F32)
+            ).astype(BF16)
+
+
+def add_both(keep, *got):
     _, count, parts, size, width = keep.shape
-    spec = pl.BlockSpec((2, count, 1, size, width), lambda i: (0, 0, i, 0, 0))
+    step = parts // 4
+    spec = pl.BlockSpec((2, count, step, size, width), lambda i: (0, 0, i, 0, 0))
+    half = pl.BlockSpec((2, 1, step, size, width), lambda i: (0, 0, i, 0, 0))
     return pl.pallas_call(
         both_kernel,
-        grid=(parts,),
-        in_specs=[spec, spec],
-        out_specs=pl.BlockSpec((1, 2, count, size, width), lambda i: (i, 0, 0, 0, 0)),
+        grid=(4,),
+        in_specs=[spec, half, half],
+        out_specs=pl.BlockSpec((step, 2, count, size, width), lambda i: (i, 0, 0, 0, 0)),
         out_shape=struct((parts, 2, count, size, width), BF16),
         compiler_params=pltpu.CompilerParams(vmem_limit_bytes=VMEM_ROOM),
-        cost_estimate=lasting(60),
-    )(keep, got)
+        cost_estimate=lasting(80),
+    )(keep, *got)
 
 
 def scatter_both(block):
@@ -795,11 +800,11 @@
             ).astype(BF16)
 
 
-def add_third(near, y_got, rest, x_got):
+def add_third(micros, near, y_got, rest, x_got):
     count, _, size, wide = near.shape
     return call(
         third_kernel, [struct((4, count, size, 2 * wide), BF16)], (near, y_got, rest, x_got),
-        micros=60,
+        micros=micros,
     )[0]
 
 
@@ -849,8 +854,10 @@
         )
         self.y_got, self.x_got = to_y(y_send), to_x(x_send)
 
-    def third(self):
-        whole = self.line.run(add_third, self.near, self.y_got, self.rest, self.x_got)
+    def third(self, micros):
+        whole = self.line.run(
+            partial(add_third, micros), self.near, self.y_got, self.rest, self.x_got
+        )
         self.shard = lax.psum_scatter(
             whole, "dp", scatter_dimension=0, tiled=True, axis_index_groups=ALONG
         )[0]
@@ -865,10 +872,9 @@
         self.shard = self.line.run(add_last, self.parts[0], *self.z_got)
 
 
-def finish_kernel(*refs):
-    attn, ffn, (rest_ref, qkv_ref, out_ref, up_ref, down_ref) = refs[:4], refs[4:8], refs[8:]
+def finish_kernel(a0, a1, a2, a3, f1_ref, rest_ref, qkv_ref, out_ref, up_ref, down_ref):
     here = lax.axis_index("section")
-    size, width = rest_ref.shape[-2:]
+    size, width = f1_ref.shape[-2:]
 
     def put(l, b, found):
         if b < 3:
@@ -876,20 +882,17 @@
         else:
             out_ref[l] = found.astype(F32)
 
-    def put_ffn(l, b, ups, downs):
-        up_ref[l, :, b * width : (b + 1) * width] = ups.astype(F32)
-        down_ref[l, b * size : (b + 1) * size] = downs.astype(F32)
-
     for m in range(4):
         @pl.when(here == m)
         def _():
             for b in range(4):
-                put(0, b, attn[m ^ b][0])
-                put_ffn(0, b, ffn[m ^ b][0], ffn[m ^ b][1])
+                put(0, b, (a0, a1, a2, a3)[m ^ b][0])
 
     for b in range(4):
         put(1, b, rest_ref[b, 2])
-        put_ffn(1, b, rest_ref[b, 0], rest_ref[b, 1])
+        for l, ref in enumerate((f1_ref, rest_ref)):
+            up_ref[l, :, b * width : (b + 1) * width] = ref[b, 0].astype(F32)
+            down_ref[l, b * size : (b + 1) * size] = ref[b, 1].astype(F32)
 
 
 def finish(*held):
@@ -933,13 +936,14 @@
             stacked, (cell, 0, half * rows, 0), (1, 1, rows, width)
         ).reshape(rows, width)
 
-    stream = mine(tokens)
-    length = lax.dynamic_slice(lengths, (cell, 0), (1, 1)).reshape(())
-    lens = jnp.stack([length - half * rows, length - (1 - half) * rows])
-
-    def attn_first(l, vec, blocks):
-        normed, queries, own = line.run(qkv_part, stream, vec, blocks)
-        return normed, queries, own, to_core(own)
+    def pinned():
+        length = lax.dynamic_slice(lengths, (cell, 0), (1, 1)).reshape(())
+        return line.run(
+            lambda one, two, size: (
+                mine(one), mine(two), jnp.stack([size - half * rows, size - (1 - half) * rows])
+            ),
+            tokens, cotangent, length,
+        )
 
     if direct:
         a1_block, f1_block, rest_block = line.run(
@@ -951,12 +955,13 @@
         rest = lax.all_gather(rest_block, ("dp", "section"), axis=0, tiled=False)
         rest = rest.reshape(8, 4, 3, size, width)
         a1 = Gather(line, *line.run(lambda near: split_near(near, (1,)), a1_near), size)
+        stream, grad, lens = pinned()
         a1.middle()
         u1_d1 = line.run(lambda near: split_near(near, (1, 1)), f1_near)
         u1 = Gather(line, *u1_d1[:2], size)
         d1 = Gather(line, *u1_d1[2:], size)
-        vecs = a1.whole()[0]
-        vec1, vec2 = vecs[0], vecs[1]
+        vec1, vec2 = a1.whole()
+        u1.middle()
         attn1 = (a1.pair, 0)
     else:
         def gather(block, axis):
@@ -998,30 +1003,36 @@
         attn1, ups1, downs1 = [(blocks(0), 0) for blocks in (attn_blocks, up_blocks, down_blocks)]
         attn2, ups2, downs2 = [(blocks(1), 0) for blocks in (attn_blocks, up_blocks, down_blocks)]
 
-    def redistribute_start(block):
+    def redistribute_start(*blocks):
         quarter = rows // 2
         route_a = [(2 * c + h, 2 * h + c) for c in range(2) for h in range(2)]
         route_b = [(2 * c + h, 2 * h + 1 - c) for c in range(2) for h in range(2)]
-        low_half, high_half = block[:quarter], block[quarter:]
         first = cell == 0
-        send_a, send_b = line.run(
-            lambda low, high: (jnp.where(first, low, high), jnp.where(first, high, low)),
-            low_half, high_half,
-        )
+
+        def choose(*items):
+            low = jnp.stack([item[:quarter] for item in items])
+            high = jnp.stack([item[quarter:] for item in items])
+            return jnp.where(first, low, high), jnp.where(first, high, low)
+
+        send_a, send_b = line.run(choose, *blocks)
         return lax.ppermute(send_a, "section", route_a), lax.ppermute(send_b, "section", route_b)
 
     def redistribute_end(got_a, got_b):
         even = section_id % 2 == 0
-        return line.run(
-            lambda a, b: jnp.stack([jnp.where(even, a, b), jnp.where(even, b, a)])[:, None],
-            got_a, got_b,
-        )
+
+        def place(a, b):
+            pair = jnp.where(even, a, b), jnp.where(even, b, a)
+            return tuple(jnp.stack([item[n] for item in pair])[:, None] for n in range(2))
+
+        return line.run(place, got_a, got_b)
+
+    if not direct:
+        stream, grad, lens = pinned()
 
     attn_in1 = stream
     normed1, queries1, own1 = line.run(qkv_part, stream, vec1, attn1)
     peer1 = to_core(own1)
     if direct:
-        u1.middle()
         d1.middle()
     mixed1, raised1, scale1 = line.run(attend, queries1, own1, peer1, lens)
     if direct:
@@ -1043,73 +1054,85 @@
     normed2_2, hidden2, slope2 = line.run(up_part, ffn_in2, vec2, ups2)
     stream = line.run(down_part, ffn_in2, hidden2, vec2, downs2)
 
-    encoded_got = redistribute_start(stream)
-    grad = mine(cotangent)
-    grad, grad_mixed, f2_keep, f2_send, f2_vec = line.run(
+    encoded_mine = stream
+    grad, grad_mixed, f2_keep, f2_up, f2_down, f2_vec = line.run(
         ffn_back, grad, ffn_in2, normed2_2, hidden2, slope2, vec2, ups2, downs2, attn2
     )
-    encoded = redistribute_end(*encoded_got)
     if direct:
-        f2_got = to_core(f2_send)
+        f2_got = to_core(f2_up), to_core(f2_down)
     grad_q, kv_own, kv_peer = line.run(
         attend_back, queries2, own2, peer2, mixed2, grad_mixed, raised2, scale2
     )
     kv_got = to_core(kv_peer)
     if direct:
-        f2_part = scatter_both(line.run(add_both, f2_keep, f2_got))
+        f2_part = scatter_both(line.run(add_both, f2_keep, *f2_got))
     grad, a2_keep, a2_send, a2_vec = line.run(
         qkv_back, grad, attn_in2, normed2, mixed2, (grad_q, kv_own, kv_got), vec2, attn2
     )
     if direct:
         a2_got = to_core(a2_send)
-    grad, grad_mixed, f1_keep, f1_send, f1_vec = line.run(
+        a2r = Reduce(line, *line.run(add_first, a2_keep, a2_got))
+    grad, grad_mixed, f1_keep, f1_up, f1_down, f1_vec = line.run(
         ffn_back, grad, ffn_in1, normed2_1, hidden1, slope1, vec1, ups1, downs1, attn1
     )
     if direct:
-        f1_got = to_core(f1_send)
-        a2r = Reduce(line, *line.run(add_first, a2_keep, a2_got))
+        f1_got = to_core(f1_up), to_core(f1_down)
+        a2r.second()
+        f1r = Reduce(line, *line.run(add_first, f1_keep, *f1_got))
     grad_q, kv_own, kv_peer = line.run(
         attend_back, queries1, own1, peer1, mixed1, grad_mixed, raised1, scale1
     )
     kv_got = to_core(kv_peer)
     if direct:
-        a2r.second()
-        f1r = Reduce(line, *line.run(add_first, f1_keep, f1_got))
+        f1r.second()
+        a2r.third(2)
     grad, a1_keep, a1_send, a1_vec = line.run(
         qkv_back, grad, attn_in1, normed1, mixed1, (grad_q, kv_own, kv_got), vec1, attn1
     )
+
+    def vector_shares(a, b, c, d):
+        total = jnp.stack([jnp.concatenate([a, b]), jnp.concatenate([c, d])])
+
+        def share(lo, hi):
+            wide = total[:, lo:hi].reshape(layers, group, hi - lo, size)
+            return wide.transpose(1, 0, 2, 3)
+
+        def each(lo, hi):
+            wide = total[:, lo:hi].reshape(layers, hi - lo, group, size)
+            return wide.transpose(2, 0, 1, 3)
+
+        return jnp.concatenate(
+            [each(0, 2), share(2, 4), each(4, 10), share(10, 14), each(14, 16)], axis=2
+        )
+
     if direct:
         a1_got = to_core(a1_send)
-        f1r.second()
-        a2r.third()
-        vec_grads = line.run(
-            lambda a, b, c, d: jnp.stack([jnp.concatenate([a, b]), jnp.concatenate([c, d])]),
+        f2_near, f2_send = line.run(lambda part: (part[0], part[1]), f2_part)
+        f1r.third(120)
+        a1r = Reduce(line, *line.run(add_first, a1_keep, a1_got))
+        f2_far = to_x(f2_send)
+        rest_own = line.run(
+            lambda near, far, attn: jnp.concatenate([near + far, attn]), f2_near, f2_far, a2r.shard
+        )
+        rest_held = lax.all_gather(rest_own, "section", axis=0)
+        a1r.second()
+        shares = line.run(
+            lambda *vecs: jnp.broadcast_to(
+                vector_shares(*vecs)[:, None], (group, section_count, layers, 16, size)
+            ).reshape(group * section_count, layers, 16, size),
             a1_vec, f1_vec, a2_vec, f2_vec,
         )
-        vec_all = lax.all_gather(vec_grads, ("dp", "section"), axis=0, tiled=False)
-        a1r = Reduce(line, *line.run(add_first, a1_keep, a1_got))
-        f1r.third_split()
-        a1r.second()
-        f1r.last()
-        f1_held = across(f1r.shard)
+        shares = lax.all_to_all(shares, ("dp", "section"), 0, 0, tiled=True)
         a1r.third_split()
-        tokens_got = redistribute_start(grad)
-        f2_far = to_x(f2_part[1])
-        rest_own = line.run(
-            lambda near, far, attn: jnp.concatenate([near[0] + far, attn]), f2_part, f2_far, a2r.shard
-        )
-        rest_held = lax.all_gather(rest_own, "section", axis=0)
+        moved = redistribute_start(encoded_mine, grad)
+        my_vec = line.run(lambda got: jnp.sum(got, axis=0), shares)
+        f1_held = lax.all_gather(f1r.shard, "section", axis=0)
         a1r.last()
         a1_held = across(a1r.shard)
-        grad_tokens = redistribute_end(*tokens_got)
-        total = line.run(lambda a: jnp.sum(a, axis=0), vec_all)
-        g_qkv, g_out, g_up, g_down = line.run(finish, *a1_held, *f1_held, rest_held)
+        encoded, grad_tokens = redistribute_end(*moved)
+        g_qkv, g_out, g_up, g_down = line.run(finish, *a1_held, f1_held, rest_held)
     else:
-        grad_tokens = redistribute_end(*redistribute_start(grad))
-        vec_grads = jnp.stack(
-            [jnp.concatenate([a1_vec, f1_vec]), jnp.concatenate([a2_vec, f2_vec])]
-        )
-
+        encoded, grad_tokens = redistribute_end(*redistribute_start(encoded_mine, grad))
         def canonical(keep, send):
             blocks = jnp.stack([keep[0], send[0], keep[1], send[1]])
             return jnp.stack([pick_row(blocks, section_id ^ n) for n in range(4)])
@@ -1122,8 +1145,8 @@
             return blocks.transpose(1, 2, 0, 3).reshape(width, 4 * width)
 
         both = [
-            (canonical(a1_keep, a1_send), canonical(f1_keep, f1_send)),
-            (canonical(a2_keep, a2_send), canonical(f2_keep, f2_send)),
+            (canonical(a1_keep, a1_send), canonical(f1_keep, jnp.concatenate([f1_up, f1_down], axis=1))),
+            (canonical(a2_keep, a2_send), canonical(f2_keep, jnp.concatenate([f2_up, f2_down], axis=1))),
         ]
         attn_all = jnp.stack([scatter(wide(attn[:, 0])) for attn, _ in both])
         g_qkv, g_out = attn_all[:, :, :width3], attn_all[:, :, width3:]
@@ -1131,15 +1154,14 @@
         g_down = jnp.stack(
             [scatter(ffn[:, 1].transpose(1, 0, 2, 3).reshape(4 * width, width)) for _, ffn in both]
         )
-        total = lax.psum(vec_grads, ("dp", "section"))
-
-    total = total + line.token
-    my_vec = lax.dynamic_slice_in_dim(total, dp_id * size, size, 2)
-    qv = lax.dynamic_slice_in_dim(total[:, 2:4].reshape(layers, 2 * width), dp_id * 2 * size, 2 * size, 1)
-    ups = lax.dynamic_slice_in_dim(total[:, 10:14].reshape(layers, 4 * width), dp_id * 4 * size, 4 * size, 1)
+        shares = lax.psum(vector_shares(a1_vec, f1_vec, a2_vec, f2_vec), ("dp", "section"))
+        my_vec = pick_row(shares, dp_id)
+
+    my_vec = my_vec + line.token
     return (
-        encoded, grad_tokens, my_vec[:, 0], my_vec[:, 1], g_qkv, qv, g_out, my_vec[:, 4],
-        my_vec[:, 8], my_vec[:, 9], g_up, ups, g_down, my_vec[:, 14],
+        encoded, grad_tokens, my_vec[:, 0], my_vec[:, 1], g_qkv,
+        my_vec[:, 2:4].reshape(layers, 2 * size), g_out, my_vec[:, 4], my_vec[:, 8], my_vec[:, 9],
+        g_up, my_vec[:, 10:14].reshape(layers, 4 * size), g_down, my_vec[:, 14],
     )
 
 

time: 608 us -> 516 us (0.85)
  waiting for transfers between devices: 187 us -> 110 us
  starting transfers between devices: 57 us -> 44.1 us
  local copies, waits for them, and re-layouts: 37.6 us -> 44.2 us
    all_gather x1, waiting for transfers between devices: 35.5 us -> 0.02 us  [local(): f1_held = lax.all_gather(f1r.shard, 'section', axis=0)]
    ppermute x48 -> x44, waiting for transfers between devices: 110 us -> 91.7 us  [over(): return lax.ppermute(block, axis, [(i, move(i)) for i in range(count)])]
    all_gather x1, waiting for transfers between devices: 16.8 us -> 0.02 us  [local(): rest_held = lax.all_gather(rest_own, 'section', axis=0)]
    ppermute x48 -> x44, starting transfers between devices: 48.7 us -> 35.9 us  [over(): return lax.ppermute(block, axis, [(i, move(i)) for i in range(count)])]
    reduce_scatter x1 -> x2, waiting for transfers between devices: 14 us -> 3.81 us  [third(): lax.psum_scatter(whole, 'dp', scatter_dimension=0, tiled=True, axis_index...]
    all_gather x1, waiting for transfers between devices: 0.02 us -> 9.61 us  [local(): rest = lax.all_gather(rest_block, ('dp', 'section'), axis=0, tiled=False)]
    ppermute x2 -> x1, waiting for transfers between devices: 9.46 us -> 0.01 us  [redistribute_start(): lax.ppermute(send_b, 'section', route_b)]
    unnamed x136 -> x130, local copies, waits for them, and re-layouts: 28.3 us -> 36.4 us
  transfers between devices with their start and end apart: 58 -> 54, of which waited for: 22 -> 17; matrix products, arithmetic and copies ran while one was open for 2% -> 2% of each run, Pallas kernels for 30% -> 34%
where the time goes in v3:
time: 516 us; the launch traced here: 509 us
  Pallas kernels  260 us (50%)
  waiting for transfers between devices  110 us (21%)
  local copies, waits for them, and re-layouts  44.2 us (9%)
  starting transfers between devices  44.1 us (9%)
  blocking collectives  28.9 us (6%)
  between operations  16.5 us (3%)
  other arithmetic  5.3 us (1%)
    pallas_call x32, Pallas kernels, call(): pl.pallas_call(body, in_specs=[PLACED if n in placed else WHOLE for n in...  184 us
    ppermute x44, waiting for transfers between devices, over(): return lax.ppermute(block, axis, [(i, move(i)) for i in range(count)])  91.7 us
    unnamed x130, local copies, waits for them, and re-layouts  36.4 us
    ppermute x44, starting transfers between devices, over(): return lax.ppermute(block, axis, [(i, move(i)) for i in range(count)])  35.9 us
    pallas_call x2, Pallas kernels, attend_back(): pl.pallas_call(attend_back_kernel, grid=(pairs,), in_specs=[block, key, k...  35.6 us
    pallas_call x2, Pallas kernels, attend(): pl.pallas_call(attend_kernel, grid_spec=pltpu.PrefetchScalarGridSpec(num_...  34.7 us
    all_gather x1, blocking collectives, gather_along(): return lax.all_gather(block, 'dp', axis=0, axis_index_groups=ALONG)  28.9 us
  transfers between devices with their start and end apart: 54, of which 17 were waited for; matrix products, arithmetic and copies ran while one was open for 2% of the time, Pallas kernels for 34%

profile of v3, /device:TPU:0, one launch (start us, length us, event | category | flops | bytes accessed | tf_op | source)
XLA Modules:
  0.0 509.1 jit_solution(17605732137224973750)
XLA Ops:
  7.2 3.1 shard_map.254
  11.2 28.9 %all-gather = bf16[512,768]{1,0:T(8,128)(2,1)} all-gather(bf16[128,768]{1,0:T(8,128)(2,1)} %get-tuple-element.520), channel_id=2, replica_groups={{0,8,16,24},{4,12,20,28},{1,9,17,25},{5,13,21,29},{2,10,18,26},{6,14,22..., dimensions={0}, use_global_device_ids=true | all-gather | bytes 983040 | tf_op jit(solution)/shard_map/all_gather | solution.py:561
  40.1 2.0 shard_map.255
  42.1 1.5 collective-permute-start
  47.0 2.6 dynamic-slice_bitcast_fusion
  50.1 1.5 collective-permute-done.1.right_got
  52.3 2.6 shard_map.256
  57.1 2.3 shard_map.257
  62.0 16.7 %collective-permute-done.2.x_got = bf16[8,1,128,384]{3,2,1,0:T(8,128)(2,1)S(1)} collective-permute-done((bf16[8,1,128,384]{3,2,1,0:T(8,128)(2,1)}, bf16[8,1,128,384]{3,2,1,0:T(8,128)(2,1)S(1)}, u32[]{:S(2)}, u32[]{:S(2)}) %collective-permute-start.2) | collective-permute-done | bytes 786464 | tf_op jit(solution)/shard_map/ppermute | solution.py:538
  81.1 3.5 shard_map.258
  86.0 2.3 shard_map.259
  91.3 6.1 %shard_map.260 = (bf16[512,768]{1,0:T(8,128)(2,1)}, bf16[512,768]{1,0:T(8,128)(2,1)}, bf16[2,512,768]{2,1,0:T(8,128)(2,1)}) custom-call(bf16[512,768]{1,0:T(8,128)(2,1)} %get-tuple-element.862.h_ref, f32[16,768]{1,0:T(8,128)} %get-tuple-element.868.vec_ref, bf16[1,2,8,96,768]{4,3,2,1,0:T(8,128)(2,1)} %get-tuple-element.869.refs_0_.refs_4_, ...), custom_call_target="tpu_custom_call" | custom-call | flops 1342177280 | bytes 65536 | tf_op jit(solution)/shard_map/pallas_call | solution.py:43
  98.3 2.4 shard_map.261
  104.3 17.2 %shard_map.262 = (bf16[512,768]{1,0:T(8,128)(2,1)S(1)}, bf16[12,1024,512]{2,1,0:T(8,128)(2,1)}, f32[512,768]{1,0:T(8,128)S(1)}) custom-call(s32[2]{0:T(128)S(1)} %pad_add_fusion.lens_ref, bf16[512,768]{1,0:T(8,128)(2,1)S(1)} %copy-done.10, bf16[2,512,768]{2,1,0:T(8,128)(2,1)S(1)} %copy-done.6, bf16[2,512,768]{2,1,0:T(8,128)(2,1)} %copy-done.19, ...), custom_call_target="tpu_custom_call" | custom-call | flops 4294967296 | bytes 65536 | tf_op jit(solution)/shard_map/pallas_call | solution.py:103
  125.3 3.2 shard_map.263.refs_0_
  128.5 4.3 shard_map.264.h_ref
  133.7 3.3 shard_map.265.refs_0_.refs_2_
  138.8 9.4 %shard_map.266 = (bf16[512,768]{1,0:T(8,128)(2,1)}, bf16[4,512,768]{2,1,0:T(8,128)(2,1)}, bf16[4,512,768]{2,1,0:T(8,128)(2,1)}) custom-call(bf16[512,768]{1,0:T(8,128)(2,1)} %shard_map.264.h_ref, f32[16,768]{1,0:T(8,128)} %get-tuple-element.868.vec_ref, bf16[1,2,8,96,768]{4,3,2,1,0:T(8,128)(2,1)} %shard_map.263.refs_0_, bf16[1,2,8,96,768]{4,3,2,1,0:T(8,128)(2,1)} %copy-done.22), custom_call_target="tpu_custom_call" | custom-call | flops 2415919104 | bytes 65536 | tf_op jit(solution)/shard_map/pallas_call | solution.py:43
  149.6 9.0 %shard_map.267.h_ref = bf16[512,768]{1,0:T(8,128)(2,1)} custom-call(bf16[512,768]{1,0:T(8,128)(2,1)} %shard_map.264.h_ref, bf16[4,512,768]{2,1,0:T(8,128)(2,1)} %get-tuple-element.774.g_hbm, f32[16,768]{1,0:T(8,128)} %get-tuple-element.868.vec_ref, bf16[1,2,8,96,768]{4,3,2,1,0:T(8,128)(2,1)} %shard_map.265.refs_0_.refs_2_, bf16[1,2,8,96,768]{4,3,2,1,0:T(8,128)(2,1)} %copy-done.18), custom_call_target="tpu_custom_call" | custom-call | flops 1610612736 | bytes 65536 | tf_op jit(solution)/shard_map/pallas_call | solution.py:43
  158.7 9.6 %all-gather.13.cloned.1.call-done = bf16[96,96,768]{2,1,0:T(8,128)(2,1)} async-done(((bf16[3,96,768]{2,1,0:T(8,128)(2,1)}), bf16[96,96,768]{2,1,0:T(8,128)(2,1)}) %all-gather.13.cloned.1.call-update) | async-done | bytes 14155792 | tf_op jit(solution)/shard_map/all_gather | solution.py:955
  168.3 6.1 %shard_map.268 = (bf16[512,768]{1,0:T(8,128)(2,1)}, bf16[512,768]{1,0:T(8,128)(2,1)}, bf16[2,512,768]{2,1,0:T(8,128)(2,1)}) custom-call(bf16[512,768]{1,0:T(8,128)(2,1)} %shard_map.267.h_ref, f32[16,768]{1,0:T(8,128)} %get-tuple-element.750.vec_ref, bf16[8,4,3,96,768]{4,3,2,1,0:T(8,128)(2,1)} %bitcast.55), custom_call_target="tpu_custom_call" | custom-call | flops 1342177280 | bytes 65536 | tf_op jit(solution)/shard_map/pallas_call | solution.py:43
  174.7 3.4 collective-permute-done.16.kp_ref.vp_ref
  181.8 17.5 %shard_map.269 = (bf16[512,768]{1,0:T(8,128)(2,1)S(1)}, bf16[12,1024,512]{2,1,0:T(8,128)(2,1)}, f32[512,768]{1,0:T(8,128)S(1)}) custom-call(s32[2]{0:T(128)S(1)} %pad_add_fusion.lens_ref, bf16[512,768]{1,0:T(8,128)(2,1)S(1)} %copy-done.12, bf16[2,512,768]{2,1,0:T(8,128)(2,1)S(1)} %copy-done.7, bf16[2,512,768]{2,1,0:T(8,128)(2,1)} %copy-done.20, ...), custom_call_target="tpu_custom_call" | custom-call | flops 4294967296 | bytes 65536 | tf_op jit(solution)/shard_map/pallas_call | solution.py:103
  201.3 4.3 shard_map.270.h_ref
  205.7 9.5 %shard_map.271 = (bf16[512,768]{1,0:T(8,128)(2,1)}, bf16[4,512,768]{2,1,0:T(8,128)(2,1)}, bf16[4,512,768]{2,1,0:T(8,128)(2,1)}) custom-call(bf16[512,768]{1,0:T(8,128)(2,1)} %shard_map.270.h_ref, f32[16,768]{1,0:T(8,128)} %get-tuple-element.750.vec_ref, bf16[8,4,3,96,768]{4,3,2,1,0:T(8,128)(2,1)} %bitcast.57), custom_call_target="tpu_custom_call" | custom-call | flops 2415919104 | bytes 65536 | tf_op jit(solution)/shard_map/pallas_call | solution.py:43
  215.2 8.9 %shard_map.272 = bf16[512,768]{1,0:T(8,128)(2,1)} custom-call(bf16[512,768]{1,0:T(8,128)(2,1)} %shard_map.270.h_ref, bf16[4,512,768]{2,1,0:T(8,128)(2,1)} %get-tuple-element.701.g_hbm, f32[16,768]{1,0:T(8,128)} %get-tuple-element.750.vec_ref, bf16[8,4,3,96,768]{4,3,2,1,0:T(8,128)(2,1)} %bitcast.58), custom_call_target="tpu_custom_call" | custom-call | flops 1610612736 | bytes 65536 | tf_op jit(solution)/shard_map/pallas_call | solution.py:43
  224.1 20.3 %shard_map.273 = (bf16[512,768]{1,0:T(8,128)(2,1)}, bf16[512,768]{1,0:T(8,128)(2,1)}, bf16[2,2,8,96,768]{4,3,2,1,0:T(8,128)(2,1)}, bf16[2,1,8,96,768]{4,3,2,1,0:...) custom-call(bf16[512,768]{1,0:T(8,128)(2,1)} %get-tuple-element.698.gy_ref, ...), custom_call_target="tpu_custom_call" | custom-call | flops 5368709120 | bytes 65536 | tf_op jit(solution)/shard_map/pallas_call | solution.py:43
  246.1 17.7 %shard_map.274 = (bf16[512,768]{1,0:T(8,128)(2,1)S(1)}, f32[2,512,768]{2,1,0:T(8,128)}, bf16[2,512,768]{2,1,0:T(8,128)(2,1)}) custom-call(bf16[512,768]{1,0:T(8,128)(2,1)S(1)} %copy-done.13, bf16[2,512,768]{2,1,0:T(8,128)(2,1)} %get-tuple-element.721.ko_ref.vo_ref, bf16[2,512,768]{2,1,0:T(8,128)(2,1)} %copy-done.20, ...), custom_call_target="tpu_custom_call" | custom-call | flops 4294967296 | bytes 65536 | tf_op jit(solution)/shard_map/pallas_call | solution.py:166
  265.0 6.4 %shard_map.275 = bf16[8,2,2,96,768]{4,3,2,1,0:T(8,128)(2,1)} custom-call(bf16[2,2,8,96,768]{4,3,2,1,0:T(8,128)(2,1)} %get-tuple-element.738.keep_ref, bf16[2,1,8,96,768]{4,3,2,1,0:T(8,128)(2,1)} %collective-permute-done.18.up_ref, bf16[2,1,8,96,768]{4,3,2,1,0:T(8,128)(2,1)} %collective-permute-done.19.down_ref), custom_call_target="tpu_custom_call" | custom-call | flops 21474836480 | bytes 65536 | tf_op jit(solution)/shard_map/pallas_call | solution.py:758
  272.6 10.9 %shard_map.276 = (bf16[512,768]{1,0:T(8,128)(2,1)}, bf16[2,1,8,96,768]{4,3,2,1,0:T(8,128)(2,1)}, bf16[2,1,8,96,768]{4,3,2,1,0:T(8,128)(2,1)}, f32[8,768]{1,0:T(8,128)}) custom-call(bf16[512,768]{1,0:T(8,128)(2,1)} %get-tuple-element.743.gy_ref, bf16[512,768]{1,0:T(8,128)(2,1)} %shard_map.267.h_ref, bf16[512,768]{1,0:T(8,128)(2,1)} %get-tuple-element.745.a_ref, ...), custom_call_target="tpu_custom_call" | custom-call | flops 2684354560 | bytes 65536 | tf_op jit(solution)/shard_map/pallas_call | solution.py:43
  284.3 4.0 collective-permute-done.20.refs_0_
  288.3 1.5 copy-done.38
  289.7 4.1 shard_map.277
  295.5 19.2 %shard_map.278 = (bf16[512,768]{1,0:T(8,128)(2,1)}, bf16[512,768]{1,0:T(8,128)(2,1)}, bf16[2,2,8,96,768]{4,3,2,1,0:T(8,128)(2,1)}, bf16[2,1,8,96,768]{4,3,2,1,0:...) custom-call(bf16[512,768]{1,0:T(8,128)(2,1)} %get-tuple-element.771.gy_ref, ...), custom_call_target="tpu_custom_call" | custom-call | flops 5368709120 | bytes 65536 | tf_op jit(solution)/shard_map/pallas_call | solution.py:43
  316.9 2.9 shard_map.279
  319.8 3.0 collective-permute-done.22.refs_1_
  324.3 6.4 %shard_map.280 = (bf16[2,8,96,384]{3,2,1,0:T(8,128)(2,1)}, bf16[2,2,4,96,384]{4,3,2,1,0:T(8,128)(2,1)}, bf16[2,8,96,384]{3,2,1,0:T(8,128)(2,1)}, bf16[2,2,4,96,384]{4,3,2,1,0:T(8,128)(2,1)}) custom-call(bf16[2,2,8,96,768]{4,3,2,1,0:T(8,128)(2,1)} %get-tuple-element.813.keep_ref, bf16[2,1,8,96,768]{4,3,2,1,0:T(8,128)(2,1)} %copy-done.23, ...), custom_call_target="tpu_custom_call" | custom-call | flops 1342177280 | bytes 65536 | tf_op jit(solution)/shard_map/pallas_call | solution.py:43
  330.7 2.0 collective-permute-start.28
  333.1 1.7 collective-permute-start.26
  334.7 17.8 %shard_map.281 = (bf16[512,768]{1,0:T(8,128)(2,1)S(1)}, f32[2,512,768]{2,1,0:T(8,128)}, bf16[2,512,768]{2,1,0:T(8,128)(2,1)}) custom-call(bf16[512,768]{1,0:T(8,128)(2,1)S(1)} %copy-done.10, bf16[2,512,768]{2,1,0:T(8,128)(2,1)} %get-tuple-element.823.ko_ref.vo_ref, bf16[2,512,768]{2,1,0:T(8,128)(2,1)} %copy-done.19, ...), custom_call_target="tpu_custom_call" | custom-call | flops 4294967296 | bytes 65536 | tf_op jit(solution)/shard_map/pallas_call | solution.py:166
  352.6 7.0 %collective-permute-done.28.x_got = bf16[2,8,96,384]{3,2,1,0:T(8,128)(2,1)S(1)} collective-permute-done((bf16[2,8,96,384]{3,2,1,0:T(8,128)(2,1)}, bf16[2,8,96,384]{3,2,1,0:T(8,128)(2,1)S(1)}, u32[]{:S(2)}, u32[]{:S(2)}) %collective-permute-start.28) | collective-permute-done | bytes 1179680 | tf_op jit(solution)/shard_map/ppermute | solution.py:538
  359.7 9.4 %collective-permute-done.29.y_got = bf16[2,2,4,96,384]{4,3,2,1,0:T(8,128)(2,1)S(1)} collective-permute-done((bf16[2,2,4,96,384]{4,3,2,1,0:T(8,128)(2,1)}, bf16[2,2,4,96,384]{4,3,2,1,0:T(8,128)(2,1)S(1)}, u32[]{:S(2)}, u32[]{:S(2)}) %collective-permute-start.29) | collective-permute-done | bytes 1179680 | tf_op jit(solution)/shard_map/ppermute | solution.py:538
  370.1 4.1 shard_map.282
  375.6 5.1 collective-permute-done.26.y_got
  382.2 2.2 shard_map.283
  385.6 12.5 %shard_map.284 = (bf16[512,768]{1,0:T(8,128)(2,1)}, bf16[2,1,8,96,768]{4,3,2,1,0:T(8,128)(2,1)}, bf16[2,1,8,96,768]{4,3,2,1,0:T(8,128)(2,1)}, f32[8,768]{1,0:T(8,128)}) custom-call(bf16[512,768]{1,0:T(8,128)(2,1)} %get-tuple-element.861.gy_ref, bf16[512,768]{1,0:T(8,128)(2,1)} %get-tuple-element.862.h_ref, bf16[512,768]{1,0:T(8,128)(2,1)} %get-tuple-element.863.a_ref, ...), custom_call_target="tpu_custom_call" | custom-call | flops 2684354560 | bytes 65536 | tf_op jit(solution)/shard_map/pallas_call | solution.py:43
  400.1 2.9 shard_map.285
  404.7 3.9 shard_map.286
  411.0 3.8 reduce-scatter.6.cloned.1.call-done
  414.8 16.0 %collective-permute-done.35 = bf16[2,96,768]{2,1,0:T(8,128)(2,1)S(1)} collective-permute-done((bf16[2,96,768]{2,1,0:T(8,128)(2,1)S(1)}, bf16[2,96,768]{2,1,0:T(8,128)(2,1)S(1)}, u32[]{:S(2)}, u32[]{:S(2)}) %collective-permute-start.35) | collective-permute-done | bytes 294944 | tf_op jit(solution)/shard_map/ppermute | solution.py:538
  430.9 1.7 pad_maximum_fusion.2
  434.4 2.8 shard_map.287
  440.4 3.2 all-to-all-start
  443.7 2.9 collective-permute-done.36.y_got
  448.0 2.1 shard_map.288
  451.1 3.4 collective-permute-start.39
  454.6 2.1 collective-permute-start.40
  456.7 2.3 collective-permute-start.41
  458.9 2.8 collective-permute-start.42
  461.8 3.8 all-to-all-done
  465.7 3.1 collective-permute-done.41.o2
  468.7 1.9 shard_map.289.a0
  472.0 18.8 %collective-permute-done.44.a2 = bf16[1,96,768]{2,1,0:T(8,128)(2,1)S(1)} collective-permute-done((bf16[1,96,768]{2,1,0:T(8,128)(2,1)}, bf16[1,96,768]{2,1,0:T(8,128)(2,1)S(1)}, u32[]{:S(2)}, u32[]{:S(2)}) %collective-permute-start.44) | collective-permute-done | bytes 147488 | tf_op jit(solution)/shard_map/ppermute | solution.py:538
  494.9 5.2 %shard_map.290 = (f32[2,96,2304]{2,1,0:T(8,128)}, f32[2,96,768]{2,1,0:T(8,128)}, f32[2,96,3072]{2,1,0:T(8,128)}, f32[2,384,768]{2,1,0:T(8,128)}) custom-call(bf16[1,96,768]{2,1,0:T(8,128)(2,1)} %shard_map.289.a0, bf16[1,96,768]{2,1,0:T(8,128)(2,1)} %copy-done.60, bf16[1,96,768]{2,1,0:T(8,128)(2,1)} %copy-done.59, bf16[1,96,768]{2,1,0:T(8,128)(2,1)} %copy-done.61, ...), custom_call_target="tpu_custom_call" | custom-call | flops 1342177280 | bytes 65536 | tf_op jit(solution)/shard_map/pallas_call | solution.py:43
  (254 shorter events, 70.6 us)
Async XLA Ops:
  7.2 37.8 %copy-start = (s32[2,1]{0,1:T(1,128)S(1)}, s32[2,1]{0,1:T(1,128)}, u32[]{:S(2)}) copy-start(s32[2,1]{0,1:T(1,128)} %param.16) | copy-start | bytes 28
  7.2 49.9 %all-gather.11.cloned.1.call-start = ((), (), s32[]{:S(2)}) async-start(), calls=%async_computation.8 | async-start | bytes 1474560 | tf_op jit(solution)/shard_map/all_gather | solution.py:561
  10.4 157.9 %all-gather.13.cloned.1.call-start = ((), (), s32[]{:S(2)}) async-start(), calls=%async_computation.9 | async-start | bytes 14598144 | tf_op jit(solution)/shard_map/all_gather | solution.py:955
  11.1 387.0 %reduce-scatter.4.cloned.1.call-start = ((), (), s32[]{:S(2)}) async-start(), calls=%async_computation.4 | async-start | bytes 5308416 | tf_op jit(solution)/shard_map/reduce_scatter | solution.py:770
  42.1 8.0 %collective-permute-start = (bf16[4,1,128,384]{3,2,1,0:T(8,128)(2,1)}, bf16[4,1,128,384]{3,2,1,0:T(8,128)(2,1)S(1)}, u32[]{:S(2)}, u32[]{:S(2)}) collective-permute-start(bf16[4,1,128,384]{3,2,1,0:T(8,128)(2,1)} %get-tuple-element.535.left_ref), channel_id=1, source_target_pairs={{0,4},{4,0},{8,12},{12,8},{16,20},{20,16},{24,28},{28,24},{1,5},{5... | collective-permute-start | bytes 1179656 | tf_op jit(solution)/shard_map/ppermute | solution.py:538
  43.6 8.0 %collective-permute-start.1 = (bf16[4,1,128,384]{3,2,1,0:T(8,128)(2,1)}, bf16[4,1,128,384]{3,2,1,0:T(8,128)(2,1)S(1)}, u32[]{:S(2)}, u32[]{:S(2)}) collective-permute-start(bf16[4,1,128,384]{3,2,1,0:T(8,128)(2,1)} %get-tuple-element.537.right_ref), channel_id=1, source_target_pairs={{0,2},{1,3},{2,0},{3,1},{4,6},{5,7},{6,4},{7,5},{8,10},{9,11},{10,... | collective-permute-start | bytes 1179656 | tf_op jit(solution)/shard_map/ppermute | solution.py:538
  54.9 23.8 %collective-permute-start.2 = (bf16[8,1,128,384]{3,2,1,0:T(8,128)(2,1)}, bf16[8,1,128,384]{3,2,1,0:T(8,128)(2,1)S(1)}, u32[]{:S(2)}, u32[]{:S(2)}) collective-permute-start(bf16[8,1,128,384]{3,2,1,0:T(8,128)(2,1)} %get-tuple-element.553.x_ref), channel_id=1, source_target_pairs={{0,2},{1,3},{2,0},{3,1},{4,6},{5,7},{6,4},{7,5},{8,10},{9,11},{10,... | collective-permute-start | bytes 2359304 | tf_op jit(solution)/shard_map/ppermute | solution.py:538
  56.3 23.9 %collective-permute-start.3 = (bf16[2,4,1,128,384]{4,3,2,1,0:T(8,128)(2,1)}, bf16[2,4,1,128,384]{4,3,2,1,0:T(8,128)(2,1)S(1)}, u32[]{:S(2)}, u32[]{:S(2)}) collective-permute-start(bf16[2,4,1,128,384]{4,3,2,1,0:T(8,128)(2,1)} %get-tuple-element.555.y_ref), channel_id=1, source_target_pairs={{0,4},{4,0},{8,12},{12,8},{16,20},{20,16},{24,28},{28,24},{1,5},{5... | collective-permute-start | bytes 2359304 | tf_op jit(solution)/shard_map/ppermute | solution.py:538
  59.4 25.1 %collective-permute-start.5 = (bf16[4,1,96,384]{3,2,1,0:T(8,128)(2,1)}, bf16[4,1,96,384]{3,2,1,0:T(8,128)(2,1)S(1)}, u32[]{:S(2)}, u32[]{:S(2)}) collective-permute-start(bf16[4,1,96,384]{3,2,1,0:T(8,128)(2,1)} %get-tuple-element.566.left_ref), channel_id=1, source_target_pairs={{0,4},{4,0},{8,12},{12,8},{16,20},{20,16},{24,28},{28,24},{1,5},{5... | collective-permute-start | bytes 884744 | tf_op jit(solution)/shard_map/ppermute | solution.py:538
  60.7 23.9 %collective-permute-start.6 = (bf16[4,1,96,384]{3,2,1,0:T(8,128)(2,1)}, bf16[4,1,96,384]{3,2,1,0:T(8,128)(2,1)S(1)}, u32[]{:S(2)}, u32[]{:S(2)}) collective-permute-start(bf16[4,1,96,384]{3,2,1,0:T(8,128)(2,1)} %get-tuple-element.568.right_ref), channel_id=1, source_target_pairs={{0,2},{1,3},{2,0},{3,1},{4,6},{5,7},{6,4},{7,5},{8,10},{9,11},{10,... | collective-permute-start | bytes 884744 | tf_op jit(solution)/shard_map/ppermute | solution.py:538
  61.3 36.2 %collective-permute-start.8 = (bf16[4,1,96,384]{3,2,1,0:T(8,128)(2,1)}, bf16[4,1,96,384]{3,2,1,0:T(8,128)(2,1)S(1)}, u32[]{:S(2)}, u32[]{:S(2)}) collective-permute-start(bf16[4,1,96,384]{3,2,1,0:T(8,128)(2,1)} %get-tuple-element.588.left_ref), channel_id=1, source_target_pairs={{0,4},{4,0},{8,12},{12,8},{16,20},{20,16},{24,28},{28,24},{1,5},{5... | collective-permute-start | bytes 884744 | tf_op jit(solution)/shard_map/ppermute | solution.py:538
  78.7 18.8 %collective-permute-start.9 = (bf16[4,1,96,384]{3,2,1,0:T(8,128)(2,1)}, bf16[4,1,96,384]{3,2,1,0:T(8,128)(2,1)S(1)}, u32[]{:S(2)}, u32[]{:S(2)}) collective-permute-start(bf16[4,1,96,384]{3,2,1,0:T(8,128)(2,1)} %get-tuple-element.590.right_ref), channel_id=1, source_target_pairs={{0,2},{1,3},{2,0},{3,1},{4,6},{5,7},{6,4},{7,5},{8,10},{9,11},{10,... | collective-permute-start | bytes 884744 | tf_op jit(solution)/shard_map/ppermute | solution.py:538
  84.5 5.4 %collective-permute-start.4 = (bf16[1,2,8,96,768]{4,3,2,1,0:T(8,128)(2,1)}, bf16[1,2,8,96,768]{4,3,2,1,0:T(8,128)(2,1)S(1)}, u32[]{:S(2)}, u32[]{:S(2)}) collective-permute-start(bf16[1,2,8,96,768]{4,3,2,1,0:T(8,128)(2,1)} %get-tuple-element.869.refs_0_.refs_4_), channel_id=1, source_target_pairs={{0,1},{1,0},{2,3},{3,2},{4,5},{5,4},{6,7},{7,6},{8,9},{9,8},{10,11... | collective-permute-start | bytes 7077896 | tf_op jit(solution)/shard_map/ppermute | solution.py:538
  88.3 35.3 %collective-permute-start.10 = (bf16[8,1,96,384]{3,2,1,0:T(8,128)(2,1)}, bf16[8,1,96,384]{3,2,1,0:T(8,128)(2,1)S(1)}, u32[]{:S(2)}, u32[]{:S(2)}) collective-permute-start(bf16[8,1,96,384]{3,2,1,0:T(8,128)(2,1)} %get-tuple-element.608.x_ref), channel_id=1, source_target_pairs={{0,2},{1,3},{2,0},{3,1},{4,6},{5,7},{6,4},{7,5},{8,10},{9,11},{10,... | collective-permute-start | bytes 1769480 | tf_op jit(solution)/shard_map/ppermute | solution.py:538
  89.2 34.4 %collective-permute-start.11 = (bf16[2,4,1,96,384]{4,3,2,1,0:T(8,128)(2,1)}, bf16[2,4,1,96,384]{4,3,2,1,0:T(8,128)(2,1)S(1)}, u32[]{:S(2)}, u32[]{:S(2)}) collective-permute-start(bf16[2,4,1,96,384]{4,3,2,1,0:T(8,128)(2,1)} %get-tuple-element.610.y_ref), channel_id=1, source_target_pairs={{0,4},{4,0},{8,12},{12,8},{16,20},{20,16},{24,28},{28,24},{1,5},{5... | collective-permute-start | bytes 1769480 | tf_op jit(solution)/shard_map/ppermute | solution.py:538
  97.4 6.9 %copy-start.6 = (bf16[2,512,768]{2,1,0:T(8,128)(2,1)S(1)}, bf16[2,512,768]{2,1,0:T(8,128)(2,1)}, u32[]{:S(2)}) copy-start(bf16[2,512,768]{2,1,0:T(8,128)(2,1)} %get-tuple-element.823.ko_ref.vo_ref) | copy-start | bytes 4718596
  97.5 5.6 %collective-permute-start.7 = (bf16[2,512,768]{2,1,0:T(8,128)(2,1)}, bf16[2,512,768]{2,1,0:T(8,128)(2,1)S(1)}, u32[]{:S(2)}, u32[]{:S(2)}) collective-permute-start(bf16[2,512,768]{2,1,0:T(8,128)(2,1)} %get-tuple-element.823.ko_ref.vo_ref), channel_id=1, source_target_pairs={{0,1},{1,0},{2,3},{3,2},{4,5},{5,4},{6,7},{7,6},{8,9},{9,8},{10,11... | collective-permute-start | bytes 4718600 | tf_op jit(solution)/shard_map/ppermute | solution.py:538
  100.7 32.2 %collective-permute-start.13 = (bf16[8,1,96,384]{3,2,1,0:T(8,128)(2,1)}, bf16[8,1,96,384]{3,2,1,0:T(8,128)(2,1)S(1)}, u32[]{:S(2)}, u32[]{:S(2)}) collective-permute-start(bf16[8,1,96,384]{3,2,1,0:T(8,128)(2,1)} %get-tuple-element.625.x_ref), channel_id=1, source_target_pairs={{0,2},{1,3},{2,0},{3,1},{4,6},{5,7},{6,4},{7,5},{8,10},{9,11},{10,... | collective-permute-start | bytes 1769480 | tf_op jit(solution)/shard_map/ppermute | solution.py:538
  101.8 31.1 %collective-permute-start.14 = (bf16[2,4,1,96,384]{4,3,2,1,0:T(8,128)(2,1)}, bf16[2,4,1,96,384]{4,3,2,1,0:T(8,128)(2,1)}, u32[]{:S(2)}, u32[]{:S(2)}) collective-permute-start(bf16[2,4,1,96,384]{4,3,2,1,0:T(8,128)(2,1)} %get-tuple-element.627.y_ref), channel_id=1, source_target_pairs={{0,4},{4,0},{8,12},{12,8},{16,20},{20,16},{24,28},{28,24},{1,5},{5... | collective-permute-start | bytes 1769480 | tf_op jit(solution)/shard_map/ppermute | solution.py:538
  128.5 8.9 %collective-permute-start.12 = (bf16[1,2,8,96,768]{4,3,2,1,0:T(8,128)(2,1)}, bf16[1,2,8,96,768]{4,3,2,1,0:T(8,128)(2,1)S(1)}, u32[]{:S(2)}, u32[]{:S(2)}) collective-permute-start(bf16[1,2,8,96,768]{4,3,2,1,0:T(8,128)(2,1)} %shard_map.263.refs_0_), channel_id=1, source_target_pairs={{0,1},{1,0},{2,3},{3,2},{4,5},{5,4},{6,7},{7,6},{8,9},{9,8},{10,11... | collective-permute-start | bytes 7077896 | tf_op jit(solution)/shard_map/ppermute | solution.py:538
  136.9 11.3 %collective-permute-start.15 = (bf16[1,2,8,96,768]{4,3,2,1,0:T(8,128)(2,1)}, bf16[1,2,8,96,768]{4,3,2,1,0:T(8,128)(2,1)S(1)}, u32[]{:S(2)}, u32[]{:S(2)}) collective-permute-start(bf16[1,2,8,96,768]{4,3,2,1,0:T(8,128)(2,1)} %shard_map.265.refs_0_.refs_2_), channel_id=1, source_target_pairs={{0,1},{1,0},{2,3},{3,2},{4,5},{5,4},{6,7},{7,6},{8,9},{9,8},{10,11... | collective-permute-start | bytes 7077896 | tf_op jit(solution)/shard_map/ppermute | solution.py:538
  174.4 3.7 collective-permute-start.16
  224.1 20.9 %copy-start.3 = (bf16[512,768]{1,0:T(8,128)(2,1)S(1)}, bf16[512,768]{1,0:T(8,128)(2,1)}, u32[]{:S(2)}) copy-start(bf16[512,768]{1,0:T(8,128)(2,1)} %copy-done.2) | copy-start | bytes 2359300
  224.1 20.9 %copy-start.13 = (bf16[512,768]{1,0:T(8,128)(2,1)S(1)}, bf16[512,768]{1,0:T(8,128)(2,1)}, u32[]{:S(2)}) copy-start(bf16[512,768]{1,0:T(8,128)(2,1)} %get-tuple-element.720.q_ref) | copy-start | bytes 2359300
  244.4 20.6 %collective-permute-start.18 = (bf16[2,1,8,96,768]{4,3,2,1,0:T(8,128)(2,1)}, bf16[2,1,8,96,768]{4,3,2,1,0:T(8,128)(2,1)}, u32[]{:S(2)}, u32[]{:S(2)}) collective-permute-start(bf16[2,1,8,96,768]{4,3,2,1,0:T(8,128)(2,1)} %get-tuple-element.735), channel_id=1, source_target_pairs={{0,1},{1,0},{2,3},{3,2},{4,5},{5,4},{6,7},{7,6},{8,9},{9,8},{10,11... | collective-permute-start | bytes 7077896 | tf_op jit(solution)/shard_map/ppermute | solution.py:538
  244.7 20.3 %collective-permute-start.19 = (bf16[2,1,8,96,768]{4,3,2,1,0:T(8,128)(2,1)}, bf16[2,1,8,96,768]{4,3,2,1,0:T(8,128)(2,1)}, u32[]{:S(2)}, u32[]{:S(2)}) collective-permute-start(bf16[2,1,8,96,768]{4,3,2,1,0:T(8,128)(2,1)} %get-tuple-element.736), channel_id=1, source_target_pairs={{0,1},{1,0},{2,3},{3,2},{4,5},{5,4},{6,7},{7,6},{8,9},{9,8},{10,11... | collective-permute-start | bytes 7077896 | tf_op jit(solution)/shard_map/ppermute | solution.py:538
  264.7 6.7 %collective-permute-start.17 = (bf16[2,512,768]{2,1,0:T(8,128)(2,1)}, bf16[2,512,768]{2,1,0:T(8,128)(2,1)S(1)}, u32[]{:S(2)}, u32[]{:S(2)}) collective-permute-start(bf16[2,512,768]{2,1,0:T(8,128)(2,1)} %get-tuple-element.733), channel_id=1, source_target_pairs={{0,1},{1,0},{2,3},{3,2},{4,5},{5,4},{6,7},{7,6},{8,9},{9,8},{10,11... | collective-permute-start | bytes 4718600 | tf_op jit(solution)/shard_map/ppermute | solution.py:538
  283.5 4.8 collective-permute-start.20
  283.8 131.0 %reduce-scatter.6.cloned.1.call-start = ((), (), s32[]{:S(2)}) async-start(), calls=%async_computation.5 | async-start | bytes 737280 | tf_op jit(solution)/shard_map/reduce_scatter | solution.py:861
  293.8 21.4 %collective-permute-start.23 = (bf16[1,8,96,384]{3,2,1,0:T(8,128)(2,1)}, bf16[1,8,96,384]{3,2,1,0:T(8,128)(2,1)S(1)}, u32[]{:S(2)}, u32[]{:S(2)}) collective-permute-start(bf16[1,8,96,384]{3,2,1,0:T(8,128)(2,1)} %get-tuple-element.799), channel_id=1, source_target_pairs={{0,2},{1,3},{2,0},{3,1},{4,6},{5,7},{6,4},{7,5},{8,10},{9,11},{10,... | collective-permute-start | bytes 1769480 | tf_op jit(solution)/shard_map/ppermute | solution.py:538
  295.2 20.1 %collective-permute-start.24 = (bf16[2,1,4,96,384]{4,3,2,1,0:T(8,128)(2,1)}, bf16[2,1,4,96,384]{4,3,2,1,0:T(8,128)(2,1)S(1)}, u32[]{:S(2)}, u32[]{:S(2)}) collective-permute-start(bf16[2,1,4,96,384]{4,3,2,1,0:T(8,128)(2,1)} %get-tuple-element.801), channel_id=1, source_target_pairs={{0,4},{4,0},{8,12},{12,8},{16,20},{20,16},{24,28},{28,24},{1,5},{5... | collective-permute-start | bytes 1769480 | tf_op jit(solution)/shard_map/ppermute | solution.py:538
  314.7 5.2 %collective-permute-start.21 = (bf16[2,1,8,96,768]{4,3,2,1,0:T(8,128)(2,1)}, bf16[2,1,8,96,768]{4,3,2,1,0:T(8,128)(2,1)S(1)}, u32[]{:S(2)}, u32[]{:S(2)}) collective-permute-start(bf16[2,1,8,96,768]{4,3,2,1,0:T(8,128)(2,1)} %get-tuple-element.796), channel_id=1, source_target_pairs={{0,1},{1,0},{2,3},{3,2},{4,5},{5,4},{6,7},{7,6},{8,9},{9,8},{10,11... | collective-permute-start | bytes 7077896 | tf_op jit(solution)/shard_map/ppermute | solution.py:538
  314.8 8.1 %collective-permute-start.22 = (bf16[2,1,8,96,768]{4,3,2,1,0:T(8,128)(2,1)}, bf16[2,1,8,96,768]{4,3,2,1,0:T(8,128)(2,1)S(1)}, u32[]{:S(2)}, u32[]{:S(2)}) collective-permute-start(bf16[2,1,8,96,768]{4,3,2,1,0:T(8,128)(2,1)} %get-tuple-element.797), channel_id=1, source_target_pairs={{0,1},{1,0},{2,3},{3,2},{4,5},{5,4},{6,7},{7,6},{8,9},{9,8},{10,11... | collective-permute-start | bytes 7077896 | tf_op jit(solution)/shard_map/ppermute | solution.py:538
  319.8 14.9 %copy-start.5 = (bf16[512,768]{1,0:T(8,128)(2,1)S(1)}, bf16[512,768]{1,0:T(8,128)(2,1)}, u32[]{:S(2)}) copy-start(bf16[512,768]{1,0:T(8,128)(2,1)} %copy-done.4) | copy-start | bytes 2359300
  319.8 14.9 %copy-start.11 = (bf16[512,768]{1,0:T(8,128)(2,1)S(1)}, bf16[512,768]{1,0:T(8,128)(2,1)}, u32[]{:S(2)}) copy-start(bf16[512,768]{1,0:T(8,128)(2,1)} %get-tuple-element.826.go_ref) | copy-start | bytes 2359300
  330.7 29.0 %collective-permute-start.28 = (bf16[2,8,96,384]{3,2,1,0:T(8,128)(2,1)}, bf16[2,8,96,384]{3,2,1,0:T(8,128)(2,1)S(1)}, u32[]{:S(2)}, u32[]{:S(2)}) collective-permute-start(bf16[2,8,96,384]{3,2,1,0:T(8,128)(2,1)} %get-tuple-element.841), channel_id=1, source_target_pairs={{0,2},{1,3},{2,0},{3,1},{4,6},{5,7},{6,4},{7,5},{8,10},{9,11},{10,... | collective-permute-start | bytes 3538952 | tf_op jit(solution)/shard_map/ppermute | solution.py:538
  332.7 36.4 %collective-permute-start.29 = (bf16[2,2,4,96,384]{4,3,2,1,0:T(8,128)(2,1)}, bf16[2,2,4,96,384]{4,3,2,1,0:T(8,128)(2,1)S(1)}, u32[]{:S(2)}, u32[]{:S(2)}) collective-permute-start(bf16[2,2,4,96,384]{4,3,2,1,0:T(8,128)(2,1)} %get-tuple-element.843), channel_id=1, source_target_pairs={{0,4},{4,0},{8,12},{12,8},{16,20},{20,16},{24,28},{28,24},{1,5},{5... | collective-permute-start | bytes 3538952 | tf_op jit(solution)/shard_map/ppermute | solution.py:538
  333.1 47.7 %collective-permute-start.26 = (bf16[1,4,96,384]{3,2,1,0:T(8,128)(2,1)}, bf16[1,4,96,384]{3,2,1,0:T(8,128)(2,1)S(1)}, u32[]{:S(2)}, u32[]{:S(2)}) collective-permute-start(bf16[1,4,96,384]{3,2,1,0:T(8,128)(2,1)} %get-tuple-element.837), channel_id=1, source_target_pairs={{0,4},{4,0},{8,12},{12,8},{16,20},{20,16},{24,28},{28,24},{1,5},{5... | collective-permute-start | bytes 884744 | tf_op jit(solution)/shard_map/ppermute | solution.py:538
  334.7 46.0 %collective-permute-start.27 = (bf16[1,4,96,384]{3,2,1,0:T(8,128)(2,1)}, bf16[1,4,96,384]{3,2,1,0:T(8,128)(2,1)S(1)}, u32[]{:S(2)}, u32[]{:S(2)}) collective-permute-start(bf16[1,4,96,384]{3,2,1,0:T(8,128)(2,1)} %get-tuple-element.839), channel_id=1, source_target_pairs={{0,2},{1,3},{2,0},{3,1},{4,6},{5,7},{6,4},{7,5},{8,10},{9,11},{10,... | collective-permute-start | bytes 884744 | tf_op jit(solution)/shard_map/ppermute | solution.py:538
  352.6 21.6 %copy-start.16 = (bf16[512,768]{1,0:T(8,128)(2,1)}, bf16[512,768]{1,0:T(8,128)(2,1)S(1)}, u32[]{:S(2)}) copy-start(bf16[512,768]{1,0:T(8,128)(2,1)S(1)} %get-tuple-element.865.gq_ref) | copy-start | bytes 2359300
  352.6 31.8 %collective-permute-start.25 = (bf16[2,512,768]{2,1,0:T(8,128)(2,1)}, bf16[2,512,768]{2,1,0:T(8,128)(2,1)S(1)}, u32[]{:S(2)}, u32[]{:S(2)}) collective-permute-start(bf16[2,512,768]{2,1,0:T(8,128)(2,1)} %get-tuple-element.835), channel_id=1, source_target_pairs={{0,1},{1,0},{2,3},{3,2},{4,5},{5,4},{6,7},{7,6},{8,9},{9,8},{10,11... | collective-permute-start | bytes 4718600 | tf_op jit(solution)/shard_map/ppermute | solution.py:538
  359.7 9.4 %copy-start.39 = (bf16[2,8,96,384]{3,2,1,0:T(8,128)(2,1)}, bf16[2,8,96,384]{3,2,1,0:T(8,128)(2,1)S(1)}, u32[]{:S(2)}) copy-start(bf16[2,8,96,384]{3,2,1,0:T(8,128)(2,1)S(1)} %collective-permute-done.28.x_got) | copy-start | bytes 3538948
  374.2 25.1 %collective-permute-start.31 = (bf16[2,4,96,384]{3,2,1,0:T(8,128)(2,1)}, bf16[2,4,96,384]{3,2,1,0:T(8,128)(2,1)S(1)}, u32[]{:S(2)}, u32[]{:S(2)}) collective-permute-start(bf16[2,4,96,384]{3,2,1,0:T(8,128)(2,1)} %get-tuple-element.880), channel_id=1, source_target_pairs={{0,4},{4,0},{8,12},{12,8},{16,20},{20,16},{24,28},{28,24},{1,5},{5... | collective-permute-start | bytes 1769480 | tf_op jit(solution)/shard_map/ppermute | solution.py:538
  374.6 24.7 %collective-permute-start.32 = (bf16[2,4,96,384]{3,2,1,0:T(8,128)(2,1)}, bf16[2,4,96,384]{3,2,1,0:T(8,128)(2,1)}, u32[]{:S(2)}, u32[]{:S(2)}) collective-permute-start(bf16[2,4,96,384]{3,2,1,0:T(8,128)(2,1)} %get-tuple-element.882), channel_id=1, source_target_pairs={{0,2},{1,3},{2,0},{3,1},{4,6},{5,7},{6,4},{7,5},{8,10},{9,11},{10,... | collective-permute-start | bytes 1769480 | tf_op jit(solution)/shard_map/ppermute | solution.py:538
  384.4 70.2 %reduce-scatter.8.cloned.1.call-start = ((), (), s32[]{:S(2)}) async-start(), calls=%async_computation.6 | async-start | bytes 1474560 | tf_op jit(solution)/shard_map/reduce_scatter | solution.py:861
  398.0 5.2 %collective-permute-start.30 = (bf16[2,1,8,96,768]{4,3,2,1,0:T(8,128)(2,1)}, bf16[2,1,8,96,768]{4,3,2,1,0:T(8,128)(2,1)S(1)}, u32[]{:S(2)}, u32[]{:S(2)}) collective-permute-start(bf16[2,1,8,96,768]{4,3,2,1,0:T(8,128)(2,1)} %get-tuple-element.878), channel_id=1, source_target_pairs={{0,1},{1,0},{2,3},{3,2},{4,5},{5,4},{6,7},{7,6},{8,9},{9,8},{10,11... | collective-permute-start | bytes 7077896 | tf_op jit(solution)/shard_map/ppermute | solution.py:538
  403.0 91.2 %all-gather.15.cloned.1.call-start = ((), (), s32[]{:S(2)}) async-start(), calls=%async_computation.10 | async-start | bytes 2211840 | tf_op jit(solution)/shard_map/all_gather | solution.py:1117
  408.6 24.1 %collective-permute-start.33 = (bf16[1,8,96,384]{3,2,1,0:T(8,128)(2,1)}, bf16[1,8,96,384]{3,2,1,0:T(8,128)(2,1)S(1)}, u32[]{:S(2)}, u32[]{:S(2)}) collective-permute-start(bf16[1,8,96,384]{3,2,1,0:T(8,128)(2,1)} %get-tuple-element.902), channel_id=1, source_target_pairs={{0,2},{1,3},{2,0},{3,1},{4,6},{5,7},{6,4},{7,5},{8,10},{9,11},{10,... | collective-permute-start | bytes 1769480 | tf_op jit(solution)/shard_map/ppermute | solution.py:538
  409.3 23.4 %collective-permute-start.34 = (bf16[2,1,4,96,384]{4,3,2,1,0:T(8,128)(2,1)}, bf16[2,1,4,96,384]{4,3,2,1,0:T(8,128)(2,1)S(1)}, u32[]{:S(2)}, u32[]{:S(2)}) collective-permute-start(bf16[2,1,4,96,384]{4,3,2,1,0:T(8,128)(2,1)} %get-tuple-element.904), channel_id=1, source_target_pairs={{0,4},{4,0},{8,12},{12,8},{16,20},{20,16},{24,28},{28,24},{1,5},{5... | collective-permute-start | bytes 1769480 | tf_op jit(solution)/shard_map/ppermute | solution.py:538
  410.4 20.5 %collective-permute-start.35 = (bf16[2,96,768]{2,1,0:T(8,128)(2,1)S(1)}, bf16[2,96,768]{2,1,0:T(8,128)(2,1)S(1)}, u32[]{:S(2)}, u32[]{:S(2)}) collective-permute-start(bf16[2,96,768]{2,1,0:T(8,128)(2,1)S(1)} %get-tuple-element.906), channel_id=1, source_target_pairs={{0,2},{1,3},{2,0},{3,1},{4,6},{5,7},{6,4},{7,5},{8,10},{9,11},{10,... | collective-permute-start | bytes 884744 | tf_op jit(solution)/shard_map/ppermute | solution.py:538
  437.6 8.9 %collective-permute-start.36 = (bf16[1,4,96,384]{3,2,1,0:T(8,128)(2,1)}, bf16[1,4,96,384]{3,2,1,0:T(8,128)(2,1)S(1)}, u32[]{:S(2)}, u32[]{:S(2)}) collective-permute-start(bf16[1,4,96,384]{3,2,1,0:T(8,128)(2,1)} %get-tuple-element.924), channel_id=1, source_target_pairs={{0,4},{4,0},{8,12},{12,8},{16,20},{20,16},{24,28},{28,24},{1,5},{5... | collective-permute-start | bytes 884744 | tf_op jit(solution)/shard_map/ppermute | solution.py:538
  438.0 8.8 %collective-permute-start.37 = (bf16[1,4,96,384]{3,2,1,0:T(8,128)(2,1)}, bf16[1,4,96,384]{3,2,1,0:T(8,128)(2,1)S(1)}, u32[]{:S(2)}, u32[]{:S(2)}) collective-permute-start(bf16[1,4,96,384]{3,2,1,0:T(8,128)(2,1)} %get-tuple-element.926), channel_id=1, source_target_pairs={{0,2},{1,3},{2,0},{3,1},{4,6},{5,7},{6,4},{7,5},{8,10},{9,11},{10,... | collective-permute-start | bytes 884744 | tf_op jit(solution)/shard_map/ppermute | solution.py:538
  440.4 25.2 %all-to-all-start = ((f32[32,2,16,96]{3,2,1,0:T(8,128)}), f32[32,2,16,96]{3,2,1,0:T(8,128)S(1)}, u32[]{:S(2)}, u32[]{:S(2)}) async-start(f32[32,2,16,96]{3,2,1,0:T(8,128)} %bitcast.19), calls=%async_computation.2 | async-start | bytes 1048576 | tf_op jit(solution)/shard_map/all_to_all | solution.py:1125
  443.6 50.6 %all-gather.9.cloned.1.call-start = ((), (), s32[]{:S(2)}) async-start(), calls=%async_computation.7 | async-start | bytes 1474560 | tf_op jit(solution)/shard_map/all_gather | solution.py:1129
  450.1 8.8 %copy-start.56 = (bf16[1,96,768]{2,1,0:T(8,128)(2,1)S(1)}, bf16[1,96,768]{2,1,0:T(8,128)(2,1)}, u32[]{:S(2)}) copy-start(bf16[1,96,768]{2,1,0:T(8,128)(2,1)} %get-tuple-element.956) | copy-start | bytes 442372
  450.4 40.5 %collective-permute-start.38 = (bf16[2,256,768]{2,1,0:T(8,128)(2,1)S(1)}, bf16[2,256,768]{2,1,0:T(8,128)(2,1)S(1)}, u32[]{:S(2)}, u32[]{:S(2)}) collective-permute-start(bf16[2,256,768]{2,1,0:T(8,128)(2,1)S(1)} %get-tuple-element.951), channel_id=1, source_target_pairs={{0,0},{1,2},{2,1},{3,3},{4,4},{5,6},{6,5},{7,7},{8,8},{9,10},{10,9... | collective-permute-start | bytes 2359304 | tf_op jit(solution)/shard_map/ppermute | solution.py:1018
  451.1 39.7 %collective-permute-start.39 = (bf16[2,256,768]{2,1,0:T(8,128)(2,1)S(1)}, bf16[2,256,768]{2,1,0:T(8,128)(2,1)}, u32[]{:S(2)}, u32[]{:S(2)}) collective-permute-start(bf16[2,256,768]{2,1,0:T(8,128)(2,1)S(1)} %get-tuple-element.952), channel_id=1, source_target_pairs={{0,1},{1,3},{2,0},{3,2},{4,5},{5,7},{6,4},{7,6},{8,9},{9,11},{10,8... | collective-permute-start | bytes 2359304 | tf_op jit(solution)/shard_map/ppermute | solution.py:1018
  454.6 11.1 %collective-permute-start.40 = (bf16[1,96,768]{2,1,0:T(8,128)(2,1)S(1)}, bf16[1,96,768]{2,1,0:T(8,128)(2,1)S(1)}, u32[]{:S(2)}, u32[]{:S(2)}) collective-permute-start(bf16[1,96,768]{2,1,0:T(8,128)(2,1)S(1)} %copy-done.58), channel_id=1, source_target_pairs={{0,8},{4,12},{8,16},{12,20},{16,24},{20,28},{24,0},{28,4},{1,9},{5... | collective-permute-start | bytes 442376 | tf_op jit(solution)/shard_map/ppermute | solution.py:538
  456.7 12.0 %collective-permute-start.41 = (bf16[1,96,768]{2,1,0:T(8,128)(2,1)S(1)}, bf16[1,96,768]{2,1,0:T(8,128)(2,1)}, u32[]{:S(2)}, u32[]{:S(2)}) collective-permute-start(bf16[1,96,768]{2,1,0:T(8,128)(2,1)S(1)} %copy-done.57), channel_id=1, source_target_pairs={{0,16},{4,20},{8,24},{12,28},{16,0},{20,4},{24,8},{28,12},{1,17},{... | collective-permute-start | bytes 442376 | tf_op jit(solution)/shard_map/ppermute | solution.py:538
  458.9 9.8 %collective-permute-start.42 = (bf16[1,96,768]{2,1,0:T(8,128)(2,1)S(1)}, bf16[1,96,768]{2,1,0:T(8,128)(2,1)}, u32[]{:S(2)}, u32[]{:S(2)}) collective-permute-start(bf16[1,96,768]{2,1,0:T(8,128)(2,1)S(1)} %copy-done.56), channel_id=1, source_target_pairs={{0,24},{4,28},{8,0},{12,4},{16,8},{20,12},{24,16},{28,20},{1,25},{... | collective-permute-start | bytes 442376 | tf_op jit(solution)/shard_map/ppermute | solution.py:538
  470.6 20.2 %collective-permute-start.44 = (bf16[1,96,768]{2,1,0:T(8,128)(2,1)}, bf16[1,96,768]{2,1,0:T(8,128)(2,1)S(1)}, u32[]{:S(2)}, u32[]{:S(2)}) collective-permute-start(bf16[1,96,768]{2,1,0:T(8,128)(2,1)} %shard_map.289.a0), channel_id=1, source_target_pairs={{0,2},{1,3},{2,0},{3,1},{4,6},{5,7},{6,4},{7,5},{8,10},{9,11},{10,... | collective-permute-start | bytes 442376 | tf_op jit(solution)/shard_map/ppermute | solution.py:538
  472.0 22.2 %collective-permute-start.43 = (bf16[1,96,768]{2,1,0:T(8,128)(2,1)}, bf16[1,96,768]{2,1,0:T(8,128)(2,1)S(1)}, u32[]{:S(2)}, u32[]{:S(2)}) collective-permute-start(bf16[1,96,768]{2,1,0:T(8,128)(2,1)} %shard_map.289.a0), channel_id=1, source_target_pairs={{0,1},{1,0},{2,3},{3,2},{4,5},{5,4},{6,7},{7,6},{8,9},{9,8},{10,11... | collective-permute-start | bytes 442376 | tf_op jit(solution)/shard_map/ppermute | solution.py:538
  490.8 3.4 collective-permute-start.45
  494.2 7.8 %copy-start.1 = (s32[2,1]{0,1:T(1,128)S(1)}, s32[2,1]{0,1:T(1,128)}, u32[]{:S(2)}) copy-start(s32[2,1]{0,1:T(1,128)} %param.16) | copy-start | bytes 28
  (53 other events, 97.1 us)
Sparse Core Ops, SparseCore 0:
  10.5 39.8 all-gather.10
  53.2 114.9 all-gather.12
  283.9 108.1 reduce-scatter.3
  394.3 20.4 reduce-scatter.5
  417.5 27.4 reduce-scatter.7
  447.1 24.9 all-gather.14
  473.6 19.9 all-gather.8

commit v4 on v3

--- a/solution.py
+++ b/solution.py
@@ -583,7 +583,7 @@
 
 def pick_kernel(
     qkv_ref, out_ref, up_ref, down_ref, again, ashift, qvb, outb, fgain, fshift, upb, downb,
-    a1, f1, rest, ride,
+    a1, f1, rest, last, ride,
 ):
     size, width = f1.shape[1:]
     here = lax.axis_index("section")
@@ -613,13 +613,13 @@
         def _():
             for l in range(2):
                 attn = qkv_ref[l, :, m * width : (m + 1) * width] if m < 3 else out_ref[l]
-                ffn = f1 if l == 0 else rest
-                ffn[0] = up_ref[l, :, m * width : (m + 1) * width]
-                ffn[1] = down_ref[l, m * size : (m + 1) * size]
+                ups, downs = (f1.at[0], f1.at[1]) if l == 0 else (rest.at[0], last.at[0])
+                ups[...] = up_ref[l, :, m * width : (m + 1) * width]
+                downs[...] = down_ref[l, m * size : (m + 1) * size]
                 if l == 0:
                     a1[:size] = attn
                 else:
-                    rest[2] = attn
+                    rest[1] = attn
 
 
 def pick_blocks(*operands):
@@ -629,7 +629,7 @@
         pick_kernel,
         [
             struct((size + 32, width), BF16), struct((2, size, width), BF16),
-            struct((3, size, width), BF16),
+            struct((2, size, width), BF16), struct((1, size, width), BF16),
         ],
         operands, (), (pltpu.VMEM((32, width), F32),), micros=4,
     )
@@ -946,14 +946,18 @@
         )
 
     if direct:
-        a1_block, f1_block, rest_block = line.run(
+        a1_block, f1_block, rest_block, last_block = line.run(
             pick_blocks, qkv_weight, out_weight, up_weight, down_weight,
             attn_gain, attn_shift, qv_bias, out_bias, ffn_gain, ffn_shift, up_bias, down_bias,
         )
         a1_near = gather_along(a1_block[None])
         f1_near = gather_along(f1_block)
-        rest = lax.all_gather(rest_block, ("dp", "section"), axis=0, tiled=False)
-        rest = rest.reshape(8, 4, 3, size, width)
+        rest, last = [
+            lax.all_gather(item, ("dp", "section"), axis=0, tiled=False).reshape(
+                8, 4, item.shape[0], size, width
+            )
+            for item in (rest_block, last_block)
+        ]
         a1 = Gather(line, *line.run(lambda near: split_near(near, (1,)), a1_near), size)
         stream, grad, lens = pinned()
         a1.middle()
@@ -1046,7 +1050,7 @@
     stream = line.run(down_part, ffn_in1, hidden1, vec1, downs1)
     attn_in2 = stream
     if direct:
-        ups2, downs2, attn2 = ((rest,), 0), ((rest,), 1), ((rest,), 2)
+        ups2, downs2, attn2 = ((rest,), 0), ((last,), 0), ((rest,), 1)
     normed2, queries2, own2 = line.run(qkv_part, stream, vec2, attn2)
     peer2 = to_core(own2)
     mixed2, raised2, scale2 = line.run(attend, queries2, own2, peer2, lens)
@@ -1111,11 +1115,6 @@
         f1r.third(120)
         a1r = Reduce(line, *line.run(add_first, a1_keep, a1_got))
         f2_far = to_x(f2_send)
-        rest_own = line.run(
-            lambda near, far, attn: jnp.concatenate([near + far, attn]), f2_near, f2_far, a2r.shard
-        )
-        rest_held = lax.all_gather(rest_own, "section", axis=0)
-        a1r.second()
         shares = line.run(
             lambda *vecs: jnp.broadcast_to(
                 vector_shares(*vecs)[:, None], (group, section_count, layers, 16, size)
@@ -1123,12 +1122,17 @@
             a1_vec, f1_vec, a2_vec, f2_vec,
         )
         shares = lax.all_to_all(shares, ("dp", "section"), 0, 0, tiled=True)
+        a1r.second()
+        moved = redistribute_start(encoded_mine, grad)
+        rest_own = line.run(
+            lambda near, far, attn: jnp.concatenate([near + far, attn]), f2_near, f2_far, a2r.shard
+        )
+        rest_held = lax.all_gather(rest_own, "section", axis=0)
         a1r.third_split()
-        moved = redistribute_start(encoded_mine, grad)
-        my_vec = line.run(lambda got: jnp.sum(got, axis=0), shares)
         f1_held = lax.all_gather(f1r.shard, "section", axis=0)
         a1r.last()
         a1_held = across(a1r.shard)
+        my_vec = line.run(lambda got: jnp.sum(got, axis=0), shares)
         encoded, grad_tokens = redistribute_end(*moved)
         g_qkv, g_out, g_up, g_down = line.run(finish, *a1_held, f1_held, rest_held)
     else:

time: 516 us -> 511 us (level)
    all_gather x1, waiting for transfers between devices: 0.02 us -> 5.66 us  [local(): f1_held = lax.all_gather(f1r.shard, 'section', axis=0)]
    unnamed x130 -> x126, local copies, waits for them, and re-layouts: 36.4 us -> 35.3 us
    all_gather x1 -> x2, waiting for transfers between devices: 9.61 us -> 10.7 us  [local(): lax.all_gather(item, ('dp', 'section'), axis=0, tiled=False)]
  transfers between devices with their start and end apart: 54 -> 55, of which waited for: 17 -> 15; matrix products, arithmetic and copies ran while one was open for 2% -> 2% of each run, Pallas kernels for 34% -> 42%
where the time goes in v4:
time: 511 us; the launch traced here: 504 us
  Pallas kernels  261 us (51%)
  waiting for transfers between devices  105 us (21%)
  starting transfers between devices  44.6 us (9%)
  local copies, waits for them, and re-layouts  43.1 us (8%)
  blocking collectives  28.9 us (6%)
  between operations  16.4 us (3%)
  other arithmetic  5.3 us (1%)
    pallas_call x32, Pallas kernels, call(): pl.pallas_call(body, in_specs=[PLACED if n in placed else WHOLE for n in...  184 us
    ppermute x44, waiting for transfers between devices, over(): return lax.ppermute(block, axis, [(i, move(i)) for i in range(count)])  88 us
    ppermute x44, starting transfers between devices, over(): return lax.ppermute(block, axis, [(i, move(i)) for i in range(count)])  36.5 us
    pallas_call x2, Pallas kernels, attend_back(): pl.pallas_call(attend_back_kernel, grid=(pairs,), in_specs=[block, key, k...  35.6 us
    unnamed x126, local copies, waits for them, and re-layouts  35.3 us
    pallas_call x2, Pallas kernels, attend(): pl.pallas_call(attend_kernel, grid_spec=pltpu.PrefetchScalarGridSpec(num_...  34.7 us
    all_gather x1, blocking collectives, gather_along(): return lax.all_gather(block, 'dp', axis=0, axis_index_groups=ALONG)  28.9 us
    all_gather x2, waiting for transfers between devices, local(): lax.all_gather(item, ('dp', 'section'), axis=0, tiled=False)  10.7 us
  transfers between devices with their start and end apart: 55, of which 15 were waited for; matrix products, arithmetic and copies ran while one was open for 2% of the time, Pallas kernels for 42%

profile of v4, /device:TPU:0, one launch (start us, length us, event | category | flops | bytes accessed | tf_op | source)
XLA Modules:
  0.0 504.2 jit_solution(9210678322734553994)
XLA Ops:
  7.2 3.1 shard_map.254
  11.2 28.9 %all-gather = bf16[512,768]{1,0:T(8,128)(2,1)} all-gather(bf16[128,768]{1,0:T(8,128)(2,1)} %get-tuple-element.523), channel_id=2, replica_groups={{0,8,16,24},{4,12,20,28},{1,9,17,25},{5,13,21,29},{2,10,18,26},{6,14,22..., dimensions={0}, use_global_device_ids=true | all-gather | bytes 983040 | tf_op jit(solution)/shard_map/all_gather | solution.py:561
  40.1 2.0 shard_map.255
  42.1 1.5 collective-permute-start
  47.0 2.6 dynamic-slice_bitcast_fusion
  50.1 1.5 collective-permute-done.1.right_got
  52.3 2.6 shard_map.256
  57.1 2.4 shard_map.257
  62.2 15.5 %collective-permute-done.2.x_got = bf16[8,1,128,384]{3,2,1,0:T(8,128)(2,1)S(1)} collective-permute-done((bf16[8,1,128,384]{3,2,1,0:T(8,128)(2,1)}, bf16[8,1,128,384]{3,2,1,0:T(8,128)(2,1)S(1)}, u32[]{:S(2)}, u32[]{:S(2)}) %collective-permute-start.2) | collective-permute-done | bytes 786464 | tf_op jit(solution)/shard_map/ppermute | solution.py:538
  80.0 3.5 shard_map.258
  85.0 2.3 shard_map.259
  90.3 6.1 %shard_map.260 = (bf16[512,768]{1,0:T(8,128)(2,1)}, bf16[512,768]{1,0:T(8,128)(2,1)}, bf16[2,512,768]{2,1,0:T(8,128)(2,1)}) custom-call(bf16[512,768]{1,0:T(8,128)(2,1)} %get-tuple-element.866.h_ref, f32[16,768]{1,0:T(8,128)} %get-tuple-element.872.vec_ref, bf16[1,2,8,96,768]{4,3,2,1,0:T(8,128)(2,1)} %get-tuple-element.873.refs_0_.refs_4_, ...), custom_call_target="tpu_custom_call" | custom-call | flops 1342177280 | bytes 65536 | tf_op jit(solution)/shard_map/pallas_call | solution.py:43
  97.3 2.4 shard_map.261
  103.3 17.2 %shard_map.262 = (bf16[512,768]{1,0:T(8,128)(2,1)S(1)}, bf16[12,1024,512]{2,1,0:T(8,128)(2,1)}, f32[512,768]{1,0:T(8,128)S(1)}) custom-call(s32[2]{0:T(128)S(1)} %pad_add_fusion.lens_ref, bf16[512,768]{1,0:T(8,128)(2,1)S(1)} %copy-done.10, bf16[2,512,768]{2,1,0:T(8,128)(2,1)S(1)} %copy-done.6, bf16[2,512,768]{2,1,0:T(8,128)(2,1)} %copy-done.19, ...), custom_call_target="tpu_custom_call" | custom-call | flops 4294967296 | bytes 65536 | tf_op jit(solution)/shard_map/pallas_call | solution.py:103
  124.3 3.2 shard_map.263.refs_0_
  127.6 4.4 shard_map.264.h_ref
  132.8 3.3 shard_map.265.refs_0_.refs_2_
  138.0 9.4 %shard_map.266 = (bf16[512,768]{1,0:T(8,128)(2,1)}, bf16[4,512,768]{2,1,0:T(8,128)(2,1)}, bf16[4,512,768]{2,1,0:T(8,128)(2,1)}) custom-call(bf16[512,768]{1,0:T(8,128)(2,1)} %shard_map.264.h_ref, f32[16,768]{1,0:T(8,128)} %get-tuple-element.872.vec_ref, bf16[1,2,8,96,768]{4,3,2,1,0:T(8,128)(2,1)} %shard_map.263.refs_0_, bf16[1,2,8,96,768]{4,3,2,1,0:T(8,128)(2,1)} %copy-done.22), custom_call_target="tpu_custom_call" | custom-call | flops 2415919104 | bytes 65536 | tf_op jit(solution)/shard_map/pallas_call | solution.py:43
  148.8 9.0 %shard_map.267.h_ref = bf16[512,768]{1,0:T(8,128)(2,1)} custom-call(bf16[512,768]{1,0:T(8,128)(2,1)} %shard_map.264.h_ref, bf16[4,512,768]{2,1,0:T(8,128)(2,1)} %get-tuple-element.778.g_hbm, f32[16,768]{1,0:T(8,128)} %get-tuple-element.872.vec_ref, bf16[1,2,8,96,768]{4,3,2,1,0:T(8,128)(2,1)} %shard_map.265.refs_0_.refs_2_, bf16[1,2,8,96,768]{4,3,2,1,0:T(8,128)(2,1)} %copy-done.18), custom_call_target="tpu_custom_call" | custom-call | flops 1610612736 | bytes 65536 | tf_op jit(solution)/shard_map/pallas_call | solution.py:43
  157.8 6.1 %shard_map.268 = (bf16[512,768]{1,0:T(8,128)(2,1)}, bf16[512,768]{1,0:T(8,128)(2,1)}, bf16[2,512,768]{2,1,0:T(8,128)(2,1)}) custom-call(bf16[512,768]{1,0:T(8,128)(2,1)} %shard_map.267.h_ref, f32[16,768]{1,0:T(8,128)} %get-tuple-element.754.vec_ref, bf16[8,4,2,96,768]{4,3,2,1,0:T(8,128)(2,1)} %bitcast.56), custom_call_target="tpu_custom_call" | custom-call | flops 1342177280 | bytes 65536 | tf_op jit(solution)/shard_map/pallas_call | solution.py:43
  164.0 3.6 collective-permute-done.16.kp_ref.vp_ref
  171.4 17.5 %shard_map.269 = (bf16[512,768]{1,0:T(8,128)(2,1)S(1)}, bf16[12,1024,512]{2,1,0:T(8,128)(2,1)}, f32[512,768]{1,0:T(8,128)S(1)}) custom-call(s32[2]{0:T(128)S(1)} %pad_add_fusion.lens_ref, bf16[512,768]{1,0:T(8,128)(2,1)S(1)} %copy-done.12, bf16[2,512,768]{2,1,0:T(8,128)(2,1)S(1)} %copy-done.7, bf16[2,512,768]{2,1,0:T(8,128)(2,1)} %copy-done.20, ...), custom_call_target="tpu_custom_call" | custom-call | flops 4294967296 | bytes 65536 | tf_op jit(solution)/shard_map/pallas_call | solution.py:103
  191.0 4.3 shard_map.270.h_ref
  195.3 9.7 %shard_map.271 = (bf16[512,768]{1,0:T(8,128)(2,1)}, bf16[4,512,768]{2,1,0:T(8,128)(2,1)}, bf16[4,512,768]{2,1,0:T(8,128)(2,1)}) custom-call(bf16[512,768]{1,0:T(8,128)(2,1)} %shard_map.270.h_ref, f32[16,768]{1,0:T(8,128)} %get-tuple-element.754.vec_ref, bf16[8,4,2,96,768]{4,3,2,1,0:T(8,128)(2,1)} %bitcast.58), custom_call_target="tpu_custom_call" | custom-call | flops 2415919104 | bytes 65536 | tf_op jit(solution)/shard_map/pallas_call | solution.py:43
  205.0 10.7 %all-gather.17.cloned.1.call-done = bf16[32,96,768]{2,1,0:T(8,128)(2,1)} async-done(((bf16[1,96,768]{2,1,0:T(8,128)(2,1)}), bf16[32,96,768]{2,1,0:T(8,128)(2,1)}) %all-gather.17.cloned.1.call-update) | async-done | bytes 4718608 | tf_op jit(solution)/shard_map/all_gather | solution.py:956
  215.7 8.9 %shard_map.272 = bf16[512,768]{1,0:T(8,128)(2,1)} custom-call(bf16[512,768]{1,0:T(8,128)(2,1)} %shard_map.270.h_ref, bf16[4,512,768]{2,1,0:T(8,128)(2,1)} %get-tuple-element.705.g_hbm, f32[16,768]{1,0:T(8,128)} %get-tuple-element.754.vec_ref, bf16[8,4,1,96,768]{4,3,2,1,0:T(8,128)(2,1)} %bitcast.62), custom_call_target="tpu_custom_call" | custom-call | flops 1610612736 | bytes 65536 | tf_op jit(solution)/shard_map/pallas_call | solution.py:43
  224.6 20.3 %shard_map.273 = (bf16[512,768]{1,0:T(8,128)(2,1)}, bf16[512,768]{1,0:T(8,128)(2,1)}, bf16[2,2,8,96,768]{4,3,2,1,0:T(8,128)(2,1)}, bf16[2,1,8,96,768]{4,3,2,1,0:...) custom-call(bf16[512,768]{1,0:T(8,128)(2,1)} %get-tuple-element.702.gy_ref, ...), custom_call_target="tpu_custom_call" | custom-call | flops 5368709120 | bytes 65536 | tf_op jit(solution)/shard_map/pallas_call | solution.py:43
  246.7 17.8 %shard_map.274 = (bf16[512,768]{1,0:T(8,128)(2,1)S(1)}, f32[2,512,768]{2,1,0:T(8,128)}, bf16[2,512,768]{2,1,0:T(8,128)(2,1)}) custom-call(bf16[512,768]{1,0:T(8,128)(2,1)S(1)} %copy-done.13, bf16[2,512,768]{2,1,0:T(8,128)(2,1)} %get-tuple-element.725.ko_ref.vo_ref, bf16[2,512,768]{2,1,0:T(8,128)(2,1)} %copy-done.20, ...), custom_call_target="tpu_custom_call" | custom-call | flops 4294967296 | bytes 65536 | tf_op jit(solution)/shard_map/pallas_call | solution.py:166
  265.6 6.4 %shard_map.275 = bf16[8,2,2,96,768]{4,3,2,1,0:T(8,128)(2,1)} custom-call(bf16[2,2,8,96,768]{4,3,2,1,0:T(8,128)(2,1)} %get-tuple-element.742.keep_ref, bf16[2,1,8,96,768]{4,3,2,1,0:T(8,128)(2,1)} %collective-permute-done.18.up_ref, bf16[2,1,8,96,768]{4,3,2,1,0:T(8,128)(2,1)} %collective-permute-done.19.down_ref), custom_call_target="tpu_custom_call" | custom-call | flops 21474836480 | bytes 65536 | tf_op jit(solution)/shard_map/pallas_call | solution.py:758
  273.2 10.9 %shard_map.276 = (bf16[512,768]{1,0:T(8,128)(2,1)}, bf16[2,1,8,96,768]{4,3,2,1,0:T(8,128)(2,1)}, bf16[2,1,8,96,768]{4,3,2,1,0:T(8,128)(2,1)}, f32[8,768]{1,0:T(8,128)}) custom-call(bf16[512,768]{1,0:T(8,128)(2,1)} %get-tuple-element.747.gy_ref, bf16[512,768]{1,0:T(8,128)(2,1)} %shard_map.267.h_ref, bf16[512,768]{1,0:T(8,128)(2,1)} %get-tuple-element.749.a_ref, ...), custom_call_target="tpu_custom_call" | custom-call | flops 2684354560 | bytes 65536 | tf_op jit(solution)/shard_map/pallas_call | solution.py:43
  284.9 4.0 collective-permute-done.20.refs_0_
  290.3 4.0 shard_map.277
  294.3 1.6 collective-permute-start.23
  296.7 19.1 %shard_map.278 = (bf16[512,768]{1,0:T(8,128)(2,1)}, bf16[512,768]{1,0:T(8,128)(2,1)}, bf16[2,2,8,96,768]{4,3,2,1,0:T(8,128)(2,1)}, bf16[2,1,8,96,768]{4,3,2,1,0:...) custom-call(bf16[512,768]{1,0:T(8,128)(2,1)} %get-tuple-element.775.gy_ref, ...), custom_call_target="tpu_custom_call" | custom-call | flops 5368709120 | bytes 65536 | tf_op jit(solution)/shard_map/pallas_call | solution.py:43
  318.0 2.9 shard_map.279
  321.0 3.0 collective-permute-done.22.refs_1_
  325.4 6.5 %shard_map.280 = (bf16[2,8,96,384]{3,2,1,0:T(8,128)(2,1)}, bf16[2,2,4,96,384]{4,3,2,1,0:T(8,128)(2,1)}, bf16[2,8,96,384]{3,2,1,0:T(8,128)(2,1)}, bf16[2,2,4,96,384]{4,3,2,1,0:T(8,128)(2,1)}) custom-call(bf16[2,2,8,96,768]{4,3,2,1,0:T(8,128)(2,1)} %get-tuple-element.817.keep_ref, bf16[2,1,8,96,768]{4,3,2,1,0:T(8,128)(2,1)} %copy-done.23, ...), custom_call_target="tpu_custom_call" | custom-call | flops 1342177280 | bytes 65536 | tf_op jit(solution)/shard_map/pallas_call | solution.py:43
  333.5 1.6 collective-permute-start.26
  335.9 17.9 %shard_map.281 = (bf16[512,768]{1,0:T(8,128)(2,1)S(1)}, f32[2,512,768]{2,1,0:T(8,128)}, bf16[2,512,768]{2,1,0:T(8,128)(2,1)}) custom-call(bf16[512,768]{1,0:T(8,128)(2,1)S(1)} %copy-done.10, bf16[2,512,768]{2,1,0:T(8,128)(2,1)} %get-tuple-element.827.ko_ref.vo_ref, bf16[2,512,768]{2,1,0:T(8,128)(2,1)} %copy-done.19, ...), custom_call_target="tpu_custom_call" | custom-call | flops 4294967296 | bytes 65536 | tf_op jit(solution)/shard_map/pallas_call | solution.py:166
  353.8 7.0 %collective-permute-done.28.x_got = bf16[2,8,96,384]{3,2,1,0:T(8,128)(2,1)S(1)} collective-permute-done((bf16[2,8,96,384]{3,2,1,0:T(8,128)(2,1)}, bf16[2,8,96,384]{3,2,1,0:T(8,128)(2,1)S(1)}, u32[]{:S(2)}, u32[]{:S(2)}) %collective-permute-start.28) | collective-permute-done | bytes 1179680 | tf_op jit(solution)/shard_map/ppermute | solution.py:538
  360.9 10.1 %collective-permute-done.29.y_got = bf16[2,2,4,96,384]{4,3,2,1,0:T(8,128)(2,1)S(1)} collective-permute-done((bf16[2,2,4,96,384]{4,3,2,1,0:T(8,128)(2,1)}, bf16[2,2,4,96,384]{4,3,2,1,0:T(8,128)(2,1)S(1)}, u32[]{:S(2)}, u32[]{:S(2)}) %collective-permute-start.29) | collective-permute-done | bytes 1179680 | tf_op jit(solution)/shard_map/ppermute | solution.py:538
  372.1 4.1 shard_map.282
  376.7 1.6 collective-permute-start.32
  378.3 2.9 collective-permute-done.26.y_got
  382.6 2.2 shard_map.283
  386.0 12.5 %shard_map.284 = (bf16[512,768]{1,0:T(8,128)(2,1)}, bf16[2,1,8,96,768]{4,3,2,1,0:T(8,128)(2,1)}, bf16[2,1,8,96,768]{4,3,2,1,0:T(8,128)(2,1)}, f32[8,768]{1,0:T(8,128)}) custom-call(bf16[512,768]{1,0:T(8,128)(2,1)} %get-tuple-element.865.gy_ref, bf16[512,768]{1,0:T(8,128)(2,1)} %get-tuple-element.866.h_ref, bf16[512,768]{1,0:T(8,128)(2,1)} %get-tuple-element.867.a_ref, ...), custom_call_target="tpu_custom_call" | custom-call | flops 2684354560 | bytes 65536 | tf_op jit(solution)/shard_map/pallas_call | solution.py:43
  400.5 2.9 shard_map.285
  404.9 3.9 shard_map.286
  412.9 18.1 %collective-permute-done.33.x_got = bf16[1,8,96,384]{3,2,1,0:T(8,128)(2,1)S(1)} collective-permute-done((bf16[1,8,96,384]{3,2,1,0:T(8,128)(2,1)}, bf16[1,8,96,384]{3,2,1,0:T(8,128)(2,1)S(1)}, u32[]{:S(2)}, u32[]{:S(2)}) %collective-permute-start.33) | collective-permute-done | bytes 589856 | tf_op jit(solution)/shard_map/ppermute | solution.py:538
  431.8 2.7 shard_map.287
  435.0 1.7 pad_maximum_fusion.2
  437.2 1.7 collective-permute-start.38
  438.8 3.6 all-to-all-start
  443.2 3.1 collective-permute-start.36
  446.3 2.1 shard_map.288
  448.4 2.9 collective-permute-start.40
  452.3 2.2 collective-permute-start.42
  454.5 4.7 collective-permute-done.40.o1
  459.2 8.2 %collective-permute-done.41.o2 = bf16[1,96,768]{2,1,0:T(8,128)(2,1)S(1)} collective-permute-done((bf16[1,96,768]{2,1,0:T(8,128)(2,1)}, bf16[1,96,768]{2,1,0:T(8,128)(2,1)S(1)}, u32[]{:S(2)}, u32[]{:S(2)}) %collective-permute-start.41) | collective-permute-done | bytes 147488 | tf_op jit(solution)/shard_map/ppermute | solution.py:538
  468.7 1.9 shard_map.289.a0
  470.5 1.5 collective-permute-start.44
  472.1 8.8 %collective-permute-done.44.a2 = bf16[1,96,768]{2,1,0:T(8,128)(2,1)S(1)} collective-permute-done((bf16[1,96,768]{2,1,0:T(8,128)(2,1)}, bf16[1,96,768]{2,1,0:T(8,128)(2,1)S(1)}, u32[]{:S(2)}, u32[]{:S(2)}) %collective-permute-start.44) | collective-permute-done | bytes 147488 | tf_op jit(solution)/shard_map/ppermute | solution.py:538
  484.3 5.7 %all-gather.11.cloned.1.call-done.f1_ref = bf16[4,2,96,768]{3,2,1,0:T(8,128)(2,1)} async-done(((bf16[1,2,96,768]{3,2,1,0:T(8,128)(2,1)}), bf16[4,2,96,768]{3,2,1,0:T(8,128)(2,1)}) %all-gather.11.cloned.1.call-update) | async-done | bytes 1179664 | tf_op jit(solution)/shard_map/all_gather | solution.py:1132
  490.0 5.2 %shard_map.290 = (f32[2,96,2304]{2,1,0:T(8,128)}, f32[2,96,768]{2,1,0:T(8,128)}, f32[2,96,3072]{2,1,0:T(8,128)}, f32[2,384,768]{2,1,0:T(8,128)}) custom-call(bf16[1,96,768]{2,1,0:T(8,128)(2,1)} %shard_map.289.a0, bf16[1,96,768]{2,1,0:T(8,128)(2,1)} %copy-done.56, bf16[1,96,768]{2,1,0:T(8,128)(2,1)} %copy-done.55, bf16[1,96,768]{2,1,0:T(8,128)(2,1)} %copy-done.57, ...), custom_call_target="tpu_custom_call" | custom-call | flops 1342177280 | bytes 65536 | tf_op jit(solution)/shard_map/pallas_call | solution.py:43
  (253 shorter events, 69.0 us)
Async XLA Ops:
  7.2 37.8 %copy-start = (s32[2,1]{0,1:T(1,128)S(1)}, s32[2,1]{0,1:T(1,128)}, u32[]{:S(2)}) copy-start(s32[2,1]{0,1:T(1,128)} %param.16) | copy-start | bytes 28
  7.2 49.9 %all-gather.13.cloned.1.call-start = ((), (), s32[]{:S(2)}) async-start(), calls=%async_computation.8 | async-start | bytes 1474560 | tf_op jit(solution)/shard_map/all_gather | solution.py:561
  10.4 147.5 %all-gather.15.cloned.1.call-start = ((), (), s32[]{:S(2)}) async-start(), calls=%async_computation.9 | async-start | bytes 9732096 | tf_op jit(solution)/shard_map/all_gather | solution.py:956
  11.1 204.6 %all-gather.17.cloned.1.call-start = ((), (), s32[]{:S(2)}) async-start(), calls=%async_computation.10 | async-start | bytes 4866048 | tf_op jit(solution)/shard_map/all_gather | solution.py:956
  42.1 8.0 %collective-permute-start = (bf16[4,1,128,384]{3,2,1,0:T(8,128)(2,1)}, bf16[4,1,128,384]{3,2,1,0:T(8,128)(2,1)S(1)}, u32[]{:S(2)}, u32[]{:S(2)}) collective-permute-start(bf16[4,1,128,384]{3,2,1,0:T(8,128)(2,1)} %get-tuple-element.538.left_ref), channel_id=1, source_target_pairs={{0,4},{4,0},{8,12},{12,8},{16,20},{20,16},{24,28},{28,24},{1,5},{5... | collective-permute-start | bytes 1179656 | tf_op jit(solution)/shard_map/ppermute | solution.py:538
  43.6 8.0 %collective-permute-start.1 = (bf16[4,1,128,384]{3,2,1,0:T(8,128)(2,1)}, bf16[4,1,128,384]{3,2,1,0:T(8,128)(2,1)S(1)}, u32[]{:S(2)}, u32[]{:S(2)}) collective-permute-start(bf16[4,1,128,384]{3,2,1,0:T(8,128)(2,1)} %get-tuple-element.540.right_ref), channel_id=1, source_target_pairs={{0,2},{1,3},{2,0},{3,1},{4,6},{5,7},{6,4},{7,5},{8,10},{9,11},{10,... | collective-permute-start | bytes 1179656 | tf_op jit(solution)/shard_map/ppermute | solution.py:538
  54.9 22.8 %collective-permute-start.2 = (bf16[8,1,128,384]{3,2,1,0:T(8,128)(2,1)}, bf16[8,1,128,384]{3,2,1,0:T(8,128)(2,1)S(1)}, u32[]{:S(2)}, u32[]{:S(2)}) collective-permute-start(bf16[8,1,128,384]{3,2,1,0:T(8,128)(2,1)} %get-tuple-element.556.x_ref), channel_id=1, source_target_pairs={{0,2},{1,3},{2,0},{3,1},{4,6},{5,7},{6,4},{7,5},{8,10},{9,11},{10,... | collective-permute-start | bytes 2359304 | tf_op jit(solution)/shard_map/ppermute | solution.py:538
  56.3 22.8 %collective-permute-start.3 = (bf16[2,4,1,128,384]{4,3,2,1,0:T(8,128)(2,1)}, bf16[2,4,1,128,384]{4,3,2,1,0:T(8,128)(2,1)S(1)}, u32[]{:S(2)}, u32[]{:S(2)}) collective-permute-start(bf16[2,4,1,128,384]{4,3,2,1,0:T(8,128)(2,1)} %get-tuple-element.558.y_ref), channel_id=1, source_target_pairs={{0,4},{4,0},{8,12},{12,8},{16,20},{20,16},{24,28},{28,24},{1,5},{5... | collective-permute-start | bytes 2359304 | tf_op jit(solution)/shard_map/ppermute | solution.py:538
  59.5 24.1 %collective-permute-start.5 = (bf16[4,1,96,384]{3,2,1,0:T(8,128)(2,1)}, bf16[4,1,96,384]{3,2,1,0:T(8,128)(2,1)S(1)}, u32[]{:S(2)}, u32[]{:S(2)}) collective-permute-start(bf16[4,1,96,384]{3,2,1,0:T(8,128)(2,1)} %get-tuple-element.569.left_ref), channel_id=1, source_target_pairs={{0,4},{4,0},{8,12},{12,8},{16,20},{20,16},{24,28},{28,24},{1,5},{5... | collective-permute-start | bytes 884744 | tf_op jit(solution)/shard_map/ppermute | solution.py:538
  60.7 22.9 %collective-permute-start.6 = (bf16[4,1,96,384]{3,2,1,0:T(8,128)(2,1)}, bf16[4,1,96,384]{3,2,1,0:T(8,128)(2,1)S(1)}, u32[]{:S(2)}, u32[]{:S(2)}) collective-permute-start(bf16[4,1,96,384]{3,2,1,0:T(8,128)(2,1)} %get-tuple-element.571.right_ref), channel_id=1, source_target_pairs={{0,2},{1,3},{2,0},{3,1},{4,6},{5,7},{6,4},{7,5},{8,10},{9,11},{10,... | collective-permute-start | bytes 884744 | tf_op jit(solution)/shard_map/ppermute | solution.py:538
  61.3 337.3 %reduce-scatter.4.cloned.1.call-start = ((), (), s32[]{:S(2)}) async-start(), calls=%async_computation.4 | async-start | bytes 5308416 | tf_op jit(solution)/shard_map/reduce_scatter | solution.py:770
  61.4 35.1 %collective-permute-start.8 = (bf16[4,1,96,384]{3,2,1,0:T(8,128)(2,1)}, bf16[4,1,96,384]{3,2,1,0:T(8,128)(2,1)S(1)}, u32[]{:S(2)}, u32[]{:S(2)}) collective-permute-start(bf16[4,1,96,384]{3,2,1,0:T(8,128)(2,1)} %get-tuple-element.591.left_ref), channel_id=1, source_target_pairs={{0,4},{4,0},{8,12},{12,8},{16,20},{20,16},{24,28},{28,24},{1,5},{5... | collective-permute-start | bytes 884744 | tf_op jit(solution)/shard_map/ppermute | solution.py:538
  77.7 18.8 %collective-permute-start.9 = (bf16[4,1,96,384]{3,2,1,0:T(8,128)(2,1)}, bf16[4,1,96,384]{3,2,1,0:T(8,128)(2,1)S(1)}, u32[]{:S(2)}, u32[]{:S(2)}) collective-permute-start(bf16[4,1,96,384]{3,2,1,0:T(8,128)(2,1)} %get-tuple-element.593.right_ref), channel_id=1, source_target_pairs={{0,2},{1,3},{2,0},{3,1},{4,6},{5,7},{6,4},{7,5},{8,10},{9,11},{10,... | collective-permute-start | bytes 884744 | tf_op jit(solution)/shard_map/ppermute | solution.py:538
  83.6 5.3 %collective-permute-start.4 = (bf16[1,2,8,96,768]{4,3,2,1,0:T(8,128)(2,1)}, bf16[1,2,8,96,768]{4,3,2,1,0:T(8,128)(2,1)S(1)}, u32[]{:S(2)}, u32[]{:S(2)}) collective-permute-start(bf16[1,2,8,96,768]{4,3,2,1,0:T(8,128)(2,1)} %get-tuple-element.873.refs_0_.refs_4_), channel_id=1, source_target_pairs={{0,1},{1,0},{2,3},{3,2},{4,5},{5,4},{6,7},{7,6},{8,9},{9,8},{10,11... | collective-permute-start | bytes 7077896 | tf_op jit(solution)/shard_map/ppermute | solution.py:538
  87.3 35.4 %collective-permute-start.10 = (bf16[8,1,96,384]{3,2,1,0:T(8,128)(2,1)}, bf16[8,1,96,384]{3,2,1,0:T(8,128)(2,1)S(1)}, u32[]{:S(2)}, u32[]{:S(2)}) collective-permute-start(bf16[8,1,96,384]{3,2,1,0:T(8,128)(2,1)} %get-tuple-element.611.x_ref), channel_id=1, source_target_pairs={{0,2},{1,3},{2,0},{3,1},{4,6},{5,7},{6,4},{7,5},{8,10},{9,11},{10,... | collective-permute-start | bytes 1769480 | tf_op jit(solution)/shard_map/ppermute | solution.py:538
  88.1 34.5 %collective-permute-start.11 = (bf16[2,4,1,96,384]{4,3,2,1,0:T(8,128)(2,1)}, bf16[2,4,1,96,384]{4,3,2,1,0:T(8,128)(2,1)S(1)}, u32[]{:S(2)}, u32[]{:S(2)}) collective-permute-start(bf16[2,4,1,96,384]{4,3,2,1,0:T(8,128)(2,1)} %get-tuple-element.613.y_ref), channel_id=1, source_target_pairs={{0,4},{4,0},{8,12},{12,8},{16,20},{20,16},{24,28},{28,24},{1,5},{5... | collective-permute-start | bytes 1769480 | tf_op jit(solution)/shard_map/ppermute | solution.py:538
  96.5 5.7 %collective-permute-start.7 = (bf16[2,512,768]{2,1,0:T(8,128)(2,1)}, bf16[2,512,768]{2,1,0:T(8,128)(2,1)S(1)}, u32[]{:S(2)}, u32[]{:S(2)}) collective-permute-start(bf16[2,512,768]{2,1,0:T(8,128)(2,1)} %get-tuple-element.827.ko_ref.vo_ref), channel_id=1, source_target_pairs={{0,1},{1,0},{2,3},{3,2},{4,5},{5,4},{6,7},{7,6},{8,9},{9,8},{10,11... | collective-permute-start | bytes 4718600 | tf_op jit(solution)/shard_map/ppermute | solution.py:538
  99.7 32.3 %collective-permute-start.13 = (bf16[8,1,96,384]{3,2,1,0:T(8,128)(2,1)}, bf16[8,1,96,384]{3,2,1,0:T(8,128)(2,1)S(1)}, u32[]{:S(2)}, u32[]{:S(2)}) collective-permute-start(bf16[8,1,96,384]{3,2,1,0:T(8,128)(2,1)} %get-tuple-element.628.x_ref), channel_id=1, source_target_pairs={{0,2},{1,3},{2,0},{3,1},{4,6},{5,7},{6,4},{7,5},{8,10},{9,11},{10,... | collective-permute-start | bytes 1769480 | tf_op jit(solution)/shard_map/ppermute | solution.py:538
  100.9 31.1 %collective-permute-start.14 = (bf16[2,4,1,96,384]{4,3,2,1,0:T(8,128)(2,1)}, bf16[2,4,1,96,384]{4,3,2,1,0:T(8,128)(2,1)}, u32[]{:S(2)}, u32[]{:S(2)}) collective-permute-start(bf16[2,4,1,96,384]{4,3,2,1,0:T(8,128)(2,1)} %get-tuple-element.630.y_ref), channel_id=1, source_target_pairs={{0,4},{4,0},{8,12},{12,8},{16,20},{20,16},{24,28},{28,24},{1,5},{5... | collective-permute-start | bytes 1769480 | tf_op jit(solution)/shard_map/ppermute | solution.py:538
  127.6 9.0 %collective-permute-start.12 = (bf16[1,2,8,96,768]{4,3,2,1,0:T(8,128)(2,1)}, bf16[1,2,8,96,768]{4,3,2,1,0:T(8,128)(2,1)S(1)}, u32[]{:S(2)}, u32[]{:S(2)}) collective-permute-start(bf16[1,2,8,96,768]{4,3,2,1,0:T(8,128)(2,1)} %shard_map.263.refs_0_), channel_id=1, source_target_pairs={{0,1},{1,0},{2,3},{3,2},{4,5},{5,4},{6,7},{7,6},{8,9},{9,8},{10,11... | collective-permute-start | bytes 7077896 | tf_op jit(solution)/shard_map/ppermute | solution.py:538
  136.1 11.3 %collective-permute-start.15 = (bf16[1,2,8,96,768]{4,3,2,1,0:T(8,128)(2,1)}, bf16[1,2,8,96,768]{4,3,2,1,0:T(8,128)(2,1)S(1)}, u32[]{:S(2)}, u32[]{:S(2)}) collective-permute-start(bf16[1,2,8,96,768]{4,3,2,1,0:T(8,128)(2,1)} %shard_map.265.refs_0_.refs_2_), channel_id=1, source_target_pairs={{0,1},{1,0},{2,3},{3,2},{4,5},{5,4},{6,7},{7,6},{8,9},{9,8},{10,11... | collective-permute-start | bytes 7077896 | tf_op jit(solution)/shard_map/ppermute | solution.py:538
  164.0 3.7 collective-permute-start.16
  224.6 20.9 %copy-start.3 = (bf16[512,768]{1,0:T(8,128)(2,1)S(1)}, bf16[512,768]{1,0:T(8,128)(2,1)}, u32[]{:S(2)}) copy-start(bf16[512,768]{1,0:T(8,128)(2,1)} %copy-done.2) | copy-start | bytes 2359300
  224.6 20.9 %copy-start.13 = (bf16[512,768]{1,0:T(8,128)(2,1)S(1)}, bf16[512,768]{1,0:T(8,128)(2,1)}, u32[]{:S(2)}) copy-start(bf16[512,768]{1,0:T(8,128)(2,1)} %get-tuple-element.724.q_ref) | copy-start | bytes 2359300
  245.0 20.7 %collective-permute-start.18 = (bf16[2,1,8,96,768]{4,3,2,1,0:T(8,128)(2,1)}, bf16[2,1,8,96,768]{4,3,2,1,0:T(8,128)(2,1)}, u32[]{:S(2)}, u32[]{:S(2)}) collective-permute-start(bf16[2,1,8,96,768]{4,3,2,1,0:T(8,128)(2,1)} %get-tuple-element.739), channel_id=1, source_target_pairs={{0,1},{1,0},{2,3},{3,2},{4,5},{5,4},{6,7},{7,6},{8,9},{9,8},{10,11... | collective-permute-start | bytes 7077896 | tf_op jit(solution)/shard_map/ppermute | solution.py:538
  245.3 20.3 %collective-permute-start.19 = (bf16[2,1,8,96,768]{4,3,2,1,0:T(8,128)(2,1)}, bf16[2,1,8,96,768]{4,3,2,1,0:T(8,128)(2,1)}, u32[]{:S(2)}, u32[]{:S(2)}) collective-permute-start(bf16[2,1,8,96,768]{4,3,2,1,0:T(8,128)(2,1)} %get-tuple-element.740), channel_id=1, source_target_pairs={{0,1},{1,0},{2,3},{3,2},{4,5},{5,4},{6,7},{7,6},{8,9},{9,8},{10,11... | collective-permute-start | bytes 7077896 | tf_op jit(solution)/shard_map/ppermute | solution.py:538
  265.3 6.7 %collective-permute-start.17 = (bf16[2,512,768]{2,1,0:T(8,128)(2,1)}, bf16[2,512,768]{2,1,0:T(8,128)(2,1)S(1)}, u32[]{:S(2)}, u32[]{:S(2)}) collective-permute-start(bf16[2,512,768]{2,1,0:T(8,128)(2,1)} %get-tuple-element.737), channel_id=1, source_target_pairs={{0,1},{1,0},{2,3},{3,2},{4,5},{5,4},{6,7},{7,6},{8,9},{9,8},{10,11... | collective-permute-start | bytes 4718600 | tf_op jit(solution)/shard_map/ppermute | solution.py:538
  284.1 4.8 collective-permute-start.20
  284.4 150.5 %reduce-scatter.6.cloned.1.call-start = ((), (), s32[]{:S(2)}) async-start(), calls=%async_computation.5 | async-start | bytes 737280 | tf_op jit(solution)/shard_map/reduce_scatter | solution.py:861
  294.3 22.1 %collective-permute-start.23 = (bf16[1,8,96,384]{3,2,1,0:T(8,128)(2,1)}, bf16[1,8,96,384]{3,2,1,0:T(8,128)(2,1)S(1)}, u32[]{:S(2)}, u32[]{:S(2)}) collective-permute-start(bf16[1,8,96,384]{3,2,1,0:T(8,128)(2,1)} %get-tuple-element.803), channel_id=1, source_target_pairs={{0,2},{1,3},{2,0},{3,1},{4,6},{5,7},{6,4},{7,5},{8,10},{9,11},{10,... | collective-permute-start | bytes 1769480 | tf_op jit(solution)/shard_map/ppermute | solution.py:538
  295.9 20.5 %collective-permute-start.24 = (bf16[2,1,4,96,384]{4,3,2,1,0:T(8,128)(2,1)}, bf16[2,1,4,96,384]{4,3,2,1,0:T(8,128)(2,1)S(1)}, u32[]{:S(2)}, u32[]{:S(2)}) collective-permute-start(bf16[2,1,4,96,384]{4,3,2,1,0:T(8,128)(2,1)} %get-tuple-element.805), channel_id=1, source_target_pairs={{0,4},{4,0},{8,12},{12,8},{16,20},{20,16},{24,28},{28,24},{1,5},{5... | collective-permute-start | bytes 1769480 | tf_op jit(solution)/shard_map/ppermute | solution.py:538
  315.8 5.2 %collective-permute-start.21 = (bf16[2,1,8,96,768]{4,3,2,1,0:T(8,128)(2,1)}, bf16[2,1,8,96,768]{4,3,2,1,0:T(8,128)(2,1)S(1)}, u32[]{:S(2)}, u32[]{:S(2)}) collective-permute-start(bf16[2,1,8,96,768]{4,3,2,1,0:T(8,128)(2,1)} %get-tuple-element.800), channel_id=1, source_target_pairs={{0,1},{1,0},{2,3},{3,2},{4,5},{5,4},{6,7},{7,6},{8,9},{9,8},{10,11... | collective-permute-start | bytes 7077896 | tf_op jit(solution)/shard_map/ppermute | solution.py:538
  315.9 8.1 %collective-permute-start.22 = (bf16[2,1,8,96,768]{4,3,2,1,0:T(8,128)(2,1)}, bf16[2,1,8,96,768]{4,3,2,1,0:T(8,128)(2,1)S(1)}, u32[]{:S(2)}, u32[]{:S(2)}) collective-permute-start(bf16[2,1,8,96,768]{4,3,2,1,0:T(8,128)(2,1)} %get-tuple-element.801), channel_id=1, source_target_pairs={{0,1},{1,0},{2,3},{3,2},{4,5},{5,4},{6,7},{7,6},{8,9},{9,8},{10,11... | collective-permute-start | bytes 7077896 | tf_op jit(solution)/shard_map/ppermute | solution.py:538
  321.0 14.9 %copy-start.5 = (bf16[512,768]{1,0:T(8,128)(2,1)S(1)}, bf16[512,768]{1,0:T(8,128)(2,1)}, u32[]{:S(2)}) copy-start(bf16[512,768]{1,0:T(8,128)(2,1)} %copy-done.4) | copy-start | bytes 2359300
  321.0 14.9 %copy-start.11 = (bf16[512,768]{1,0:T(8,128)(2,1)S(1)}, bf16[512,768]{1,0:T(8,128)(2,1)}, u32[]{:S(2)}) copy-start(bf16[512,768]{1,0:T(8,128)(2,1)} %get-tuple-element.830.go_ref) | copy-start | bytes 2359300
  331.8 29.0 %collective-permute-start.28 = (bf16[2,8,96,384]{3,2,1,0:T(8,128)(2,1)}, bf16[2,8,96,384]{3,2,1,0:T(8,128)(2,1)S(1)}, u32[]{:S(2)}, u32[]{:S(2)}) collective-permute-start(bf16[2,8,96,384]{3,2,1,0:T(8,128)(2,1)} %get-tuple-element.845), channel_id=1, source_target_pairs={{0,2},{1,3},{2,0},{3,1},{4,6},{5,7},{6,4},{7,5},{8,10},{9,11},{10,... | collective-permute-start | bytes 3538952 | tf_op jit(solution)/shard_map/ppermute | solution.py:538
  333.1 37.9 %collective-permute-start.29 = (bf16[2,2,4,96,384]{4,3,2,1,0:T(8,128)(2,1)}, bf16[2,2,4,96,384]{4,3,2,1,0:T(8,128)(2,1)S(1)}, u32[]{:S(2)}, u32[]{:S(2)}) collective-permute-start(bf16[2,2,4,96,384]{4,3,2,1,0:T(8,128)(2,1)} %get-tuple-element.847), channel_id=1, source_target_pairs={{0,4},{4,0},{8,12},{12,8},{16,20},{20,16},{24,28},{28,24},{1,5},{5... | collective-permute-start | bytes 3538952 | tf_op jit(solution)/shard_map/ppermute | solution.py:538
  333.5 47.6 %collective-permute-start.26 = (bf16[1,4,96,384]{3,2,1,0:T(8,128)(2,1)}, bf16[1,4,96,384]{3,2,1,0:T(8,128)(2,1)S(1)}, u32[]{:S(2)}, u32[]{:S(2)}) collective-permute-start(bf16[1,4,96,384]{3,2,1,0:T(8,128)(2,1)} %get-tuple-element.841), channel_id=1, source_target_pairs={{0,4},{4,0},{8,12},{12,8},{16,20},{20,16},{24,28},{28,24},{1,5},{5... | collective-permute-start | bytes 884744 | tf_op jit(solution)/shard_map/ppermute | solution.py:538
  335.2 46.0 %collective-permute-start.27 = (bf16[1,4,96,384]{3,2,1,0:T(8,128)(2,1)}, bf16[1,4,96,384]{3,2,1,0:T(8,128)(2,1)S(1)}, u32[]{:S(2)}, u32[]{:S(2)}) collective-permute-start(bf16[1,4,96,384]{3,2,1,0:T(8,128)(2,1)} %get-tuple-element.843), channel_id=1, source_target_pairs={{0,2},{1,3},{2,0},{3,1},{4,6},{5,7},{6,4},{7,5},{8,10},{9,11},{10,... | collective-permute-start | bytes 884744 | tf_op jit(solution)/shard_map/ppermute | solution.py:538
  353.8 22.4 %copy-start.16 = (bf16[512,768]{1,0:T(8,128)(2,1)}, bf16[512,768]{1,0:T(8,128)(2,1)S(1)}, u32[]{:S(2)}) copy-start(bf16[512,768]{1,0:T(8,128)(2,1)S(1)} %get-tuple-element.869.gq_ref) | copy-start | bytes 2359300
  353.8 31.1 %collective-permute-start.25 = (bf16[2,512,768]{2,1,0:T(8,128)(2,1)}, bf16[2,512,768]{2,1,0:T(8,128)(2,1)S(1)}, u32[]{:S(2)}, u32[]{:S(2)}) collective-permute-start(bf16[2,512,768]{2,1,0:T(8,128)(2,1)} %get-tuple-element.839), channel_id=1, source_target_pairs={{0,1},{1,0},{2,3},{3,2},{4,5},{5,4},{6,7},{7,6},{8,9},{9,8},{10,11... | collective-permute-start | bytes 4718600 | tf_op jit(solution)/shard_map/ppermute | solution.py:538
  360.9 10.1 %copy-start.39 = (bf16[2,8,96,384]{3,2,1,0:T(8,128)(2,1)}, bf16[2,8,96,384]{3,2,1,0:T(8,128)(2,1)S(1)}, u32[]{:S(2)}) copy-start(bf16[2,8,96,384]{3,2,1,0:T(8,128)(2,1)S(1)} %collective-permute-done.28.x_got) | copy-start | bytes 3538948
  376.2 23.5 %collective-permute-start.31 = (bf16[2,4,96,384]{3,2,1,0:T(8,128)(2,1)}, bf16[2,4,96,384]{3,2,1,0:T(8,128)(2,1)S(1)}, u32[]{:S(2)}, u32[]{:S(2)}) collective-permute-start(bf16[2,4,96,384]{3,2,1,0:T(8,128)(2,1)} %get-tuple-element.884), channel_id=1, source_target_pairs={{0,4},{4,0},{8,12},{12,8},{16,20},{20,16},{24,28},{28,24},{1,5},{5... | collective-permute-start | bytes 1769480 | tf_op jit(solution)/shard_map/ppermute | solution.py:538
  376.7 23.1 %collective-permute-start.32 = (bf16[2,4,96,384]{3,2,1,0:T(8,128)(2,1)}, bf16[2,4,96,384]{3,2,1,0:T(8,128)(2,1)}, u32[]{:S(2)}, u32[]{:S(2)}) collective-permute-start(bf16[2,4,96,384]{3,2,1,0:T(8,128)(2,1)} %get-tuple-element.886), channel_id=1, source_target_pairs={{0,2},{1,3},{2,0},{3,1},{4,6},{5,7},{6,4},{7,5},{8,10},{9,11},{10,... | collective-permute-start | bytes 1769480 | tf_op jit(solution)/shard_map/ppermute | solution.py:538
  384.8 61.4 %reduce-scatter.8.cloned.1.call-start = ((), (), s32[]{:S(2)}) async-start(), calls=%async_computation.6 | async-start | bytes 1474560 | tf_op jit(solution)/shard_map/reduce_scatter | solution.py:861
  398.5 4.9 collective-permute-start.30
  408.9 26.0 %collective-permute-start.39 = (bf16[2,96,768]{2,1,0:T(8,128)(2,1)S(1)}, bf16[2,96,768]{2,1,0:T(8,128)(2,1)S(1)}, u32[]{:S(2)}, u32[]{:S(2)}) collective-permute-start(bf16[2,96,768]{2,1,0:T(8,128)(2,1)S(1)} %get-tuple-element.941), channel_id=1, source_target_pairs={{0,2},{1,3},{2,0},{3,1},{4,6},{5,7},{6,4},{7,5},{8,10},{9,11},{10,... | collective-permute-start | bytes 884744 | tf_op jit(solution)/shard_map/ppermute | solution.py:538
  410.4 20.6 %collective-permute-start.33 = (bf16[1,8,96,384]{3,2,1,0:T(8,128)(2,1)}, bf16[1,8,96,384]{3,2,1,0:T(8,128)(2,1)S(1)}, u32[]{:S(2)}, u32[]{:S(2)}) collective-permute-start(bf16[1,8,96,384]{3,2,1,0:T(8,128)(2,1)} %get-tuple-element.906), channel_id=1, source_target_pairs={{0,2},{1,3},{2,0},{3,1},{4,6},{5,7},{6,4},{7,5},{8,10},{9,11},{10,... | collective-permute-start | bytes 1769480 | tf_op jit(solution)/shard_map/ppermute | solution.py:538
  411.5 19.5 %collective-permute-start.34 = (bf16[2,1,4,96,384]{4,3,2,1,0:T(8,128)(2,1)}, bf16[2,1,4,96,384]{4,3,2,1,0:T(8,128)(2,1)}, u32[]{:S(2)}, u32[]{:S(2)}) collective-permute-start(bf16[2,1,4,96,384]{4,3,2,1,0:T(8,128)(2,1)} %get-tuple-element.908), channel_id=1, source_target_pairs={{0,4},{4,0},{8,12},{12,8},{16,20},{20,16},{24,28},{28,24},{1,5},{5... | collective-permute-start | bytes 1769480 | tf_op jit(solution)/shard_map/ppermute | solution.py:538
  412.9 21.7 %copy-start.21 = (bf16[512,768]{1,0:T(8,128)(2,1)S(1)}, bf16[512,768]{1,0:T(8,128)(2,1)}, u32[]{:S(2)}) copy-start(bf16[512,768]{1,0:T(8,128)(2,1)} %shard_map.272) | copy-start | bytes 2359300
  412.9 21.7 %copy-start.27 = (bf16[512,768]{1,0:T(8,128)(2,1)S(1)}, bf16[512,768]{1,0:T(8,128)(2,1)}, u32[]{:S(2)}) copy-start(bf16[512,768]{1,0:T(8,128)(2,1)} %get-tuple-element.931) | copy-start | bytes 2359300
  412.9 71.4 %all-gather.19.cloned.1.call-start = ((), (), s32[]{:S(2)}) async-start(), calls=%async_computation.11 | async-start | bytes 2211840 | tf_op jit(solution)/shard_map/all_gather | solution.py:1130
  436.7 9.6 %collective-permute-start.37 = (bf16[1,4,96,384]{3,2,1,0:T(8,128)(2,1)S(1)}, bf16[1,4,96,384]{3,2,1,0:T(8,128)(2,1)}, u32[]{:S(2)}, u32[]{:S(2)}) collective-permute-start(bf16[1,4,96,384]{3,2,1,0:T(8,128)(2,1)S(1)} %copy-done.48), channel_id=1, source_target_pairs={{0,4},{4,0},{8,12},{12,8},{16,20},{20,16},{24,28},{28,24},{1,5},{5... | collective-permute-start | bytes 884744 | tf_op jit(solution)/shard_map/ppermute | solution.py:538
  437.2 9.1 %collective-permute-start.38 = (bf16[1,4,96,384]{3,2,1,0:T(8,128)(2,1)S(1)}, bf16[1,4,96,384]{3,2,1,0:T(8,128)(2,1)}, u32[]{:S(2)}, u32[]{:S(2)}) collective-permute-start(bf16[1,4,96,384]{3,2,1,0:T(8,128)(2,1)S(1)} %copy-done.47), channel_id=1, source_target_pairs={{0,2},{1,3},{2,0},{3,1},{4,6},{5,7},{6,4},{7,5},{8,10},{9,11},{10,... | collective-permute-start | bytes 884744 | tf_op jit(solution)/shard_map/ppermute | solution.py:538
  438.8 33.2 %all-to-all-start = ((f32[32,2,16,96]{3,2,1,0:T(8,128)}), f32[32,2,16,96]{3,2,1,0:T(8,128)S(1)}, u32[]{:S(2)}, u32[]{:S(2)}) async-start(f32[32,2,16,96]{3,2,1,0:T(8,128)} %bitcast.19), calls=%async_computation.1 | async-start | bytes 1048576 | tf_op jit(solution)/shard_map/all_to_all | solution.py:1124
  442.4 47.6 %all-gather.11.cloned.1.call-start = ((), (), s32[]{:S(2)}) async-start(), calls=%async_computation.7 | async-start | bytes 1474560 | tf_op jit(solution)/shard_map/all_gather | solution.py:1132
  442.5 38.5 %collective-permute-start.35 = (bf16[2,256,768]{2,1,0:T(8,128)(2,1)S(1)}, bf16[2,256,768]{2,1,0:T(8,128)(2,1)S(1)}, u32[]{:S(2)}, u32[]{:S(2)}) collective-permute-start(bf16[2,256,768]{2,1,0:T(8,128)(2,1)S(1)} %get-tuple-element.933), channel_id=1, source_target_pairs={{0,0},{1,2},{2,1},{3,3},{4,4},{5,6},{6,5},{7,7},{8,8},{9,10},{10,9... | collective-permute-start | bytes 2359304 | tf_op jit(solution)/shard_map/ppermute | solution.py:1022
  443.2 37.8 %collective-permute-start.36 = (bf16[2,256,768]{2,1,0:T(8,128)(2,1)S(1)}, bf16[2,256,768]{2,1,0:T(8,128)(2,1)}, u32[]{:S(2)}, u32[]{:S(2)}) collective-permute-start(bf16[2,256,768]{2,1,0:T(8,128)(2,1)S(1)} %get-tuple-element.934), channel_id=1, source_target_pairs={{0,1},{1,3},{2,0},{3,2},{4,5},{5,7},{6,4},{7,6},{8,9},{9,11},{10,8... | collective-permute-start | bytes 2359304 | tf_op jit(solution)/shard_map/ppermute | solution.py:1022
  448.4 10.8 %collective-permute-start.40 = (bf16[1,96,768]{2,1,0:T(8,128)(2,1)}, bf16[1,96,768]{2,1,0:T(8,128)(2,1)S(1)}, u32[]{:S(2)}, u32[]{:S(2)}) collective-permute-start(bf16[1,96,768]{2,1,0:T(8,128)(2,1)} %get-tuple-element.959), channel_id=1, source_target_pairs={{0,8},{4,12},{8,16},{12,20},{16,24},{20,28},{24,0},{28,4},{1,9},{5... | collective-permute-start | bytes 442376 | tf_op jit(solution)/shard_map/ppermute | solution.py:538
  451.3 16.1 %collective-permute-start.41 = (bf16[1,96,768]{2,1,0:T(8,128)(2,1)}, bf16[1,96,768]{2,1,0:T(8,128)(2,1)S(1)}, u32[]{:S(2)}, u32[]{:S(2)}) collective-permute-start(bf16[1,96,768]{2,1,0:T(8,128)(2,1)} %get-tuple-element.960), channel_id=1, source_target_pairs={{0,16},{4,20},{8,24},{12,28},{16,0},{20,4},{24,8},{28,12},{1,17},{... | collective-permute-start | bytes 442376 | tf_op jit(solution)/shard_map/ppermute | solution.py:538
  452.3 15.1 %collective-permute-start.42 = (bf16[1,96,768]{2,1,0:T(8,128)(2,1)}, bf16[1,96,768]{2,1,0:T(8,128)(2,1)S(1)}, u32[]{:S(2)}, u32[]{:S(2)}) collective-permute-start(bf16[1,96,768]{2,1,0:T(8,128)(2,1)} %get-tuple-element.961), channel_id=1, source_target_pairs={{0,24},{4,28},{8,0},{12,4},{16,8},{20,12},{24,16},{28,20},{1,25},{... | collective-permute-start | bytes 442376 | tf_op jit(solution)/shard_map/ppermute | solution.py:538
  470.5 10.4 %collective-permute-start.44 = (bf16[1,96,768]{2,1,0:T(8,128)(2,1)}, bf16[1,96,768]{2,1,0:T(8,128)(2,1)S(1)}, u32[]{:S(2)}, u32[]{:S(2)}) collective-permute-start(bf16[1,96,768]{2,1,0:T(8,128)(2,1)} %shard_map.289.a0), channel_id=1, source_target_pairs={{0,2},{1,3},{2,0},{3,1},{4,6},{5,7},{6,4},{7,5},{8,10},{9,11},{10,... | collective-permute-start | bytes 442376 | tf_op jit(solution)/shard_map/ppermute | solution.py:538
  472.0 12.3 %collective-permute-start.43 = (bf16[1,96,768]{2,1,0:T(8,128)(2,1)}, bf16[1,96,768]{2,1,0:T(8,128)(2,1)S(1)}, u32[]{:S(2)}, u32[]{:S(2)}) collective-permute-start(bf16[1,96,768]{2,1,0:T(8,128)(2,1)} %shard_map.289.a0), channel_id=1, source_target_pairs={{0,1},{1,0},{2,3},{3,2},{4,5},{5,4},{6,7},{7,6},{8,9},{9,8},{10,11... | collective-permute-start | bytes 442376 | tf_op jit(solution)/shard_map/ppermute | solution.py:538
  480.9 3.4 collective-permute-start.45
  (52 other events, 110.0 us)
Sparse Core Ops, SparseCore 0:
  10.5 39.8 all-gather.12
  53.2 95.4 all-gather.14
  151.7 63.9 all-gather.16
  284.5 106.5 reduce-scatter.3
  393.2 20.4 reduce-scatter.5
  416.5 27.5 reduce-scatter.7
  446.2 24.9 all-gather.18
  472.7 17.1 all-gather.10

commit v5 on v4

--- a/solution.py
+++ b/solution.py
@@ -752,12 +752,12 @@
 
 def add_both(keep, *got):
     _, count, parts, size, width = keep.shape
-    step = parts // 4
+    step = parts // 2
     spec = pl.BlockSpec((2, count, step, size, width), lambda i: (0, 0, i, 0, 0))
     half = pl.BlockSpec((2, 1, step, size, width), lambda i: (0, 0, i, 0, 0))
     return pl.pallas_call(
         both_kernel,
-        grid=(4,),
+        grid=(2,),
         in_specs=[spec, half, half],
         out_specs=pl.BlockSpec((step, 2, count, size, width), lambda i: (i, 0, 0, 0, 0)),
         out_shape=struct((parts, 2, count, size, width), BF16),

time: 511 us -> 511 us (level)
  no operation moved by 1% of the time
where the time goes in v5:
time: 511 us; the launch traced here: 503 us
  Pallas kernels  260 us (51%)
  waiting for transfers between devices  105 us (21%)
  starting transfers between devices  44.6 us (9%)
  local copies, waits for them, and re-layouts  43.1 us (8%)
  blocking collectives  28.9 us (6%)
  between operations  16.4 us (3%)
  other arithmetic  5.3 us (1%)
    pallas_call x32, Pallas kernels, call(): pl.pallas_call(body, in_specs=[PLACED if n in placed else WHOLE for n in...  184 us
    ppermute x44, waiting for transfers between devices, over(): return lax.ppermute(block, axis, [(i, move(i)) for i in range(count)])  88 us
    ppermute x44, starting transfers between devices, over(): return lax.ppermute(block, axis, [(i, move(i)) for i in range(count)])  36.5 us
    pallas_call x2, Pallas kernels, attend_back(): pl.pallas_call(attend_back_kernel, grid=(pairs,), in_specs=[block, key, k...  35.6 us
    unnamed x126, local copies, waits for them, and re-layouts  35.3 us
    pallas_call x2, Pallas kernels, attend(): pl.pallas_call(attend_kernel, grid_spec=pltpu.PrefetchScalarGridSpec(num_...  34.7 us
    all_gather x1, blocking collectives, gather_along(): return lax.all_gather(block, 'dp', axis=0, axis_index_groups=ALONG)  28.9 us
    all_gather x2, waiting for transfers between devices, local(): lax.all_gather(item, ('dp', 'section'), axis=0, tiled=False)  10.7 us
  transfers between devices with their start and end apart: 55, of which 15 were waited for; matrix products, arithmetic and copies ran while one was open for 2% of the time, Pallas kernels for 42%

profile of v5, /device:TPU:0, one launch (start us, length us, event | category | flops | bytes accessed | tf_op | source)
XLA Modules:
  0.0 503.4 jit_solution(14300360223595728089)
XLA Ops:
  7.2 3.1 shard_map.254
  11.2 28.9 %all-gather = bf16[512,768]{1,0:T(8,128)(2,1)} all-gather(bf16[128,768]{1,0:T(8,128)(2,1)} %get-tuple-element.523), channel_id=2, replica_groups={{0,8,16,24},{4,12,20,28},{1,9,17,25},{5,13,21,29},{2,10,18,26},{6,14,22..., dimensions={0}, use_global_device_ids=true | all-gather | bytes 983040 | tf_op jit(solution)/shard_map/all_gather | solution.py:561
  40.1 2.0 shard_map.255
  42.1 1.5 collective-permute-start
  47.0 2.6 dynamic-slice_bitcast_fusion
  50.1 1.5 collective-permute-done.1.right_got
  52.3 2.6 shard_map.256
  57.1 2.4 shard_map.257
  62.2 15.5 %collective-permute-done.2.x_got = bf16[8,1,128,384]{3,2,1,0:T(8,128)(2,1)S(1)} collective-permute-done((bf16[8,1,128,384]{3,2,1,0:T(8,128)(2,1)}, bf16[8,1,128,384]{3,2,1,0:T(8,128)(2,1)S(1)}, u32[]{:S(2)}, u32[]{:S(2)}) %collective-permute-start.2) | collective-permute-done | bytes 786464 | tf_op jit(solution)/shard_map/ppermute | solution.py:538
  80.0 3.5 shard_map.258
  85.0 2.3 shard_map.259
  90.3 6.1 %shard_map.260 = (bf16[512,768]{1,0:T(8,128)(2,1)}, bf16[512,768]{1,0:T(8,128)(2,1)}, bf16[2,512,768]{2,1,0:T(8,128)(2,1)}) custom-call(bf16[512,768]{1,0:T(8,128)(2,1)} %get-tuple-element.866.h_ref, f32[16,768]{1,0:T(8,128)} %get-tuple-element.872.vec_ref, bf16[1,2,8,96,768]{4,3,2,1,0:T(8,128)(2,1)} %get-tuple-element.873.refs_0_.refs_4_, ...), custom_call_target="tpu_custom_call" | custom-call | flops 1342177280 | bytes 65536 | tf_op jit(solution)/shard_map/pallas_call | solution.py:43
  97.3 2.4 shard_map.261
  103.3 17.2 %shard_map.262 = (bf16[512,768]{1,0:T(8,128)(2,1)S(1)}, bf16[12,1024,512]{2,1,0:T(8,128)(2,1)}, f32[512,768]{1,0:T(8,128)S(1)}) custom-call(s32[2]{0:T(128)S(1)} %pad_add_fusion.lens_ref, bf16[512,768]{1,0:T(8,128)(2,1)S(1)} %copy-done.10, bf16[2,512,768]{2,1,0:T(8,128)(2,1)S(1)} %copy-done.6, bf16[2,512,768]{2,1,0:T(8,128)(2,1)} %copy-done.19, ...), custom_call_target="tpu_custom_call" | custom-call | flops 4294967296 | bytes 65536 | tf_op jit(solution)/shard_map/pallas_call | solution.py:103
  124.3 3.2 shard_map.263.refs_0_
  127.6 4.4 shard_map.264.h_ref
  132.8 3.3 shard_map.265.refs_0_.refs_2_
  138.0 9.4 %shard_map.266 = (bf16[512,768]{1,0:T(8,128)(2,1)}, bf16[4,512,768]{2,1,0:T(8,128)(2,1)}, bf16[4,512,768]{2,1,0:T(8,128)(2,1)}) custom-call(bf16[512,768]{1,0:T(8,128)(2,1)} %shard_map.264.h_ref, f32[16,768]{1,0:T(8,128)} %get-tuple-element.872.vec_ref, bf16[1,2,8,96,768]{4,3,2,1,0:T(8,128)(2,1)} %shard_map.263.refs_0_, bf16[1,2,8,96,768]{4,3,2,1,0:T(8,128)(2,1)} %copy-done.22), custom_call_target="tpu_custom_call" | custom-call | flops 2415919104 | bytes 65536 | tf_op jit(solution)/shard_map/pallas_call | solution.py:43
  148.8 9.0 %shard_map.267.h_ref = bf16[512,768]{1,0:T(8,128)(2,1)} custom-call(bf16[512,768]{1,0:T(8,128)(2,1)} %shard_map.264.h_ref, bf16[4,512,768]{2,1,0:T(8,128)(2,1)} %get-tuple-element.778.g_hbm, f32[16,768]{1,0:T(8,128)} %get-tuple-element.872.vec_ref, bf16[1,2,8,96,768]{4,3,2,1,0:T(8,128)(2,1)} %shard_map.265.refs_0_.refs_2_, bf16[1,2,8,96,768]{4,3,2,1,0:T(8,128)(2,1)} %copy-done.18), custom_call_target="tpu_custom_call" | custom-call | flops 1610612736 | bytes 65536 | tf_op jit(solution)/shard_map/pallas_call | solution.py:43
  157.8 6.1 %shard_map.268 = (bf16[512,768]{1,0:T(8,128)(2,1)}, bf16[512,768]{1,0:T(8,128)(2,1)}, bf16[2,512,768]{2,1,0:T(8,128)(2,1)}) custom-call(bf16[512,768]{1,0:T(8,128)(2,1)} %shard_map.267.h_ref, f32[16,768]{1,0:T(8,128)} %get-tuple-element.754.vec_ref, bf16[8,4,2,96,768]{4,3,2,1,0:T(8,128)(2,1)} %bitcast.56), custom_call_target="tpu_custom_call" | custom-call | flops 1342177280 | bytes 65536 | tf_op jit(solution)/shard_map/pallas_call | solution.py:43
  164.0 3.6 collective-permute-done.16.kp_ref.vp_ref
  171.4 17.5 %shard_map.269 = (bf16[512,768]{1,0:T(8,128)(2,1)S(1)}, bf16[12,1024,512]{2,1,0:T(8,128)(2,1)}, f32[512,768]{1,0:T(8,128)S(1)}) custom-call(s32[2]{0:T(128)S(1)} %pad_add_fusion.lens_ref, bf16[512,768]{1,0:T(8,128)(2,1)S(1)} %copy-done.12, bf16[2,512,768]{2,1,0:T(8,128)(2,1)S(1)} %copy-done.7, bf16[2,512,768]{2,1,0:T(8,128)(2,1)} %copy-done.20, ...), custom_call_target="tpu_custom_call" | custom-call | flops 4294967296 | bytes 65536 | tf_op jit(solution)/shard_map/pallas_call | solution.py:103
  191.0 4.3 shard_map.270.h_ref
  195.3 9.7 %shard_map.271 = (bf16[512,768]{1,0:T(8,128)(2,1)}, bf16[4,512,768]{2,1,0:T(8,128)(2,1)}, bf16[4,512,768]{2,1,0:T(8,128)(2,1)}) custom-call(bf16[512,768]{1,0:T(8,128)(2,1)} %shard_map.270.h_ref, f32[16,768]{1,0:T(8,128)} %get-tuple-element.754.vec_ref, bf16[8,4,2,96,768]{4,3,2,1,0:T(8,128)(2,1)} %bitcast.58), custom_call_target="tpu_custom_call" | custom-call | flops 2415919104 | bytes 65536 | tf_op jit(solution)/shard_map/pallas_call | solution.py:43
  205.0 10.7 %all-gather.17.cloned.1.call-done = bf16[32,96,768]{2,1,0:T(8,128)(2,1)} async-done(((bf16[1,96,768]{2,1,0:T(8,128)(2,1)}), bf16[32,96,768]{2,1,0:T(8,128)(2,1)}) %all-gather.17.cloned.1.call-update) | async-done | bytes 4718608 | tf_op jit(solution)/shard_map/all_gather | solution.py:956
  215.7 8.9 %shard_map.272 = bf16[512,768]{1,0:T(8,128)(2,1)} custom-call(bf16[512,768]{1,0:T(8,128)(2,1)} %shard_map.270.h_ref, bf16[4,512,768]{2,1,0:T(8,128)(2,1)} %get-tuple-element.705.g_hbm, f32[16,768]{1,0:T(8,128)} %get-tuple-element.754.vec_ref, bf16[8,4,1,96,768]{4,3,2,1,0:T(8,128)(2,1)} %bitcast.62), custom_call_target="tpu_custom_call" | custom-call | flops 1610612736 | bytes 65536 | tf_op jit(solution)/shard_map/pallas_call | solution.py:43
  224.6 20.3 %shard_map.273 = (bf16[512,768]{1,0:T(8,128)(2,1)}, bf16[512,768]{1,0:T(8,128)(2,1)}, bf16[2,2,8,96,768]{4,3,2,1,0:T(8,128)(2,1)}, bf16[2,1,8,96,768]{4,3,2,1,0:...) custom-call(bf16[512,768]{1,0:T(8,128)(2,1)} %get-tuple-element.702.gy_ref, ...), custom_call_target="tpu_custom_call" | custom-call | flops 5368709120 | bytes 65536 | tf_op jit(solution)/shard_map/pallas_call | solution.py:43
  246.7 17.8 %shard_map.274 = (bf16[512,768]{1,0:T(8,128)(2,1)S(1)}, f32[2,512,768]{2,1,0:T(8,128)}, bf16[2,512,768]{2,1,0:T(8,128)(2,1)}) custom-call(bf16[512,768]{1,0:T(8,128)(2,1)S(1)} %copy-done.13, bf16[2,512,768]{2,1,0:T(8,128)(2,1)} %get-tuple-element.725.ko_ref.vo_ref, bf16[2,512,768]{2,1,0:T(8,128)(2,1)} %copy-done.20, ...), custom_call_target="tpu_custom_call" | custom-call | flops 4294967296 | bytes 65536 | tf_op jit(solution)/shard_map/pallas_call | solution.py:166
  265.6 5.7 %shard_map.275 = bf16[8,2,2,96,768]{4,3,2,1,0:T(8,128)(2,1)} custom-call(bf16[2,2,8,96,768]{4,3,2,1,0:T(8,128)(2,1)} %get-tuple-element.742.keep_ref, bf16[2,1,8,96,768]{4,3,2,1,0:T(8,128)(2,1)} %collective-permute-done.18.up_ref, bf16[2,1,8,96,768]{4,3,2,1,0:T(8,128)(2,1)} %collective-permute-done.19.down_ref), custom_call_target="tpu_custom_call" | custom-call | flops 21474836480 | bytes 65536 | tf_op jit(solution)/shard_map/pallas_call | solution.py:758
  272.5 10.9 %shard_map.276 = (bf16[512,768]{1,0:T(8,128)(2,1)}, bf16[2,1,8,96,768]{4,3,2,1,0:T(8,128)(2,1)}, bf16[2,1,8,96,768]{4,3,2,1,0:T(8,128)(2,1)}, f32[8,768]{1,0:T(8,128)}) custom-call(bf16[512,768]{1,0:T(8,128)(2,1)} %get-tuple-element.747.gy_ref, bf16[512,768]{1,0:T(8,128)(2,1)} %shard_map.267.h_ref, bf16[512,768]{1,0:T(8,128)(2,1)} %get-tuple-element.749.a_ref, ...), custom_call_target="tpu_custom_call" | custom-call | flops 2684354560 | bytes 65536 | tf_op jit(solution)/shard_map/pallas_call | solution.py:43
  284.1 4.0 collective-permute-done.20.refs_0_
  289.6 4.0 shard_map.277
  293.5 1.6 collective-permute-start.23
  295.9 19.1 %shard_map.278 = (bf16[512,768]{1,0:T(8,128)(2,1)}, bf16[512,768]{1,0:T(8,128)(2,1)}, bf16[2,2,8,96,768]{4,3,2,1,0:T(8,128)(2,1)}, bf16[2,1,8,96,768]{4,3,2,1,0:...) custom-call(bf16[512,768]{1,0:T(8,128)(2,1)} %get-tuple-element.775.gy_ref, ...), custom_call_target="tpu_custom_call" | custom-call | flops 5368709120 | bytes 65536 | tf_op jit(solution)/shard_map/pallas_call | solution.py:43
  317.3 2.9 shard_map.279
  320.3 3.0 collective-permute-done.22.refs_1_
  324.7 6.5 %shard_map.280 = (bf16[2,8,96,384]{3,2,1,0:T(8,128)(2,1)}, bf16[2,2,4,96,384]{4,3,2,1,0:T(8,128)(2,1)}, bf16[2,8,96,384]{3,2,1,0:T(8,128)(2,1)}, bf16[2,2,4,96,384]{4,3,2,1,0:T(8,128)(2,1)}) custom-call(bf16[2,2,8,96,768]{4,3,2,1,0:T(8,128)(2,1)} %get-tuple-element.817.keep_ref, bf16[2,1,8,96,768]{4,3,2,1,0:T(8,128)(2,1)} %copy-done.23, ...), custom_call_target="tpu_custom_call" | custom-call | flops 1342177280 | bytes 65536 | tf_op jit(solution)/shard_map/pallas_call | solution.py:43
  332.8 1.6 collective-permute-start.26
  335.2 17.9 %shard_map.281 = (bf16[512,768]{1,0:T(8,128)(2,1)S(1)}, f32[2,512,768]{2,1,0:T(8,128)}, bf16[2,512,768]{2,1,0:T(8,128)(2,1)}) custom-call(bf16[512,768]{1,0:T(8,128)(2,1)S(1)} %copy-done.10, bf16[2,512,768]{2,1,0:T(8,128)(2,1)} %get-tuple-element.827.ko_ref.vo_ref, bf16[2,512,768]{2,1,0:T(8,128)(2,1)} %copy-done.19, ...), custom_call_target="tpu_custom_call" | custom-call | flops 4294967296 | bytes 65536 | tf_op jit(solution)/shard_map/pallas_call | solution.py:166
  353.1 7.0 %collective-permute-done.28.x_got = bf16[2,8,96,384]{3,2,1,0:T(8,128)(2,1)S(1)} collective-permute-done((bf16[2,8,96,384]{3,2,1,0:T(8,128)(2,1)}, bf16[2,8,96,384]{3,2,1,0:T(8,128)(2,1)S(1)}, u32[]{:S(2)}, u32[]{:S(2)}) %collective-permute-start.28) | collective-permute-done | bytes 1179680 | tf_op jit(solution)/shard_map/ppermute | solution.py:538
  360.1 10.1 %collective-permute-done.29.y_got = bf16[2,2,4,96,384]{4,3,2,1,0:T(8,128)(2,1)S(1)} collective-permute-done((bf16[2,2,4,96,384]{4,3,2,1,0:T(8,128)(2,1)}, bf16[2,2,4,96,384]{4,3,2,1,0:T(8,128)(2,1)S(1)}, u32[]{:S(2)}, u32[]{:S(2)}) %collective-permute-start.29) | collective-permute-done | bytes 1179680 | tf_op jit(solution)/shard_map/ppermute | solution.py:538
  371.4 4.1 shard_map.282
  375.9 1.6 collective-permute-start.32
  377.5 2.9 collective-permute-done.26.y_got
  381.9 2.2 shard_map.283
  385.3 12.5 %shard_map.284 = (bf16[512,768]{1,0:T(8,128)(2,1)}, bf16[2,1,8,96,768]{4,3,2,1,0:T(8,128)(2,1)}, bf16[2,1,8,96,768]{4,3,2,1,0:T(8,128)(2,1)}, f32[8,768]{1,0:T(8,128)}) custom-call(bf16[512,768]{1,0:T(8,128)(2,1)} %get-tuple-element.865.gy_ref, bf16[512,768]{1,0:T(8,128)(2,1)} %get-tuple-element.866.h_ref, bf16[512,768]{1,0:T(8,128)(2,1)} %get-tuple-element.867.a_ref, ...), custom_call_target="tpu_custom_call" | custom-call | flops 2684354560 | bytes 65536 | tf_op jit(solution)/shard_map/pallas_call | solution.py:43
  399.8 2.9 shard_map.285
  404.1 3.9 shard_map.286
  412.2 18.1 %collective-permute-done.33.x_got = bf16[1,8,96,384]{3,2,1,0:T(8,128)(2,1)S(1)} collective-permute-done((bf16[1,8,96,384]{3,2,1,0:T(8,128)(2,1)}, bf16[1,8,96,384]{3,2,1,0:T(8,128)(2,1)S(1)}, u32[]{:S(2)}, u32[]{:S(2)}) %collective-permute-start.33) | collective-permute-done | bytes 589856 | tf_op jit(solution)/shard_map/ppermute | solution.py:538
  431.1 2.7 shard_map.287
  434.2 1.7 pad_maximum_fusion.2
  436.4 1.7 collective-permute-start.38
  438.1 3.6 all-to-all-start
  442.4 3.1 collective-permute-start.36
  445.6 2.1 shard_map.288
  447.7 2.9 collective-permute-start.40
  451.5 2.2 collective-permute-start.42
  453.8 4.7 collective-permute-done.40.o1
  458.4 8.2 %collective-permute-done.41.o2 = bf16[1,96,768]{2,1,0:T(8,128)(2,1)S(1)} collective-permute-done((bf16[1,96,768]{2,1,0:T(8,128)(2,1)}, bf16[1,96,768]{2,1,0:T(8,128)(2,1)S(1)}, u32[]{:S(2)}, u32[]{:S(2)}) %collective-permute-start.41) | collective-permute-done | bytes 147488 | tf_op jit(solution)/shard_map/ppermute | solution.py:538
  467.9 1.9 shard_map.289.a0
  469.8 1.5 collective-permute-start.44
  471.3 8.8 %collective-permute-done.44.a2 = bf16[1,96,768]{2,1,0:T(8,128)(2,1)S(1)} collective-permute-done((bf16[1,96,768]{2,1,0:T(8,128)(2,1)}, bf16[1,96,768]{2,1,0:T(8,128)(2,1)S(1)}, u32[]{:S(2)}, u32[]{:S(2)}) %collective-permute-start.44) | collective-permute-done | bytes 147488 | tf_op jit(solution)/shard_map/ppermute | solution.py:538
  483.6 5.7 %all-gather.11.cloned.1.call-done.f1_ref = bf16[4,2,96,768]{3,2,1,0:T(8,128)(2,1)} async-done(((bf16[1,2,96,768]{3,2,1,0:T(8,128)(2,1)}), bf16[4,2,96,768]{3,2,1,0:T(8,128)(2,1)}) %all-gather.11.cloned.1.call-update) | async-done | bytes 1179664 | tf_op jit(solution)/shard_map/all_gather | solution.py:1132
  489.2 5.2 %shard_map.290 = (f32[2,96,2304]{2,1,0:T(8,128)}, f32[2,96,768]{2,1,0:T(8,128)}, f32[2,96,3072]{2,1,0:T(8,128)}, f32[2,384,768]{2,1,0:T(8,128)}) custom-call(bf16[1,96,768]{2,1,0:T(8,128)(2,1)} %shard_map.289.a0, bf16[1,96,768]{2,1,0:T(8,128)(2,1)} %copy-done.56, bf16[1,96,768]{2,1,0:T(8,128)(2,1)} %copy-done.55, bf16[1,96,768]{2,1,0:T(8,128)(2,1)} %copy-done.57, ...), custom_call_target="tpu_custom_call" | custom-call | flops 1342177280 | bytes 65536 | tf_op jit(solution)/shard_map/pallas_call | solution.py:43
  (253 shorter events, 69.0 us)
Async XLA Ops:
  7.2 37.8 %copy-start = (s32[2,1]{0,1:T(1,128)S(1)}, s32[2,1]{0,1:T(1,128)}, u32[]{:S(2)}) copy-start(s32[2,1]{0,1:T(1,128)} %param.16) | copy-start | bytes 28
  7.2 49.9 %all-gather.13.cloned.1.call-start = ((), (), s32[]{:S(2)}) async-start(), calls=%async_computation.8 | async-start | bytes 1474560 | tf_op jit(solution)/shard_map/all_gather | solution.py:561
  10.4 147.5 %all-gather.15.cloned.1.call-start = ((), (), s32[]{:S(2)}) async-start(), calls=%async_computation.9 | async-start | bytes 9732096 | tf_op jit(solution)/shard_map/all_gather | solution.py:956
  11.1 204.6 %all-gather.17.cloned.1.call-start = ((), (), s32[]{:S(2)}) async-start(), calls=%async_computation.10 | async-start | bytes 4866048 | tf_op jit(solution)/shard_map/all_gather | solution.py:956
  42.1 8.0 %collective-permute-start = (bf16[4,1,128,384]{3,2,1,0:T(8,128)(2,1)}, bf16[4,1,128,384]{3,2,1,0:T(8,128)(2,1)S(1)}, u32[]{:S(2)}, u32[]{:S(2)}) collective-permute-start(bf16[4,1,128,384]{3,2,1,0:T(8,128)(2,1)} %get-tuple-element.538.left_ref), channel_id=1, source_target_pairs={{0,4},{4,0},{8,12},{12,8},{16,20},{20,16},{24,28},{28,24},{1,5},{5... | collective-permute-start | bytes 1179656 | tf_op jit(solution)/shard_map/ppermute | solution.py:538
  43.6 8.0 %collective-permute-start.1 = (bf16[4,1,128,384]{3,2,1,0:T(8,128)(2,1)}, bf16[4,1,128,384]{3,2,1,0:T(8,128)(2,1)S(1)}, u32[]{:S(2)}, u32[]{:S(2)}) collective-permute-start(bf16[4,1,128,384]{3,2,1,0:T(8,128)(2,1)} %get-tuple-element.540.right_ref), channel_id=1, source_target_pairs={{0,2},{1,3},{2,0},{3,1},{4,6},{5,7},{6,4},{7,5},{8,10},{9,11},{10,... | collective-permute-start | bytes 1179656 | tf_op jit(solution)/shard_map/ppermute | solution.py:538
  54.9 22.8 %collective-permute-start.2 = (bf16[8,1,128,384]{3,2,1,0:T(8,128)(2,1)}, bf16[8,1,128,384]{3,2,1,0:T(8,128)(2,1)S(1)}, u32[]{:S(2)}, u32[]{:S(2)}) collective-permute-start(bf16[8,1,128,384]{3,2,1,0:T(8,128)(2,1)} %get-tuple-element.556.x_ref), channel_id=1, source_target_pairs={{0,2},{1,3},{2,0},{3,1},{4,6},{5,7},{6,4},{7,5},{8,10},{9,11},{10,... | collective-permute-start | bytes 2359304 | tf_op jit(solution)/shard_map/ppermute | solution.py:538
  56.3 22.8 %collective-permute-start.3 = (bf16[2,4,1,128,384]{4,3,2,1,0:T(8,128)(2,1)}, bf16[2,4,1,128,384]{4,3,2,1,0:T(8,128)(2,1)S(1)}, u32[]{:S(2)}, u32[]{:S(2)}) collective-permute-start(bf16[2,4,1,128,384]{4,3,2,1,0:T(8,128)(2,1)} %get-tuple-element.558.y_ref), channel_id=1, source_target_pairs={{0,4},{4,0},{8,12},{12,8},{16,20},{20,16},{24,28},{28,24},{1,5},{5... | collective-permute-start | bytes 2359304 | tf_op jit(solution)/shard_map/ppermute | solution.py:538
  59.5 24.1 %collective-permute-start.5 = (bf16[4,1,96,384]{3,2,1,0:T(8,128)(2,1)}, bf16[4,1,96,384]{3,2,1,0:T(8,128)(2,1)S(1)}, u32[]{:S(2)}, u32[]{:S(2)}) collective-permute-start(bf16[4,1,96,384]{3,2,1,0:T(8,128)(2,1)} %get-tuple-element.569.left_ref), channel_id=1, source_target_pairs={{0,4},{4,0},{8,12},{12,8},{16,20},{20,16},{24,28},{28,24},{1,5},{5... | collective-permute-start | bytes 884744 | tf_op jit(solution)/shard_map/ppermute | solution.py:538
  60.7 22.9 %collective-permute-start.6 = (bf16[4,1,96,384]{3,2,1,0:T(8,128)(2,1)}, bf16[4,1,96,384]{3,2,1,0:T(8,128)(2,1)S(1)}, u32[]{:S(2)}, u32[]{:S(2)}) collective-permute-start(bf16[4,1,96,384]{3,2,1,0:T(8,128)(2,1)} %get-tuple-element.571.right_ref), channel_id=1, source_target_pairs={{0,2},{1,3},{2,0},{3,1},{4,6},{5,7},{6,4},{7,5},{8,10},{9,11},{10,... | collective-permute-start | bytes 884744 | tf_op jit(solution)/shard_map/ppermute | solution.py:538
  61.3 336.6 %reduce-scatter.4.cloned.1.call-start = ((), (), s32[]{:S(2)}) async-start(), calls=%async_computation.4 | async-start | bytes 5308416 | tf_op jit(solution)/shard_map/reduce_scatter | solution.py:770
  61.4 35.1 %collective-permute-start.8 = (bf16[4,1,96,384]{3,2,1,0:T(8,128)(2,1)}, bf16[4,1,96,384]{3,2,1,0:T(8,128)(2,1)S(1)}, u32[]{:S(2)}, u32[]{:S(2)}) collective-permute-start(bf16[4,1,96,384]{3,2,1,0:T(8,128)(2,1)} %get-tuple-element.591.left_ref), channel_id=1, source_target_pairs={{0,4},{4,0},{8,12},{12,8},{16,20},{20,16},{24,28},{28,24},{1,5},{5... | collective-permute-start | bytes 884744 | tf_op jit(solution)/shard_map/ppermute | solution.py:538
  77.7 18.8 %collective-permute-start.9 = (bf16[4,1,96,384]{3,2,1,0:T(8,128)(2,1)}, bf16[4,1,96,384]{3,2,1,0:T(8,128)(2,1)S(1)}, u32[]{:S(2)}, u32[]{:S(2)}) collective-permute-start(bf16[4,1,96,384]{3,2,1,0:T(8,128)(2,1)} %get-tuple-element.593.right_ref), channel_id=1, source_target_pairs={{0,2},{1,3},{2,0},{3,1},{4,6},{5,7},{6,4},{7,5},{8,10},{9,11},{10,... | collective-permute-start | bytes 884744 | tf_op jit(solution)/shard_map/ppermute | solution.py:538
  83.6 5.3 %collective-permute-start.4 = (bf16[1,2,8,96,768]{4,3,2,1,0:T(8,128)(2,1)}, bf16[1,2,8,96,768]{4,3,2,1,0:T(8,128)(2,1)S(1)}, u32[]{:S(2)}, u32[]{:S(2)}) collective-permute-start(bf16[1,2,8,96,768]{4,3,2,1,0:T(8,128)(2,1)} %get-tuple-element.873.refs_0_.refs_4_), channel_id=1, source_target_pairs={{0,1},{1,0},{2,3},{3,2},{4,5},{5,4},{6,7},{7,6},{8,9},{9,8},{10,11... | collective-permute-start | bytes 7077896 | tf_op jit(solution)/shard_map/ppermute | solution.py:538
  87.3 35.4 %collective-permute-start.10 = (bf16[8,1,96,384]{3,2,1,0:T(8,128)(2,1)}, bf16[8,1,96,384]{3,2,1,0:T(8,128)(2,1)S(1)}, u32[]{:S(2)}, u32[]{:S(2)}) collective-permute-start(bf16[8,1,96,384]{3,2,1,0:T(8,128)(2,1)} %get-tuple-element.611.x_ref), channel_id=1, source_target_pairs={{0,2},{1,3},{2,0},{3,1},{4,6},{5,7},{6,4},{7,5},{8,10},{9,11},{10,... | collective-permute-start | bytes 1769480 | tf_op jit(solution)/shard_map/ppermute | solution.py:538
  88.1 34.5 %collective-permute-start.11 = (bf16[2,4,1,96,384]{4,3,2,1,0:T(8,128)(2,1)}, bf16[2,4,1,96,384]{4,3,2,1,0:T(8,128)(2,1)S(1)}, u32[]{:S(2)}, u32[]{:S(2)}) collective-permute-start(bf16[2,4,1,96,384]{4,3,2,1,0:T(8,128)(2,1)} %get-tuple-element.613.y_ref), channel_id=1, source_target_pairs={{0,4},{4,0},{8,12},{12,8},{16,20},{20,16},{24,28},{28,24},{1,5},{5... | collective-permute-start | bytes 1769480 | tf_op jit(solution)/shard_map/ppermute | solution.py:538
  96.5 5.7 %collective-permute-start.7 = (bf16[2,512,768]{2,1,0:T(8,128)(2,1)}, bf16[2,512,768]{2,1,0:T(8,128)(2,1)S(1)}, u32[]{:S(2)}, u32[]{:S(2)}) collective-permute-start(bf16[2,512,768]{2,1,0:T(8,128)(2,1)} %get-tuple-element.827.ko_ref.vo_ref), channel_id=1, source_target_pairs={{0,1},{1,0},{2,3},{3,2},{4,5},{5,4},{6,7},{7,6},{8,9},{9,8},{10,11... | collective-permute-start | bytes 4718600 | tf_op jit(solution)/shard_map/ppermute | solution.py:538
  99.7 32.3 %collective-permute-start.13 = (bf16[8,1,96,384]{3,2,1,0:T(8,128)(2,1)}, bf16[8,1,96,384]{3,2,1,0:T(8,128)(2,1)S(1)}, u32[]{:S(2)}, u32[]{:S(2)}) collective-permute-start(bf16[8,1,96,384]{3,2,1,0:T(8,128)(2,1)} %get-tuple-element.628.x_ref), channel_id=1, source_target_pairs={{0,2},{1,3},{2,0},{3,1},{4,6},{5,7},{6,4},{7,5},{8,10},{9,11},{10,... | collective-permute-start | bytes 1769480 | tf_op jit(solution)/shard_map/ppermute | solution.py:538
  100.9 31.1 %collective-permute-start.14 = (bf16[2,4,1,96,384]{4,3,2,1,0:T(8,128)(2,1)}, bf16[2,4,1,96,384]{4,3,2,1,0:T(8,128)(2,1)}, u32[]{:S(2)}, u32[]{:S(2)}) collective-permute-start(bf16[2,4,1,96,384]{4,3,2,1,0:T(8,128)(2,1)} %get-tuple-element.630.y_ref), channel_id=1, source_target_pairs={{0,4},{4,0},{8,12},{12,8},{16,20},{20,16},{24,28},{28,24},{1,5},{5... | collective-permute-start | bytes 1769480 | tf_op jit(solution)/shard_map/ppermute | solution.py:538
  127.6 9.0 %collective-permute-start.12 = (bf16[1,2,8,96,768]{4,3,2,1,0:T(8,128)(2,1)}, bf16[1,2,8,96,768]{4,3,2,1,0:T(8,128)(2,1)S(1)}, u32[]{:S(2)}, u32[]{:S(2)}) collective-permute-start(bf16[1,2,8,96,768]{4,3,2,1,0:T(8,128)(2,1)} %shard_map.263.refs_0_), channel_id=1, source_target_pairs={{0,1},{1,0},{2,3},{3,2},{4,5},{5,4},{6,7},{7,6},{8,9},{9,8},{10,11... | collective-permute-start | bytes 7077896 | tf_op jit(solution)/shard_map/ppermute | solution.py:538
  136.1 11.3 %collective-permute-start.15 = (bf16[1,2,8,96,768]{4,3,2,1,0:T(8,128)(2,1)}, bf16[1,2,8,96,768]{4,3,2,1,0:T(8,128)(2,1)S(1)}, u32[]{:S(2)}, u32[]{:S(2)}) collective-permute-start(bf16[1,2,8,96,768]{4,3,2,1,0:T(8,128)(2,1)} %shard_map.265.refs_0_.refs_2_), channel_id=1, source_target_pairs={{0,1},{1,0},{2,3},{3,2},{4,5},{5,4},{6,7},{7,6},{8,9},{9,8},{10,11... | collective-permute-start | bytes 7077896 | tf_op jit(solution)/shard_map/ppermute | solution.py:538
  164.0 3.7 collective-permute-start.16
  224.6 20.9 %copy-start.3 = (bf16[512,768]{1,0:T(8,128)(2,1)S(1)}, bf16[512,768]{1,0:T(8,128)(2,1)}, u32[]{:S(2)}) copy-start(bf16[512,768]{1,0:T(8,128)(2,1)} %copy-done.2) | copy-start | bytes 2359300
  224.6 20.9 %copy-start.13 = (bf16[512,768]{1,0:T(8,128)(2,1)S(1)}, bf16[512,768]{1,0:T(8,128)(2,1)}, u32[]{:S(2)}) copy-start(bf16[512,768]{1,0:T(8,128)(2,1)} %get-tuple-element.724.q_ref) | copy-start | bytes 2359300
  245.0 20.7 %collective-permute-start.18 = (bf16[2,1,8,96,768]{4,3,2,1,0:T(8,128)(2,1)}, bf16[2,1,8,96,768]{4,3,2,1,0:T(8,128)(2,1)}, u32[]{:S(2)}, u32[]{:S(2)}) collective-permute-start(bf16[2,1,8,96,768]{4,3,2,1,0:T(8,128)(2,1)} %get-tuple-element.739), channel_id=1, source_target_pairs={{0,1},{1,0},{2,3},{3,2},{4,5},{5,4},{6,7},{7,6},{8,9},{9,8},{10,11... | collective-permute-start | bytes 7077896 | tf_op jit(solution)/shard_map/ppermute | solution.py:538
  245.3 20.3 %collective-permute-start.19 = (bf16[2,1,8,96,768]{4,3,2,1,0:T(8,128)(2,1)}, bf16[2,1,8,96,768]{4,3,2,1,0:T(8,128)(2,1)}, u32[]{:S(2)}, u32[]{:S(2)}) collective-permute-start(bf16[2,1,8,96,768]{4,3,2,1,0:T(8,128)(2,1)} %get-tuple-element.740), channel_id=1, source_target_pairs={{0,1},{1,0},{2,3},{3,2},{4,5},{5,4},{6,7},{7,6},{8,9},{9,8},{10,11... | collective-permute-start | bytes 7077896 | tf_op jit(solution)/shard_map/ppermute | solution.py:538
  265.3 6.0 %collective-permute-start.17 = (bf16[2,512,768]{2,1,0:T(8,128)(2,1)}, bf16[2,512,768]{2,1,0:T(8,128)(2,1)S(1)}, u32[]{:S(2)}, u32[]{:S(2)}) collective-permute-start(bf16[2,512,768]{2,1,0:T(8,128)(2,1)} %get-tuple-element.737), channel_id=1, source_target_pairs={{0,1},{1,0},{2,3},{3,2},{4,5},{5,4},{6,7},{7,6},{8,9},{9,8},{10,11... | collective-permute-start | bytes 4718600 | tf_op jit(solution)/shard_map/ppermute | solution.py:538
  283.3 4.8 collective-permute-start.20
  283.7 150.5 %reduce-scatter.6.cloned.1.call-start = ((), (), s32[]{:S(2)}) async-start(), calls=%async_computation.5 | async-start | bytes 737280 | tf_op jit(solution)/shard_map/reduce_scatter | solution.py:861
  293.5 22.1 %collective-permute-start.23 = (bf16[1,8,96,384]{3,2,1,0:T(8,128)(2,1)}, bf16[1,8,96,384]{3,2,1,0:T(8,128)(2,1)S(1)}, u32[]{:S(2)}, u32[]{:S(2)}) collective-permute-start(bf16[1,8,96,384]{3,2,1,0:T(8,128)(2,1)} %get-tuple-element.803), channel_id=1, source_target_pairs={{0,2},{1,3},{2,0},{3,1},{4,6},{5,7},{6,4},{7,5},{8,10},{9,11},{10,... | collective-permute-start | bytes 1769480 | tf_op jit(solution)/shard_map/ppermute | solution.py:538
  295.2 20.5 %collective-permute-start.24 = (bf16[2,1,4,96,384]{4,3,2,1,0:T(8,128)(2,1)}, bf16[2,1,4,96,384]{4,3,2,1,0:T(8,128)(2,1)S(1)}, u32[]{:S(2)}, u32[]{:S(2)}) collective-permute-start(bf16[2,1,4,96,384]{4,3,2,1,0:T(8,128)(2,1)} %get-tuple-element.805), channel_id=1, source_target_pairs={{0,4},{4,0},{8,12},{12,8},{16,20},{20,16},{24,28},{28,24},{1,5},{5... | collective-permute-start | bytes 1769480 | tf_op jit(solution)/shard_map/ppermute | solution.py:538
  315.1 5.2 %collective-permute-start.21 = (bf16[2,1,8,96,768]{4,3,2,1,0:T(8,128)(2,1)}, bf16[2,1,8,96,768]{4,3,2,1,0:T(8,128)(2,1)S(1)}, u32[]{:S(2)}, u32[]{:S(2)}) collective-permute-start(bf16[2,1,8,96,768]{4,3,2,1,0:T(8,128)(2,1)} %get-tuple-element.800), channel_id=1, source_target_pairs={{0,1},{1,0},{2,3},{3,2},{4,5},{5,4},{6,7},{7,6},{8,9},{9,8},{10,11... | collective-permute-start | bytes 7077896 | tf_op jit(solution)/shard_map/ppermute | solution.py:538
  315.2 8.1 %collective-permute-start.22 = (bf16[2,1,8,96,768]{4,3,2,1,0:T(8,128)(2,1)}, bf16[2,1,8,96,768]{4,3,2,1,0:T(8,128)(2,1)S(1)}, u32[]{:S(2)}, u32[]{:S(2)}) collective-permute-start(bf16[2,1,8,96,768]{4,3,2,1,0:T(8,128)(2,1)} %get-tuple-element.801), channel_id=1, source_target_pairs={{0,1},{1,0},{2,3},{3,2},{4,5},{5,4},{6,7},{7,6},{8,9},{9,8},{10,11... | collective-permute-start | bytes 7077896 | tf_op jit(solution)/shard_map/ppermute | solution.py:538
  320.2 14.9 %copy-start.5 = (bf16[512,768]{1,0:T(8,128)(2,1)S(1)}, bf16[512,768]{1,0:T(8,128)(2,1)}, u32[]{:S(2)}) copy-start(bf16[512,768]{1,0:T(8,128)(2,1)} %copy-done.4) | copy-start | bytes 2359300
  320.2 14.9 %copy-start.11 = (bf16[512,768]{1,0:T(8,128)(2,1)S(1)}, bf16[512,768]{1,0:T(8,128)(2,1)}, u32[]{:S(2)}) copy-start(bf16[512,768]{1,0:T(8,128)(2,1)} %get-tuple-element.830.go_ref) | copy-start | bytes 2359300
  331.1 29.0 %collective-permute-start.28 = (bf16[2,8,96,384]{3,2,1,0:T(8,128)(2,1)}, bf16[2,8,96,384]{3,2,1,0:T(8,128)(2,1)S(1)}, u32[]{:S(2)}, u32[]{:S(2)}) collective-permute-start(bf16[2,8,96,384]{3,2,1,0:T(8,128)(2,1)} %get-tuple-element.845), channel_id=1, source_target_pairs={{0,2},{1,3},{2,0},{3,1},{4,6},{5,7},{6,4},{7,5},{8,10},{9,11},{10,... | collective-permute-start | bytes 3538952 | tf_op jit(solution)/shard_map/ppermute | solution.py:538
  332.4 37.9 %collective-permute-start.29 = (bf16[2,2,4,96,384]{4,3,2,1,0:T(8,128)(2,1)}, bf16[2,2,4,96,384]{4,3,2,1,0:T(8,128)(2,1)S(1)}, u32[]{:S(2)}, u32[]{:S(2)}) collective-permute-start(bf16[2,2,4,96,384]{4,3,2,1,0:T(8,128)(2,1)} %get-tuple-element.847), channel_id=1, source_target_pairs={{0,4},{4,0},{8,12},{12,8},{16,20},{20,16},{24,28},{28,24},{1,5},{5... | collective-permute-start | bytes 3538952 | tf_op jit(solution)/shard_map/ppermute | solution.py:538
  332.8 47.6 %collective-permute-start.26 = (bf16[1,4,96,384]{3,2,1,0:T(8,128)(2,1)}, bf16[1,4,96,384]{3,2,1,0:T(8,128)(2,1)S(1)}, u32[]{:S(2)}, u32[]{:S(2)}) collective-permute-start(bf16[1,4,96,384]{3,2,1,0:T(8,128)(2,1)} %get-tuple-element.841), channel_id=1, source_target_pairs={{0,4},{4,0},{8,12},{12,8},{16,20},{20,16},{24,28},{28,24},{1,5},{5... | collective-permute-start | bytes 884744 | tf_op jit(solution)/shard_map/ppermute | solution.py:538
  334.4 46.0 %collective-permute-start.27 = (bf16[1,4,96,384]{3,2,1,0:T(8,128)(2,1)}, bf16[1,4,96,384]{3,2,1,0:T(8,128)(2,1)S(1)}, u32[]{:S(2)}, u32[]{:S(2)}) collective-permute-start(bf16[1,4,96,384]{3,2,1,0:T(8,128)(2,1)} %get-tuple-element.843), channel_id=1, source_target_pairs={{0,2},{1,3},{2,0},{3,1},{4,6},{5,7},{6,4},{7,5},{8,10},{9,11},{10,... | collective-permute-start | bytes 884744 | tf_op jit(solution)/shard_map/ppermute | solution.py:538
  353.0 22.4 %copy-start.16 = (bf16[512,768]{1,0:T(8,128)(2,1)}, bf16[512,768]{1,0:T(8,128)(2,1)S(1)}, u32[]{:S(2)}) copy-start(bf16[512,768]{1,0:T(8,128)(2,1)S(1)} %get-tuple-element.869.gq_ref) | copy-start | bytes 2359300
  353.0 31.1 %collective-permute-start.25 = (bf16[2,512,768]{2,1,0:T(8,128)(2,1)}, bf16[2,512,768]{2,1,0:T(8,128)(2,1)S(1)}, u32[]{:S(2)}, u32[]{:S(2)}) collective-permute-start(bf16[2,512,768]{2,1,0:T(8,128)(2,1)} %get-tuple-element.839), channel_id=1, source_target_pairs={{0,1},{1,0},{2,3},{3,2},{4,5},{5,4},{6,7},{7,6},{8,9},{9,8},{10,11... | collective-permute-start | bytes 4718600 | tf_op jit(solution)/shard_map/ppermute | solution.py:538
  360.1 10.1 %copy-start.39 = (bf16[2,8,96,384]{3,2,1,0:T(8,128)(2,1)}, bf16[2,8,96,384]{3,2,1,0:T(8,128)(2,1)S(1)}, u32[]{:S(2)}) copy-start(bf16[2,8,96,384]{3,2,1,0:T(8,128)(2,1)S(1)} %collective-permute-done.28.x_got) | copy-start | bytes 3538948
  375.5 23.5 %collective-permute-start.31 = (bf16[2,4,96,384]{3,2,1,0:T(8,128)(2,1)}, bf16[2,4,96,384]{3,2,1,0:T(8,128)(2,1)S(1)}, u32[]{:S(2)}, u32[]{:S(2)}) collective-permute-start(bf16[2,4,96,384]{3,2,1,0:T(8,128)(2,1)} %get-tuple-element.884), channel_id=1, source_target_pairs={{0,4},{4,0},{8,12},{12,8},{16,20},{20,16},{24,28},{28,24},{1,5},{5... | collective-permute-start | bytes 1769480 | tf_op jit(solution)/shard_map/ppermute | solution.py:538
  375.9 23.1 %collective-permute-start.32 = (bf16[2,4,96,384]{3,2,1,0:T(8,128)(2,1)}, bf16[2,4,96,384]{3,2,1,0:T(8,128)(2,1)}, u32[]{:S(2)}, u32[]{:S(2)}) collective-permute-start(bf16[2,4,96,384]{3,2,1,0:T(8,128)(2,1)} %get-tuple-element.886), channel_id=1, source_target_pairs={{0,2},{1,3},{2,0},{3,1},{4,6},{5,7},{6,4},{7,5},{8,10},{9,11},{10,... | collective-permute-start | bytes 1769480 | tf_op jit(solution)/shard_map/ppermute | solution.py:538
  384.1 61.4 %reduce-scatter.8.cloned.1.call-start = ((), (), s32[]{:S(2)}) async-start(), calls=%async_computation.6 | async-start | bytes 1474560 | tf_op jit(solution)/shard_map/reduce_scatter | solution.py:861
  397.8 4.9 collective-permute-start.30
  408.2 26.0 %collective-permute-start.39 = (bf16[2,96,768]{2,1,0:T(8,128)(2,1)S(1)}, bf16[2,96,768]{2,1,0:T(8,128)(2,1)S(1)}, u32[]{:S(2)}, u32[]{:S(2)}) collective-permute-start(bf16[2,96,768]{2,1,0:T(8,128)(2,1)S(1)} %get-tuple-element.941), channel_id=1, source_target_pairs={{0,2},{1,3},{2,0},{3,1},{4,6},{5,7},{6,4},{7,5},{8,10},{9,11},{10,... | collective-permute-start | bytes 884744 | tf_op jit(solution)/shard_map/ppermute | solution.py:538
  409.7 20.6 %collective-permute-start.33 = (bf16[1,8,96,384]{3,2,1,0:T(8,128)(2,1)}, bf16[1,8,96,384]{3,2,1,0:T(8,128)(2,1)S(1)}, u32[]{:S(2)}, u32[]{:S(2)}) collective-permute-start(bf16[1,8,96,384]{3,2,1,0:T(8,128)(2,1)} %get-tuple-element.906), channel_id=1, source_target_pairs={{0,2},{1,3},{2,0},{3,1},{4,6},{5,7},{6,4},{7,5},{8,10},{9,11},{10,... | collective-permute-start | bytes 1769480 | tf_op jit(solution)/shard_map/ppermute | solution.py:538
  410.8 19.5 %collective-permute-start.34 = (bf16[2,1,4,96,384]{4,3,2,1,0:T(8,128)(2,1)}, bf16[2,1,4,96,384]{4,3,2,1,0:T(8,128)(2,1)}, u32[]{:S(2)}, u32[]{:S(2)}) collective-permute-start(bf16[2,1,4,96,384]{4,3,2,1,0:T(8,128)(2,1)} %get-tuple-element.908), channel_id=1, source_target_pairs={{0,4},{4,0},{8,12},{12,8},{16,20},{20,16},{24,28},{28,24},{1,5},{5... | collective-permute-start | bytes 1769480 | tf_op jit(solution)/shard_map/ppermute | solution.py:538
  412.1 21.7 %copy-start.21 = (bf16[512,768]{1,0:T(8,128)(2,1)S(1)}, bf16[512,768]{1,0:T(8,128)(2,1)}, u32[]{:S(2)}) copy-start(bf16[512,768]{1,0:T(8,128)(2,1)} %shard_map.272) | copy-start | bytes 2359300
  412.1 21.7 %copy-start.27 = (bf16[512,768]{1,0:T(8,128)(2,1)S(1)}, bf16[512,768]{1,0:T(8,128)(2,1)}, u32[]{:S(2)}) copy-start(bf16[512,768]{1,0:T(8,128)(2,1)} %get-tuple-element.931) | copy-start | bytes 2359300
  412.1 71.4 %all-gather.19.cloned.1.call-start = ((), (), s32[]{:S(2)}) async-start(), calls=%async_computation.11 | async-start | bytes 2211840 | tf_op jit(solution)/shard_map/all_gather | solution.py:1130
  436.0 9.6 %collective-permute-start.37 = (bf16[1,4,96,384]{3,2,1,0:T(8,128)(2,1)S(1)}, bf16[1,4,96,384]{3,2,1,0:T(8,128)(2,1)}, u32[]{:S(2)}, u32[]{:S(2)}) collective-permute-start(bf16[1,4,96,384]{3,2,1,0:T(8,128)(2,1)S(1)} %copy-done.48), channel_id=1, source_target_pairs={{0,4},{4,0},{8,12},{12,8},{16,20},{20,16},{24,28},{28,24},{1,5},{5... | collective-permute-start | bytes 884744 | tf_op jit(solution)/shard_map/ppermute | solution.py:538
  436.4 9.1 %collective-permute-start.38 = (bf16[1,4,96,384]{3,2,1,0:T(8,128)(2,1)S(1)}, bf16[1,4,96,384]{3,2,1,0:T(8,128)(2,1)}, u32[]{:S(2)}, u32[]{:S(2)}) collective-permute-start(bf16[1,4,96,384]{3,2,1,0:T(8,128)(2,1)S(1)} %copy-done.47), channel_id=1, source_target_pairs={{0,2},{1,3},{2,0},{3,1},{4,6},{5,7},{6,4},{7,5},{8,10},{9,11},{10,... | collective-permute-start | bytes 884744 | tf_op jit(solution)/shard_map/ppermute | solution.py:538
  438.1 33.2 %all-to-all-start = ((f32[32,2,16,96]{3,2,1,0:T(8,128)}), f32[32,2,16,96]{3,2,1,0:T(8,128)S(1)}, u32[]{:S(2)}, u32[]{:S(2)}) async-start(f32[32,2,16,96]{3,2,1,0:T(8,128)} %bitcast.19), calls=%async_computation.1 | async-start | bytes 1048576 | tf_op jit(solution)/shard_map/all_to_all | solution.py:1124
  441.7 47.6 %all-gather.11.cloned.1.call-start = ((), (), s32[]{:S(2)}) async-start(), calls=%async_computation.7 | async-start | bytes 1474560 | tf_op jit(solution)/shard_map/all_gather | solution.py:1132
  441.7 38.5 %collective-permute-start.35 = (bf16[2,256,768]{2,1,0:T(8,128)(2,1)S(1)}, bf16[2,256,768]{2,1,0:T(8,128)(2,1)S(1)}, u32[]{:S(2)}, u32[]{:S(2)}) collective-permute-start(bf16[2,256,768]{2,1,0:T(8,128)(2,1)S(1)} %get-tuple-element.933), channel_id=1, source_target_pairs={{0,0},{1,2},{2,1},{3,3},{4,4},{5,6},{6,5},{7,7},{8,8},{9,10},{10,9... | collective-permute-start | bytes 2359304 | tf_op jit(solution)/shard_map/ppermute | solution.py:1022
  442.4 37.8 %collective-permute-start.36 = (bf16[2,256,768]{2,1,0:T(8,128)(2,1)S(1)}, bf16[2,256,768]{2,1,0:T(8,128)(2,1)}, u32[]{:S(2)}, u32[]{:S(2)}) collective-permute-start(bf16[2,256,768]{2,1,0:T(8,128)(2,1)S(1)} %get-tuple-element.934), channel_id=1, source_target_pairs={{0,1},{1,3},{2,0},{3,2},{4,5},{5,7},{6,4},{7,6},{8,9},{9,11},{10,8... | collective-permute-start | bytes 2359304 | tf_op jit(solution)/shard_map/ppermute | solution.py:1022
  447.7 10.8 %collective-permute-start.40 = (bf16[1,96,768]{2,1,0:T(8,128)(2,1)}, bf16[1,96,768]{2,1,0:T(8,128)(2,1)S(1)}, u32[]{:S(2)}, u32[]{:S(2)}) collective-permute-start(bf16[1,96,768]{2,1,0:T(8,128)(2,1)} %get-tuple-element.959), channel_id=1, source_target_pairs={{0,8},{4,12},{8,16},{12,20},{16,24},{20,28},{24,0},{28,4},{1,9},{5... | collective-permute-start | bytes 442376 | tf_op jit(solution)/shard_map/ppermute | solution.py:538
  450.5 16.1 %collective-permute-start.41 = (bf16[1,96,768]{2,1,0:T(8,128)(2,1)}, bf16[1,96,768]{2,1,0:T(8,128)(2,1)S(1)}, u32[]{:S(2)}, u32[]{:S(2)}) collective-permute-start(bf16[1,96,768]{2,1,0:T(8,128)(2,1)} %get-tuple-element.960), channel_id=1, source_target_pairs={{0,16},{4,20},{8,24},{12,28},{16,0},{20,4},{24,8},{28,12},{1,17},{... | collective-permute-start | bytes 442376 | tf_op jit(solution)/shard_map/ppermute | solution.py:538
  451.5 15.1 %collective-permute-start.42 = (bf16[1,96,768]{2,1,0:T(8,128)(2,1)}, bf16[1,96,768]{2,1,0:T(8,128)(2,1)S(1)}, u32[]{:S(2)}, u32[]{:S(2)}) collective-permute-start(bf16[1,96,768]{2,1,0:T(8,128)(2,1)} %get-tuple-element.961), channel_id=1, source_target_pairs={{0,24},{4,28},{8,0},{12,4},{16,8},{20,12},{24,16},{28,20},{1,25},{... | collective-permute-start | bytes 442376 | tf_op jit(solution)/shard_map/ppermute | solution.py:538
  469.8 10.4 %collective-permute-start.44 = (bf16[1,96,768]{2,1,0:T(8,128)(2,1)}, bf16[1,96,768]{2,1,0:T(8,128)(2,1)S(1)}, u32[]{:S(2)}, u32[]{:S(2)}) collective-permute-start(bf16[1,96,768]{2,1,0:T(8,128)(2,1)} %shard_map.289.a0), channel_id=1, source_target_pairs={{0,2},{1,3},{2,0},{3,1},{4,6},{5,7},{6,4},{7,5},{8,10},{9,11},{10,... | collective-permute-start | bytes 442376 | tf_op jit(solution)/shard_map/ppermute | solution.py:538
  471.3 12.3 %collective-permute-start.43 = (bf16[1,96,768]{2,1,0:T(8,128)(2,1)}, bf16[1,96,768]{2,1,0:T(8,128)(2,1)S(1)}, u32[]{:S(2)}, u32[]{:S(2)}) collective-permute-start(bf16[1,96,768]{2,1,0:T(8,128)(2,1)} %shard_map.289.a0), channel_id=1, source_target_pairs={{0,1},{1,0},{2,3},{3,2},{4,5},{5,4},{6,7},{7,6},{8,9},{9,8},{10,11... | collective-permute-start | bytes 442376 | tf_op jit(solution)/shard_map/ppermute | solution.py:538
  480.2 3.4 collective-permute-start.45
  (52 other events, 110.0 us)
Sparse Core Ops, SparseCore 0:
  10.5 39.8 all-gather.12
  53.2 95.4 all-gather.14
  151.7 63.9 all-gather.16
  283.8 106.5 reduce-scatter.3
  392.5 20.4 reduce-scatter.5
  415.8 27.5 reduce-scatter.7
  445.4 24.9 all-gather.18
  472.0 17.1 all-gather.10
